TPU v7x, 128 devices: a whole 4x4x4 slice. The times are simulated.
128 devices in a mesh: seq: 32 (over z, x, core), head: 4 (over y).
Axes of the slice: x: 4, y: 4, z: 4, core: 2. Of those that a mesh axis runs over, the one named last changes fastest.
Arguments:
- queries: bfloat16 [16384, 4096], P('seq', 'head'), may hold values from -6 to 6
- keys: bfloat16 [16384, 4096], P('seq', 'head'), may hold values from -6 to 6
- values: bfloat16 [16384, 4096], P('seq', 'head'), may hold values from -6 to 6
- log_decay: float32 [32, 16384], P('head', 'seq'), may hold values from -3 to 0
- beta: float32 [32, 16384], P('head', 'seq'), may hold values from 0.001 to 0.03
- level_weights: float32 [10, 32, 16384], P(None, 'head', 'seq'), may hold values from 0.25 to 2
- doc_start: int32 [256], P('seq'), may hold values from 0 to 1, as said below
- norm_gain: float32 [4096], P('head'), may hold values from 0.25 to 1.75
- out_weight: bfloat16 [4096, 4096], P('head'), may hold values from -0.09375 to 0.09375
Outputs:
- mixed: bfloat16 [16384, 4096], P(('seq', 'head'))
Inputs may be any that keep to these rules, and one draw needn't show every extreme that they name: doc_start is 0 on the first 128 spans; the second half holds at least one 1.
All inputs are finite; a program needn't handle non-finite values.
Results may differ from a plain program's by a relative error of at most 0.014.
Values may be sent and summed in bfloat16 or wider, within the bound.
No kernel may reach another device: no remote copies, remote signals or barrier semaphores. Data moves between devices by JAX's collectives and lax.ppermute only.
A program may use at most 128 MiB of HBM per device.

v0:
```python
import functools

import jax
import jax.numpy as jnp
from jax import lax
from jax.experimental import pallas as pl
from jax.experimental.pallas import tpu as pltpu
from jax.sharding import PartitionSpec as P

SPAN = 64
SUPER = 128
HEAD_DIM = 128
LOCAL_LEVELS = 4
F32 = jnp.float32
BF16 = jnp.bfloat16


def mm(a, b):
    return jnp.dot(a, b, preferred_element_type=F32)


def mm_t(a, b):
    return lax.dot_general(a, b, (((1,), (1,)), ((), ())), preferred_element_type=F32)


def local_kernel(flags, q_ref, k_ref, v_ref, log_ref, beta_ref, weight_ref,
                 near_ref, far_ref, map_ref, cols_ref, rows_ref):
    head = pl.program_id(0)
    tokens = q_ref.shape[0]
    heads = log_ref.shape[0]
    supers = tokens // SUPER
    spans = tokens // SPAN
    row_i = lax.broadcasted_iota(jnp.int32, (SUPER, SUPER), 0)
    col_i = lax.broadcasted_iota(jnp.int32, (SUPER, SUPER), 1)
    same = (row_i // SPAN) == (col_i // SPAN)
    lower = same & (row_i >= col_i)
    strict = same & (row_i > col_i)
    eye = (row_i == col_i).astype(F32)

    @pl.when(head == 0)
    def _():
        upto = (same & (row_i <= col_i)).astype(F32)
        after = strict.astype(F32)
        both = jnp.concatenate([upto, after], axis=1)
        pieces = [
            jnp.dot(log_ref[:, s * SUPER:(s + 1) * SUPER], both,
                    precision=lax.Precision.HIGHEST, preferred_element_type=F32)
            for s in range(supers)
        ]
        cum = jnp.concatenate([p[:, :SUPER] for p in pieces], axis=1)
        tail = jnp.concatenate([p[:, SUPER:] for p in pieces], axis=1)
        span_i = lax.broadcasted_iota(jnp.int32, (heads, tokens), 1) // SPAN
        keep = jnp.ones((heads, tokens), F32)
        for j in range(spans):
            keep = jnp.where(span_i == j, (1 - flags[j]).astype(F32), keep)
        decay = jnp.exp(cum) * keep
        rows_ref[0] = cum
        rows_ref[1] = jnp.exp(tail)
        rows_ref[2] = decay
        rows_ref[3] = beta_ref[...] * decay
        rows_ref[4] = beta_ref[...]

    def row(i):
        return rows_ref[i, pl.ds(head, 1), :]

    wanted = [row(i) for i in range(5)]
    wanted += [weight_ref[level, pl.ds(head, 1), :] for level in range(9)]
    wanted += [jnp.zeros((2, tokens), F32)]
    cols = jnp.transpose(jnp.concatenate(wanted, axis=0))
    cols_ref[...] = cols

    cum_row = row(0)
    tail_row = row(1)

    readers, outs, maps = [], [], []
    for s in range(supers):
        t0 = s * SUPER
        c = cols[t0:t0 + SUPER, :]
        cum_c, decay_c, bdecay_c, beta_c, w0_c = (c[:, i:i + 1] for i in (0, 2, 3, 4, 5))
        qf = q_ref[t0:t0 + SUPER, :].astype(F32)
        kf = k_ref[t0:t0 + SUPER, :].astype(F32)
        vf = v_ref[t0:t0 + SUPER, :].astype(F32)
        qn = qf * lax.rsqrt(jnp.sum(qf * qf, axis=1, keepdims=True) + 1e-06)
        kn = kf * lax.rsqrt(jnp.sum(kf * kf, axis=1, keepdims=True) + 1e-06)
        qb = qn.astype(BF16)
        kb = kn.astype(BF16)
        k_t = jnp.transpose(kn)
        grams = mm_t(jnp.concatenate([qb, kb], axis=0), kb)
        ratio = jnp.exp(jnp.where(lower, cum_c - cum_row[:, t0:t0 + SUPER], -jnp.inf))
        scores = (ratio * grams[:SUPER]).astype(BF16)
        power = jnp.where(strict, -(beta_c * ratio) * grams[SUPER:], 0.0)
        inverse = eye + power
        pb = power.astype(BF16)
        pb = mm(pb, pb).astype(BF16)
        for step in range(4):
            both = mm(pb, jnp.concatenate([pb, inverse.astype(BF16)], axis=1))
            pb = both[:, :SUPER].astype(BF16)
            inverse = inverse + both[:, SUPER:]
        inverse = inverse + mm(pb, inverse.astype(BF16))
        rhs = jnp.concatenate([beta_c * vf, bdecay_c * kn], axis=1).astype(BF16)
        solved = mm(inverse.astype(BF16), rhs).astype(BF16)
        read = mm(scores, solved)
        outs.append(w0_c * read[:, :HEAD_DIM])
        readers.append((decay_c * qn - read[:, HEAD_DIM:]).astype(BF16))
        tails = (k_t * tail_row[:, t0:t0 + SUPER]).astype(BF16)
        for half in range(SUPER // SPAN):
            a, b = half * SPAN, (half + 1) * SPAN
            summary = mm(tails[:, a:b], solved[a:b, :])
            last = decay_c[b - 1:b, :]
            maps.append((summary[:, :HEAD_DIM], eye * last - summary[:, HEAD_DIM:]))

    outs = [o[a:a + SPAN] for o in outs for a in range(0, SUPER, SPAN)]
    readers = [r[a:a + SPAN] for r in readers for a in range(0, SUPER, SPAN)]
    for level in range(1, LOCAL_LEVELS):
        new_outs, new_readers, new_maps = [], [], []
        for i in range(0, len(maps), 2):
            (s_lo, t_lo), (s_hi, t_hi) = maps[i], maps[i + 1]
            r_hi = readers[i + 1]
            n = r_hi.shape[0]
            t0 = (i + 1) * n
            w_c = cols[t0:t0 + n, 5 + level:6 + level]
            both = mm(jnp.concatenate([r_hi, t_hi.astype(BF16)], axis=0),
                      jnp.concatenate([s_lo.astype(BF16), t_lo.astype(BF16)], axis=1))
            new_outs.append(jnp.concatenate([outs[i], outs[i + 1] + w_c * both[:n, :HEAD_DIM]], axis=0))
            new_readers.append(jnp.concatenate([readers[i], both[:n, HEAD_DIM:].astype(BF16)], axis=0))
            new_maps.append((both[n:, :HEAD_DIM] + s_hi, both[n:, HEAD_DIM:]))
        outs, readers, maps = new_outs, new_readers, new_maps
    near_ref[...] = outs[0]
    far_ref[...] = readers[0]
    map_ref[0] = jnp.concatenate(maps[0], axis=1).astype(BF16)


def local_part(flags, queries, keys, values, log_decay, beta, weights):
    tokens, width = queries.shape
    heads = log_decay.shape[0]
    block = pl.BlockSpec((tokens, HEAD_DIM), lambda h, f: (0, h))
    whole2 = pl.BlockSpec((heads, tokens), lambda h, f: (0, 0))
    whole3 = pl.BlockSpec(weights.shape, lambda h, f: (0, 0, 0))
    return pl.pallas_call(
        local_kernel,
        grid_spec=pltpu.PrefetchScalarGridSpec(
            num_scalar_prefetch=1,
            grid=(heads,),
            in_specs=[block, block, block, whole2, whole2, whole3],
            out_specs=[block, block,
                       pl.BlockSpec((1, HEAD_DIM, 2 * HEAD_DIM), lambda h, f: (h, 0, 0)),
                       pl.BlockSpec((tokens, 16), lambda h, f: (h, 0))],
            scratch_shapes=[pltpu.VMEM((5, heads, tokens), F32)],
        ),
        out_shape=[
            jax.ShapeDtypeStruct((tokens, width), F32),
            jax.ShapeDtypeStruct((tokens, width), BF16),
            jax.ShapeDtypeStruct((heads, HEAD_DIM, 2 * HEAD_DIM), BF16),
            jax.ShapeDtypeStruct((heads * tokens, 16), F32),
        ],
        name="local_part",
    )(flags, queries, keys, values, log_decay, beta, weights)


def pair_kernel(bits, mine_ref, sib_ref, cur_ref):
    core = bits[0]
    half = cur_ref.shape[0]

    def run(first, second):
        for g in range(half):
            h = half * core + g
            later = second[h]
            both = mm(later[:, HEAD_DIM:], first[h])
            cur_ref[g, :, :HEAD_DIM] = (both[:, :HEAD_DIM] + later[:, :HEAD_DIM].astype(F32)).astype(BF16)
            cur_ref[g, :, HEAD_DIM:] = both[:, HEAD_DIM:].astype(BF16)

    @pl.when(core == 1)
    def _():
        run(sib_ref, mine_ref)

    @pl.when(core == 0)
    def _():
        run(mine_ref, sib_ref)


def level_kernel(level, bits, *refs):
    if level == 1:
        sib_ref, cur_ref, new_ref, x_ref, carry_ref = refs
    else:
        sib_ref, cur_ref, carried_ref, new_ref, x_ref, carry_ref = refs
    bit = bits[level]
    half = cur_ref.shape[0]

    def store(g, both, later):
        new_ref[g, :, :HEAD_DIM] = (both[:, :HEAD_DIM] + later[:, :HEAD_DIM].astype(F32)).astype(BF16)
        new_ref[g, :, HEAD_DIM:] = both[:, HEAD_DIM:].astype(BF16)

    @pl.when(bit == 1)
    def _():
        for g in range(half):
            later, sib = cur_ref[g], sib_ref[g]
            if level == 1:
                store(g, mm(later[:, HEAD_DIM:], sib), later)
                x_ref[g] = sib[:, :HEAD_DIM]
                carry_ref[g] = sib[:, HEAD_DIM:]
            else:
                both = mm(jnp.concatenate([later[:, HEAD_DIM:], carried_ref[g]], axis=0), sib)
                store(g, both[:HEAD_DIM], later)
                x_ref[g] = both[HEAD_DIM:, :HEAD_DIM].astype(BF16)
                carry_ref[g] = both[HEAD_DIM:, HEAD_DIM:].astype(BF16)

    @pl.when(bit == 0)
    def _():
        row_i = lax.broadcasted_iota(jnp.int32, (HEAD_DIM, HEAD_DIM), 0)
        col_i = lax.broadcasted_iota(jnp.int32, (HEAD_DIM, HEAD_DIM), 1)
        eye = (row_i == col_i).astype(F32).astype(BF16)
        for g in range(half):
            later = sib_ref[g]
            store(g, mm(later[:, HEAD_DIM:], cur_ref[g]), later)
            x_ref[g] = jnp.zeros((HEAD_DIM, HEAD_DIM), BF16)
            carry_ref[g] = eye if level == 1 else carried_ref[g]


def top_kernel(level, bits, sib_ref, carried_ref, x_ref):
    bit = bits[level]

    @pl.when(bit == 1)
    def _():
        for g in range(x_ref.shape[0]):
            x_ref[g] = mm(carried_ref[g], sib_ref[g]).astype(BF16)

    @pl.when(bit == 0)
    def _():
        x_ref[...] = jnp.zeros(x_ref.shape, BF16)


def small_call(kernel, bits, args, outs, name):
    spec = [pl.BlockSpec(a.shape, lambda i, b, n=a.ndim: (0,) * n) for a in args]
    flops = 2 * 256 * 128 * 256 * args[0].shape[0]
    return pl.pallas_call(
        kernel,
        grid_spec=pltpu.PrefetchScalarGridSpec(
            num_scalar_prefetch=1,
            grid=(1,),
            in_specs=spec,
            out_specs=[pl.BlockSpec(o.shape, lambda i, b, n=len(o.shape): (0,) * n) for o in outs],
        ),
        out_shape=outs,
        cost_estimate=pl.CostEstimate(flops=flops, bytes_accessed=1 << 20, transcendentals=0),
        name=name,
    )(bits, *args)


def final_kernel(bits, near_ref, far_ref, sib_ref, cols_ref, gain_ref, *refs):
    head = pl.program_id(0)
    core = bits[0]
    levels = (len(refs) - 1) // 2
    mine, other, z_ref = refs[:levels], refs[levels:2 * levels], refs[-1]
    half = pl.num_programs(0) // 2
    is_mine = (head // half) == core
    states = jnp.concatenate(
        [jnp.where(is_mine, m[0], o[0]) for m, o in zip(mine, other)], axis=1)
    first = 5 + LOCAL_LEVELS
    rows = 128
    for t0 in range(0, near_ref.shape[0], rows):
        cut = slice(t0, t0 + rows)
        far = far_ref[cut, :]
        both = mm(far, sib_ref[0])
        c = cols_ref[cut, :]
        y = near_ref[cut, :] + jnp.where(core == 1, c[:, first:first + 1], 0.0) * both[:, :HEAD_DIM]
        far = jnp.where(core == 1, both[:, HEAD_DIM:].astype(BF16), far)
        reads = mm(far, states)
        for i in range(levels):
            y = y + c[:, first + 1 + i:first + 2 + i] * reads[:, i * HEAD_DIM:(i + 1) * HEAD_DIM]
        scale = lax.rsqrt(jnp.mean(y * y, axis=1, keepdims=True) + 1e-06)
        z_ref[cut, :] = (y * scale * gain_ref[...]).astype(BF16)


def final_part(bits, near, far, sib, cols, gain, mine, other):
    tokens, width = near.shape
    heads = sib.shape[0]
    half = heads // 2
    block = pl.BlockSpec((tokens, HEAD_DIM), lambda h, b: (0, h))
    state = pl.BlockSpec((1, HEAD_DIM, HEAD_DIM), lambda h, b: (h % half, 0, 0))
    return pl.pallas_call(
        final_kernel,
        grid_spec=pltpu.PrefetchScalarGridSpec(
            num_scalar_prefetch=1,
            grid=(heads,),
            in_specs=[block, block,
                      pl.BlockSpec((1, HEAD_DIM, 2 * HEAD_DIM), lambda h, b: (h, 0, 0)),
                      pl.BlockSpec((tokens, 16), lambda h, b: (h, 0)),
                      pl.BlockSpec((1, HEAD_DIM), lambda h, b: (0, h))]
                     + [state] * (2 * len(mine)),
            out_specs=block,
        ),
        out_shape=jax.ShapeDtypeStruct((tokens, width), BF16),
        name="final_part",
    )(bits, near, far, sib, cols, gain.reshape(1, width), *mine, *other)


def partner(value, bit):
    size = lax.axis_size("seq")
    return lax.ppermute(value, "seq", [(i, i ^ (1 << bit)) for i in range(size)])


def project(z, out_weight):
    size = lax.axis_size("head")
    me = lax.axis_index("head")
    rows = z.shape[0] // size
    cols = out_weight.shape[1] // 2
    up = [(j, (j + 1) % size) for j in range(size)]
    down = [(j, (j - 1) % size) for j in range(size)]

    def term(block, side):
        part = lax.dynamic_slice_in_dim(z, (block % size) * rows, rows, 0)
        w = out_weight[:, side * cols:(side + 1) * cols]
        return jnp.dot(part, w, preferred_element_type=F32).astype(BF16)

    a = term(me + size - 1, 0)
    b = term(me + 1, 1)
    for s in range(size - 1):
        got_a = lax.ppermute(a, "head", up)
        got_b = lax.ppermute(b, "head", down)
        own_a = lax.optimization_barrier(term(me + 2 * size - 2 - s, 0))
        own_b = lax.optimization_barrier(term(me + 2 + s, 1))
        a = (got_a.astype(F32) + own_a.astype(F32)).astype(BF16)
        b = (got_b.astype(F32) + own_b.astype(F32)).astype(BF16)
    return jnp.concatenate([a, b], axis=1)


def body(queries, keys, values, log_decay, beta, level_weights, doc_start, norm_gain, out_weight):
    heads = log_decay.shape[0]
    half = heads // 2
    nbits = lax.axis_size("seq").bit_length() - 1
    index = lax.axis_index("seq")
    bits = jnp.stack([(index >> b) & 1 for b in range(nbits)]).astype(jnp.int32)
    near, far, mine, cols = local_part(doc_start, queries, keys, values, log_decay, beta, level_weights)
    sib0 = partner(mine, 0)
    wide = jax.ShapeDtypeStruct((half, HEAD_DIM, 2 * HEAD_DIM), BF16)
    square = jax.ShapeDtypeStruct((half, HEAD_DIM, HEAD_DIM), BF16)
    cur = small_call(pair_kernel, bits, [mine, sib0], [wide], "pair")[0]
    carried = None
    states, others = [], []
    for level in range(1, nbits):
        if level < nbits - 1:
            sib = partner(cur, level)
            args = [sib, cur] if level == 1 else [sib, cur, carried]
            cur, x, carried = small_call(
                functools.partial(level_kernel, level), bits, args, [wide, square, square], f"level{level}")
        else:
            sib = partner(cur[:, :, :HEAD_DIM], level)
            x = small_call(functools.partial(top_kernel, level), bits, [sib, carried], [square], "top")[0]
        states.append(x)
        others.append(partner(x, 0))
    z = final_part(bits, near, far, sib0, cols, norm_gain, states, others)
    return project(z, out_weight)


def solution(mesh):
    placed = (
        P("seq", "head"),
        P("seq", "head"),
        P("seq", "head"),
        P("head", "seq"),
        P("head", "seq"),
        P(None, "head", "seq"),
        P("seq"),
        P("head"),
        P("head", None),
    )
    return jax.shard_map(
        body, mesh=mesh, in_specs=placed, out_specs=P(("seq", "head"), None), check_vma=False
    )
```

profile of v0, /device:TPU:28, one launch (start us, length us, event | category | flops | bytes accessed | tf_op | source)
XLA Modules:
  0.0 168.4 jit_solution(6943830522038954379)
XLA Ops:
  0.0 48.0 %local_part.1 = (f32[512,1024]{1,0:T(8,128)}, bf16[512,1024]{1,0:T(8,128)(2,1)}, bf16[8,128,256]{2,1,0:T(8,128)(2,1)}, f32[4096,16]{1,0:T(8,128)}) custom-call(s32[8]{0:T(128)} %flags.1, bf16[512,1024]{1,0:T(8,128)(2,1)} %q_ref.1, bf16[512,1024]{1,0:T(8,128)(2,1)} %k_ref.1, bf16[512,1024]{1,0:T(8,128)(2,1)} %v_ref.1, f32[8,512]{1,0:T(8,128)} %log_ref.1, ...), custom_call_target="tpu_custom_call" | custom-call | tf_op jit(solution)/shard_map/local_part/pallas_call | solution.py:139
  48.1 0.6 stack.23.bits
  48.7 1.5 collective-permute-done.sib_ref
  50.2 0.8 copy-done
  51.0 2.8 %pair.1.refs_1_ = bf16[4,128,256]{2,1,0:T(8,128)(2,1)} custom-call(s32[5]{0:T(128)} %stack.23.bits, bf16[8,128,256]{2,1,0:T(8,128)(2,1)} %get-tuple-element.20.mine_ref, bf16[8,128,256]{2,1,0:T(8,128)(2,1)} %copy-done), custom_call_target="tpu_custom_call" | custom-call | flops 134217728 | bytes 1048576 | tf_op jit(solution)/shard_map/pair/pallas_call | solution.py:235
  53.8 1.2 collective-permute-start.1
  55.0 7.4 %collective-permute-done.1.refs_0_ = bf16[4,128,256]{2,1,0:T(8,128)(2,1)S(1)} collective-permute-done((bf16[4,128,256]{2,1,0:T(8,128)(2,1)}, bf16[4,128,256]{2,1,0:T(8,128)(2,1)S(1)}, u32[]{:S(2)}, u32[]{:S(2)}) %collective-permute-start.1) | collective-permute-done | bytes 262176 | tf_op jit(solution)/shard_map/ppermute | solution.py:299
  62.3 0.7 copy-done.2
  63.0 2.7 %level1.1 = (bf16[4,128,256]{2,1,0:T(8,128)(2,1)}, bf16[4,128,128]{2,1,0:T(8,128)(2,1)}, bf16[4,128,128]{2,1,0:T(8,128)(2,1)}) custom-call(s32[5]{0:T(128)} %stack.23.bits, bf16[4,128,256]{2,1,0:T(8,128)(2,1)} %copy-done.2, bf16[4,128,256]{2,1,0:T(8,128)(2,1)} %pair.1.refs_1_), custom_call_target="tpu_custom_call" | custom-call | flops 67108864 | bytes 1048576 | tf_op jit(solution)/shard_map/level1/pallas_call | solution.py:235
  65.8 0.5 collective-permute-start.2
  66.3 8.7 %collective-permute-done.2.refs_0_ = bf16[4,128,256]{2,1,0:T(8,128)(2,1)S(1)} collective-permute-done((bf16[4,128,256]{2,1,0:T(8,128)(2,1)}, bf16[4,128,256]{2,1,0:T(8,128)(2,1)S(1)}, u32[]{:S(2)}, u32[]{:S(2)}) %collective-permute-start.2) | collective-permute-done | bytes 262176 | tf_op jit(solution)/shard_map/ppermute | solution.py:299
  75.0 0.7 copy-done.3
  75.7 2.8 %level2.1 = (bf16[4,128,256]{2,1,0:T(8,128)(2,1)}, bf16[4,128,128]{2,1,0:T(8,128)(2,1)}, bf16[4,128,128]{2,1,0:T(8,128)(2,1)}) custom-call(s32[5]{0:T(128)} %stack.23.bits, bf16[4,128,256]{2,1,0:T(8,128)(2,1)} %copy-done.3, bf16[4,128,256]{2,1,0:T(8,128)(2,1)} %get-tuple-element.23.refs_1_, bf16[4,128,128]{2,1,0:T(8,128)(2,1)} %get-tuple-element.24.refs_2_), custom_call_target="tpu_custom_call" | custom-call | flops 67108864 | bytes 1048576 | tf_op jit(solution)/shard_map/level2/pallas_call | solution.py:235
  78.5 1.9 %collective-permute-start.3 = (bf16[4,128,256]{2,1,0:T(8,128)(2,1)}, bf16[4,128,256]{2,1,0:T(8,128)(2,1)S(1)}, u32[]{:S(2)}, u32[]{:S(2)}) collective-permute-start(bf16[4,128,256]{2,1,0:T(8,128)(2,1)} %get-tuple-element.26.refs_1_), channel_id=1, source_target_pairs={{0,32},{4,36},{8,40},{12,44},{16,48},{20,52},{24,56},{28,60},{32,0... | collective-permute-start | bytes 786440 | tf_op jit(solution)/shard_map/ppermute | solution.py:299
  80.4 5.1 %collective-permute-done.3.refs_0_ = bf16[4,128,256]{2,1,0:T(8,128)(2,1)S(1)} collective-permute-done((bf16[4,128,256]{2,1,0:T(8,128)(2,1)}, bf16[4,128,256]{2,1,0:T(8,128)(2,1)S(1)}, u32[]{:S(2)}, u32[]{:S(2)}) %collective-permute-start.3) | collective-permute-done | bytes 262176 | tf_op jit(solution)/shard_map/ppermute | solution.py:299
  85.5 0.7 copy-done.4
  86.2 2.8 %level3.1 = (bf16[4,128,256]{2,1,0:T(8,128)(2,1)}, bf16[4,128,128]{2,1,0:T(8,128)(2,1)}, bf16[4,128,128]{2,1,0:T(8,128)(2,1)}) custom-call(s32[5]{0:T(128)} %stack.23.bits, bf16[4,128,256]{2,1,0:T(8,128)(2,1)} %copy-done.4, bf16[4,128,256]{2,1,0:T(8,128)(2,1)} %get-tuple-element.26.refs_1_, bf16[4,128,128]{2,1,0:T(8,128)(2,1)} %get-tuple-element.27.refs_2_), custom_call_target="tpu_custom_call" | custom-call | flops 67108864 | bytes 1048576 | tf_op jit(solution)/shard_map/level3/pallas_call | solution.py:235
  89.0 0.9 slice.6
  89.9 3.8 %collective-permute-start.4 = (bf16[4,128,128]{2,1,0:T(8,128)(2,1)S(1)}, bf16[4,128,128]{2,1,0:T(8,128)(2,1)S(1)}, u32[]{:S(2)}, u32[]{:S(2)}) collective-permute-start(bf16[4,128,128]{2,1,0:T(8,128)(2,1)S(1)} %slice.6), channel_id=1, source_target_pairs={{0,64},{4,68},{8,72},{12,76},{16,80},{20,84},{24,88},{28,92},{32,9... | collective-permute-start | bytes 393224 | tf_op jit(solution)/shard_map/ppermute | solution.py:299
  93.7 0.5 collective-permute-start.6
  94.2 2.4 %collective-permute-done.4.sib_ref = bf16[4,128,128]{2,1,0:T(8,128)(2,1)S(1)} collective-permute-done((bf16[4,128,128]{2,1,0:T(8,128)(2,1)S(1)}, bf16[4,128,128]{2,1,0:T(8,128)(2,1)S(1)}, u32[]{:S(2)}, u32[]{:S(2)}) %collective-permute-start.4) | collective-permute-done | bytes 131104 | tf_op jit(solution)/shard_map/ppermute | solution.py:299
  96.7 0.7 copy-done.9
  97.3 2.3 %top.1.refs_3_ = bf16[4,128,128]{2,1,0:T(8,128)(2,1)} custom-call(s32[5]{0:T(128)} %stack.23.bits, bf16[4,128,128]{2,1,0:T(8,128)(2,1)} %copy-done.9, bf16[4,128,128]{2,1,0:T(8,128)(2,1)} %get-tuple-element.30.carried_ref), custom_call_target="tpu_custom_call" | custom-call | flops 67108864 | bytes 1048576 | tf_op jit(solution)/shard_map/top/pallas_call | solution.py:235
  99.7 1.5 collective-permute-done.8.refs_7_
  101.2 0.6 copy-done.8
  101.8 11.4 %final_part.1 = bf16[512,1024]{1,0:T(8,128)(2,1)} custom-call(s32[5]{0:T(128)} %stack.23.bits, f32[512,1024]{1,0:T(8,128)} %get-tuple-element.18.near_ref, bf16[512,1024]{1,0:T(8,128)(2,1)} %get-tuple-element.19.far_ref, bf16[8,128,256]{2,1,0:T(8,128)(2,1)} %copy-done, f32[4096,16]{1,0:T(8,128)} %get-tuple-element.21.cols_ref, f32[1,1024]{1,0:T(1,128)} %bitcast.6, ...), custom_call_target="tpu_custom_call" | custom-call | tf_op jit(solution)/shard_map/final_part/pallas_call | solution.py:280
  113.3 3.1 %fusion.16 = bf16[128,2048]{1,0:T(8,128)(2,1)S(1)} fusion(bf16[1024,4096]{1,0:T(8,128)(2,1)} %param.17, bf16[512,1024]{1,0:T(8,128)(2,1)} %final_part.1, s32[]{:T(128)S(6)} %select_n.52), kind=kOutput, calls=%fused_computation.16 | convolution fusion | flops 537133056 | bytes 4980740 | tf_op jit(solution)/shard_map/dot_general | solution.py:313
  116.4 3.1 %fusion.34 = bf16[128,2048]{1,0:T(8,128)(2,1)S(1)} fusion(bf16[1024,4096]{1,0:T(8,128)(2,1)} %param.17, bf16[512,1024]{1,0:T(8,128)(2,1)S(1)} %copy-done.1, s32[]{:T(128)S(6)} %select_n.52), kind=kOutput, calls=%fused_computation.22 | convolution fusion | flops 537133056 | bytes 4980740 | tf_op jit(solution)/shard_map/dot_general | solution.py:313
  119.5 0.3 collective-permute-start.9
  119.8 2.9 %fusion.19 = bf16[128,2048]{1,0:T(8,128)(2,1)S(1)} fusion(bf16[1024,4096]{1,0:T(8,128)(2,1)} %param.17, bf16[512,1024]{1,0:T(8,128)(2,1)S(1)} %copy-done.1, s32[]{:T(128)S(6)} %select_n.54), kind=kOutput, calls=%fused_computation.17 | convolution fusion | flops 537133056 | bytes 4980740 | tf_op jit(solution)/shard_map/dot_general | solution.py:313
  122.7 0.7 fusion.22
  123.5 0.7 fusion.28
  124.2 2.1 %collective-permute-start.12 = (bf16[128,2048]{1,0:T(8,128)(2,1)S(1)}, bf16[128,2048]{1,0:T(8,128)(2,1)S(1)}, u32[]{:S(2)}, u32[]{:S(2)}) collective-permute-start(bf16[128,2048]{1,0:T(8,128)(2,1)S(1)} %fusion.28), channel_id=1, source_target_pairs={{0,3},{1,0},{2,1},{3,2},{4,7},{5,4},{6,5},{7,6},{8,11},{9,8},{10,9... | collective-permute-start | bytes 1572872 | tf_op jit(solution)/shard_map/ppermute | solution.py:319
  126.3 0.7 fusion.31
  127.0 6.5 %collective-permute-done.9 = bf16[128,2048]{1,0:T(8,128)(2,1)S(1)} collective-permute-done((bf16[128,2048]{1,0:T(8,128)(2,1)S(1)}, bf16[128,2048]{1,0:T(8,128)(2,1)S(1)}, u32[]{:S(2)}, u32[]{:S(2)}) %collective-permute-start.9) | collective-permute-done | bytes 524320 | tf_op jit(solution)/shard_map/ppermute | solution.py:318
  133.6 0.1 add_convert_fusion.5
  133.7 1.6 collective-permute-start.10
  135.2 4.2 %collective-permute-done.12 = bf16[128,2048]{1,0:T(8,128)(2,1)S(1)} collective-permute-done((bf16[128,2048]{1,0:T(8,128)(2,1)S(1)}, bf16[128,2048]{1,0:T(8,128)(2,1)S(1)}, u32[]{:S(2)}, u32[]{:S(2)}) %collective-permute-start.12) | collective-permute-done | bytes 524320 | tf_op jit(solution)/shard_map/ppermute | solution.py:319
  139.5 0.1 add_convert_fusion.2
  139.6 0.6 collective-permute-start.13
  140.2 0.7 fusion.25
  140.9 6.0 %collective-permute-done.10 = bf16[128,2048]{1,0:T(8,128)(2,1)S(1)} collective-permute-done((bf16[128,2048]{1,0:T(8,128)(2,1)S(1)}, bf16[128,2048]{1,0:T(8,128)(2,1)S(1)}, u32[]{:S(2)}, u32[]{:S(2)}) %collective-permute-start.10) | collective-permute-done | bytes 524320 | tf_op jit(solution)/shard_map/ppermute | solution.py:318
  147.0 2.8 %collective-permute-start.11 = (bf16[128,2048]{1,0:T(8,128)(2,1)S(1)}, bf16[128,2048]{1,0:T(8,128)(2,1)S(1)}, u32[]{:S(2)}, u32[]{:S(2)}) collective-permute-start(bf16[128,2048]{1,0:T(8,128)(2,1)S(1)} %add_convert_fusion.4), channel_id=1, source_target_pairs={{0,1},{1,2},{2,3},{3,0},{4,5},{5,6},{6,7},{7,4},{8,9},{9,10},{10,1... | collective-permute-start | bytes 1572872 | tf_op jit(solution)/shard_map/ppermute | solution.py:318
  149.8 3.9 %collective-permute-done.13 = bf16[128,2048]{1,0:T(8,128)(2,1)S(1)} collective-permute-done((bf16[128,2048]{1,0:T(8,128)(2,1)S(1)}, bf16[128,2048]{1,0:T(8,128)(2,1)S(1)}, u32[]{:S(2)}, u32[]{:S(2)}) %collective-permute-start.13) | collective-permute-done | bytes 524320 | tf_op jit(solution)/shard_map/ppermute | solution.py:319
  154.0 0.7 fusion.37
  154.7 5.0 %collective-permute-done.11 = bf16[128,2048]{1,0:T(8,128)(2,1)S(1)} collective-permute-done((bf16[128,2048]{1,0:T(8,128)(2,1)S(1)}, bf16[128,2048]{1,0:T(8,128)(2,1)S(1)}, u32[]{:S(2)}, u32[]{:S(2)}) %collective-permute-start.11) | collective-permute-done | bytes 524320 | tf_op jit(solution)/shard_map/ppermute | solution.py:318
  159.8 7.4 %collective-permute-done.14 = bf16[128,2048]{1,0:T(8,128)(2,1)S(1)} collective-permute-done((bf16[128,2048]{1,0:T(8,128)(2,1)S(1)}, bf16[128,2048]{1,0:T(8,128)(2,1)S(1)}, u32[]{:S(2)}, u32[]{:S(2)}) %collective-permute-start.14) | collective-permute-done | bytes 524320 | tf_op jit(solution)/shard_map/ppermute | solution.py:319
  167.4 1.0 pad_maximum_fusion
  (31 shorter events, 0.7 us)
Async XLA Ops:
  48.0 2.2 %collective-permute-start = (bf16[8,128,256]{2,1,0:T(8,128)(2,1)}, bf16[8,128,256]{2,1,0:T(8,128)(2,1)S(1)}, u32[]{:S(2)}, u32[]{:S(2)}) collective-permute-start(bf16[8,128,256]{2,1,0:T(8,128)(2,1)} %get-tuple-element.20.mine_ref), channel_id=1, source_target_pairs={{0,4},{4,0},{8,12},{12,8},{16,20},{20,16},{24,28},{28,24},{32,36},... | collective-permute-start | bytes 1572872 | tf_op jit(solution)/shard_map/ppermute | solution.py:299
  50.2 0.8 copy-start
  53.8 8.6 %collective-permute-start.1 = (bf16[4,128,256]{2,1,0:T(8,128)(2,1)}, bf16[4,128,256]{2,1,0:T(8,128)(2,1)S(1)}, u32[]{:S(2)}, u32[]{:S(2)}) collective-permute-start(bf16[4,128,256]{2,1,0:T(8,128)(2,1)} %pair.1.refs_1_), channel_id=1, source_target_pairs={{0,8},{4,12},{8,0},{12,4},{16,24},{20,28},{24,16},{28,20},{32,40},... | collective-permute-start | bytes 786440 | tf_op jit(solution)/shard_map/ppermute | solution.py:299
  62.3 0.7 copy-start.2
  65.8 9.2 %collective-permute-start.2 = (bf16[4,128,256]{2,1,0:T(8,128)(2,1)}, bf16[4,128,256]{2,1,0:T(8,128)(2,1)S(1)}, u32[]{:S(2)}, u32[]{:S(2)}) collective-permute-start(bf16[4,128,256]{2,1,0:T(8,128)(2,1)} %get-tuple-element.23.refs_1_), channel_id=1, source_target_pairs={{0,16},{4,20},{8,24},{12,28},{16,0},{20,4},{24,8},{28,12},{32,48},... | collective-permute-start | bytes 786440 | tf_op jit(solution)/shard_map/ppermute | solution.py:299
  75.0 0.7 copy-start.3
  78.5 7.0 %collective-permute-start.3 = (bf16[4,128,256]{2,1,0:T(8,128)(2,1)}, bf16[4,128,256]{2,1,0:T(8,128)(2,1)S(1)}, u32[]{:S(2)}, u32[]{:S(2)}) collective-permute-start(bf16[4,128,256]{2,1,0:T(8,128)(2,1)} %get-tuple-element.26.refs_1_), channel_id=1, source_target_pairs={{0,32},{4,36},{8,40},{12,44},{16,48},{20,52},{24,56},{28,60},{32,0... | collective-permute-start | bytes 786440 | tf_op jit(solution)/shard_map/ppermute | solution.py:299
  85.5 0.7 copy-start.4
  89.9 6.7 %collective-permute-start.4 = (bf16[4,128,128]{2,1,0:T(8,128)(2,1)S(1)}, bf16[4,128,128]{2,1,0:T(8,128)(2,1)S(1)}, u32[]{:S(2)}, u32[]{:S(2)}) collective-permute-start(bf16[4,128,128]{2,1,0:T(8,128)(2,1)S(1)} %slice.6), channel_id=1, source_target_pairs={{0,64},{4,68},{8,72},{12,76},{16,80},{20,84},{24,88},{28,92},{32,9... | collective-permute-start | bytes 393224 | tf_op jit(solution)/shard_map/ppermute | solution.py:299
  93.7 5.9 %collective-permute-start.5 = (bf16[4,128,128]{2,1,0:T(8,128)(2,1)}, bf16[4,128,128]{2,1,0:T(8,128)(2,1)S(1)}, u32[]{:S(2)}, u32[]{:S(2)}) collective-permute-start(bf16[4,128,128]{2,1,0:T(8,128)(2,1)} %get-tuple-element.22.refs_0_), channel_id=1, source_target_pairs={{0,4},{4,0},{8,12},{12,8},{16,20},{20,16},{24,28},{28,24},{32,36},... | collective-permute-start | bytes 393224 | tf_op jit(solution)/shard_map/ppermute | solution.py:299
  93.7 5.9 %collective-permute-start.6 = (bf16[4,128,128]{2,1,0:T(8,128)(2,1)}, bf16[4,128,128]{2,1,0:T(8,128)(2,1)S(1)}, u32[]{:S(2)}, u32[]{:S(2)}) collective-permute-start(bf16[4,128,128]{2,1,0:T(8,128)(2,1)} %get-tuple-element.25.refs_1_), channel_id=1, source_target_pairs={{0,4},{4,0},{8,12},{12,8},{16,20},{20,16},{24,28},{28,24},{32,36},... | collective-permute-start | bytes 393224 | tf_op jit(solution)/shard_map/ppermute | solution.py:299
  94.2 5.4 %collective-permute-start.7 = (bf16[4,128,128]{2,1,0:T(8,128)(2,1)}, bf16[4,128,128]{2,1,0:T(8,128)(2,1)S(1)}, u32[]{:S(2)}, u32[]{:S(2)}) collective-permute-start(bf16[4,128,128]{2,1,0:T(8,128)(2,1)} %get-tuple-element.28.refs_2_), channel_id=1, source_target_pairs={{0,4},{4,0},{8,12},{12,8},{16,20},{20,16},{24,28},{28,24},{32,36},... | collective-permute-start | bytes 393224 | tf_op jit(solution)/shard_map/ppermute | solution.py:299
  96.7 0.7 copy-start.9
  99.6 1.6 collective-permute-start.8
  99.6 1.6 copy-start.5
  99.7 1.5 copy-start.6
  99.7 1.5 copy-start.7
  101.2 0.7 copy-start.8
  113.2 3.2 %copy-start.1 = (bf16[512,1024]{1,0:T(8,128)(2,1)S(1)}, bf16[512,1024]{1,0:T(8,128)(2,1)}, u32[]{:S(2)}) copy-start(bf16[512,1024]{1,0:T(8,128)(2,1)} %final_part.1) | copy-start | bytes 3145732
  113.2 9.5 %slice-start = ((s8[8388608]{0:T(1024)(128)(4,1)}), s8[4194304]{0:T(1024)(128)(4,1)S(1)}, s32[]{:S(2)}) async-start(s8[8388608]{0:T(1024)(128)(4,1)} %bitcast.7), calls=%async_computation | async-start | bytes 8388608
  116.4 6.3 %slice-start.1 = ((s8[8388608]{0:T(1024)(128)(4,1)}), s8[4194304]{0:T(1024)(128)(4,1)S(1)}, s32[]{:S(2)}) async-start(s8[8388608]{0:T(1024)(128)(4,1)} %bitcast.7), calls=%async_computation.1 | async-start | bytes 8388608
  119.5 14.0 %collective-permute-start.9 = (bf16[128,2048]{1,0:T(8,128)(2,1)S(1)}, bf16[128,2048]{1,0:T(8,128)(2,1)S(1)}, u32[]{:S(2)}, u32[]{:S(2)}) collective-permute-start(bf16[128,2048]{1,0:T(8,128)(2,1)S(1)} %fusion.16), channel_id=1, source_target_pairs={{0,1},{1,2},{2,3},{3,0},{4,5},{5,6},{6,7},{7,4},{8,9},{9,10},{10,1... | collective-permute-start | bytes 1572872 | tf_op jit(solution)/shard_map/ppermute | solution.py:318
  124.2 15.2 %collective-permute-start.12 = (bf16[128,2048]{1,0:T(8,128)(2,1)S(1)}, bf16[128,2048]{1,0:T(8,128)(2,1)S(1)}, u32[]{:S(2)}, u32[]{:S(2)}) collective-permute-start(bf16[128,2048]{1,0:T(8,128)(2,1)S(1)} %fusion.28), channel_id=1, source_target_pairs={{0,3},{1,0},{2,1},{3,2},{4,7},{5,4},{6,5},{7,6},{8,11},{9,8},{10,9... | collective-permute-start | bytes 1572872 | tf_op jit(solution)/shard_map/ppermute | solution.py:319
  133.7 13.2 %collective-permute-start.10 = (bf16[128,2048]{1,0:T(8,128)(2,1)S(1)}, bf16[128,2048]{1,0:T(8,128)(2,1)S(1)}, u32[]{:S(2)}, u32[]{:S(2)}) collective-permute-start(bf16[128,2048]{1,0:T(8,128)(2,1)S(1)} %add_convert_fusion.5), channel_id=1, source_target_pairs={{0,1},{1,2},{2,3},{3,0},{4,5},{5,6},{6,7},{7,4},{8,9},{9,10},{10,1... | collective-permute-start | bytes 1572872 | tf_op jit(solution)/shard_map/ppermute | solution.py:318
  139.6 14.2 %collective-permute-start.13 = (bf16[128,2048]{1,0:T(8,128)(2,1)S(1)}, bf16[128,2048]{1,0:T(8,128)(2,1)S(1)}, u32[]{:S(2)}, u32[]{:S(2)}) collective-permute-start(bf16[128,2048]{1,0:T(8,128)(2,1)S(1)} %add_convert_fusion.2), channel_id=1, source_target_pairs={{0,3},{1,0},{2,1},{3,2},{4,7},{5,4},{6,5},{7,6},{8,11},{9,8},{10,9... | collective-permute-start | bytes 1572872 | tf_op jit(solution)/shard_map/ppermute | solution.py:319
  147.0 12.7 %collective-permute-start.11 = (bf16[128,2048]{1,0:T(8,128)(2,1)S(1)}, bf16[128,2048]{1,0:T(8,128)(2,1)S(1)}, u32[]{:S(2)}, u32[]{:S(2)}) collective-permute-start(bf16[128,2048]{1,0:T(8,128)(2,1)S(1)} %add_convert_fusion.4), channel_id=1, source_target_pairs={{0,1},{1,2},{2,3},{3,0},{4,5},{5,6},{6,7},{7,4},{8,9},{9,10},{10,1... | collective-permute-start | bytes 1572872 | tf_op jit(solution)/shard_map/ppermute | solution.py:318
  153.9 13.3 %collective-permute-start.14 = (bf16[128,2048]{1,0:T(8,128)(2,1)S(1)}, bf16[128,2048]{1,0:T(8,128)(2,1)S(1)}, u32[]{:S(2)}, u32[]{:S(2)}) collective-permute-start(bf16[128,2048]{1,0:T(8,128)(2,1)S(1)} %add_convert_fusion.1), channel_id=1, source_target_pairs={{0,3},{1,0},{2,1},{3,2},{4,7},{5,4},{6,5},{7,6},{8,11},{9,8},{10,9... | collective-permute-start | bytes 1572872 | tf_op jit(solution)/shard_map/ppermute | solution.py:319
where the time goes:
time: 169 us; the launch traced here: 168 us
  Pallas kernels  72.8 us (43%)
  waiting for transfers between devices  59.6 us (35%)
  starting transfers between devices  15.4 us (9%)
  matrix products  12.8 us (8%)
  local copies, waits for them, and re-layouts  5.81 us (3%)
  other arithmetic  1.8 us (1%)
    pallas_call x1, Pallas kernels, local_part(): pl.pallas_call(local_kernel, grid_spec=pltpu.PrefetchScalarGridSpec(num_s...  48 us
    ppermute x9, waiting for transfers between devices, partner(): return lax.ppermute(value, 'seq', [(i, i ^ 1 << bit) for i in range(size)])  26.6 us
    ppermute x3, waiting for transfers between devices, project(): got_a = lax.ppermute(a, 'head', up)  17.5 us
    ppermute x3, waiting for transfers between devices, project(): got_b = lax.ppermute(b, 'head', down)  15.6 us
    pallas_call x5, Pallas kernels, small_call(): pl.pallas_call(kernel, grid_spec=pltpu.PrefetchScalarGridSpec(num_scalar_...  13.4 us
    dot_general x8, matrix products, term(): return jnp.dot(part, w, preferred_element_type=F32).astype(BF16)  12.8 us
    pallas_call x1, Pallas kernels, final_part(): pl.pallas_call(final_kernel, grid_spec=pltpu.PrefetchScalarGridSpec(num_s...  11.4 us
    ppermute x9, starting transfers between devices, partner(): return lax.ppermute(value, 'seq', [(i, i ^ 1 << bit) for i in range(size)])  8 us
  transfers between devices with their start and end apart: 15, of which 12 were waited for; matrix products, arithmetic and copies ran while one was open for 5% of the time, Pallas kernels for 1%

commit v1 on v0

v1 whole, which is shorter than its diff:
```python
import functools
import jax
import jax.numpy as jnp
from jax import lax
from jax.experimental import pallas as pl
from jax.experimental.pallas import tpu as pltpu
from jax.sharding import PartitionSpec as P

SPAN = 64
SUPER = 128
HEAD_DIM = 128
LOCAL_LEVELS = 4
TOGETHER = 2
CHUNKS = 2
PIECES = 2
EPS = 1e-06
F32 = jnp.float32
BF16 = jnp.bfloat16


def mm(a, b):
    return jnp.dot(a, b, preferred_element_type=F32)


def local_kernel(chunk, flags, q_ref, k_ref, v_ref, log_ref, beta_ref, weight_ref,
                 near_ref, far_ref, map_ref, cols_ref, rows_ref):
    step = pl.program_id(0)
    tokens = q_ref.shape[0]
    heads = log_ref.shape[0]
    supers = tokens // SUPER
    spans = tokens // SPAN
    row_i = lax.broadcasted_iota(jnp.int32, (SUPER, SUPER), 0)
    col_i = lax.broadcasted_iota(jnp.int32, (SUPER, SUPER), 1)
    same = (row_i >> 6) == (col_i >> 6)
    lower = same & (row_i >= col_i)
    strict = same & (row_i > col_i)
    eye = (row_i == col_i).astype(F32)

    @pl.when(step == 0)
    def _():
        upto = (same & (row_i <= col_i)).astype(F32)
        both = jnp.concatenate([upto, strict.astype(F32)], axis=1)
        pieces = [
            jnp.dot(log_ref[:, s * SUPER:(s + 1) * SUPER], both,
                    precision=lax.Precision.HIGHEST, preferred_element_type=F32)
            for s in range(supers)
        ]
        cum = jnp.concatenate([p[:, :SUPER] for p in pieces], axis=1)
        tail = jnp.concatenate([p[:, SUPER:] for p in pieces], axis=1)
        span_i = lax.broadcasted_iota(jnp.int32, (heads, tokens), 1) >> 6
        keep = jnp.ones((heads, tokens), F32)
        for j in range(spans):
            keep = jnp.where(span_i == j, (1 - flags[j]).astype(F32), keep)
        rows_ref[0] = cum
        rows_ref[1] = jnp.exp(tail)
        rows_ref[2] = jnp.exp(cum) * keep

    units = [(g, s) for g in range(TOGETHER) for s in range(supers)]
    cols, cum_rows, tail_rows, beta_rows = [], [], [], []
    for g in range(TOGETHER):
        head = TOGETHER * (CHUNKS * step + chunk) + g
        take = pl.ds(head, 1)
        beta_row = beta_ref[take, :]
        wanted = [rows_ref[0, take, :], rows_ref[2, take, :], beta_row]
        wanted += [weight_ref[level, take, :] for level in range(9)]
        wanted += [jnp.zeros((4, tokens), F32)]
        c = jnp.transpose(jnp.concatenate(wanted, axis=0))
        cols_ref[g * tokens:(g + 1) * tokens, :] = c
        cols.append(c)
        cum_rows.append(rows_ref[0, take, :])
        tail_rows.append(rows_ref[1, take, :])
        beta_rows.append(beta_row)

    def cut(s):
        return slice(s * SUPER, (s + 1) * SUPER)

    def lanes(g):
        return slice(g * HEAD_DIM, (g + 1) * HEAD_DIM)

    def col(g, s, i):
        return cols[g][cut(s), i:i + 1]

    scores, powers, inverses, right, tails, queries = [], [], [], [], [], []
    for g, s in units:
        q = q_ref[cut(s), lanes(g)]
        k = k_ref[cut(s), lanes(g)]
        k_t = jnp.transpose(k)
        grams = mm(jnp.concatenate([q, k], axis=0), k_t)
        qf, kf, ktf = q.astype(F32), k.astype(F32), k_t.astype(F32)
        rq = lax.rsqrt(jnp.sum(qf * qf, axis=1, keepdims=True) + EPS)
        rk = lax.rsqrt(jnp.sum(kf * kf, axis=1, keepdims=True) + EPS)
        rk_row = lax.rsqrt(jnp.sum(ktf * ktf, axis=0, keepdims=True) + EPS)
        spread = col(g, s, 0) - cum_rows[g][:, cut(s)]
        ratio = jnp.exp(jnp.where(lower, spread, -1e30)) * rk_row
        scores.append((ratio * (rq * grams[:SUPER])).astype(BF16))
        power = jnp.where(strict, (-col(g, s, 2) * rk) * ratio * grams[SUPER:], 0.0)
        inverses.append(eye + power)
        powers.append(power.astype(BF16))
        decay = col(g, s, 1)
        right.append(jnp.concatenate([v_ref[cut(s), lanes(g)], (decay * rk * kf).astype(BF16)], axis=1))
        tails.append((ktf * (rk_row * tail_rows[g][:, cut(s)])).astype(BF16))
        queries.append(decay * rq * qf)

    n = len(units)
    powers = [mm(p, p).astype(BF16) for p in powers]
    for _ in range(4):
        both = [mm(powers[u], jnp.concatenate([powers[u], inverses[u].astype(BF16)], axis=1)) for u in range(n)]
        powers = [b[:, :SUPER].astype(BF16) for b in both]
        inverses = [inverses[u] + both[u][:, SUPER:] for u in range(n)]
    inverses = [inverses[u] + mm(powers[u], inverses[u].astype(BF16)) for u in range(n)]
    solved = []
    for u, (g, s) in enumerate(units):
        scaled = (inverses[u] * beta_rows[g][:, cut(s)]).astype(BF16)
        solved.append(mm(scaled, right[u]).astype(BF16))
    leaves = [[] for _ in range(TOGETHER)]
    for u, (g, s) in enumerate(units):
        for half in range(SUPER // SPAN):
            a, b = half * SPAN, (half + 1) * SPAN
            summary = mm(tails[u][:, a:b], solved[u][a:b, :])
            t = s * SUPER + b - 1
            last = jnp.broadcast_to(cols[g][t:t + 1, 1:2], (1, HEAD_DIM))
            leaves[g].append((summary[:, :HEAD_DIM], summary[:, HEAD_DIM:], last))
    outs = [[] for _ in range(TOGETHER)]
    readers = [[] for _ in range(TOGETHER)]
    for u, (g, s) in enumerate(units):
        read = mm(scores[u], solved[u])
        out = col(g, s, 3) * read[:, :HEAD_DIM]
        reader = queries[u] - read[:, HEAD_DIM:]
        for half in range(SUPER // SPAN):
            a, b = half * SPAN, (half + 1) * SPAN
            outs[g].append(out[a:b])
            readers[g].append(reader[a:b])

    for level in range(1, LOCAL_LEVELS):
        for g in range(TOGETHER):
            maps = leaves[g]
            new_outs, new_readers, new_maps = [], [], []
            for i in range(0, len(maps), 2):
                (s_lo, e_lo, d_lo), (s_hi, e_hi, d_hi) = maps[i], maps[i + 1]
                r_hi = readers[g][i + 1]
                m = r_hi.shape[0]
                t0 = (i + 1) * m
                w_c = cols[g][t0:t0 + m, 3 + level:4 + level]
                both = mm(jnp.concatenate([r_hi.astype(BF16), e_hi.astype(BF16)], axis=0),
                          jnp.concatenate([s_lo.astype(BF16), e_lo.astype(BF16)], axis=1))
                new_outs.append(jnp.concatenate(
                    [outs[g][i], outs[g][i + 1] + w_c * both[:m, :HEAD_DIM]], axis=0))
                new_readers.append(jnp.concatenate(
                    [readers[g][i], d_lo * r_hi - both[:m, HEAD_DIM:]], axis=0))
                new_maps.append((d_hi * s_lo + s_hi - both[m:, :HEAD_DIM],
                                 d_hi * e_lo + d_lo * e_hi - both[m:, HEAD_DIM:],
                                 d_lo * d_hi))
            outs[g], readers[g], leaves[g] = new_outs, new_readers, new_maps
    for g in range(TOGETHER):
        total, erase, decay = leaves[g][0]
        near_ref[:, lanes(g)] = outs[g][0]
        far_ref[:, lanes(g)] = readers[g][0].astype(BF16)
        map_ref[g] = jnp.concatenate([total, eye * decay - erase], axis=1).astype(BF16)


def local_part(chunk, flags, queries, keys, values, log_decay, beta, weights):
    tokens, width = queries.shape
    heads = log_decay.shape[0]
    steps = heads // (TOGETHER * CHUNKS)
    wide = TOGETHER * HEAD_DIM
    block = pl.BlockSpec((tokens, wide), lambda h, f: (0, CHUNKS * h + chunk))
    out = pl.BlockSpec((tokens, wide), lambda h, f: (0, h))
    whole2 = pl.BlockSpec((heads, tokens), lambda h, f: (0, 0))
    whole3 = pl.BlockSpec(weights.shape, lambda h, f: (0, 0, 0))
    part = steps * TOGETHER
    return pl.pallas_call(
        functools.partial(local_kernel, chunk),
        grid_spec=pltpu.PrefetchScalarGridSpec(
            num_scalar_prefetch=1,
            grid=(steps,),
            in_specs=[block, block, block, whole2, whole2, whole3],
            out_specs=[out, out,
                       pl.BlockSpec((TOGETHER, HEAD_DIM, 2 * HEAD_DIM), lambda h, f: (h, 0, 0)),
                       pl.BlockSpec((TOGETHER * tokens, 16), lambda h, f: (h, 0))],
            scratch_shapes=[pltpu.VMEM((3, heads, tokens), F32)],
        ),
        out_shape=[
            jax.ShapeDtypeStruct((tokens, part * HEAD_DIM), F32),
            jax.ShapeDtypeStruct((tokens, part * HEAD_DIM), BF16),
            jax.ShapeDtypeStruct((part, HEAD_DIM, 2 * HEAD_DIM), BF16),
            jax.ShapeDtypeStruct((part * tokens, 16), F32),
        ],
        compiler_params=pltpu.CompilerParams(vmem_limit_bytes=24 << 20),
        cost_estimate=pl.CostEstimate(flops=part * 1500000000, bytes_accessed=8 << 20, transcendentals=0),
        name=f"local{chunk}",
    )(flags, queries, keys, values, log_decay, beta, weights)


def pair_kernel(bits, mine_ref, sib_ref, cur_ref):
    core = bits[0]
    half = cur_ref.shape[0]

    def run(first, second):
        for g in range(half):
            later = second[half * core + g]
            both = mm(later[:, HEAD_DIM:], first[half * core + g])
            cur_ref[g, :, :HEAD_DIM] = (both[:, :HEAD_DIM] + later[:, :HEAD_DIM].astype(F32)).astype(BF16)
            cur_ref[g, :, HEAD_DIM:] = both[:, HEAD_DIM:].astype(BF16)

    @pl.when(core == 1)
    def _():
        run(sib_ref, mine_ref)

    @pl.when(core == 0)
    def _():
        run(mine_ref, sib_ref)


def level_kernel(level, bits, *refs):
    if level == 1:
        sib_ref, cur_ref, new_ref, x_ref, carry_ref = refs
    else:
        sib_ref, cur_ref, carried_ref, new_ref, x_ref, carry_ref = refs
    bit = bits[level]
    half = cur_ref.shape[0]

    def store(g, both, later):
        new_ref[g, :, :HEAD_DIM] = (both[:, :HEAD_DIM] + later[:, :HEAD_DIM].astype(F32)).astype(BF16)
        new_ref[g, :, HEAD_DIM:] = both[:, HEAD_DIM:].astype(BF16)

    @pl.when(bit == 1)
    def _():
        for g in range(half):
            later, sib = cur_ref[g], sib_ref[g]
            if level == 1:
                store(g, mm(later[:, HEAD_DIM:], sib), later)
                x_ref[g] = sib[:, :HEAD_DIM]
                carry_ref[g] = sib[:, HEAD_DIM:]
            else:
                both = mm(jnp.concatenate([later[:, HEAD_DIM:], carried_ref[g]], axis=0), sib)
                store(g, both[:HEAD_DIM], later)
                x_ref[g] = both[HEAD_DIM:, :HEAD_DIM].astype(BF16)
                carry_ref[g] = both[HEAD_DIM:, HEAD_DIM:].astype(BF16)

    @pl.when(bit == 0)
    def _():
        row_i = lax.broadcasted_iota(jnp.int32, (HEAD_DIM, HEAD_DIM), 0)
        col_i = lax.broadcasted_iota(jnp.int32, (HEAD_DIM, HEAD_DIM), 1)
        eye = (row_i == col_i).astype(F32).astype(BF16)
        for g in range(half):
            later = sib_ref[g]
            store(g, mm(later[:, HEAD_DIM:], cur_ref[g]), later)
            x_ref[g] = jnp.zeros((HEAD_DIM, HEAD_DIM), BF16)
            carry_ref[g] = eye if level == 1 else carried_ref[g]


def top_kernel(level, bits, sib_ref, carried_ref, x_ref):
    bit = bits[level]

    @pl.when(bit == 1)
    def _():
        for g in range(x_ref.shape[0]):
            x_ref[g] = mm(carried_ref[g], sib_ref[g]).astype(BF16)

    @pl.when(bit == 0)
    def _():
        x_ref[...] = jnp.zeros(x_ref.shape, BF16)


def small_call(kernel, bits, args, outs, name):
    return pl.pallas_call(
        kernel,
        grid_spec=pltpu.PrefetchScalarGridSpec(
            num_scalar_prefetch=1,
            grid=(1,),
            in_specs=[pl.BlockSpec(a.shape, lambda i, b, n=a.ndim: (0,) * n) for a in args],
            out_specs=[pl.BlockSpec(o.shape, lambda i, b, n=len(o.shape): (0,) * n) for o in outs],
        ),
        out_shape=outs,
        compiler_params=pltpu.CompilerParams(vmem_limit_bytes=6 << 20),
        cost_estimate=pl.CostEstimate(flops=600000000, bytes_accessed=1 << 20, transcendentals=0),
        name=name,
    )(bits, *args)


def final_kernel(levels, bits, near_ref, far_ref, sib_ref, cols_ref, gain_ref, *refs):
    core = bits[0]
    mine, other, z_ref = refs[:levels], refs[levels:2 * levels], refs[-1]
    tokens = near_ref.shape[0]
    is_mine = pl.program_id(0) == core
    first = 3 + LOCAL_LEVELS
    upper = core == 1
    units = [(g, t) for g in range(TOGETHER) for t in range(0, tokens, SUPER)]
    states = [jnp.concatenate([jnp.where(is_mine, m[g], o[g]) for m, o in zip(mine, other)], axis=1)
              for g in range(TOGETHER)]

    def lanes(g):
        return slice(g * HEAD_DIM, (g + 1) * HEAD_DIM)

    def cols(g, t, i):
        return cols_ref[g * tokens + t:g * tokens + t + SUPER, i:i + 1]

    fars = [far_ref[t:t + SUPER, lanes(g)] for g, t in units]
    both = [mm(fars[u], sib_ref[g]) for u, (g, t) in enumerate(units)]
    ys = [near_ref[t:t + SUPER, lanes(g)]
          + jnp.where(upper, cols(g, t, first), 0.0) * both[u][:, :HEAD_DIM] for u, (g, t) in enumerate(units)]
    fars = [jnp.where(upper, both[u][:, HEAD_DIM:].astype(BF16), fars[u]) for u in range(len(units))]
    for u, (g, t) in enumerate(units):
        reads = mm(fars[u], states[g])
        y = ys[u]
        for i in range(levels):
            y = y + cols(g, t, first + 1 + i) * reads[:, i * HEAD_DIM:(i + 1) * HEAD_DIM]
        scale = lax.rsqrt(jnp.mean(y * y, axis=1, keepdims=True) + EPS)
        z_ref[t:t + SUPER, lanes(g)] = (y * scale * gain_ref[:, lanes(g)]).astype(BF16)


def final_part(chunk, bits, near, far, sib, cols, gain, mine, other, before):
    tokens, width = near.shape
    wide = TOGETHER * HEAD_DIM
    steps = width // wide
    levels = len(mine)
    block = pl.BlockSpec((tokens, wide), lambda h, b: (0, h))
    placed = lambda h, b: (0, CHUNKS * h + chunk)
    state = pl.BlockSpec((TOGETHER, HEAD_DIM, HEAD_DIM), lambda h, b: (0, 0, 0))
    in_specs = [block, block,
                pl.BlockSpec((TOGETHER, HEAD_DIM, 2 * HEAD_DIM), lambda h, b: (h, 0, 0)),
                pl.BlockSpec((TOGETHER * tokens, 16), lambda h, b: (h, 0)),
                pl.BlockSpec((1, wide), placed)] + [state] * (2 * levels)
    args = [bits, near, far, sib, cols, gain, *mine, *other]
    aliases = {}
    if before is not None:
        aliases = {len(args): 0}
        args.append(before)
        in_specs.append(pl.BlockSpec(memory_space=pl.ANY))
    return pl.pallas_call(
        functools.partial(final_kernel, levels),
        grid_spec=pltpu.PrefetchScalarGridSpec(
            num_scalar_prefetch=1,
            grid=(steps,),
            in_specs=in_specs,
            out_specs=pl.BlockSpec((tokens, wide), placed),
        ),
        out_shape=jax.ShapeDtypeStruct((tokens, CHUNKS * width), BF16),
        input_output_aliases=aliases,
        compiler_params=pltpu.CompilerParams(vmem_limit_bytes=20 << 20),
        cost_estimate=pl.CostEstimate(flops=3000000000, bytes_accessed=8 << 20, transcendentals=0),
        name=f"final{chunk}",
    )(*args)


def partner(value, bit):
    size = lax.axis_size("seq")
    return lax.ppermute(value, "seq", [(i, i ^ (1 << bit)) for i in range(size)])


def project(z, out_weight):
    size = lax.axis_size("head")
    me = lax.axis_index("head")
    rows = z.shape[0] // size
    cols = out_weight.shape[1] // (2 * PIECES)
    up = [(j, (j + 1) % size) for j in range(size)]
    down = [(j, (j - 1) % size) for j in range(size)]

    def term(block, piece):
        part = lax.dynamic_slice_in_dim(z, (block % size) * rows, rows, 0)
        w = out_weight[:, piece * cols:(piece + 1) * cols]
        return jnp.dot(part, w, preferred_element_type=F32).astype(BF16)

    order = [p for i in range(PIECES) for p in (i, PIECES + i)]
    sums = {p: term(me + size - 1 if p < PIECES else me + 1, p) for p in order}
    for s in range(size - 1):
        got = {p: lax.ppermute(sums[p], "head", up if p < PIECES else down) for p in order}
        own = {p: lax.optimization_barrier(
            term(me + 2 * size - 2 - s if p < PIECES else me + 2 + s, p)) for p in order}
        sums = {p: (got[p].astype(F32) + own[p].astype(F32)).astype(BF16) for p in order}
    return jnp.concatenate([sums[p] for p in range(2 * PIECES)], axis=1)


def body(queries, keys, values, log_decay, beta, level_weights, doc_start, norm_gain, out_weight):
    heads = log_decay.shape[0]
    mine_heads = heads // (2 * CHUNKS)
    nbits = lax.axis_size("seq").bit_length() - 1
    index = lax.axis_index("seq")
    bits = jnp.stack([(index >> b) & 1 for b in range(nbits)]).astype(jnp.int32)
    gain = norm_gain.reshape(1, -1)
    wide = jax.ShapeDtypeStruct((mine_heads, HEAD_DIM, 2 * HEAD_DIM), BF16)
    square = jax.ShapeDtypeStruct((mine_heads, HEAD_DIM, HEAD_DIM), BF16)
    local, sibs, curs = [], [], []
    for chunk in range(CHUNKS):
        local.append(local_part(chunk, doc_start, queries, keys, values, log_decay, beta, level_weights))
        mine = local[chunk][2]
        sibs.append(partner(mine, 0))
        curs.append(small_call(pair_kernel, bits, [mine, sibs[chunk]], [wide], f"pair{chunk}")[0])
    carried = [None] * CHUNKS
    states = [[] for _ in range(CHUNKS)]
    others = [[] for _ in range(CHUNKS)]
    for level in range(1, nbits):
        for c in range(CHUNKS):
            if level < nbits - 1:
                sib = partner(curs[c], level)
                args = [sib, curs[c]] if level == 1 else [sib, curs[c], carried[c]]
                curs[c], x, carried[c] = small_call(
                    functools.partial(level_kernel, level), bits, args, [wide, square, square],
                    f"level{level}{c}")
            else:
                sib = partner(curs[c][:, :, :HEAD_DIM], level)
                x = small_call(functools.partial(top_kernel, level), bits, [sib, carried[c]], [square],
                               f"top{c}")[0]
            states[c].append(x)
            others[c].append(partner(x, 0))
    z = None
    for c in range(CHUNKS):
        near, far, _, cols = local[c]
        z = final_part(c, bits, near, far, sibs[c], cols, gain, states[c], others[c], z)
    return project(z, out_weight)


def solution(mesh):
    placed = (
        P("seq", "head"),
        P("seq", "head"),
        P("seq", "head"),
        P("head", "seq"),
        P("head", "seq"),
        P(None, "head", "seq"),
        P("seq"),
        P("head"),
        P("head", None),
    )
    return jax.shard_map(
        body, mesh=mesh, in_specs=placed, out_specs=P(("seq", "head"), None), check_vma=False
    )
```

time: 169 us -> 119 us (0.70)
  Pallas kernels: 72.8 us -> 30.6 us
  waiting for transfers between devices: 59.6 us -> 41.1 us
  starting transfers between devices: 15.4 us -> 28 us
  matrix products: 12.8 us -> 7.15 us
  local copies, waits for them, and re-layouts: 5.81 us -> 9.42 us
    pallas_call x2 -> x4, Pallas kernels: 59.4 us -> 23.5 us  [the longest x2 14.8 us: local_part(): pl.pallas_call(functools.partial(local_kernel, chunk), grid_spec=pltpu.Pr...]
    ppermute x9 -> x18, waiting for transfers between devices: 26.6 us -> 13.8 us  [partner(): return lax.ppermute(value, 'seq', [(i, i ^ 1 << bit) for i in range(size)])]
    ppermute x9 -> x18, starting transfers between devices: 8 us -> 15.4 us  [partner(): return lax.ppermute(value, 'seq', [(i, i ^ 1 << bit) for i in range(size)])]
    pallas_call x5 -> x10, Pallas kernels: 13.4 us -> 7.14 us  [small_call(): pl.pallas_call(kernel, grid_spec=pltpu.PrefetchScalarGridSpec(num_scalar_...]
    ppermute x6 -> x12, waiting for transfers between devices: 33 us -> 27.3 us  [project(): lax.ppermute(sums[p], 'head', up if p < PIECES else down)]
    dot_general x8 -> x16, matrix products: 12.8 us -> 7.15 us  [term(): return jnp.dot(part, w, preferred_element_type=F32).astype(BF16)]
    ppermute x6 -> x12, starting transfers between devices: 7.41 us -> 12.6 us  [project(): lax.ppermute(sums[p], 'head', up if p < PIECES else down)]
    unnamed x24 -> x36, local copies, waits for them, and re-layouts: 4.29 us -> 9.32 us
  transfers between devices with their start and end apart: 15 -> 30, of which waited for: 12 -> 15; matrix products, arithmetic and copies ran while one was open for 5% -> 1% of each run, Pallas kernels for 1% -> 16%
where the time goes in v1:
time: 119 us
  waiting for transfers between devices  41.1 us (35%)
  Pallas kernels  30.6 us (26%)
  starting transfers between devices  28 us (24%)
  local copies, waits for them, and re-layouts  9.42 us (8%)
  matrix products  7.15 us (6%)
  other arithmetic  1.84 us (2%)
    ppermute x12, waiting for transfers between devices, project(): lax.ppermute(sums[p], 'head', up if p < PIECES else down)  27.3 us
    ppermute x18, starting transfers between devices, partner(): return lax.ppermute(value, 'seq', [(i, i ^ 1 << bit) for i in range(size)])  15.4 us
    pallas_call x2, Pallas kernels, local_part(): pl.pallas_call(functools.partial(local_kernel, chunk), grid_spec=pltpu.Pr...  14.8 us
    ppermute x18, waiting for transfers between devices, partner(): return lax.ppermute(value, 'seq', [(i, i ^ 1 << bit) for i in range(size)])  13.8 us
    ppermute x12, starting transfers between devices, project(): lax.ppermute(sums[p], 'head', up if p < PIECES else down)  12.6 us
    unnamed x36, local copies, waits for them, and re-layouts  9.32 us
    pallas_call x2, Pallas kernels, final_part(): pl.pallas_call(functools.partial(final_kernel, levels), grid_spec=pltpu.P...  8.74 us
    dot_general x16, matrix products, term(): return jnp.dot(part, w, preferred_element_type=F32).astype(BF16)  7.15 us
  transfers between devices with their start and end apart: 30, of which 15 were waited for; matrix products, arithmetic and copies ran while one was open for 1% of the time, Pallas kernels for 16%

profile of v1, /device:TPU:28, one launch (start us, length us, event | category | flops | bytes accessed | tf_op | source)
XLA Modules:
  0.0 118.7 jit_solution(8449622889299933817)
XLA Ops:
  0.0 1.2 %copy-done = bf16[512,1024]{1,0:T(8,128)(2,1)S(1)} copy-done((bf16[512,1024]{1,0:T(8,128)(2,1)S(1)}, bf16[512,1024]{1,0:T(8,128)(2,1)}, u32[]{:S(2)}) %copy-start) | copy-done | bytes 1048600
  1.2 1.2 %copy-done.1 = bf16[512,1024]{1,0:T(8,128)(2,1)S(1)} copy-done((bf16[512,1024]{1,0:T(8,128)(2,1)S(1)}, bf16[512,1024]{1,0:T(8,128)(2,1)}, u32[]{:S(2)}) %copy-start.1) | copy-done | bytes 1048600
  2.5 1.2 %copy-done.2 = bf16[512,1024]{1,0:T(8,128)(2,1)S(1)} copy-done((bf16[512,1024]{1,0:T(8,128)(2,1)S(1)}, bf16[512,1024]{1,0:T(8,128)(2,1)}, u32[]{:S(2)}) %copy-start.2) | copy-done | bytes 1048600
  3.7 0.9 copy-done.3
  4.6 0.7 copy-done.4
  5.3 0.7 copy-done.5
  6.7 7.4 %local0.1 = (f32[512,512]{1,0:T(8,128)S(1)}, bf16[512,512]{1,0:T(8,128)(2,1)S(1)}, bf16[4,128,256]{2,1,0:T(8,128)(2,1)S(1)}, f32[2048,16]{1,0:T(8,128)S(1)}) custom-call(s32[8]{0:T(128)S(1)} %copy-done.7, bf16[512,1024]{1,0:T(8,128)(2,1)S(1)} %copy-done, bf16[512,1024]{1,0:T(8,128)(2,1)S(1)} %copy-done.1, bf16[512,1024]{1,0:T(8,128)(2,1)S(1)} %copy-done.2, ...), custom_call_target="tpu_custom_call" | custom-call | flops 6000000000 | bytes 8388608 | tf_op jit(solution)/shard_map/local0/pallas_call | solution.py:171
  14.1 0.8 copy-done.14
  14.9 7.4 %local1.1 = (f32[512,512]{1,0:T(8,128)S(1)}, bf16[512,512]{1,0:T(8,128)(2,1)S(1)}, bf16[4,128,256]{2,1,0:T(8,128)(2,1)S(1)}, f32[2048,16]{1,0:T(8,128)S(1)}) custom-call(s32[8]{0:T(128)S(1)} %copy-done.7, bf16[512,1024]{1,0:T(8,128)(2,1)S(1)} %copy-done, bf16[512,1024]{1,0:T(8,128)(2,1)S(1)} %copy-done.1, bf16[512,1024]{1,0:T(8,128)(2,1)S(1)} %copy-done.2, ...), custom_call_target="tpu_custom_call" | custom-call | flops 6000000000 | bytes 8388608 | tf_op jit(solution)/shard_map/local1/pallas_call | solution.py:171
  22.3 0.8 copy-done.12
  23.7 0.7 pair0.1.refs_1_
  24.4 1.3 %collective-permute-start.10 = (bf16[2,128,256]{2,1,0:T(8,128)(2,1)S(1)}, bf16[2,128,256]{2,1,0:T(8,128)(2,1)S(1)}, u32[]{:S(2)}, u32[]{:S(2)}) collective-permute-start(bf16[2,128,256]{2,1,0:T(8,128)(2,1)S(1)} %pair0.1.refs_1_), channel_id=1, source_target_pairs={{0,8},{4,12},{8,0},{12,4},{16,24},{20,28},{24,16},{28,20},{32,40},... | collective-permute-start | bytes 393224 | tf_op jit(solution)/shard_map/ppermute | solution.py:348
  25.7 0.7 pair1.1.refs_1_
  26.4 0.9 collective-permute-start.1
  27.3 3.5 %collective-permute-done.10.refs_0_ = bf16[2,128,256]{2,1,0:T(8,128)(2,1)S(1)} collective-permute-done((bf16[2,128,256]{2,1,0:T(8,128)(2,1)S(1)}, bf16[2,128,256]{2,1,0:T(8,128)(2,1)S(1)}, u32[]{:S(2)}, u32[]{:S(2)}) %collective-permute-start.10) | collective-permute-done | bytes 131104 | tf_op jit(solution)/shard_map/ppermute | solution.py:348
  30.9 0.7 level10.1
  32.7 0.7 level11.1
  33.4 2.6 %collective-permute-start.2 = (bf16[2,128,256]{2,1,0:T(8,128)(2,1)S(1)}, bf16[2,128,256]{2,1,0:T(8,128)(2,1)S(1)}, u32[]{:S(2)}, u32[]{:S(2)}) collective-permute-start(bf16[2,128,256]{2,1,0:T(8,128)(2,1)S(1)} %get-tuple-element.36.refs_1_), channel_id=1, source_target_pairs={{0,16},{4,20},{8,24},{12,28},{16,0},{20,4},{24,8},{28,12},{32,48},... | collective-permute-start | bytes 393224 | tf_op jit(solution)/shard_map/ppermute | solution.py:348
  36.0 3.5 %collective-permute-done.11.refs_0_ = bf16[2,128,256]{2,1,0:T(8,128)(2,1)S(1)} collective-permute-done((bf16[2,128,256]{2,1,0:T(8,128)(2,1)S(1)}, bf16[2,128,256]{2,1,0:T(8,128)(2,1)S(1)}, u32[]{:S(2)}, u32[]{:S(2)}) %collective-permute-start.11) | collective-permute-done | bytes 131104 | tf_op jit(solution)/shard_map/ppermute | solution.py:348
  39.5 0.8 level20.1
  40.3 2.0 %collective-permute-start.12 = (bf16[2,128,256]{2,1,0:T(8,128)(2,1)S(1)}, bf16[2,128,256]{2,1,0:T(8,128)(2,1)S(1)}, u32[]{:S(2)}, u32[]{:S(2)}) collective-permute-start(bf16[2,128,256]{2,1,0:T(8,128)(2,1)S(1)} %get-tuple-element.52.refs_1_), channel_id=1, source_target_pairs={{0,32},{4,36},{8,40},{12,44},{16,48},{20,52},{24,56},{28,60},{32,0... | collective-permute-start | bytes 393224 | tf_op jit(solution)/shard_map/ppermute | solution.py:348
  42.3 0.8 level21.1
  43.7 2.4 %collective-permute-done.12.refs_0_ = bf16[2,128,256]{2,1,0:T(8,128)(2,1)S(1)} collective-permute-done((bf16[2,128,256]{2,1,0:T(8,128)(2,1)S(1)}, bf16[2,128,256]{2,1,0:T(8,128)(2,1)S(1)}, u32[]{:S(2)}, u32[]{:S(2)}) %collective-permute-start.12) | collective-permute-done | bytes 131104 | tf_op jit(solution)/shard_map/ppermute | solution.py:348
  46.1 0.7 level30.1
  46.9 4.5 %collective-permute-start.13 = (bf16[2,128,128]{2,1,0:T(8,128)(2,1)S(1)}, bf16[2,128,128]{2,1,0:T(8,128)(2,1)S(1)}, u32[]{:S(2)}, u32[]{:S(2)}) collective-permute-start(bf16[2,128,128]{2,1,0:T(8,128)(2,1)S(1)} %slice.13), channel_id=1, source_target_pairs={{0,64},{4,68},{8,72},{12,76},{16,80},{20,84},{24,88},{28,92},{32,9... | collective-permute-start | bytes 196616 | tf_op jit(solution)/shard_map/ppermute | solution.py:348
  51.4 0.7 level31.1
  53.6 0.7 top0.1.refs_3_
  54.6 3.3 %collective-permute-done.4.sib_ref = bf16[2,128,128]{2,1,0:T(8,128)(2,1)S(1)} collective-permute-done((bf16[2,128,128]{2,1,0:T(8,128)(2,1)S(1)}, bf16[2,128,128]{2,1,0:T(8,128)(2,1)S(1)}, u32[]{:S(2)}, u32[]{:S(2)}) %collective-permute-start.4) | collective-permute-done | bytes 65568 | tf_op jit(solution)/shard_map/ppermute | solution.py:348
  59.7 1.0 copy-done.15
  60.7 4.4 %final0.1.refs_8_ = bf16[512,1024]{1,0:T(8,128)(2,1)S(1)} custom-call(s32[5]{0:T(128)S(1)} %stack.23.bits, f32[512,512]{1,0:T(8,128)S(1)} %copy-done.9, bf16[512,512]{1,0:T(8,128)(2,1)S(1)} %copy-done.15, bf16[4,128,256]{2,1,0:T(8,128)(2,1)S(1)} %collective-permute-done.9.sib_ref, f32[2048,16]{1,0:T(8,128)S(1)} %copy-done.11, f32[1,1024]{1,0:T(1,128)S(1)} %bitcast.6, ...), custom_call_target="tpu_custom_call" | custom-call | flops 3000000000 | bytes 8388608 | tf_op jit(solution)/shard_map/final0/pallas_call | solution.py:330
  65.1 4.4 %final1.1 = bf16[512,1024]{1,0:T(8,128)(2,1)S(1)} custom-call(s32[5]{0:T(128)S(1)} %stack.23.bits, f32[512,512]{1,0:T(8,128)S(1)} %get-tuple-element.31.near_ref, bf16[512,512]{1,0:T(8,128)(2,1)S(1)} %copy-done.13, bf16[4,128,256]{2,1,0:T(8,128)(2,1)S(1)} %collective-permute-done.sib_ref, ...), custom_call_target="tpu_custom_call", output_to_operand_aliasing={{}: (14, {})} | custom-call | flops 3000000000 | bytes 8388608 | tf_op jit(solution)/shard_map/final1/pallas_call | solution.py:330
  76.7 1.6 %collective-permute-start.21 = (bf16[128,1024]{1,0:T(8,128)(2,1)S(1)}, bf16[128,1024]{1,0:T(8,128)(2,1)S(1)}, u32[]{:S(2)}, u32[]{:S(2)}) collective-permute-start(bf16[128,1024]{1,0:T(8,128)(2,1)S(1)} %fusion.44), channel_id=1, source_target_pairs={{0,1},{1,2},{2,3},{3,0},{4,5},{5,6},{6,7},{7,4},{8,9},{9,10},{10,1... | collective-permute-start | bytes 786440 | tf_op jit(solution)/shard_map/ppermute | solution.py:367
  79.2 1.8 %collective-permute-start.27 = (bf16[128,1024]{1,0:T(8,128)(2,1)S(1)}, bf16[128,1024]{1,0:T(8,128)(2,1)S(1)}, u32[]{:S(2)}, u32[]{:S(2)}) collective-permute-start(bf16[128,1024]{1,0:T(8,128)(2,1)S(1)} %fusion.68), channel_id=1, source_target_pairs={{0,3},{1,0},{2,1},{3,2},{4,7},{5,4},{6,5},{7,6},{8,11},{9,8},{10,9... | collective-permute-start | bytes 786440 | tf_op jit(solution)/shard_map/ppermute | solution.py:367
  81.0 4.6 %collective-permute-done.18 = bf16[128,1024]{1,0:T(8,128)(2,1)S(1)} collective-permute-done((bf16[128,1024]{1,0:T(8,128)(2,1)S(1)}, bf16[128,1024]{1,0:T(8,128)(2,1)S(1)}, u32[]{:S(2)}, u32[]{:S(2)}) %collective-permute-start.18) | collective-permute-done | bytes 262176 | tf_op jit(solution)/shard_map/ppermute | solution.py:367
  85.7 1.7 %collective-permute-start.19 = (bf16[128,1024]{1,0:T(8,128)(2,1)S(1)}, bf16[128,1024]{1,0:T(8,128)(2,1)S(1)}, u32[]{:S(2)}, u32[]{:S(2)}) collective-permute-start(bf16[128,1024]{1,0:T(8,128)(2,1)S(1)} %add_convert_fusion.11), channel_id=1, source_target_pairs={{0,1},{1,2},{2,3},{3,0},{4,5},{5,6},{6,7},{7,4},{8,9},{9,10},{10,1... | collective-permute-start | bytes 786440 | tf_op jit(solution)/shard_map/ppermute | solution.py:367
  87.4 3.8 %collective-permute-done.21 = bf16[128,1024]{1,0:T(8,128)(2,1)S(1)} collective-permute-done((bf16[128,1024]{1,0:T(8,128)(2,1)S(1)}, bf16[128,1024]{1,0:T(8,128)(2,1)S(1)}, u32[]{:S(2)}, u32[]{:S(2)}) %collective-permute-start.21) | collective-permute-done | bytes 262176 | tf_op jit(solution)/shard_map/ppermute | solution.py:367
  91.3 1.5 %collective-permute-start.22 = (bf16[128,1024]{1,0:T(8,128)(2,1)S(1)}, bf16[128,1024]{1,0:T(8,128)(2,1)S(1)}, u32[]{:S(2)}, u32[]{:S(2)}) collective-permute-start(bf16[128,1024]{1,0:T(8,128)(2,1)S(1)} %add_convert_fusion.8), channel_id=1, source_target_pairs={{0,1},{1,2},{2,3},{3,0},{4,5},{5,6},{6,7},{7,4},{8,9},{9,10},{10,1... | collective-permute-start | bytes 786440 | tf_op jit(solution)/shard_map/ppermute | solution.py:367
  93.6 0.8 collective-permute-start.28
  94.4 2.4 %collective-permute-done.19 = bf16[128,1024]{1,0:T(8,128)(2,1)S(1)} collective-permute-done((bf16[128,1024]{1,0:T(8,128)(2,1)S(1)}, bf16[128,1024]{1,0:T(8,128)(2,1)S(1)}, u32[]{:S(2)}, u32[]{:S(2)}) %collective-permute-start.19) | collective-permute-done | bytes 262176 | tf_op jit(solution)/shard_map/ppermute | solution.py:367
  96.9 1.5 %collective-permute-start.20 = (bf16[128,1024]{1,0:T(8,128)(2,1)S(1)}, bf16[128,1024]{1,0:T(8,128)(2,1)S(1)}, u32[]{:S(2)}, u32[]{:S(2)}) collective-permute-start(bf16[128,1024]{1,0:T(8,128)(2,1)S(1)} %add_convert_fusion.10), channel_id=1, source_target_pairs={{0,1},{1,2},{2,3},{3,0},{4,5},{5,6},{6,7},{7,4},{8,9},{9,10},{10,1... | collective-permute-start | bytes 786440 | tf_op jit(solution)/shard_map/ppermute | solution.py:367
  98.4 4.0 %collective-permute-done.22 = bf16[128,1024]{1,0:T(8,128)(2,1)S(1)} collective-permute-done((bf16[128,1024]{1,0:T(8,128)(2,1)S(1)}, bf16[128,1024]{1,0:T(8,128)(2,1)S(1)}, u32[]{:S(2)}, u32[]{:S(2)}) %collective-permute-start.22) | collective-permute-done | bytes 262176 | tf_op jit(solution)/shard_map/ppermute | solution.py:367
  102.5 1.5 %collective-permute-start.23 = (bf16[128,1024]{1,0:T(8,128)(2,1)S(1)}, bf16[128,1024]{1,0:T(8,128)(2,1)S(1)}, u32[]{:S(2)}, u32[]{:S(2)}) collective-permute-start(bf16[128,1024]{1,0:T(8,128)(2,1)S(1)} %add_convert_fusion.7), channel_id=1, source_target_pairs={{0,1},{1,2},{2,3},{3,0},{4,5},{5,6},{6,7},{7,4},{8,9},{9,10},{10,1... | collective-permute-start | bytes 786440 | tf_op jit(solution)/shard_map/ppermute | solution.py:367
  104.8 1.5 %collective-permute-done.28 = bf16[128,1024]{1,0:T(8,128)(2,1)S(1)} collective-permute-done((bf16[128,1024]{1,0:T(8,128)(2,1)S(1)}, bf16[128,1024]{1,0:T(8,128)(2,1)S(1)}, u32[]{:S(2)}, u32[]{:S(2)}) %collective-permute-start.28) | collective-permute-done | bytes 262176 | tf_op jit(solution)/shard_map/ppermute | solution.py:367
  106.5 1.6 %collective-permute-done.20 = bf16[128,1024]{1,0:T(8,128)(2,1)S(1)} collective-permute-done((bf16[128,1024]{1,0:T(8,128)(2,1)S(1)}, bf16[128,1024]{1,0:T(8,128)(2,1)S(1)}, u32[]{:S(2)}, u32[]{:S(2)}) %collective-permute-start.20) | collective-permute-done | bytes 262176 | tf_op jit(solution)/shard_map/ppermute | solution.py:367
  108.2 4.7 %collective-permute-done.23 = bf16[128,1024]{1,0:T(8,128)(2,1)S(1)} collective-permute-done((bf16[128,1024]{1,0:T(8,128)(2,1)S(1)}, bf16[128,1024]{1,0:T(8,128)(2,1)S(1)}, u32[]{:S(2)}, u32[]{:S(2)}) %collective-permute-start.23) | collective-permute-done | bytes 262176 | tf_op jit(solution)/shard_map/ppermute | solution.py:367
  113.0 1.6 %collective-permute-done.26 = bf16[128,1024]{1,0:T(8,128)(2,1)S(1)} collective-permute-done((bf16[128,1024]{1,0:T(8,128)(2,1)S(1)}, bf16[128,1024]{1,0:T(8,128)(2,1)S(1)}, u32[]{:S(2)}, u32[]{:S(2)}) %collective-permute-start.26) | collective-permute-done | bytes 262176 | tf_op jit(solution)/shard_map/ppermute | solution.py:367
  114.7 2.9 %collective-permute-done.29 = bf16[128,1024]{1,0:T(8,128)(2,1)S(1)} collective-permute-done((bf16[128,1024]{1,0:T(8,128)(2,1)S(1)}, bf16[128,1024]{1,0:T(8,128)(2,1)S(1)}, u32[]{:S(2)}, u32[]{:S(2)}) %collective-permute-start.29) | collective-permute-done | bytes 262176 | tf_op jit(solution)/shard_map/ppermute | solution.py:367
  117.6 1.0 pad_maximum_fusion
  (95 shorter events, 16.7 us)
Async XLA Ops:
  0.0 1.2 %copy-start = (bf16[512,1024]{1,0:T(8,128)(2,1)S(1)}, bf16[512,1024]{1,0:T(8,128)(2,1)}, u32[]{:S(2)}) copy-start(bf16[512,1024]{1,0:T(8,128)(2,1)} %q_ref.3) | copy-start | bytes 3145732
  1.2 1.2 %copy-start.1 = (bf16[512,1024]{1,0:T(8,128)(2,1)S(1)}, bf16[512,1024]{1,0:T(8,128)(2,1)}, u32[]{:S(2)}) copy-start(bf16[512,1024]{1,0:T(8,128)(2,1)} %k_ref.3) | copy-start | bytes 3145732
  2.5 1.2 %copy-start.2 = (bf16[512,1024]{1,0:T(8,128)(2,1)S(1)}, bf16[512,1024]{1,0:T(8,128)(2,1)}, u32[]{:S(2)}) copy-start(bf16[512,1024]{1,0:T(8,128)(2,1)} %v_ref.3) | copy-start | bytes 3145732
  3.7 0.9 copy-start.3
  4.6 0.7 copy-start.4
  5.3 0.7 copy-start.5
  6.0 0.7 copy-start.7
  14.1 0.8 copy-start.14
  14.9 7.4 %copy-start.8 = (f32[512,512]{1,0:T(8,128)}, f32[512,512]{1,0:T(8,128)S(1)}, u32[]{:S(2)}) copy-start(f32[512,512]{1,0:T(8,128)S(1)} %get-tuple-element.44.near_ref) | copy-start | bytes 3145732
  14.9 7.4 %copy-start.10 = (f32[2048,16]{1,0:T(8,128)}, f32[2048,16]{1,0:T(8,128)S(1)}, u32[]{:S(2)}) copy-start(f32[2048,16]{1,0:T(8,128)S(1)} %get-tuple-element.47.cols_ref) | copy-start | bytes 393220
  14.9 8.8 %collective-permute-start.9 = (bf16[4,128,256]{2,1,0:T(8,128)(2,1)S(1)}, bf16[4,128,256]{2,1,0:T(8,128)(2,1)S(1)}, u32[]{:S(2)}, u32[]{:S(2)}) collective-permute-start(bf16[4,128,256]{2,1,0:T(8,128)(2,1)S(1)} %get-tuple-element.46.mine_ref), channel_id=1, source_target_pairs={{0,4},{4,0},{8,12},{12,8},{16,20},{20,16},{24,28},{28,24},{32,36},... | collective-permute-start | bytes 786440 | tf_op jit(solution)/shard_map/ppermute | solution.py:348
  22.3 0.8 copy-start.12
  23.1 2.6 %collective-permute-start = (bf16[4,128,256]{2,1,0:T(8,128)(2,1)S(1)}, bf16[4,128,256]{2,1,0:T(8,128)(2,1)S(1)}, u32[]{:S(2)}, u32[]{:S(2)}) collective-permute-start(bf16[4,128,256]{2,1,0:T(8,128)(2,1)S(1)} %get-tuple-element.33.mine_ref), channel_id=1, source_target_pairs={{0,4},{4,0},{8,12},{12,8},{16,20},{20,16},{24,28},{28,24},{32,36},... | collective-permute-start | bytes 786440 | tf_op jit(solution)/shard_map/ppermute | solution.py:348
  24.4 6.4 %collective-permute-start.10 = (bf16[2,128,256]{2,1,0:T(8,128)(2,1)S(1)}, bf16[2,128,256]{2,1,0:T(8,128)(2,1)S(1)}, u32[]{:S(2)}, u32[]{:S(2)}) collective-permute-start(bf16[2,128,256]{2,1,0:T(8,128)(2,1)S(1)} %pair0.1.refs_1_), channel_id=1, source_target_pairs={{0,8},{4,12},{8,0},{12,4},{16,24},{20,28},{24,16},{28,20},{32,40},... | collective-permute-start | bytes 393224 | tf_op jit(solution)/shard_map/ppermute | solution.py:348
  26.4 6.3 %collective-permute-start.1 = (bf16[2,128,256]{2,1,0:T(8,128)(2,1)S(1)}, bf16[2,128,256]{2,1,0:T(8,128)(2,1)S(1)}, u32[]{:S(2)}, u32[]{:S(2)}) collective-permute-start(bf16[2,128,256]{2,1,0:T(8,128)(2,1)S(1)} %pair1.1.refs_1_), channel_id=1, source_target_pairs={{0,8},{4,12},{8,0},{12,4},{16,24},{20,28},{24,16},{28,20},{32,40},... | collective-permute-start | bytes 393224 | tf_op jit(solution)/shard_map/ppermute | solution.py:348
  31.6 7.9 %collective-permute-start.11 = (bf16[2,128,256]{2,1,0:T(8,128)(2,1)S(1)}, bf16[2,128,256]{2,1,0:T(8,128)(2,1)S(1)}, u32[]{:S(2)}, u32[]{:S(2)}) collective-permute-start(bf16[2,128,256]{2,1,0:T(8,128)(2,1)S(1)} %get-tuple-element.49.refs_1_), channel_id=1, source_target_pairs={{0,16},{4,20},{8,24},{12,28},{16,0},{20,4},{24,8},{28,12},{32,48},... | collective-permute-start | bytes 393224 | tf_op jit(solution)/shard_map/ppermute | solution.py:348
  33.4 8.8 %collective-permute-start.2 = (bf16[2,128,256]{2,1,0:T(8,128)(2,1)S(1)}, bf16[2,128,256]{2,1,0:T(8,128)(2,1)S(1)}, u32[]{:S(2)}, u32[]{:S(2)}) collective-permute-start(bf16[2,128,256]{2,1,0:T(8,128)(2,1)S(1)} %get-tuple-element.36.refs_1_), channel_id=1, source_target_pairs={{0,16},{4,20},{8,24},{12,28},{16,0},{20,4},{24,8},{28,12},{32,48},... | collective-permute-start | bytes 393224 | tf_op jit(solution)/shard_map/ppermute | solution.py:348
  40.3 5.9 %collective-permute-start.12 = (bf16[2,128,256]{2,1,0:T(8,128)(2,1)S(1)}, bf16[2,128,256]{2,1,0:T(8,128)(2,1)S(1)}, u32[]{:S(2)}, u32[]{:S(2)}) collective-permute-start(bf16[2,128,256]{2,1,0:T(8,128)(2,1)S(1)} %get-tuple-element.52.refs_1_), channel_id=1, source_target_pairs={{0,32},{4,36},{8,40},{12,44},{16,48},{20,52},{24,56},{28,60},{32,0... | collective-permute-start | bytes 393224 | tf_op jit(solution)/shard_map/ppermute | solution.py:348
  43.0 8.3 %collective-permute-start.3 = (bf16[2,128,256]{2,1,0:T(8,128)(2,1)S(1)}, bf16[2,128,256]{2,1,0:T(8,128)(2,1)S(1)}, u32[]{:S(2)}, u32[]{:S(2)}) collective-permute-start(bf16[2,128,256]{2,1,0:T(8,128)(2,1)S(1)} %get-tuple-element.39.refs_1_), channel_id=1, source_target_pairs={{0,32},{4,36},{8,40},{12,44},{16,48},{20,52},{24,56},{28,60},{32,0... | collective-permute-start | bytes 393224 | tf_op jit(solution)/shard_map/ppermute | solution.py:348
  46.9 6.7 %collective-permute-start.13 = (bf16[2,128,128]{2,1,0:T(8,128)(2,1)S(1)}, bf16[2,128,128]{2,1,0:T(8,128)(2,1)S(1)}, u32[]{:S(2)}, u32[]{:S(2)}) collective-permute-start(bf16[2,128,128]{2,1,0:T(8,128)(2,1)S(1)} %slice.13), channel_id=1, source_target_pairs={{0,64},{4,68},{8,72},{12,76},{16,80},{20,84},{24,88},{28,92},{32,9... | collective-permute-start | bytes 196616 | tf_op jit(solution)/shard_map/ppermute | solution.py:348
  52.1 5.8 %collective-permute-start.4 = (bf16[2,128,128]{2,1,0:T(8,128)(2,1)S(1)}, bf16[2,128,128]{2,1,0:T(8,128)(2,1)S(1)}, u32[]{:S(2)}, u32[]{:S(2)}) collective-permute-start(bf16[2,128,128]{2,1,0:T(8,128)(2,1)S(1)} %slice.12), channel_id=1, source_target_pairs={{0,64},{4,68},{8,72},{12,76},{16,80},{20,84},{24,88},{28,92},{32,9... | collective-permute-start | bytes 196616 | tf_op jit(solution)/shard_map/ppermute | solution.py:348
  52.8 5.8 %collective-permute-start.14 = (bf16[2,128,128]{2,1,0:T(8,128)(2,1)S(1)}, bf16[2,128,128]{2,1,0:T(8,128)(2,1)S(1)}, u32[]{:S(2)}, u32[]{:S(2)}) collective-permute-start(bf16[2,128,128]{2,1,0:T(8,128)(2,1)S(1)} %get-tuple-element.48.refs_0_), channel_id=1, source_target_pairs={{0,4},{4,0},{8,12},{12,8},{16,20},{20,16},{24,28},{28,24},{32,36},... | collective-permute-start | bytes 196616 | tf_op jit(solution)/shard_map/ppermute | solution.py:348
  52.8 6.4 %collective-permute-start.15 = (bf16[2,128,128]{2,1,0:T(8,128)(2,1)S(1)}, bf16[2,128,128]{2,1,0:T(8,128)(2,1)S(1)}, u32[]{:S(2)}, u32[]{:S(2)}) collective-permute-start(bf16[2,128,128]{2,1,0:T(8,128)(2,1)S(1)} %get-tuple-element.51.refs_1_), channel_id=1, source_target_pairs={{0,4},{4,0},{8,12},{12,8},{16,20},{20,16},{24,28},{28,24},{32,36},... | collective-permute-start | bytes 196616 | tf_op jit(solution)/shard_map/ppermute | solution.py:348
  53.3 6.0 %collective-permute-start.16 = (bf16[2,128,128]{2,1,0:T(8,128)(2,1)S(1)}, bf16[2,128,128]{2,1,0:T(8,128)(2,1)S(1)}, u32[]{:S(2)}, u32[]{:S(2)}) collective-permute-start(bf16[2,128,128]{2,1,0:T(8,128)(2,1)S(1)} %get-tuple-element.54.refs_2_), channel_id=1, source_target_pairs={{0,4},{4,0},{8,12},{12,8},{16,20},{20,16},{24,28},{28,24},{32,36},... | collective-permute-start | bytes 196616 | tf_op jit(solution)/shard_map/ppermute | solution.py:348
  53.6 6.0 %copy-start.6 = (f32[1024]{0:T(1024)S(1)}, f32[1024]{0:T(1024)}, u32[]{:S(2)}) copy-start(f32[1024]{0:T(1024)} %param.16) | copy-start | bytes 12292
  54.3 5.3 %collective-permute-start.17 = (bf16[2,128,128]{2,1,0:T(8,128)(2,1)S(1)}, bf16[2,128,128]{2,1,0:T(8,128)(2,1)S(1)}, u32[]{:S(2)}, u32[]{:S(2)}) collective-permute-start(bf16[2,128,128]{2,1,0:T(8,128)(2,1)S(1)} %top0.1.refs_3_), channel_id=1, source_target_pairs={{0,4},{4,0},{8,12},{12,8},{16,20},{20,16},{24,28},{28,24},{32,36},... | collective-permute-start | bytes 196616 | tf_op jit(solution)/shard_map/ppermute | solution.py:348
  54.6 5.0 %copy-start.9 = (f32[512,512]{1,0:T(8,128)S(1)}, f32[512,512]{1,0:T(8,128)}, u32[]{:S(2)}) copy-start(f32[512,512]{1,0:T(8,128)} %copy-done.8) | copy-start | bytes 3145732
  54.6 5.0 %copy-start.11 = (f32[2048,16]{1,0:T(8,128)S(1)}, f32[2048,16]{1,0:T(8,128)}, u32[]{:S(2)}) copy-start(f32[2048,16]{1,0:T(8,128)} %copy-done.10) | copy-start | bytes 393220
  57.9 7.1 %collective-permute-start.5 = (bf16[2,128,128]{2,1,0:T(8,128)(2,1)S(1)}, bf16[2,128,128]{2,1,0:T(8,128)(2,1)S(1)}, u32[]{:S(2)}, u32[]{:S(2)}) collective-permute-start(bf16[2,128,128]{2,1,0:T(8,128)(2,1)S(1)} %get-tuple-element.35.refs_0_), channel_id=1, source_target_pairs={{0,4},{4,0},{8,12},{12,8},{16,20},{20,16},{24,28},{28,24},{32,36},... | collective-permute-start | bytes 196616 | tf_op jit(solution)/shard_map/ppermute | solution.py:348
  58.5 6.5 %collective-permute-start.6 = (bf16[2,128,128]{2,1,0:T(8,128)(2,1)S(1)}, bf16[2,128,128]{2,1,0:T(8,128)(2,1)S(1)}, u32[]{:S(2)}, u32[]{:S(2)}) collective-permute-start(bf16[2,128,128]{2,1,0:T(8,128)(2,1)S(1)} %get-tuple-element.38.refs_1_), channel_id=1, source_target_pairs={{0,4},{4,0},{8,12},{12,8},{16,20},{20,16},{24,28},{28,24},{32,36},... | collective-permute-start | bytes 196616 | tf_op jit(solution)/shard_map/ppermute | solution.py:348
  59.1 6.0 %collective-permute-start.7 = (bf16[2,128,128]{2,1,0:T(8,128)(2,1)S(1)}, bf16[2,128,128]{2,1,0:T(8,128)(2,1)S(1)}, u32[]{:S(2)}, u32[]{:S(2)}) collective-permute-start(bf16[2,128,128]{2,1,0:T(8,128)(2,1)S(1)} %get-tuple-element.41.refs_2_), channel_id=1, source_target_pairs={{0,4},{4,0},{8,12},{12,8},{16,20},{20,16},{24,28},{28,24},{32,36},... | collective-permute-start | bytes 196616 | tf_op jit(solution)/shard_map/ppermute | solution.py:348
  59.2 5.9 %collective-permute-start.8 = (bf16[2,128,128]{2,1,0:T(8,128)(2,1)S(1)}, bf16[2,128,128]{2,1,0:T(8,128)(2,1)S(1)}, u32[]{:S(2)}, u32[]{:S(2)}) collective-permute-start(bf16[2,128,128]{2,1,0:T(8,128)(2,1)S(1)} %top1.1.refs_3_), channel_id=1, source_target_pairs={{0,4},{4,0},{8,12},{12,8},{16,20},{20,16},{24,28},{28,24},{32,36},... | collective-permute-start | bytes 196616 | tf_op jit(solution)/shard_map/ppermute | solution.py:348
  59.6 1.0 copy-start.15
  60.7 4.4 %copy-start.13 = (bf16[512,512]{1,0:T(8,128)(2,1)S(1)}, bf16[512,512]{1,0:T(8,128)(2,1)}, u32[]{:S(2)}) copy-start(bf16[512,512]{1,0:T(8,128)(2,1)} %copy-done.12) | copy-start | bytes 1572868
  60.7 8.8 %slice-start = ((s8[8388608]{0:T(1024)(128)(4,1)}), s8[4194304]{0:T(1024)(128)(4,1)S(1)}, s32[]{:S(2)}) async-start(s8[8388608]{0:T(1024)(128)(4,1)} %bitcast.8), calls=%async_computation | async-start | bytes 8388608
  65.1 4.4 %slice-start.1 = ((s8[8388608]{0:T(1024)(128)(4,1)}), s8[4194304]{0:T(1024)(128)(4,1)S(1)}, s32[]{:S(2)}) async-start(s8[8388608]{0:T(1024)(128)(4,1)} %bitcast.8), calls=%async_computation.1 | async-start | bytes 8388608
  76.4 9.2 %collective-permute-start.18 = (bf16[128,1024]{1,0:T(8,128)(2,1)S(1)}, bf16[128,1024]{1,0:T(8,128)(2,1)S(1)}, u32[]{:S(2)}, u32[]{:S(2)}) collective-permute-start(bf16[128,1024]{1,0:T(8,128)(2,1)S(1)} %fusion.32), channel_id=1, source_target_pairs={{0,1},{1,2},{2,3},{3,0},{4,5},{5,6},{6,7},{7,4},{8,9},{9,10},{10,1... | collective-permute-start | bytes 786440 | tf_op jit(solution)/shard_map/ppermute | solution.py:367
  76.7 14.6 %collective-permute-start.21 = (bf16[128,1024]{1,0:T(8,128)(2,1)S(1)}, bf16[128,1024]{1,0:T(8,128)(2,1)S(1)}, u32[]{:S(2)}, u32[]{:S(2)}) collective-permute-start(bf16[128,1024]{1,0:T(8,128)(2,1)S(1)} %fusion.44), channel_id=1, source_target_pairs={{0,1},{1,2},{2,3},{3,0},{4,5},{5,6},{6,7},{7,4},{8,9},{9,10},{10,1... | collective-permute-start | bytes 786440 | tf_op jit(solution)/shard_map/ppermute | solution.py:367
  78.7 14.1 %collective-permute-start.24 = (bf16[128,1024]{1,0:T(8,128)(2,1)S(1)}, bf16[128,1024]{1,0:T(8,128)(2,1)S(1)}, u32[]{:S(2)}, u32[]{:S(2)}) collective-permute-start(bf16[128,1024]{1,0:T(8,128)(2,1)S(1)} %fusion.56), channel_id=1, source_target_pairs={{0,3},{1,0},{2,1},{3,2},{4,7},{5,4},{6,5},{7,6},{8,11},{9,8},{10,9... | collective-permute-start | bytes 786440 | tf_op jit(solution)/shard_map/ppermute | solution.py:367
  79.2 14.3 %collective-permute-start.27 = (bf16[128,1024]{1,0:T(8,128)(2,1)S(1)}, bf16[128,1024]{1,0:T(8,128)(2,1)S(1)}, u32[]{:S(2)}, u32[]{:S(2)}) collective-permute-start(bf16[128,1024]{1,0:T(8,128)(2,1)S(1)} %fusion.68), channel_id=1, source_target_pairs={{0,3},{1,0},{2,1},{3,2},{4,7},{5,4},{6,5},{7,6},{8,11},{9,8},{10,9... | collective-permute-start | bytes 786440 | tf_op jit(solution)/shard_map/ppermute | solution.py:367
  85.7 11.2 %collective-permute-start.19 = (bf16[128,1024]{1,0:T(8,128)(2,1)S(1)}, bf16[128,1024]{1,0:T(8,128)(2,1)S(1)}, u32[]{:S(2)}, u32[]{:S(2)}) collective-permute-start(bf16[128,1024]{1,0:T(8,128)(2,1)S(1)} %add_convert_fusion.11), channel_id=1, source_target_pairs={{0,1},{1,2},{2,3},{3,0},{4,5},{5,6},{6,7},{7,4},{8,9},{9,10},{10,1... | collective-permute-start | bytes 786440 | tf_op jit(solution)/shard_map/ppermute | solution.py:367
  91.3 11.2 %collective-permute-start.22 = (bf16[128,1024]{1,0:T(8,128)(2,1)S(1)}, bf16[128,1024]{1,0:T(8,128)(2,1)S(1)}, u32[]{:S(2)}, u32[]{:S(2)}) collective-permute-start(bf16[128,1024]{1,0:T(8,128)(2,1)S(1)} %add_convert_fusion.8), channel_id=1, source_target_pairs={{0,1},{1,2},{2,3},{3,0},{4,5},{5,6},{6,7},{7,4},{8,9},{9,10},{10,1... | collective-permute-start | bytes 786440 | tf_op jit(solution)/shard_map/ppermute | solution.py:367
  92.9 11.2 %collective-permute-start.25 = (bf16[128,1024]{1,0:T(8,128)(2,1)S(1)}, bf16[128,1024]{1,0:T(8,128)(2,1)S(1)}, u32[]{:S(2)}, u32[]{:S(2)}) collective-permute-start(bf16[128,1024]{1,0:T(8,128)(2,1)S(1)} %add_convert_fusion.5), channel_id=1, source_target_pairs={{0,3},{1,0},{2,1},{3,2},{4,7},{5,4},{6,5},{7,6},{8,11},{9,8},{10,9... | collective-permute-start | bytes 786440 | tf_op jit(solution)/shard_map/ppermute | solution.py:367
  93.6 12.7 %collective-permute-start.28 = (bf16[128,1024]{1,0:T(8,128)(2,1)S(1)}, bf16[128,1024]{1,0:T(8,128)(2,1)S(1)}, u32[]{:S(2)}, u32[]{:S(2)}) collective-permute-start(bf16[128,1024]{1,0:T(8,128)(2,1)S(1)} %add_convert_fusion.2), channel_id=1, source_target_pairs={{0,3},{1,0},{2,1},{3,2},{4,7},{5,4},{6,5},{7,6},{8,11},{9,8},{10,9... | collective-permute-start | bytes 786440 | tf_op jit(solution)/shard_map/ppermute | solution.py:367
  96.9 11.2 %collective-permute-start.20 = (bf16[128,1024]{1,0:T(8,128)(2,1)S(1)}, bf16[128,1024]{1,0:T(8,128)(2,1)S(1)}, u32[]{:S(2)}, u32[]{:S(2)}) collective-permute-start(bf16[128,1024]{1,0:T(8,128)(2,1)S(1)} %add_convert_fusion.10), channel_id=1, source_target_pairs={{0,1},{1,2},{2,3},{3,0},{4,5},{5,6},{6,7},{7,4},{8,9},{9,10},{10,1... | collective-permute-start | bytes 786440 | tf_op jit(solution)/shard_map/ppermute | solution.py:367
  102.5 10.3 %collective-permute-start.23 = (bf16[128,1024]{1,0:T(8,128)(2,1)S(1)}, bf16[128,1024]{1,0:T(8,128)(2,1)S(1)}, u32[]{:S(2)}, u32[]{:S(2)}) collective-permute-start(bf16[128,1024]{1,0:T(8,128)(2,1)S(1)} %add_convert_fusion.7), channel_id=1, source_target_pairs={{0,1},{1,2},{2,3},{3,0},{4,5},{5,6},{6,7},{7,4},{8,9},{9,10},{10,1... | collective-permute-start | bytes 786440 | tf_op jit(solution)/shard_map/ppermute | solution.py:367
  104.1 10.5 %collective-permute-start.26 = (bf16[128,1024]{1,0:T(8,128)(2,1)S(1)}, bf16[128,1024]{1,0:T(8,128)(2,1)S(1)}, u32[]{:S(2)}, u32[]{:S(2)}) collective-permute-start(bf16[128,1024]{1,0:T(8,128)(2,1)S(1)} %add_convert_fusion.4), channel_id=1, source_target_pairs={{0,3},{1,0},{2,1},{3,2},{4,7},{5,4},{6,5},{7,6},{8,11},{9,8},{10,9... | collective-permute-start | bytes 786440 | tf_op jit(solution)/shard_map/ppermute | solution.py:367
  106.4 11.2 %collective-permute-start.29 = (bf16[128,1024]{1,0:T(8,128)(2,1)S(1)}, bf16[128,1024]{1,0:T(8,128)(2,1)S(1)}, u32[]{:S(2)}, u32[]{:S(2)}) collective-permute-start(bf16[128,1024]{1,0:T(8,128)(2,1)S(1)} %add_convert_fusion.1), channel_id=1, source_target_pairs={{0,3},{1,0},{2,1},{3,2},{4,7},{5,4},{6,5},{7,6},{8,11},{9,8},{10,9... | collective-permute-start | bytes 786440 | tf_op jit(solution)/shard_map/ppermute | solution.py:367

commit v2 on v1

--- a/solution.py
+++ b/solution.py
@@ -5,6 +5,7 @@
 from jax.experimental import pallas as pl
 from jax.experimental.pallas import tpu as pltpu
 from jax.sharding import PartitionSpec as P
+
 
 SPAN = 64
 SUPER = 128
@@ -22,7 +23,7 @@
     return jnp.dot(a, b, preferred_element_type=F32)
 
 
-def local_kernel(chunk, flags, q_ref, k_ref, v_ref, log_ref, beta_ref, weight_ref,
+def local_kernel(base, stride, flags, q_ref, k_ref, v_ref, log_ref, beta_ref, weight_ref,
                  near_ref, far_ref, map_ref, cols_ref, rows_ref):
     step = pl.program_id(0)
     tokens = q_ref.shape[0]
@@ -58,7 +59,7 @@
     units = [(g, s) for g in range(TOGETHER) for s in range(supers)]
     cols, cum_rows, tail_rows, beta_rows = [], [], [], []
     for g in range(TOGETHER):
-        head = TOGETHER * (CHUNKS * step + chunk) + g
+        head = TOGETHER * (base + stride * step) + g
         take = pl.ds(head, 1)
         beta_row = beta_ref[take, :]
         wanted = [rows_ref[0, take, :], rows_ref[2, take, :], beta_row]
@@ -158,18 +159,17 @@
         map_ref[g] = jnp.concatenate([total, eye * decay - erase], axis=1).astype(BF16)
 
 
-def local_part(chunk, flags, queries, keys, values, log_decay, beta, weights):
-    tokens, width = queries.shape
+def local_part(base, stride, steps, flags, queries, keys, values, log_decay, beta, weights):
+    tokens = queries.shape[0]
     heads = log_decay.shape[0]
-    steps = heads // (TOGETHER * CHUNKS)
     wide = TOGETHER * HEAD_DIM
-    block = pl.BlockSpec((tokens, wide), lambda h, f: (0, CHUNKS * h + chunk))
+    block = pl.BlockSpec((tokens, wide), lambda h, f: (0, base + stride * h))
     out = pl.BlockSpec((tokens, wide), lambda h, f: (0, h))
     whole2 = pl.BlockSpec((heads, tokens), lambda h, f: (0, 0))
     whole3 = pl.BlockSpec(weights.shape, lambda h, f: (0, 0, 0))
     part = steps * TOGETHER
     return pl.pallas_call(
-        functools.partial(local_kernel, chunk),
+        functools.partial(local_kernel, base, stride),
         grid_spec=pltpu.PrefetchScalarGridSpec(
             num_scalar_prefetch=1,
             grid=(steps,),
@@ -185,30 +185,32 @@
             jax.ShapeDtypeStruct((part, HEAD_DIM, 2 * HEAD_DIM), BF16),
             jax.ShapeDtypeStruct((part * tokens, 16), F32),
         ],
-        compiler_params=pltpu.CompilerParams(vmem_limit_bytes=24 << 20),
+        compiler_params=pltpu.CompilerParams(vmem_limit_bytes=14 << 20),
         cost_estimate=pl.CostEstimate(flops=part * 1500000000, bytes_accessed=8 << 20, transcendentals=0),
-        name=f"local{chunk}",
     )(flags, queries, keys, values, log_decay, beta, weights)
 
 
-def pair_kernel(bits, mine_ref, sib_ref, cur_ref):
+def pair_kernel(bits, *refs):
     core = bits[0]
+    cur_ref = refs[-1]
     half = cur_ref.shape[0]
-
-    def run(first, second):
+    parts = (len(refs) - 1) // 2
+    mine, sib = refs[:parts], refs[parts:2 * parts]
+
+    def run(first, second, offset):
         for g in range(half):
-            later = second[half * core + g]
-            both = mm(later[:, HEAD_DIM:], first[half * core + g])
+            later = second[offset + g]
+            both = mm(later[:, HEAD_DIM:], first[offset + g])
             cur_ref[g, :, :HEAD_DIM] = (both[:, :HEAD_DIM] + later[:, :HEAD_DIM].astype(F32)).astype(BF16)
             cur_ref[g, :, HEAD_DIM:] = both[:, HEAD_DIM:].astype(BF16)
 
     @pl.when(core == 1)
     def _():
-        run(sib_ref, mine_ref)
+        run(sib[-1], mine[-1], half if parts == 1 else 0)
 
     @pl.when(core == 0)
     def _():
-        run(mine_ref, sib_ref)
+        run(mine[0], sib[0], 0)
 
 
 def level_kernel(level, bits, *refs):
@@ -262,7 +264,7 @@
         x_ref[...] = jnp.zeros(x_ref.shape, BF16)
 
 
-def small_call(kernel, bits, args, outs, name):
+def small_call(kernel, bits, args, outs):
     return pl.pallas_call(
         kernel,
         grid_spec=pltpu.PrefetchScalarGridSpec(
@@ -272,22 +274,19 @@
             out_specs=[pl.BlockSpec(o.shape, lambda i, b, n=len(o.shape): (0,) * n) for o in outs],
         ),
         out_shape=outs,
-        compiler_params=pltpu.CompilerParams(vmem_limit_bytes=6 << 20),
+        compiler_params=pltpu.CompilerParams(vmem_limit_bytes=3 << 20),
         cost_estimate=pl.CostEstimate(flops=600000000, bytes_accessed=1 << 20, transcendentals=0),
-        name=name,
     )(bits, *args)
 
 
-def final_kernel(levels, bits, near_ref, far_ref, sib_ref, cols_ref, gain_ref, *refs):
+def read_kernel(side, fold, slots, norm, bits, near_ref, far_ref, cols_ref, *refs):
     core = bits[0]
-    mine, other, z_ref = refs[:levels], refs[levels:2 * levels], refs[-1]
+    refs = list(refs)
     tokens = near_ref.shape[0]
-    is_mine = pl.program_id(0) == core
     first = 3 + LOCAL_LEVELS
     upper = core == 1
     units = [(g, t) for g in range(TOGETHER) for t in range(0, tokens, SUPER)]
-    states = [jnp.concatenate([jnp.where(is_mine, m[g], o[g]) for m, o in zip(mine, other)], axis=1)
-              for g in range(TOGETHER)]
+    count = range(len(units))
 
     def lanes(g):
         return slice(g * HEAD_DIM, (g + 1) * HEAD_DIM)
@@ -296,56 +295,83 @@
         return cols_ref[g * tokens + t:g * tokens + t + SUPER, i:i + 1]
 
     fars = [far_ref[t:t + SUPER, lanes(g)] for g, t in units]
-    both = [mm(fars[u], sib_ref[g]) for u, (g, t) in enumerate(units)]
-    ys = [near_ref[t:t + SUPER, lanes(g)]
-          + jnp.where(upper, cols(g, t, first), 0.0) * both[u][:, :HEAD_DIM] for u, (g, t) in enumerate(units)]
-    fars = [jnp.where(upper, both[u][:, HEAD_DIM:].astype(BF16), fars[u]) for u in range(len(units))]
+    ys = [near_ref[t:t + SUPER, lanes(g)] for g, t in units]
+    if fold:
+        sib_ref = refs.pop(0)
+        both = [mm(fars[u], sib_ref[g]) for u, (g, t) in enumerate(units)]
+        ys = [ys[u] + jnp.where(upper, cols(g, t, first) * both[u][:, :HEAD_DIM], 0.0)
+              for u, (g, t) in enumerate(units)]
+        fars = [jnp.where(upper, both[u][:, HEAD_DIM:].astype(BF16), fars[u]) for u in count]
+    if slots:
+        mine, other = refs[:len(slots)], refs[len(slots):2 * len(slots)]
+        refs = refs[2 * len(slots):]
+        is_mine = core == side
+        states = [jnp.concatenate([jnp.where(is_mine, m[g], o[g]) for m, o in zip(mine, other)], axis=1)
+                  for g in range(TOGETHER)]
+        reads = [mm(fars[u], states[g]) for u, (g, t) in enumerate(units)]
+        for i, slot in enumerate(slots):
+            ys = [ys[u] + cols(g, t, first + slot) * reads[u][:, i * HEAD_DIM:(i + 1) * HEAD_DIM]
+                  for u, (g, t) in enumerate(units)]
+    if norm:
+        gain_ref, z_ref = refs[0], refs[-1]
+        for u, (g, t) in enumerate(units):
+            scale = lax.rsqrt(jnp.mean(ys[u] * ys[u], axis=1, keepdims=True) + EPS)
+            z_ref[t:t + SUPER, lanes(g)] = (ys[u] * scale * gain_ref[:, lanes(g)]).astype(BF16)
+        return
     for u, (g, t) in enumerate(units):
-        reads = mm(fars[u], states[g])
-        y = ys[u]
-        for i in range(levels):
-            y = y + cols(g, t, first + 1 + i) * reads[:, i * HEAD_DIM:(i + 1) * HEAD_DIM]
-        scale = lax.rsqrt(jnp.mean(y * y, axis=1, keepdims=True) + EPS)
-        z_ref[t:t + SUPER, lanes(g)] = (y * scale * gain_ref[:, lanes(g)]).astype(BF16)
-
-
-def final_part(chunk, bits, near, far, sib, cols, gain, mine, other, before):
-    tokens, width = near.shape
+        refs[0][t:t + SUPER, lanes(g)] = ys[u]
+        if fold:
+            refs[1][t:t + SUPER, lanes(g)] = fars[u]
+
+
+def read_part(bits, side, pair, near, far, cols, sib=None, slots=(), mine=(), other=(), gain=None, before=None):
+    tokens = near[0].shape[0]
     wide = TOGETHER * HEAD_DIM
-    steps = width // wide
-    levels = len(mine)
-    block = pl.BlockSpec((tokens, wide), lambda h, b: (0, h))
-    placed = lambda h, b: (0, CHUNKS * h + chunk)
     state = pl.BlockSpec((TOGETHER, HEAD_DIM, HEAD_DIM), lambda h, b: (0, 0, 0))
-    in_specs = [block, block,
-                pl.BlockSpec((TOGETHER, HEAD_DIM, 2 * HEAD_DIM), lambda h, b: (h, 0, 0)),
-                pl.BlockSpec((TOGETHER * tokens, 16), lambda h, b: (h, 0)),
-                pl.BlockSpec((1, wide), placed)] + [state] * (2 * levels)
-    args = [bits, near, far, sib, cols, gain, *mine, *other]
+
+    def column(index):
+        return pl.BlockSpec((tokens, wide), lambda h, b: (0, index))
+
+    in_specs = [column(near[1]), column(far[1]),
+                pl.BlockSpec((TOGETHER * tokens, 16), lambda h, b, i=cols[1]: (i, 0))]
+    args = [bits, near[0], far[0], cols[0]]
+    if sib is not None:
+        in_specs.append(pl.BlockSpec((TOGETHER, HEAD_DIM, 2 * HEAD_DIM), lambda h, b, i=sib[1]: (i, 0, 0)))
+        args.append(sib[0])
+    in_specs += [state] * (2 * len(slots))
+    args += [*mine, *other]
     aliases = {}
-    if before is not None:
-        aliases = {len(args): 0}
-        args.append(before)
-        in_specs.append(pl.BlockSpec(memory_space=pl.ANY))
+    if gain is not None:
+        in_specs.append(pl.BlockSpec((1, wide), lambda h, b: (0, pair)))
+        args.append(gain)
+        if before is not None:
+            aliases = {len(args): 0}
+            args.append(before)
+            in_specs.append(pl.BlockSpec(memory_space=pl.ANY))
+        out_specs = column(pair)
+        out_shape = jax.ShapeDtypeStruct((tokens, gain.shape[1]), BF16)
+    else:
+        out_specs = [column(0)] + ([column(0)] if sib is not None else [])
+        out_shape = [jax.ShapeDtypeStruct((tokens, wide), F32)]
+        out_shape += [jax.ShapeDtypeStruct((tokens, wide), BF16)] if sib is not None else []
     return pl.pallas_call(
-        functools.partial(final_kernel, levels),
+        functools.partial(read_kernel, side, sib is not None, slots, gain is not None),
         grid_spec=pltpu.PrefetchScalarGridSpec(
-            num_scalar_prefetch=1,
-            grid=(steps,),
-            in_specs=in_specs,
-            out_specs=pl.BlockSpec((tokens, wide), placed),
-        ),
-        out_shape=jax.ShapeDtypeStruct((tokens, CHUNKS * width), BF16),
+            num_scalar_prefetch=1, grid=(1,), in_specs=in_specs, out_specs=out_specs),
+        out_shape=out_shape,
         input_output_aliases=aliases,
-        compiler_params=pltpu.CompilerParams(vmem_limit_bytes=20 << 20),
-        cost_estimate=pl.CostEstimate(flops=3000000000, bytes_accessed=8 << 20, transcendentals=0),
-        name=f"final{chunk}",
+        compiler_params=pltpu.CompilerParams(vmem_limit_bytes=8 << 20),
+        cost_estimate=pl.CostEstimate(flops=1200000000, bytes_accessed=2 << 20, transcendentals=0),
     )(*args)
 
 
 def partner(value, bit):
     size = lax.axis_size("seq")
     return lax.ppermute(value, "seq", [(i, i ^ (1 << bit)) for i in range(size)])
+
+
+def order_pieces():
+    return [p for i in range(PIECES) for p in (i, PIECES + i)]
 
 
 def project(z, out_weight):
@@ -361,13 +387,21 @@
         w = out_weight[:, piece * cols:(piece + 1) * cols]
         return jnp.dot(part, w, preferred_element_type=F32).astype(BF16)
 
-    order = [p for i in range(PIECES) for p in (i, PIECES + i)]
-    sums = {p: term(me + size - 1 if p < PIECES else me + 1, p) for p in order}
+    order = order_pieces()
+    sums = {}
+    for p in order:
+        sums[p] = term(me + size - 1 if p < PIECES else me + 1, p)
+    last = None
     for s in range(size - 1):
-        got = {p: lax.ppermute(sums[p], "head", up if p < PIECES else down) for p in order}
-        own = {p: lax.optimization_barrier(
-            term(me + 2 * size - 2 - s if p < PIECES else me + 2 + s, p)) for p in order}
-        sums = {p: (got[p].astype(F32) + own[p].astype(F32)).astype(BF16) for p in order}
+        got, own = {}, {}
+        for p in order:
+            got[p] = lax.ppermute(sums[p], "head", up if p < PIECES else down)
+            own[p] = term(me + 2 * size - 2 - s if p < PIECES else me + 2 + s, p)
+        for p in order:
+            keep = (own[p],) if last is None else (own[p], last)
+            mine = lax.optimization_barrier(keep)[0]
+            last = (got[p].astype(F32) + mine.astype(F32)).astype(BF16)
+            sums[p] = last
     return jnp.concatenate([sums[p] for p in range(2 * PIECES)], axis=1)
 
 
@@ -380,12 +414,29 @@
     gain = norm_gain.reshape(1, -1)
     wide = jax.ShapeDtypeStruct((mine_heads, HEAD_DIM, 2 * HEAD_DIM), BF16)
     square = jax.ShapeDtypeStruct((mine_heads, HEAD_DIM, HEAD_DIM), BF16)
-    local, sibs, curs = [], [], []
-    for chunk in range(CHUNKS):
-        local.append(local_part(chunk, doc_start, queries, keys, values, log_decay, beta, level_weights))
-        mine = local[chunk][2]
-        sibs.append(partner(mine, 0))
-        curs.append(small_call(pair_kernel, bits, [mine, sibs[chunk]], [wide], f"pair{chunk}")[0])
+    in_hbm = lambda x: pltpu.with_memory_space_constraint(x, pltpu.HBM)
+    given = [in_hbm(x) for x in (queries, keys, values, log_decay, beta, level_weights)]
+    doc_start = in_hbm(doc_start)
+
+    def local(base, stride, steps, flags):
+        near, far, maps, cols = local_part(base, stride, steps, flags, *given)
+        return in_hbm(near), in_hbm(far), maps, in_hbm(cols), partner(maps, 0)
+
+    front = local(0, CHUNKS, 2, doc_start)
+    low = local(1, CHUNKS, 1, doc_start)
+    cur = small_call(pair_kernel, bits, [front[2], front[4]], [wide])[0]
+    flags = lax.optimization_barrier((doc_start, cur))[0]
+    high = local(3, CHUNKS, 1, flags)
+    settled = lax.optimization_barrier((bits, high[2]))[0]
+    curs = [cur, small_call(pair_kernel, bits, [low[2], high[2], low[4], high[4]], [wide])[0]]
+    where = [[(front, 0), (front, 1)], [(low, 0), (high, 0)]]
+    parts = [(c, h) for c in range(CHUNKS) for h in range(2)]
+    nears, fars, colss = {}, {}, {}
+    for c, h in parts:
+        (near, far, _, cols, sib), i = where[c][h]
+        colss[c, h] = (cols, i)
+        near, far = read_part(settled, h, 2 * h + c, (near, i), (far, i), (cols, i), sib=(sib, i))
+        nears[c, h], fars[c, h] = (near, 0), (far, 0)
     carried = [None] * CHUNKS
     states = [[] for _ in range(CHUNKS)]
     others = [[] for _ in range(CHUNKS)]
@@ -395,18 +446,22 @@
                 sib = partner(curs[c], level)
                 args = [sib, curs[c]] if level == 1 else [sib, curs[c], carried[c]]
                 curs[c], x, carried[c] = small_call(
-                    functools.partial(level_kernel, level), bits, args, [wide, square, square],
-                    f"level{level}{c}")
+                    functools.partial(level_kernel, level), bits, args, [wide, square, square])
             else:
                 sib = partner(curs[c][:, :, :HEAD_DIM], level)
-                x = small_call(functools.partial(top_kernel, level), bits, [sib, carried[c]], [square],
-                               f"top{c}")[0]
+                x = small_call(functools.partial(top_kernel, level), bits, [sib, carried[c]], [square])[0]
             states[c].append(x)
             others[c].append(partner(x, 0))
     z = None
-    for c in range(CHUNKS):
-        near, far, _, cols = local[c]
-        z = final_part(c, bits, near, far, sibs[c], cols, gain, states[c], others[c], z)
+    early = (nbits - 1) // 2
+    for c, h in parts:
+        near = read_part(bits, h, 2 * h + c, nears[c, h], fars[c, h], colss[c, h],
+                         slots=tuple(range(1, early + 1)), mine=states[c][:early], other=others[c][:early])[0]
+        nears[c, h] = (near, 0)
+    for c, h in parts:
+        z = read_part(bits, h, 2 * h + c, nears[c, h], fars[c, h], colss[c, h],
+                      slots=tuple(range(early + 1, nbits)), mine=states[c][early:], other=others[c][early:],
+                      gain=gain, before=z)
     return project(z, out_weight)
 
 

time: 119 us -> 126 us (1.059)
  the two profiles are of different devices: /device:TPU:28 before, /device:TPU:1 now
where the time goes in v2:
time: 126 us; the launch traced here: 125 us
  Pallas kernels  50.9 us (40%)
  starting transfers between devices  38.7 us (31%)
  waiting for transfers between devices  20.1 us (16%)
  matrix products  7.14 us (6%)
  local copies, waits for them, and re-layouts  5.66 us (4%)
  other arithmetic  1.85 us (1%)
    pallas_call x12, Pallas kernels, read_part(): pl.pallas_call(functools.partial(read_kernel, side, sib is not None, slot...  25.4 us
    ppermute x19, starting transfers between devices, partner(): return lax.ppermute(value, 'seq', [(i, i ^ 1 << bit) for i in range(size)])  21.9 us
    ppermute x12, waiting for transfers between devices, project(): got[p] = lax.ppermute(sums[p], 'head', up if p < PIECES else down)  19.3 us
    pallas_call x3, Pallas kernels, local_part(): pl.pallas_call(functools.partial(local_kernel, base, stride), grid_spec=p...  18.7 us
    ppermute x12, starting transfers between devices, project(): got[p] = lax.ppermute(sums[p], 'head', up if p < PIECES else down)  16.8 us
    dot_general x16, matrix products, term(): return jnp.dot(part, w, preferred_element_type=F32).astype(BF16)  7.14 us
    pallas_call x10, Pallas kernels, small_call(): pl.pallas_call(kernel, grid_spec=pltpu.PrefetchScalarGridSpec(num_scalar_...  6.9 us
    unnamed x24, local copies, waits for them, and re-layouts  5.56 us
  transfers between devices with their start and end apart: 31, of which 7 were waited for; matrix products, arithmetic and copies ran while one was open for 1% of the time, Pallas kernels for 30%

profile of v2, /device:TPU:1, one launch (start us, length us, event | category | flops | bytes accessed | tf_op | source)
XLA Modules:
  0.0 125.1 jit_solution(15521578395278836240)
XLA Ops:
  0.0 8.5 %shard_map.91 = (f32[512,512]{1,0:T(8,128)S(1)}, bf16[512,512]{1,0:T(8,128)(2,1)S(1)}, bf16[4,128,256]{2,1,0:T(8,128)(2,1)S(1)}, f32[2048,16]{1,0:T(8,128)S(1)}) custom-call(s32[8]{0:T(128)} %flags.4, bf16[512,1024]{1,0:T(8,128)(2,1)} %q_ref.5, bf16[512,1024]{1,0:T(8,128)(2,1)} %k_ref.5, bf16[512,1024]{1,0:T(8,128)(2,1)} %v_ref.5, f32[8,512]{1,0:T(8,128)} %log_ref.5, ...), custom_call_target="tpu_custom_call" | custom-call | flops 6000000000 | bytes 8388608 | tf_op jit(solution)/shard_map/pallas_call | solution.py:171
  8.6 1.0 copy-done.4
  9.5 0.8 copy-done.5
  10.3 1.4 %collective-permute-start = (bf16[4,128,256]{2,1,0:T(8,128)(2,1)S(1)}, bf16[4,128,256]{2,1,0:T(8,128)(2,1)S(1)}, u32[]{:S(2)}, u32[]{:S(2)}) collective-permute-start(bf16[4,128,256]{2,1,0:T(8,128)(2,1)S(1)} %get-tuple-element.56.refs_0_), channel_id=1, source_target_pairs={{0,4},{4,0},{8,12},{12,8},{16,20},{20,16},{24,28},{28,24},{32,36},... | collective-permute-start | bytes 786440 | tf_op jit(solution)/shard_map/ppermute | solution.py:370
  11.7 5.1 %shard_map.95 = (f32[512,256]{1,0:T(8,128)S(1)}, bf16[512,256]{1,0:T(8,128)(2,1)S(1)}, bf16[2,128,256]{2,1,0:T(8,128)(2,1)S(1)}, f32[1024,16]{1,0:T(8,128)S(1)}) custom-call(s32[8]{0:T(128)} %flags.4, bf16[512,1024]{1,0:T(8,128)(2,1)} %q_ref.5, bf16[512,1024]{1,0:T(8,128)(2,1)} %k_ref.5, bf16[512,1024]{1,0:T(8,128)(2,1)} %v_ref.5, f32[8,512]{1,0:T(8,128)} %log_ref.5, ...), custom_call_target="tpu_custom_call" | custom-call | flops 3000000000 | bytes 8388608 | tf_op jit(solution)/shard_map/pallas_call | solution.py:171
  16.8 0.8 copy-done.2
  17.6 0.8 copy-done.6
  19.9 1.4 %collective-permute-start.11 = (bf16[2,128,256]{2,1,0:T(8,128)(2,1)S(1)}, bf16[2,128,256]{2,1,0:T(8,128)(2,1)S(1)}, u32[]{:S(2)}, u32[]{:S(2)}) collective-permute-start(bf16[2,128,256]{2,1,0:T(8,128)(2,1)S(1)} %shard_map.92.refs_1_), channel_id=1, source_target_pairs={{0,8},{4,12},{8,0},{12,4},{16,24},{20,28},{24,16},{28,20},{32,40},... | collective-permute-start | bytes 393224 | tf_op jit(solution)/shard_map/ppermute | solution.py:370
  21.3 5.1 %shard_map.93 = (f32[512,256]{1,0:T(8,128)S(1)}, bf16[512,256]{1,0:T(8,128)(2,1)S(1)}, bf16[2,128,256]{2,1,0:T(8,128)(2,1)S(1)}, f32[1024,16]{1,0:T(8,128)S(1)}) custom-call(s32[8]{0:T(128)} %flags.4, bf16[512,1024]{1,0:T(8,128)(2,1)} %q_ref.5, bf16[512,1024]{1,0:T(8,128)(2,1)} %k_ref.5, bf16[512,1024]{1,0:T(8,128)(2,1)} %v_ref.5, f32[8,512]{1,0:T(8,128)} %log_ref.5, ...), custom_call_target="tpu_custom_call" | custom-call | flops 3000000000 | bytes 8388608 | tf_op jit(solution)/shard_map/pallas_call | solution.py:171
  26.4 0.8 copy-done.7
  27.9 0.8 collective-permute-start.1
  28.7 2.1 %shard_map.110 = (f32[512,256]{1,0:T(8,128)S(1)}, bf16[512,256]{1,0:T(8,128)(2,1)S(1)}) custom-call(s32[5]{0:T(128)S(1)} %stack.23.bits, f32[512,512]{1,0:T(8,128)} %copy-done.4, bf16[512,512]{1,0:T(8,128)(2,1)} %copy-done.5, f32[2048,16]{1,0:T(8,128)} %copy-done.1, bf16[4,128,256]{2,1,0:T(8,128)(2,1)S(1)} %collective-permute-done.refs_1_.refs_0_), custom_call_target="tpu_custom_call" | custom-call | flops 1200000000 | bytes 2097152 | tf_op jit(solution)/shard_map/pallas_call | solution.py:357
  30.8 2.1 %shard_map.104 = (f32[512,256]{1,0:T(8,128)S(1)}, bf16[512,256]{1,0:T(8,128)(2,1)S(1)}) custom-call(s32[5]{0:T(128)S(1)} %stack.23.bits, f32[512,512]{1,0:T(8,128)} %copy-done.4, bf16[512,512]{1,0:T(8,128)(2,1)} %copy-done.5, f32[2048,16]{1,0:T(8,128)} %copy-done.1, bf16[4,128,256]{2,1,0:T(8,128)(2,1)S(1)} %collective-permute-done.refs_1_.refs_0_), custom_call_target="tpu_custom_call" | custom-call | flops 1200000000 | bytes 2097152 | tf_op jit(solution)/shard_map/pallas_call | solution.py:357
  32.9 0.7 shard_map.105
  33.7 2.7 %collective-permute-start.12 = (bf16[2,128,256]{2,1,0:T(8,128)(2,1)S(1)}, bf16[2,128,256]{2,1,0:T(8,128)(2,1)S(1)}, u32[]{:S(2)}, u32[]{:S(2)}) collective-permute-start(bf16[2,128,256]{2,1,0:T(8,128)(2,1)S(1)} %get-tuple-element.86.refs_1_), channel_id=1, source_target_pairs={{0,16},{4,20},{8,24},{12,28},{16,0},{20,4},{24,8},{28,12},{32,48},... | collective-permute-start | bytes 393224 | tf_op jit(solution)/shard_map/ppermute | solution.py:370
  36.4 2.1 %shard_map.102 = (f32[512,256]{1,0:T(8,128)S(1)}, bf16[512,256]{1,0:T(8,128)(2,1)S(1)}) custom-call(s32[5]{0:T(128)S(1)} %stack.23.bits, f32[512,256]{1,0:T(8,128)} %copy-done.6, bf16[512,256]{1,0:T(8,128)(2,1)} %copy-done.8, f32[1024,16]{1,0:T(8,128)} %copy-done.2, bf16[2,128,256]{2,1,0:T(8,128)(2,1)S(1)} %collective-permute-done.2.refs_2_.refs_0_), custom_call_target="tpu_custom_call" | custom-call | flops 1200000000 | bytes 2097152 | tf_op jit(solution)/shard_map/pallas_call | solution.py:357
  39.7 0.8 collective-permute-done.12.refs_0_
  41.2 1.0 collective-permute-start.14
  42.2 2.1 %shard_map.94 = (f32[512,256]{1,0:T(8,128)S(1)}, bf16[512,256]{1,0:T(8,128)(2,1)S(1)}) custom-call(s32[5]{0:T(128)S(1)} %stack.23.bits, f32[512,256]{1,0:T(8,128)} %copy-done.7, bf16[512,256]{1,0:T(8,128)(2,1)} %copy-done.9, f32[1024,16]{1,0:T(8,128)} %copy-done.3, bf16[2,128,256]{2,1,0:T(8,128)(2,1)S(1)} %collective-permute-done.1.refs_0_.refs_3_), custom_call_target="tpu_custom_call" | custom-call | flops 1200000000 | bytes 2097152 | tf_op jit(solution)/shard_map/pallas_call | solution.py:357
  44.3 1.7 %collective-permute-start.15 = (bf16[2,128,256]{2,1,0:T(8,128)(2,1)S(1)}, bf16[2,128,256]{2,1,0:T(8,128)(2,1)S(1)}, u32[]{:S(2)}, u32[]{:S(2)}) collective-permute-start(bf16[2,128,256]{2,1,0:T(8,128)(2,1)S(1)} %get-tuple-element.89.refs_1_), channel_id=1, source_target_pairs={{0,32},{4,36},{8,40},{12,44},{16,48},{20,52},{24,56},{28,60},{32,0... | collective-permute-start | bytes 393224 | tf_op jit(solution)/shard_map/ppermute | solution.py:370
  46.0 0.7 shard_map.97
  46.7 2.6 %collective-permute-start.4 = (bf16[2,128,256]{2,1,0:T(8,128)(2,1)S(1)}, bf16[2,128,256]{2,1,0:T(8,128)(2,1)S(1)}, u32[]{:S(2)}, u32[]{:S(2)}) collective-permute-start(bf16[2,128,256]{2,1,0:T(8,128)(2,1)S(1)} %get-tuple-element.67.refs_1_), channel_id=1, source_target_pairs={{0,16},{4,20},{8,24},{12,28},{16,0},{20,4},{24,8},{28,12},{32,48},... | collective-permute-start | bytes 393224 | tf_op jit(solution)/shard_map/ppermute | solution.py:370
  49.9 2.0 %shard_map.111.near_ref = f32[512,256]{1,0:T(8,128)S(1)} custom-call(s32[5]{0:T(128)S(1)} %stack.23.bits, f32[512,256]{1,0:T(8,128)S(1)} %get-tuple-element.94.near_ref, bf16[512,256]{1,0:T(8,128)(2,1)S(1)} %get-tuple-element.95.far_ref, f32[2048,16]{1,0:T(8,128)} %copy-done.1, bf16[2,128,128]{2,1,0:T(8,128)(2,1)S(1)} %get-tuple-element.85.refs_0_, ...), custom_call_target="tpu_custom_call" | custom-call | flops 1200000000 | bytes 2097152 | tf_op jit(solution)/shard_map/pallas_call | solution.py:357
  52.6 3.4 %collective-permute-start.16 = (bf16[2,128,128]{2,1,0:T(8,128)(2,1)S(1)}, bf16[2,128,128]{2,1,0:T(8,128)(2,1)S(1)}, u32[]{:S(2)}, u32[]{:S(2)}) collective-permute-start(bf16[2,128,128]{2,1,0:T(8,128)(2,1)S(1)} %slice.13), channel_id=1, source_target_pairs={{0,64},{4,68},{8,72},{12,76},{16,80},{20,84},{24,88},{28,92},{32,9... | collective-permute-start | bytes 196616 | tf_op jit(solution)/shard_map/ppermute | solution.py:370
  57.1 2.0 %shard_map.107.near_ref = f32[512,256]{1,0:T(8,128)S(1)} custom-call(s32[5]{0:T(128)S(1)} %stack.23.bits, f32[512,256]{1,0:T(8,128)S(1)} %get-tuple-element.83.near_ref, bf16[512,256]{1,0:T(8,128)(2,1)S(1)} %get-tuple-element.84.far_ref, f32[2048,16]{1,0:T(8,128)} %copy-done.1, bf16[2,128,128]{2,1,0:T(8,128)(2,1)S(1)} %get-tuple-element.85.refs_0_, ...), custom_call_target="tpu_custom_call" | custom-call | flops 1200000000 | bytes 2097152 | tf_op jit(solution)/shard_map/pallas_call | solution.py:357
  60.3 2.0 %shard_map.103.near_ref = f32[512,256]{1,0:T(8,128)S(1)} custom-call(s32[5]{0:T(128)S(1)} %stack.23.bits, f32[512,256]{1,0:T(8,128)S(1)} %get-tuple-element.78.near_ref, bf16[512,256]{1,0:T(8,128)(2,1)S(1)} %get-tuple-element.79.far_ref, f32[1024,16]{1,0:T(8,128)} %copy-done.2, bf16[2,128,128]{2,1,0:T(8,128)(2,1)S(1)} %get-tuple-element.66.refs_0_, ...), custom_call_target="tpu_custom_call" | custom-call | flops 1200000000 | bytes 2097152 | tf_op jit(solution)/shard_map/pallas_call | solution.py:357
  62.3 2.0 %shard_map.99.near_ref = f32[512,256]{1,0:T(8,128)S(1)} custom-call(s32[5]{0:T(128)S(1)} %stack.23.bits, f32[512,256]{1,0:T(8,128)S(1)} %get-tuple-element.63.near_ref, bf16[512,256]{1,0:T(8,128)(2,1)S(1)} %get-tuple-element.64.far_ref, f32[1024,16]{1,0:T(8,128)} %copy-done.3, bf16[2,128,128]{2,1,0:T(8,128)(2,1)S(1)} %get-tuple-element.66.refs_0_, ...), custom_call_target="tpu_custom_call" | custom-call | flops 1200000000 | bytes 2097152 | tf_op jit(solution)/shard_map/pallas_call | solution.py:357
  64.3 0.7 shard_map.100
  65.1 2.5 %collective-permute-start.8 = (bf16[2,128,128]{2,1,0:T(8,128)(2,1)S(1)}, bf16[2,128,128]{2,1,0:T(8,128)(2,1)S(1)}, u32[]{:S(2)}, u32[]{:S(2)}) collective-permute-start(bf16[2,128,128]{2,1,0:T(8,128)(2,1)S(1)} %slice.12), channel_id=1, source_target_pairs={{0,64},{4,68},{8,72},{12,76},{16,80},{20,84},{24,88},{28,92},{32,9... | collective-permute-start | bytes 196616 | tf_op jit(solution)/shard_map/ppermute | solution.py:370
  67.6 2.2 %shard_map.112.refs_5_ = bf16[512,1024]{1,0:T(8,128)(2,1)S(1)} custom-call(s32[5]{0:T(128)S(1)} %stack.23.bits, f32[512,256]{1,0:T(8,128)S(1)} %shard_map.111.near_ref, bf16[512,256]{1,0:T(8,128)(2,1)S(1)} %get-tuple-element.95.far_ref, f32[2048,16]{1,0:T(8,128)} %copy-done.1, bf16[2,128,128]{2,1,0:T(8,128)(2,1)S(1)} %get-tuple-element.91.refs_0_, ...), custom_call_target="tpu_custom_call" | custom-call | flops 1200000000 | bytes 2097152 | tf_op jit(solution)/shard_map/pallas_call | solution.py:357
  70.8 2.0 %collective-permute-start.10 = (bf16[2,128,128]{2,1,0:T(8,128)(2,1)S(1)}, bf16[2,128,128]{2,1,0:T(8,128)(2,1)S(1)}, u32[]{:S(2)}, u32[]{:S(2)}) collective-permute-start(bf16[2,128,128]{2,1,0:T(8,128)(2,1)S(1)} %shard_map.101.refs_1_), channel_id=1, source_target_pairs={{0,4},{4,0},{8,12},{12,8},{16,20},{20,16},{24,28},{28,24},{32,36},... | collective-permute-start | bytes 196616 | tf_op jit(solution)/shard_map/ppermute | solution.py:370
  72.8 2.2 %shard_map.113.refs_5_ = bf16[512,1024]{1,0:T(8,128)(2,1)S(1)} custom-call(s32[5]{0:T(128)S(1)} %stack.23.bits, f32[512,256]{1,0:T(8,128)S(1)} %shard_map.107.near_ref, bf16[512,256]{1,0:T(8,128)(2,1)S(1)} %get-tuple-element.84.far_ref, f32[2048,16]{1,0:T(8,128)} %copy-done.1, ...), custom_call_target="tpu_custom_call", output_to_operand_aliasing={{}: (9, {})} | custom-call | flops 1200000000 | bytes 2097152 | tf_op jit(solution)/shard_map/pallas_call | solution.py:357
  75.0 2.5 %shard_map.114.refs_5_ = bf16[512,1024]{1,0:T(8,128)(2,1)S(1)} custom-call(s32[5]{0:T(128)S(1)} %stack.23.bits, f32[512,256]{1,0:T(8,128)S(1)} %shard_map.103.near_ref, bf16[512,256]{1,0:T(8,128)(2,1)S(1)} %get-tuple-element.79.far_ref, f32[1024,16]{1,0:T(8,128)} %copy-done.2, ...), custom_call_target="tpu_custom_call", output_to_operand_aliasing={{}: (9, {})} | custom-call | flops 1200000000 | bytes 2097152 | tf_op jit(solution)/shard_map/pallas_call | solution.py:357
  77.5 2.2 %shard_map.115 = bf16[512,1024]{1,0:T(8,128)(2,1)S(1)} custom-call(s32[5]{0:T(128)S(1)} %stack.23.bits, f32[512,256]{1,0:T(8,128)S(1)} %shard_map.99.near_ref, bf16[512,256]{1,0:T(8,128)(2,1)S(1)} %get-tuple-element.64.far_ref, f32[1024,16]{1,0:T(8,128)} %copy-done.3, ...), custom_call_target="tpu_custom_call", output_to_operand_aliasing={{}: (9, {})} | custom-call | flops 1200000000 | bytes 2097152 | tf_op jit(solution)/shard_map/pallas_call | solution.py:357
  86.5 1.4 %collective-permute-start.19 = (bf16[128,1024]{1,0:T(8,128)(2,1)S(1)}, bf16[128,1024]{1,0:T(8,128)(2,1)S(1)}, u32[]{:S(2)}, u32[]{:S(2)}) collective-permute-start(bf16[128,1024]{1,0:T(8,128)(2,1)S(1)} %fusion.32), channel_id=1, source_target_pairs={{0,1},{1,2},{2,3},{3,0},{4,5},{5,6},{6,7},{7,4},{8,9},{9,10},{10,1... | collective-permute-start | bytes 786440 | tf_op jit(solution)/shard_map/ppermute | solution.py:398
  87.9 1.5 %collective-permute-start.23 = (bf16[128,1024]{1,0:T(8,128)(2,1)S(1)}, bf16[128,1024]{1,0:T(8,128)(2,1)S(1)}, u32[]{:S(2)}, u32[]{:S(2)}) collective-permute-start(bf16[128,1024]{1,0:T(8,128)(2,1)S(1)} %fusion.68), channel_id=1, source_target_pairs={{0,3},{1,0},{2,1},{3,2},{4,7},{5,4},{6,5},{7,6},{8,11},{9,8},{10,9... | collective-permute-start | bytes 786440 | tf_op jit(solution)/shard_map/ppermute | solution.py:398
  89.9 2.7 %collective-permute-start.21 = (bf16[128,1024]{1,0:T(8,128)(2,1)S(1)}, bf16[128,1024]{1,0:T(8,128)(2,1)S(1)}, u32[]{:S(2)}, u32[]{:S(2)}) collective-permute-start(bf16[128,1024]{1,0:T(8,128)(2,1)S(1)} %fusion.44), channel_id=1, source_target_pairs={{0,3},{1,0},{2,1},{3,2},{4,7},{5,4},{6,5},{7,6},{8,11},{9,8},{10,9... | collective-permute-start | bytes 786440 | tf_op jit(solution)/shard_map/ppermute | solution.py:398
  92.6 3.2 %collective-permute-done.19 = bf16[128,1024]{1,0:T(8,128)(2,1)S(1)} collective-permute-done((bf16[128,1024]{1,0:T(8,128)(2,1)S(1)}, bf16[128,1024]{1,0:T(8,128)(2,1)S(1)}, u32[]{:S(2)}, u32[]{:S(2)}) %collective-permute-start.19) | collective-permute-done | bytes 262176 | tf_op jit(solution)/shard_map/ppermute | solution.py:398
  96.0 2.7 %collective-permute-start.27 = (bf16[128,1024]{1,0:T(8,128)(2,1)S(1)}, bf16[128,1024]{1,0:T(8,128)(2,1)S(1)}, u32[]{:S(2)}, u32[]{:S(2)}) collective-permute-start(bf16[128,1024]{1,0:T(8,128)(2,1)S(1)} %add_convert_fusion.10), channel_id=1, source_target_pairs={{0,3},{1,0},{2,1},{3,2},{4,7},{5,4},{6,5},{7,6},{8,11},{9,8},{10,9... | collective-permute-start | bytes 786440 | tf_op jit(solution)/shard_map/ppermute | solution.py:398
  98.7 2.7 %collective-permute-done.22 = bf16[128,1024]{1,0:T(8,128)(2,1)S(1)} collective-permute-done((bf16[128,1024]{1,0:T(8,128)(2,1)S(1)}, bf16[128,1024]{1,0:T(8,128)(2,1)S(1)}, u32[]{:S(2)}, u32[]{:S(2)}) %collective-permute-start.22) | collective-permute-done | bytes 262176 | tf_op jit(solution)/shard_map/ppermute | solution.py:398
  101.6 2.7 %collective-permute-start.25 = (bf16[128,1024]{1,0:T(8,128)(2,1)S(1)}, bf16[128,1024]{1,0:T(8,128)(2,1)S(1)}, u32[]{:S(2)}, u32[]{:S(2)}) collective-permute-start(bf16[128,1024]{1,0:T(8,128)(2,1)S(1)} %add_convert_fusion.8), channel_id=1, source_target_pairs={{0,3},{1,0},{2,1},{3,2},{4,7},{5,4},{6,5},{7,6},{8,11},{9,8},{10,9... | collective-permute-start | bytes 786440 | tf_op jit(solution)/shard_map/ppermute | solution.py:398
  104.3 2.7 %collective-permute-done.20 = bf16[128,1024]{1,0:T(8,128)(2,1)S(1)} collective-permute-done((bf16[128,1024]{1,0:T(8,128)(2,1)S(1)}, bf16[128,1024]{1,0:T(8,128)(2,1)S(1)}, u32[]{:S(2)}, u32[]{:S(2)}) %collective-permute-start.20) | collective-permute-done | bytes 262176 | tf_op jit(solution)/shard_map/ppermute | solution.py:398
  107.2 2.7 %collective-permute-start.29 = (bf16[128,1024]{1,0:T(8,128)(2,1)S(1)}, bf16[128,1024]{1,0:T(8,128)(2,1)S(1)}, u32[]{:S(2)}, u32[]{:S(2)}) collective-permute-start(bf16[128,1024]{1,0:T(8,128)(2,1)S(1)} %add_convert_fusion.6), channel_id=1, source_target_pairs={{0,3},{1,0},{2,1},{3,2},{4,7},{5,4},{6,5},{7,6},{8,11},{9,8},{10,9... | collective-permute-start | bytes 786440 | tf_op jit(solution)/shard_map/ppermute | solution.py:398
  110.0 2.7 %collective-permute-done.26 = bf16[128,1024]{1,0:T(8,128)(2,1)S(1)} collective-permute-done((bf16[128,1024]{1,0:T(8,128)(2,1)S(1)}, bf16[128,1024]{1,0:T(8,128)(2,1)S(1)}, u32[]{:S(2)}, u32[]{:S(2)}) %collective-permute-start.26) | collective-permute-done | bytes 262176 | tf_op jit(solution)/shard_map/ppermute | solution.py:398
  112.9 2.7 %collective-permute-start.30 = (bf16[128,1024]{1,0:T(8,128)(2,1)S(1)}, bf16[128,1024]{1,0:T(8,128)(2,1)S(1)}, u32[]{:S(2)}, u32[]{:S(2)}) collective-permute-start(bf16[128,1024]{1,0:T(8,128)(2,1)S(1)} %add_convert_fusion.4), channel_id=1, source_target_pairs={{0,3},{1,0},{2,1},{3,2},{4,7},{5,4},{6,5},{7,6},{8,11},{9,8},{10,9... | collective-permute-start | bytes 786440 | tf_op jit(solution)/shard_map/ppermute | solution.py:398
  115.6 2.7 %collective-permute-done.24 = bf16[128,1024]{1,0:T(8,128)(2,1)S(1)} collective-permute-done((bf16[128,1024]{1,0:T(8,128)(2,1)S(1)}, bf16[128,1024]{1,0:T(8,128)(2,1)S(1)}, u32[]{:S(2)}, u32[]{:S(2)}) %collective-permute-start.24) | collective-permute-done | bytes 262176 | tf_op jit(solution)/shard_map/ppermute | solution.py:398
  118.4 5.5 %collective-permute-done.28 = bf16[128,1024]{1,0:T(8,128)(2,1)S(1)} collective-permute-done((bf16[128,1024]{1,0:T(8,128)(2,1)S(1)}, bf16[128,1024]{1,0:T(8,128)(2,1)S(1)}, u32[]{:S(2)}, u32[]{:S(2)}) %collective-permute-start.28) | collective-permute-done | bytes 262176 | tf_op jit(solution)/shard_map/ppermute | solution.py:398
  124.0 1.0 pad_maximum_fusion
  (96 shorter events, 17.1 us)
Async XLA Ops:
  8.6 1.0 copy-start.4
  9.5 0.8 copy-start.5
  10.3 6.5 %copy-start.1 = (f32[2048,16]{1,0:T(8,128)}, f32[2048,16]{1,0:T(8,128)S(1)}, u32[]{:S(2)}) copy-start(f32[2048,16]{1,0:T(8,128)S(1)} %get-tuple-element.82.cols_ref) | copy-start | bytes 393220
  10.3 8.9 %collective-permute-start = (bf16[4,128,256]{2,1,0:T(8,128)(2,1)S(1)}, bf16[4,128,256]{2,1,0:T(8,128)(2,1)S(1)}, u32[]{:S(2)}, u32[]{:S(2)}) collective-permute-start(bf16[4,128,256]{2,1,0:T(8,128)(2,1)S(1)} %get-tuple-element.56.refs_0_), channel_id=1, source_target_pairs={{0,4},{4,0},{8,12},{12,8},{16,20},{20,16},{24,28},{28,24},{32,36},... | collective-permute-start | bytes 786440 | tf_op jit(solution)/shard_map/ppermute | solution.py:370
  16.8 0.8 copy-start.2
  17.6 0.8 copy-start.6
  18.4 0.7 copy-start.8
  19.1 17.3 %collective-permute-start.2 = (bf16[2,128,256]{2,1,0:T(8,128)(2,1)S(1)}, bf16[2,128,256]{2,1,0:T(8,128)(2,1)S(1)}, u32[]{:S(2)}, u32[]{:S(2)}) collective-permute-start(bf16[2,128,256]{2,1,0:T(8,128)(2,1)S(1)} %get-tuple-element.65.refs_0_), channel_id=1, source_target_pairs={{0,4},{4,0},{8,12},{12,8},{16,20},{20,16},{24,28},{28,24},{32,36},... | collective-permute-start | bytes 393224 | tf_op jit(solution)/shard_map/ppermute | solution.py:370
  19.9 13.0 %collective-permute-start.11 = (bf16[2,128,256]{2,1,0:T(8,128)(2,1)S(1)}, bf16[2,128,256]{2,1,0:T(8,128)(2,1)S(1)}, u32[]{:S(2)}, u32[]{:S(2)}) collective-permute-start(bf16[2,128,256]{2,1,0:T(8,128)(2,1)S(1)} %shard_map.92.refs_1_), channel_id=1, source_target_pairs={{0,8},{4,12},{8,0},{12,4},{16,24},{20,28},{24,16},{28,20},{32,40},... | collective-permute-start | bytes 393224 | tf_op jit(solution)/shard_map/ppermute | solution.py:370
  26.4 0.8 copy-start.7
  27.2 0.7 copy-start.9
  27.9 2.9 %copy-start.3 = (f32[1024,16]{1,0:T(8,128)}, f32[1024,16]{1,0:T(8,128)S(1)}, u32[]{:S(2)}) copy-start(f32[1024,16]{1,0:T(8,128)S(1)} %get-tuple-element.62.cols_ref) | copy-start | bytes 196612
  27.9 11.0 %collective-permute-start.1 = (bf16[2,128,256]{2,1,0:T(8,128)(2,1)S(1)}, bf16[2,128,256]{2,1,0:T(8,128)(2,1)S(1)}, u32[]{:S(2)}, u32[]{:S(2)}) collective-permute-start(bf16[2,128,256]{2,1,0:T(8,128)(2,1)S(1)} %get-tuple-element.58.refs_1_), channel_id=1, source_target_pairs={{0,4},{4,0},{8,12},{12,8},{16,20},{20,16},{24,28},{28,24},{32,36},... | collective-permute-start | bytes 393224 | tf_op jit(solution)/shard_map/ppermute | solution.py:370
  33.7 6.8 %collective-permute-start.12 = (bf16[2,128,256]{2,1,0:T(8,128)(2,1)S(1)}, bf16[2,128,256]{2,1,0:T(8,128)(2,1)S(1)}, u32[]{:S(2)}, u32[]{:S(2)}) collective-permute-start(bf16[2,128,256]{2,1,0:T(8,128)(2,1)S(1)} %get-tuple-element.86.refs_1_), channel_id=1, source_target_pairs={{0,16},{4,20},{8,24},{12,28},{16,0},{20,4},{24,8},{28,12},{32,48},... | collective-permute-start | bytes 393224 | tf_op jit(solution)/shard_map/ppermute | solution.py:370
  38.5 11.4 %collective-permute-start.13 = (bf16[2,128,128]{2,1,0:T(8,128)(2,1)S(1)}, bf16[2,128,128]{2,1,0:T(8,128)(2,1)S(1)}, u32[]{:S(2)}, u32[]{:S(2)}) collective-permute-start(bf16[2,128,128]{2,1,0:T(8,128)(2,1)S(1)} %get-tuple-element.85.refs_0_), channel_id=1, source_target_pairs={{0,4},{4,0},{8,12},{12,8},{16,20},{20,16},{24,28},{28,24},{32,36},... | collective-permute-start | bytes 196616 | tf_op jit(solution)/shard_map/ppermute | solution.py:370
  39.6 6.4 %collective-permute-start.3 = (bf16[2,128,256]{2,1,0:T(8,128)(2,1)S(1)}, bf16[2,128,256]{2,1,0:T(8,128)(2,1)S(1)}, u32[]{:S(2)}, u32[]{:S(2)}) collective-permute-start(bf16[2,128,256]{2,1,0:T(8,128)(2,1)S(1)} %shard_map.96.refs_1_), channel_id=1, source_target_pairs={{0,8},{4,12},{8,0},{12,4},{16,24},{20,28},{24,16},{28,20},{32,40},... | collective-permute-start | bytes 393224 | tf_op jit(solution)/shard_map/ppermute | solution.py:370
  41.2 8.7 %collective-permute-start.14 = (bf16[2,128,128]{2,1,0:T(8,128)(2,1)S(1)}, bf16[2,128,128]{2,1,0:T(8,128)(2,1)S(1)}, u32[]{:S(2)}, u32[]{:S(2)}) collective-permute-start(bf16[2,128,128]{2,1,0:T(8,128)(2,1)S(1)} %get-tuple-element.88.refs_1_), channel_id=1, source_target_pairs={{0,4},{4,0},{8,12},{12,8},{16,20},{20,16},{24,28},{28,24},{32,36},... | collective-permute-start | bytes 196616 | tf_op jit(solution)/shard_map/ppermute | solution.py:370
  44.3 7.6 %collective-permute-start.15 = (bf16[2,128,256]{2,1,0:T(8,128)(2,1)S(1)}, bf16[2,128,256]{2,1,0:T(8,128)(2,1)S(1)}, u32[]{:S(2)}, u32[]{:S(2)}) collective-permute-start(bf16[2,128,256]{2,1,0:T(8,128)(2,1)S(1)} %get-tuple-element.89.refs_1_), channel_id=1, source_target_pairs={{0,32},{4,36},{8,40},{12,44},{16,48},{20,52},{24,56},{28,60},{32,0... | collective-permute-start | bytes 393224 | tf_op jit(solution)/shard_map/ppermute | solution.py:370
  46.7 9.3 %collective-permute-start.4 = (bf16[2,128,256]{2,1,0:T(8,128)(2,1)S(1)}, bf16[2,128,256]{2,1,0:T(8,128)(2,1)S(1)}, u32[]{:S(2)}, u32[]{:S(2)}) collective-permute-start(bf16[2,128,256]{2,1,0:T(8,128)(2,1)S(1)} %get-tuple-element.67.refs_1_), channel_id=1, source_target_pairs={{0,16},{4,20},{8,24},{12,28},{16,0},{20,4},{24,8},{28,12},{32,48},... | collective-permute-start | bytes 393224 | tf_op jit(solution)/shard_map/ppermute | solution.py:370
  49.3 11.0 %collective-permute-start.5 = (bf16[2,128,128]{2,1,0:T(8,128)(2,1)S(1)}, bf16[2,128,128]{2,1,0:T(8,128)(2,1)S(1)}, u32[]{:S(2)}, u32[]{:S(2)}) collective-permute-start(bf16[2,128,128]{2,1,0:T(8,128)(2,1)S(1)} %get-tuple-element.66.refs_0_), channel_id=1, source_target_pairs={{0,4},{4,0},{8,12},{12,8},{16,20},{20,16},{24,28},{28,24},{32,36},... | collective-permute-start | bytes 196616 | tf_op jit(solution)/shard_map/ppermute | solution.py:370
  52.6 6.8 %collective-permute-start.16 = (bf16[2,128,128]{2,1,0:T(8,128)(2,1)S(1)}, bf16[2,128,128]{2,1,0:T(8,128)(2,1)S(1)}, u32[]{:S(2)}, u32[]{:S(2)}) collective-permute-start(bf16[2,128,128]{2,1,0:T(8,128)(2,1)S(1)} %slice.13), channel_id=1, source_target_pairs={{0,64},{4,68},{8,72},{12,76},{16,80},{20,84},{24,88},{28,92},{32,9... | collective-permute-start | bytes 196616 | tf_op jit(solution)/shard_map/ppermute | solution.py:370
  56.7 3.6 %collective-permute-start.6 = (bf16[2,128,128]{2,1,0:T(8,128)(2,1)S(1)}, bf16[2,128,128]{2,1,0:T(8,128)(2,1)S(1)}, u32[]{:S(2)}, u32[]{:S(2)}) collective-permute-start(bf16[2,128,128]{2,1,0:T(8,128)(2,1)S(1)} %get-tuple-element.69.refs_1_), channel_id=1, source_target_pairs={{0,4},{4,0},{8,12},{12,8},{16,20},{20,16},{24,28},{28,24},{32,36},... | collective-permute-start | bytes 196616 | tf_op jit(solution)/shard_map/ppermute | solution.py:370
  59.1 8.5 %collective-permute-start.17 = (bf16[2,128,128]{2,1,0:T(8,128)(2,1)S(1)}, bf16[2,128,128]{2,1,0:T(8,128)(2,1)S(1)}, u32[]{:S(2)}, u32[]{:S(2)}) collective-permute-start(bf16[2,128,128]{2,1,0:T(8,128)(2,1)S(1)} %get-tuple-element.91.refs_0_), channel_id=1, source_target_pairs={{0,4},{4,0},{8,12},{12,8},{16,20},{20,16},{24,28},{28,24},{32,36},... | collective-permute-start | bytes 196616 | tf_op jit(solution)/shard_map/ppermute | solution.py:370
  59.4 4.9 %collective-permute-start.7 = (bf16[2,128,256]{2,1,0:T(8,128)(2,1)S(1)}, bf16[2,128,256]{2,1,0:T(8,128)(2,1)S(1)}, u32[]{:S(2)}, u32[]{:S(2)}) collective-permute-start(bf16[2,128,256]{2,1,0:T(8,128)(2,1)S(1)} %get-tuple-element.70.refs_1_), channel_id=1, source_target_pairs={{0,32},{4,36},{8,40},{12,44},{16,48},{20,52},{24,56},{28,60},{32,0... | collective-permute-start | bytes 393224 | tf_op jit(solution)/shard_map/ppermute | solution.py:370
  60.0 7.6 %collective-permute-start.18 = (bf16[2,128,128]{2,1,0:T(8,128)(2,1)S(1)}, bf16[2,128,128]{2,1,0:T(8,128)(2,1)S(1)}, u32[]{:S(2)}, u32[]{:S(2)}) collective-permute-start(bf16[2,128,128]{2,1,0:T(8,128)(2,1)S(1)} %shard_map.109.refs_1_), channel_id=1, source_target_pairs={{0,4},{4,0},{8,12},{12,8},{16,20},{20,16},{24,28},{28,24},{32,36},... | collective-permute-start | bytes 196616 | tf_op jit(solution)/shard_map/ppermute | solution.py:370
  64.3 3.3 %copy-start = (f32[1024]{0:T(1024)S(1)}, f32[1024]{0:T(1024)}, u32[]{:S(2)}) copy-start(f32[1024]{0:T(1024)} %param.16) | copy-start | bytes 12292
  65.1 5.1 %collective-permute-start.8 = (bf16[2,128,128]{2,1,0:T(8,128)(2,1)S(1)}, bf16[2,128,128]{2,1,0:T(8,128)(2,1)S(1)}, u32[]{:S(2)}, u32[]{:S(2)}) collective-permute-start(bf16[2,128,128]{2,1,0:T(8,128)(2,1)S(1)} %slice.12), channel_id=1, source_target_pairs={{0,64},{4,68},{8,72},{12,76},{16,80},{20,84},{24,88},{28,92},{32,9... | collective-permute-start | bytes 196616 | tf_op jit(solution)/shard_map/ppermute | solution.py:370
  69.8 5.2 %collective-permute-start.9 = (bf16[2,128,128]{2,1,0:T(8,128)(2,1)S(1)}, bf16[2,128,128]{2,1,0:T(8,128)(2,1)S(1)}, u32[]{:S(2)}, u32[]{:S(2)}) collective-permute-start(bf16[2,128,128]{2,1,0:T(8,128)(2,1)S(1)} %get-tuple-element.72.refs_0_), channel_id=1, source_target_pairs={{0,4},{4,0},{8,12},{12,8},{16,20},{20,16},{24,28},{28,24},{32,36},... | collective-permute-start | bytes 196616 | tf_op jit(solution)/shard_map/ppermute | solution.py:370
  70.2 9.5 %slice-start = ((s8[8388608]{0:T(1024)(128)(4,1)}), s8[4194304]{0:T(1024)(128)(4,1)S(1)}, s32[]{:S(2)}) async-start(s8[8388608]{0:T(1024)(128)(4,1)} %bitcast.10), calls=%async_computation | async-start | bytes 8388608
  70.8 4.2 %collective-permute-start.10 = (bf16[2,128,128]{2,1,0:T(8,128)(2,1)S(1)}, bf16[2,128,128]{2,1,0:T(8,128)(2,1)S(1)}, u32[]{:S(2)}, u32[]{:S(2)}) collective-permute-start(bf16[2,128,128]{2,1,0:T(8,128)(2,1)S(1)} %shard_map.101.refs_1_), channel_id=1, source_target_pairs={{0,4},{4,0},{8,12},{12,8},{16,20},{20,16},{24,28},{28,24},{32,36},... | collective-permute-start | bytes 196616 | tf_op jit(solution)/shard_map/ppermute | solution.py:370
  75.0 4.7 %slice-start.1 = ((s8[8388608]{0:T(1024)(128)(4,1)}), s8[4194304]{0:T(1024)(128)(4,1)S(1)}, s32[]{:S(2)}) async-start(s8[8388608]{0:T(1024)(128)(4,1)} %bitcast.10), calls=%async_computation.1 | async-start | bytes 8388608
  86.5 9.3 %collective-permute-start.19 = (bf16[128,1024]{1,0:T(8,128)(2,1)S(1)}, bf16[128,1024]{1,0:T(8,128)(2,1)S(1)}, u32[]{:S(2)}, u32[]{:S(2)}) collective-permute-start(bf16[128,1024]{1,0:T(8,128)(2,1)S(1)} %fusion.32), channel_id=1, source_target_pairs={{0,1},{1,2},{2,3},{3,0},{4,5},{5,6},{6,7},{7,4},{8,9},{9,10},{10,1... | collective-permute-start | bytes 786440 | tf_op jit(solution)/shard_map/ppermute | solution.py:398
  87.9 8.1 %collective-permute-start.23 = (bf16[128,1024]{1,0:T(8,128)(2,1)S(1)}, bf16[128,1024]{1,0:T(8,128)(2,1)S(1)}, u32[]{:S(2)}, u32[]{:S(2)}) collective-permute-start(bf16[128,1024]{1,0:T(8,128)(2,1)S(1)} %fusion.68), channel_id=1, source_target_pairs={{0,3},{1,0},{2,1},{3,2},{4,7},{5,4},{6,5},{7,6},{8,11},{9,8},{10,9... | collective-permute-start | bytes 786440 | tf_op jit(solution)/shard_map/ppermute | solution.py:398
  89.8 11.5 %collective-permute-start.22 = (bf16[128,1024]{1,0:T(8,128)(2,1)S(1)}, bf16[128,1024]{1,0:T(8,128)(2,1)S(1)}, u32[]{:S(2)}, u32[]{:S(2)}) collective-permute-start(bf16[128,1024]{1,0:T(8,128)(2,1)S(1)} %fusion.56), channel_id=1, source_target_pairs={{0,1},{1,2},{2,3},{3,0},{4,5},{5,6},{6,7},{7,4},{8,9},{9,10},{10,1... | collective-permute-start | bytes 786440 | tf_op jit(solution)/shard_map/ppermute | solution.py:398
  89.9 11.6 %collective-permute-start.21 = (bf16[128,1024]{1,0:T(8,128)(2,1)S(1)}, bf16[128,1024]{1,0:T(8,128)(2,1)S(1)}, u32[]{:S(2)}, u32[]{:S(2)}) collective-permute-start(bf16[128,1024]{1,0:T(8,128)(2,1)S(1)} %fusion.44), channel_id=1, source_target_pairs={{0,3},{1,0},{2,1},{3,2},{4,7},{5,4},{6,5},{7,6},{8,11},{9,8},{10,9... | collective-permute-start | bytes 786440 | tf_op jit(solution)/shard_map/ppermute | solution.py:398
  95.8 11.2 %collective-permute-start.20 = (bf16[128,1024]{1,0:T(8,128)(2,1)S(1)}, bf16[128,1024]{1,0:T(8,128)(2,1)S(1)}, u32[]{:S(2)}, u32[]{:S(2)}) collective-permute-start(bf16[128,1024]{1,0:T(8,128)(2,1)S(1)} %add_convert_fusion.11), channel_id=1, source_target_pairs={{0,1},{1,2},{2,3},{3,0},{4,5},{5,6},{6,7},{7,4},{8,9},{9,10},{10,1... | collective-permute-start | bytes 786440 | tf_op jit(solution)/shard_map/ppermute | solution.py:398
  96.0 11.2 %collective-permute-start.27 = (bf16[128,1024]{1,0:T(8,128)(2,1)S(1)}, bf16[128,1024]{1,0:T(8,128)(2,1)S(1)}, u32[]{:S(2)}, u32[]{:S(2)}) collective-permute-start(bf16[128,1024]{1,0:T(8,128)(2,1)S(1)} %add_convert_fusion.10), channel_id=1, source_target_pairs={{0,3},{1,0},{2,1},{3,2},{4,7},{5,4},{6,5},{7,6},{8,11},{9,8},{10,9... | collective-permute-start | bytes 786440 | tf_op jit(solution)/shard_map/ppermute | solution.py:398
  101.5 11.2 %collective-permute-start.26 = (bf16[128,1024]{1,0:T(8,128)(2,1)S(1)}, bf16[128,1024]{1,0:T(8,128)(2,1)S(1)}, u32[]{:S(2)}, u32[]{:S(2)}) collective-permute-start(bf16[128,1024]{1,0:T(8,128)(2,1)S(1)} %add_convert_fusion.9), channel_id=1, source_target_pairs={{0,1},{1,2},{2,3},{3,0},{4,5},{5,6},{6,7},{7,4},{8,9},{9,10},{10,1... | collective-permute-start | bytes 786440 | tf_op jit(solution)/shard_map/ppermute | solution.py:398
  101.6 11.2 %collective-permute-start.25 = (bf16[128,1024]{1,0:T(8,128)(2,1)S(1)}, bf16[128,1024]{1,0:T(8,128)(2,1)S(1)}, u32[]{:S(2)}, u32[]{:S(2)}) collective-permute-start(bf16[128,1024]{1,0:T(8,128)(2,1)S(1)} %add_convert_fusion.8), channel_id=1, source_target_pairs={{0,3},{1,0},{2,1},{3,2},{4,7},{5,4},{6,5},{7,6},{8,11},{9,8},{10,9... | collective-permute-start | bytes 786440 | tf_op jit(solution)/shard_map/ppermute | solution.py:398
  107.1 11.2 %collective-permute-start.24 = (bf16[128,1024]{1,0:T(8,128)(2,1)S(1)}, bf16[128,1024]{1,0:T(8,128)(2,1)S(1)}, u32[]{:S(2)}, u32[]{:S(2)}) collective-permute-start(bf16[128,1024]{1,0:T(8,128)(2,1)S(1)} %add_convert_fusion.7), channel_id=1, source_target_pairs={{0,1},{1,2},{2,3},{3,0},{4,5},{5,6},{6,7},{7,4},{8,9},{9,10},{10,1... | collective-permute-start | bytes 786440 | tf_op jit(solution)/shard_map/ppermute | solution.py:398
  107.2 11.1 %collective-permute-start.29 = (bf16[128,1024]{1,0:T(8,128)(2,1)S(1)}, bf16[128,1024]{1,0:T(8,128)(2,1)S(1)}, u32[]{:S(2)}, u32[]{:S(2)}) collective-permute-start(bf16[128,1024]{1,0:T(8,128)(2,1)S(1)} %add_convert_fusion.6), channel_id=1, source_target_pairs={{0,3},{1,0},{2,1},{3,2},{4,7},{5,4},{6,5},{7,6},{8,11},{9,8},{10,9... | collective-permute-start | bytes 786440 | tf_op jit(solution)/shard_map/ppermute | solution.py:398
  112.7 11.2 %collective-permute-start.28 = (bf16[128,1024]{1,0:T(8,128)(2,1)S(1)}, bf16[128,1024]{1,0:T(8,128)(2,1)S(1)}, u32[]{:S(2)}, u32[]{:S(2)}) collective-permute-start(bf16[128,1024]{1,0:T(8,128)(2,1)S(1)} %add_convert_fusion.5), channel_id=1, source_target_pairs={{0,1},{1,2},{2,3},{3,0},{4,5},{5,6},{6,7},{7,4},{8,9},{9,10},{10,1... | collective-permute-start | bytes 786440 | tf_op jit(solution)/shard_map/ppermute | solution.py:398
  112.9 11.1 %collective-permute-start.30 = (bf16[128,1024]{1,0:T(8,128)(2,1)S(1)}, bf16[128,1024]{1,0:T(8,128)(2,1)S(1)}, u32[]{:S(2)}, u32[]{:S(2)}) collective-permute-start(bf16[128,1024]{1,0:T(8,128)(2,1)S(1)} %add_convert_fusion.4), channel_id=1, source_target_pairs={{0,3},{1,0},{2,1},{3,2},{4,7},{5,4},{6,5},{7,6},{8,11},{9,8},{10,9... | collective-permute-start | bytes 786440 | tf_op jit(solution)/shard_map/ppermute | solution.py:398

commit v3 on v2

--- a/solution.py
+++ b/solution.py
@@ -24,7 +24,7 @@
 
 
 def local_kernel(base, stride, flags, q_ref, k_ref, v_ref, log_ref, beta_ref, weight_ref,
-                 near_ref, far_ref, map_ref, cols_ref, rows_ref):
+                 near_ref, far_ref, map_ref, rows_ref):
     step = pl.program_id(0)
     tokens = q_ref.shape[0]
     heads = log_ref.shape[0]
@@ -63,10 +63,9 @@
         take = pl.ds(head, 1)
         beta_row = beta_ref[take, :]
         wanted = [rows_ref[0, take, :], rows_ref[2, take, :], beta_row]
-        wanted += [weight_ref[level, take, :] for level in range(9)]
-        wanted += [jnp.zeros((4, tokens), F32)]
+        wanted += [weight_ref[level, take, :] for level in range(LOCAL_LEVELS)]
+        wanted += [jnp.zeros((1, tokens), F32)]
         c = jnp.transpose(jnp.concatenate(wanted, axis=0))
-        cols_ref[g * tokens:(g + 1) * tokens, :] = c
         cols.append(c)
         cum_rows.append(rows_ref[0, take, :])
         tail_rows.append(rows_ref[1, take, :])
@@ -175,15 +174,13 @@
             grid=(steps,),
             in_specs=[block, block, block, whole2, whole2, whole3],
             out_specs=[out, out,
-                       pl.BlockSpec((TOGETHER, HEAD_DIM, 2 * HEAD_DIM), lambda h, f: (h, 0, 0)),
-                       pl.BlockSpec((TOGETHER * tokens, 16), lambda h, f: (h, 0))],
+                       pl.BlockSpec((TOGETHER, HEAD_DIM, 2 * HEAD_DIM), lambda h, f: (h, 0, 0))],
             scratch_shapes=[pltpu.VMEM((3, heads, tokens), F32)],
         ),
         out_shape=[
-            jax.ShapeDtypeStruct((tokens, part * HEAD_DIM), F32),
-            jax.ShapeDtypeStruct((tokens, part * HEAD_DIM), BF16),
+            pltpu.HBM((tokens, part * HEAD_DIM), F32),
+            pltpu.HBM((tokens, part * HEAD_DIM), BF16),
             jax.ShapeDtypeStruct((part, HEAD_DIM, 2 * HEAD_DIM), BF16),
-            jax.ShapeDtypeStruct((part * tokens, 16), F32),
         ],
         compiler_params=pltpu.CompilerParams(vmem_limit_bytes=14 << 20),
         cost_estimate=pl.CostEstimate(flops=part * 1500000000, bytes_accessed=8 << 20, transcendentals=0),
@@ -279,89 +276,84 @@
     )(bits, *args)
 
 
-def read_kernel(side, fold, slots, norm, bits, near_ref, far_ref, cols_ref, *refs):
+def final_kernel(levels, parts, chunk, bits, *refs):
     core = bits[0]
     refs = list(refs)
-    tokens = near_ref.shape[0]
-    first = 3 + LOCAL_LEVELS
+    near_refs = [refs.pop(0) for _ in range(parts)]
+    far_refs = [refs.pop(0) for _ in range(parts)]
+    sib_refs = [refs.pop(0) for _ in range(parts)]
+    weight_ref, gain_ref = refs[:2]
+    mine, other, z_ref = refs[2:2 + levels], refs[2 + levels:2 + 2 * levels], refs[-1]
+    tokens = near_refs[0].shape[0]
+    side = pl.program_id(0)
+    is_mine = side == core
     upper = core == 1
-    units = [(g, t) for g in range(TOGETHER) for t in range(0, tokens, SUPER)]
-    count = range(len(units))
+    first = LOCAL_LEVELS
 
     def lanes(g):
         return slice(g * HEAD_DIM, (g + 1) * HEAD_DIM)
 
-    def cols(g, t, i):
-        return cols_ref[g * tokens + t:g * tokens + t + SUPER, i:i + 1]
-
-    fars = [far_ref[t:t + SUPER, lanes(g)] for g, t in units]
-    ys = [near_ref[t:t + SUPER, lanes(g)] for g, t in units]
-    if fold:
-        sib_ref = refs.pop(0)
-        both = [mm(fars[u], sib_ref[g]) for u, (g, t) in enumerate(units)]
-        ys = [ys[u] + jnp.where(upper, cols(g, t, first) * both[u][:, :HEAD_DIM], 0.0)
-              for u, (g, t) in enumerate(units)]
-        fars = [jnp.where(upper, both[u][:, HEAD_DIM:].astype(BF16), fars[u]) for u in count]
-    if slots:
-        mine, other = refs[:len(slots)], refs[len(slots):2 * len(slots)]
-        refs = refs[2 * len(slots):]
-        is_mine = core == side
-        states = [jnp.concatenate([jnp.where(is_mine, m[g], o[g]) for m, o in zip(mine, other)], axis=1)
-                  for g in range(TOGETHER)]
-        reads = [mm(fars[u], states[g]) for u, (g, t) in enumerate(units)]
-        for i, slot in enumerate(slots):
-            ys = [ys[u] + cols(g, t, first + slot) * reads[u][:, i * HEAD_DIM:(i + 1) * HEAD_DIM]
-                  for u, (g, t) in enumerate(units)]
-    if norm:
-        gain_ref, z_ref = refs[0], refs[-1]
-        for u, (g, t) in enumerate(units):
-            scale = lax.rsqrt(jnp.mean(ys[u] * ys[u], axis=1, keepdims=True) + EPS)
-            z_ref[t:t + SUPER, lanes(g)] = (ys[u] * scale * gain_ref[:, lanes(g)]).astype(BF16)
-        return
+    def pick(group, where):
+        if parts == 1:
+            return group[0][where]
+        return jnp.where(side == 0, group[0][where], group[1][where])
+
+    stacks = []
+    for g in range(TOGETHER):
+        sib = pick(sib_refs, g)
+        states = jnp.concatenate([jnp.where(is_mine, m[g], o[g]) for m, o in zip(mine, other)], axis=1)
+        states = jnp.where(upper, mm(sib[:, HEAD_DIM:], states).astype(BF16), states)
+        low = jnp.where(upper, sib[:, :HEAD_DIM], jnp.zeros((HEAD_DIM, HEAD_DIM), BF16))
+        stacks.append(jnp.transpose(jnp.concatenate([low, states], axis=1)))
+    step = 2 * SUPER
+    units = [(g, t) for g in range(TOGETHER) for t in range(0, tokens, step)]
+    reads = [lax.dot_general(stacks[g], pick(far_refs, (slice(t, t + step), lanes(g))),
+                             (((1,), (1,)), ((), ())), preferred_element_type=F32) for g, t in units]
     for u, (g, t) in enumerate(units):
-        refs[0][t:t + SUPER, lanes(g)] = ys[u]
-        if fold:
-            refs[1][t:t + SUPER, lanes(g)] = fars[u]
-
-
-def read_part(bits, side, pair, near, far, cols, sib=None, slots=(), mine=(), other=(), gain=None, before=None):
-    tokens = near[0].shape[0]
+        head = TOGETHER * (CHUNKS * side + chunk) + g
+        turned = None
+        for i in range(levels + 1):
+            term = weight_ref[first + i, pl.ds(head, 1), t:t + step] * reads[u][i * HEAD_DIM:(i + 1) * HEAD_DIM]
+            turned = term if turned is None else turned + term
+        y = pick(near_refs, (slice(t, t + step), lanes(g))) + jnp.transpose(turned)
+        scale = lax.rsqrt(jnp.mean(y * y, axis=1, keepdims=True) + EPS)
+        z_ref[t:t + step, lanes(g)] = (y * scale * gain_ref[:, lanes(g)]).astype(BF16)
+
+
+def final_part(chunk, bits, nears, fars, sibs, weights, gain, mine, other, before):
+    tokens = nears[0].shape[0]
     wide = TOGETHER * HEAD_DIM
+    levels = len(mine)
+    parts = len(nears)
+    placed = lambda h, b: (0, CHUNKS * h + chunk)
     state = pl.BlockSpec((TOGETHER, HEAD_DIM, HEAD_DIM), lambda h, b: (0, 0, 0))
-
-    def column(index):
-        return pl.BlockSpec((tokens, wide), lambda h, b: (0, index))
-
-    in_specs = [column(near[1]), column(far[1]),
-                pl.BlockSpec((TOGETHER * tokens, 16), lambda h, b, i=cols[1]: (i, 0))]
-    args = [bits, near[0], far[0], cols[0]]
-    if sib is not None:
-        in_specs.append(pl.BlockSpec((TOGETHER, HEAD_DIM, 2 * HEAD_DIM), lambda h, b, i=sib[1]: (i, 0, 0)))
-        args.append(sib[0])
-    in_specs += [state] * (2 * len(slots))
-    args += [*mine, *other]
+    if parts == 1:
+        block = pl.BlockSpec((tokens, wide), lambda h, b: (0, h))
+        maps = pl.BlockSpec((TOGETHER, HEAD_DIM, 2 * HEAD_DIM), lambda h, b: (h, 0, 0))
+    else:
+        block = pl.BlockSpec((tokens, wide), lambda h, b: (0, 0))
+        maps = pl.BlockSpec((TOGETHER, HEAD_DIM, 2 * HEAD_DIM), lambda h, b: (0, 0, 0))
+    in_specs = [block] * (2 * parts) + [maps] * parts
+    in_specs += [pl.BlockSpec(weights.shape, lambda h, b: (0, 0, 0)), pl.BlockSpec((1, wide), placed)]
+    in_specs += [state] * (2 * levels)
+    args = [bits, *nears, *fars, *sibs, weights, gain, *mine, *other]
     aliases = {}
-    if gain is not None:
-        in_specs.append(pl.BlockSpec((1, wide), lambda h, b: (0, pair)))
-        args.append(gain)
-        if before is not None:
-            aliases = {len(args): 0}
-            args.append(before)
-            in_specs.append(pl.BlockSpec(memory_space=pl.ANY))
-        out_specs = column(pair)
-        out_shape = jax.ShapeDtypeStruct((tokens, gain.shape[1]), BF16)
-    else:
-        out_specs = [column(0)] + ([column(0)] if sib is not None else [])
-        out_shape = [jax.ShapeDtypeStruct((tokens, wide), F32)]
-        out_shape += [jax.ShapeDtypeStruct((tokens, wide), BF16)] if sib is not None else []
+    if before is not None:
+        aliases = {len(args): 0}
+        args.append(before)
+        in_specs.append(pl.BlockSpec(memory_space=pl.ANY))
     return pl.pallas_call(
-        functools.partial(read_kernel, side, sib is not None, slots, gain is not None),
+        functools.partial(final_kernel, levels, parts, chunk),
         grid_spec=pltpu.PrefetchScalarGridSpec(
-            num_scalar_prefetch=1, grid=(1,), in_specs=in_specs, out_specs=out_specs),
-        out_shape=out_shape,
+            num_scalar_prefetch=1,
+            grid=(2,),
+            in_specs=in_specs,
+            out_specs=pl.BlockSpec((tokens, wide), placed),
+        ),
+        out_shape=jax.ShapeDtypeStruct((tokens, gain.shape[1]), BF16),
         input_output_aliases=aliases,
-        compiler_params=pltpu.CompilerParams(vmem_limit_bytes=8 << 20),
-        cost_estimate=pl.CostEstimate(flops=1200000000, bytes_accessed=2 << 20, transcendentals=0),
+        compiler_params=pltpu.CompilerParams(vmem_limit_bytes=14 << 20),
+        cost_estimate=pl.CostEstimate(flops=2400000000, bytes_accessed=4 << 20, transcendentals=0),
     )(*args)
 
 
@@ -405,7 +397,7 @@
     return jnp.concatenate([sums[p] for p in range(2 * PIECES)], axis=1)
 
 
-def body(queries, keys, values, log_decay, beta, level_weights, doc_start, norm_gain, out_weight):
+def layer(queries, keys, values, log_decay, beta, level_weights, doc_start, norm_gain, out_weight):
     heads = log_decay.shape[0]
     mine_heads = heads // (2 * CHUNKS)
     nbits = lax.axis_size("seq").bit_length() - 1
@@ -419,24 +411,16 @@
     doc_start = in_hbm(doc_start)
 
     def local(base, stride, steps, flags):
-        near, far, maps, cols = local_part(base, stride, steps, flags, *given)
-        return in_hbm(near), in_hbm(far), maps, in_hbm(cols), partner(maps, 0)
+        near, far, maps = local_part(base, stride, steps, flags, *given)
+        return near, far, maps, partner(maps, 0)
 
     front = local(0, CHUNKS, 2, doc_start)
     low = local(1, CHUNKS, 1, doc_start)
-    cur = small_call(pair_kernel, bits, [front[2], front[4]], [wide])[0]
+    cur = small_call(pair_kernel, bits, [front[2], front[3]], [wide])[0]
     flags = lax.optimization_barrier((doc_start, cur))[0]
     high = local(3, CHUNKS, 1, flags)
-    settled = lax.optimization_barrier((bits, high[2]))[0]
-    curs = [cur, small_call(pair_kernel, bits, [low[2], high[2], low[4], high[4]], [wide])[0]]
-    where = [[(front, 0), (front, 1)], [(low, 0), (high, 0)]]
-    parts = [(c, h) for c in range(CHUNKS) for h in range(2)]
-    nears, fars, colss = {}, {}, {}
-    for c, h in parts:
-        (near, far, _, cols, sib), i = where[c][h]
-        colss[c, h] = (cols, i)
-        near, far = read_part(settled, h, 2 * h + c, (near, i), (far, i), (cols, i), sib=(sib, i))
-        nears[c, h], fars[c, h] = (near, 0), (far, 0)
+    curs = [cur, small_call(pair_kernel, bits, [low[2], high[2], low[3], high[3]], [wide])[0]]
+    sources = [[front], [low, high]]
     carried = [None] * CHUNKS
     states = [[] for _ in range(CHUNKS)]
     others = [[] for _ in range(CHUNKS)]
@@ -453,15 +437,9 @@
             states[c].append(x)
             others[c].append(partner(x, 0))
     z = None
-    early = (nbits - 1) // 2
-    for c, h in parts:
-        near = read_part(bits, h, 2 * h + c, nears[c, h], fars[c, h], colss[c, h],
-                         slots=tuple(range(1, early + 1)), mine=states[c][:early], other=others[c][:early])[0]
-        nears[c, h] = (near, 0)
-    for c, h in parts:
-        z = read_part(bits, h, 2 * h + c, nears[c, h], fars[c, h], colss[c, h],
-                      slots=tuple(range(early + 1, nbits)), mine=states[c][early:], other=others[c][early:],
-                      gain=gain, before=z)
+    for c in range(CHUNKS):
+        nears, fars, _, sibs = zip(*sources[c])
+        z = final_part(c, bits, nears, fars, sibs, given[5], gain, states[c], others[c], z)
     return project(z, out_weight)
 
 
@@ -477,6 +455,4 @@
         P("head"),
         P("head", None),
     )
-    return jax.shard_map(
-        body, mesh=mesh, in_specs=placed, out_specs=P(("seq", "head"), None), check_vma=False
-    )
+    return jax.shard_map(layer, mesh=mesh, in_specs=placed, out_specs=P(("seq", "head"), None), check_vma=False)

time: 126 us -> 110 us (0.87)
  the two profiles are of different devices: /device:TPU:1 before, /device:TPU:28 now
where the time goes in v3:
time: 110 us
  Pallas kernels  35.7 us (32%)
  waiting for transfers between devices  33.4 us (30%)
  starting transfers between devices  30.9 us (28%)
  matrix products  7.15 us (6%)
  other arithmetic  1.84 us (2%)
    ppermute x12, waiting for transfers between devices, project(): got[p] = lax.ppermute(sums[p], 'head', up if p < PIECES else down)  23.9 us
    pallas_call x3, Pallas kernels, local_part(): pl.pallas_call(functools.partial(local_kernel, base, stride), grid_spec=p...  21.2 us
    ppermute x19, starting transfers between devices, partner(): return lax.ppermute(value, 'seq', [(i, i ^ 1 << bit) for i in range(size)])  18 us
    ppermute x12, starting transfers between devices, project(): got[p] = lax.ppermute(sums[p], 'head', up if p < PIECES else down)  12.8 us
    ppermute x19, waiting for transfers between devices, partner(): return lax.ppermute(value, 'seq', [(i, i ^ 1 << bit) for i in range(size)])  9.53 us
    pallas_call x2, Pallas kernels, final_part(): pl.pallas_call(functools.partial(final_kernel, levels, parts, chunk), gri...  7.51 us
    dot_general x16, matrix products, term(): return jnp.dot(part, w, preferred_element_type=F32).astype(BF16)  7.15 us
    pallas_call x10, Pallas kernels, small_call(): pl.pallas_call(kernel, grid_spec=pltpu.PrefetchScalarGridSpec(num_scalar_...  6.95 us
  transfers between devices with their start and end apart: 31, of which 14 were waited for; matrix products, arithmetic and copies ran while one was open for 1% of the time, Pallas kernels for 21%

profile of v3, /device:TPU:28, one launch (start us, length us, event | category | flops | bytes accessed | tf_op | source)
XLA Modules:
  0.0 109.6 jit_solution(10243262557604190193)
XLA Ops:
  0.0 9.3 %shard_map.92 = (f32[512,512]{1,0:T(8,128)}, bf16[512,512]{1,0:T(8,128)(2,1)}, bf16[4,128,256]{2,1,0:T(8,128)(2,1)S(1)}) custom-call(s32[8]{0:T(128)} %flags.4, bf16[512,1024]{1,0:T(8,128)(2,1)} %q_ref.5, bf16[512,1024]{1,0:T(8,128)(2,1)} %k_ref.5, bf16[512,1024]{1,0:T(8,128)(2,1)} %v_ref.5, f32[8,512]{1,0:T(8,128)} %log_ref.5, f32[8,512]{1,0:T(8,128)} %beta_ref.5, ...), custom_call_target="tpu_custom_call" | custom-call | flops 6000000000 | bytes 8388608 | tf_op jit(solution)/shard_map/pallas_call | solution.py:170
  9.3 6.0 %shard_map.91 = (f32[512,256]{1,0:T(8,128)}, bf16[512,256]{1,0:T(8,128)(2,1)}, bf16[2,128,256]{2,1,0:T(8,128)(2,1)S(1)}) custom-call(s32[8]{0:T(128)} %flags.4, bf16[512,1024]{1,0:T(8,128)(2,1)} %q_ref.5, bf16[512,1024]{1,0:T(8,128)(2,1)} %k_ref.5, bf16[512,1024]{1,0:T(8,128)(2,1)} %v_ref.5, f32[8,512]{1,0:T(8,128)} %log_ref.5, f32[8,512]{1,0:T(8,128)} %beta_ref.5, ...), custom_call_target="tpu_custom_call" | custom-call | flops 3000000000 | bytes 8388608 | tf_op jit(solution)/shard_map/pallas_call | solution.py:170
  15.8 0.7 shard_map.93.refs_1_
  16.5 6.0 %shard_map.94 = (f32[512,256]{1,0:T(8,128)}, bf16[512,256]{1,0:T(8,128)(2,1)}, bf16[2,128,256]{2,1,0:T(8,128)(2,1)S(1)}) custom-call(s32[8]{0:T(128)} %flags.4, bf16[512,1024]{1,0:T(8,128)(2,1)} %q_ref.5, bf16[512,1024]{1,0:T(8,128)(2,1)} %k_ref.5, bf16[512,1024]{1,0:T(8,128)(2,1)} %v_ref.5, f32[8,512]{1,0:T(8,128)} %log_ref.5, f32[8,512]{1,0:T(8,128)} %beta_ref.5, ...), custom_call_target="tpu_custom_call" | custom-call | flops 3000000000 | bytes 8388608 | tf_op jit(solution)/shard_map/pallas_call | solution.py:170
  22.5 1.2 %collective-permute-start.11 = (bf16[2,128,256]{2,1,0:T(8,128)(2,1)S(1)}, bf16[2,128,256]{2,1,0:T(8,128)(2,1)S(1)}, u32[]{:S(2)}, u32[]{:S(2)}) collective-permute-start(bf16[2,128,256]{2,1,0:T(8,128)(2,1)S(1)} %shard_map.93.refs_1_), channel_id=1, source_target_pairs={{0,8},{4,12},{8,0},{12,4},{16,24},{20,28},{24,16},{28,20},{32,40},... | collective-permute-start | bytes 393224 | tf_op jit(solution)/shard_map/ppermute | solution.py:362
  23.9 0.7 shard_map.95.refs_1_
  24.6 1.3 %collective-permute-start.3 = (bf16[2,128,256]{2,1,0:T(8,128)(2,1)S(1)}, bf16[2,128,256]{2,1,0:T(8,128)(2,1)S(1)}, u32[]{:S(2)}, u32[]{:S(2)}) collective-permute-start(bf16[2,128,256]{2,1,0:T(8,128)(2,1)S(1)} %shard_map.95.refs_1_), channel_id=1, source_target_pairs={{0,8},{4,12},{8,0},{12,4},{16,24},{20,28},{24,16},{28,20},{32,40},... | collective-permute-start | bytes 393224 | tf_op jit(solution)/shard_map/ppermute | solution.py:362
  25.9 3.0 %collective-permute-done.11.refs_0_ = bf16[2,128,256]{2,1,0:T(8,128)(2,1)S(1)} collective-permute-done((bf16[2,128,256]{2,1,0:T(8,128)(2,1)S(1)}, bf16[2,128,256]{2,1,0:T(8,128)(2,1)S(1)}, u32[]{:S(2)}, u32[]{:S(2)}) %collective-permute-start.11) | collective-permute-done | bytes 131104 | tf_op jit(solution)/shard_map/ppermute | solution.py:362
  28.9 0.7 shard_map.100
  29.6 0.6 collective-permute-start.12
  30.2 1.0 collective-permute-done.3.refs_0_
  31.2 0.7 shard_map.96
  32.0 2.3 %collective-permute-start.4 = (bf16[2,128,256]{2,1,0:T(8,128)(2,1)S(1)}, bf16[2,128,256]{2,1,0:T(8,128)(2,1)S(1)}, u32[]{:S(2)}, u32[]{:S(2)}) collective-permute-start(bf16[2,128,256]{2,1,0:T(8,128)(2,1)S(1)} %get-tuple-element.53.refs_1_), channel_id=1, source_target_pairs={{0,16},{4,20},{8,24},{12,28},{16,0},{20,4},{24,8},{28,12},{32,48},... | collective-permute-start | bytes 393224 | tf_op jit(solution)/shard_map/ppermute | solution.py:362
  34.2 2.1 %collective-permute-done.12.refs_0_ = bf16[2,128,256]{2,1,0:T(8,128)(2,1)S(1)} collective-permute-done((bf16[2,128,256]{2,1,0:T(8,128)(2,1)S(1)}, bf16[2,128,256]{2,1,0:T(8,128)(2,1)S(1)}, u32[]{:S(2)}, u32[]{:S(2)}) %collective-permute-start.12) | collective-permute-done | bytes 131104 | tf_op jit(solution)/shard_map/ppermute | solution.py:362
  36.4 0.8 shard_map.101
  37.1 2.0 %collective-permute-start.13 = (bf16[2,128,256]{2,1,0:T(8,128)(2,1)S(1)}, bf16[2,128,256]{2,1,0:T(8,128)(2,1)S(1)}, u32[]{:S(2)}, u32[]{:S(2)}) collective-permute-start(bf16[2,128,256]{2,1,0:T(8,128)(2,1)S(1)} %get-tuple-element.67.refs_1_), channel_id=1, source_target_pairs={{0,32},{4,36},{8,40},{12,44},{16,48},{20,52},{24,56},{28,60},{32,0... | collective-permute-start | bytes 393224 | tf_op jit(solution)/shard_map/ppermute | solution.py:362
  39.1 0.8 shard_map.97
  39.9 1.9 %collective-permute-start.5 = (bf16[2,128,256]{2,1,0:T(8,128)(2,1)S(1)}, bf16[2,128,256]{2,1,0:T(8,128)(2,1)S(1)}, u32[]{:S(2)}, u32[]{:S(2)}) collective-permute-start(bf16[2,128,256]{2,1,0:T(8,128)(2,1)S(1)} %get-tuple-element.56.refs_1_), channel_id=1, source_target_pairs={{0,32},{4,36},{8,40},{12,44},{16,48},{20,52},{24,56},{28,60},{32,0... | collective-permute-start | bytes 393224 | tf_op jit(solution)/shard_map/ppermute | solution.py:362
  41.7 1.0 collective-permute-done.13.refs_0_
  42.8 0.7 shard_map.102
  43.5 4.1 %collective-permute-start.14 = (bf16[2,128,128]{2,1,0:T(8,128)(2,1)S(1)}, bf16[2,128,128]{2,1,0:T(8,128)(2,1)S(1)}, u32[]{:S(2)}, u32[]{:S(2)}) collective-permute-start(bf16[2,128,128]{2,1,0:T(8,128)(2,1)S(1)} %slice.13), channel_id=1, source_target_pairs={{0,64},{4,68},{8,72},{12,76},{16,80},{20,84},{24,88},{28,92},{32,9... | collective-permute-start | bytes 196616 | tf_op jit(solution)/shard_map/ppermute | solution.py:362
  47.6 0.7 shard_map.98
  48.4 2.0 %collective-permute-start.6 = (bf16[2,128,128]{2,1,0:T(8,128)(2,1)S(1)}, bf16[2,128,128]{2,1,0:T(8,128)(2,1)S(1)}, u32[]{:S(2)}, u32[]{:S(2)}) collective-permute-start(bf16[2,128,128]{2,1,0:T(8,128)(2,1)S(1)} %slice.12), channel_id=1, source_target_pairs={{0,64},{4,68},{8,72},{12,76},{16,80},{20,84},{24,88},{28,92},{32,9... | collective-permute-start | bytes 196616 | tf_op jit(solution)/shard_map/ppermute | solution.py:362
  50.9 0.6 shard_map.103.refs_8_
  51.5 0.6 collective-permute-start.18
  52.1 2.2 %collective-permute-done.6.sib_ref = bf16[2,128,128]{2,1,0:T(8,128)(2,1)S(1)} collective-permute-done((bf16[2,128,128]{2,1,0:T(8,128)(2,1)S(1)}, bf16[2,128,128]{2,1,0:T(8,128)(2,1)S(1)}, u32[]{:S(2)}, u32[]{:S(2)}) %collective-permute-start.6) | collective-permute-done | bytes 65568 | tf_op jit(solution)/shard_map/ppermute | solution.py:362
  54.8 0.6 collective-permute-start.8
  56.0 3.8 %shard_map.104.refs_16_ = bf16[512,1024]{1,0:T(8,128)(2,1)S(1)} custom-call(s32[5]{0:T(128)S(1)} %stack.23.bits, f32[512,512]{1,0:T(8,128)S(1)} %copy-done.1, bf16[512,512]{1,0:T(8,128)(2,1)S(1)} %copy-done.4, bf16[4,128,256]{2,1,0:T(8,128)(2,1)S(1)} %collective-permute-done.refs_1_.refs_2_, f32[10,8,512]{2,1,0:T(8,128)} %refs_6_.1, f32[1,1024]{1,0:T(1,128)S(1)} %bitcast.6, ...), custom_call_target="tpu_custom_call" | custom-call | flops 2400000000 | bytes 4194304 | tf_op jit(solution)/shard_map/pallas_call | solution.py:345
  59.9 3.7 %shard_map.105 = bf16[512,1024]{1,0:T(8,128)(2,1)S(1)} custom-call(s32[5]{0:T(128)S(1)} %stack.23.bits, f32[512,256]{1,0:T(8,128)S(1)} %copy-done.2, f32[512,256]{1,0:T(8,128)S(1)} %copy-done.3, bf16[512,256]{1,0:T(8,128)(2,1)S(1)} %copy-done.5, bf16[512,256]{1,0:T(8,128)(2,1)S(1)} %copy-done.6, ...), custom_call_target="tpu_custom_call", output_to_operand_aliasing={{}: (17, {})} | custom-call | flops 2400000000 | bytes 4194304 | tf_op jit(solution)/shard_map/pallas_call | solution.py:345
  70.8 1.8 %collective-permute-start.23 = (bf16[128,1024]{1,0:T(8,128)(2,1)S(1)}, bf16[128,1024]{1,0:T(8,128)(2,1)S(1)}, u32[]{:S(2)}, u32[]{:S(2)}) collective-permute-start(bf16[128,1024]{1,0:T(8,128)(2,1)S(1)} %fusion.68), channel_id=1, source_target_pairs={{0,3},{1,0},{2,1},{3,2},{4,7},{5,4},{6,5},{7,6},{8,11},{9,8},{10,9... | collective-permute-start | bytes 786440 | tf_op jit(solution)/shard_map/ppermute | solution.py:390
  73.0 1.6 %collective-permute-start.22 = (bf16[128,1024]{1,0:T(8,128)(2,1)S(1)}, bf16[128,1024]{1,0:T(8,128)(2,1)S(1)}, u32[]{:S(2)}, u32[]{:S(2)}) collective-permute-start(bf16[128,1024]{1,0:T(8,128)(2,1)S(1)} %fusion.56), channel_id=1, source_target_pairs={{0,1},{1,2},{2,3},{3,0},{4,5},{5,6},{6,7},{7,4},{8,9},{9,10},{10,1... | collective-permute-start | bytes 786440 | tf_op jit(solution)/shard_map/ppermute | solution.py:390
  75.1 4.6 %collective-permute-done.19 = bf16[128,1024]{1,0:T(8,128)(2,1)S(1)} collective-permute-done((bf16[128,1024]{1,0:T(8,128)(2,1)S(1)}, bf16[128,1024]{1,0:T(8,128)(2,1)S(1)}, u32[]{:S(2)}, u32[]{:S(2)}) %collective-permute-start.19) | collective-permute-done | bytes 262176 | tf_op jit(solution)/shard_map/ppermute | solution.py:390
  79.8 1.5 %collective-permute-start.20 = (bf16[128,1024]{1,0:T(8,128)(2,1)S(1)}, bf16[128,1024]{1,0:T(8,128)(2,1)S(1)}, u32[]{:S(2)}, u32[]{:S(2)}) collective-permute-start(bf16[128,1024]{1,0:T(8,128)(2,1)S(1)} %add_convert_fusion.11), channel_id=1, source_target_pairs={{0,1},{1,2},{2,3},{3,0},{4,5},{5,6},{6,7},{7,4},{8,9},{9,10},{10,1... | collective-permute-start | bytes 786440 | tf_op jit(solution)/shard_map/ppermute | solution.py:390
  81.4 0.7 collective-permute-start.27
  82.0 3.3 %collective-permute-done.22 = bf16[128,1024]{1,0:T(8,128)(2,1)S(1)} collective-permute-done((bf16[128,1024]{1,0:T(8,128)(2,1)S(1)}, bf16[128,1024]{1,0:T(8,128)(2,1)S(1)}, u32[]{:S(2)}, u32[]{:S(2)}) %collective-permute-start.22) | collective-permute-done | bytes 262176 | tf_op jit(solution)/shard_map/ppermute | solution.py:390
  85.4 1.5 %collective-permute-start.26 = (bf16[128,1024]{1,0:T(8,128)(2,1)S(1)}, bf16[128,1024]{1,0:T(8,128)(2,1)S(1)}, u32[]{:S(2)}, u32[]{:S(2)}) collective-permute-start(bf16[128,1024]{1,0:T(8,128)(2,1)S(1)} %add_convert_fusion.9), channel_id=1, source_target_pairs={{0,1},{1,2},{2,3},{3,0},{4,5},{5,6},{6,7},{7,4},{8,9},{9,10},{10,1... | collective-permute-start | bytes 786440 | tf_op jit(solution)/shard_map/ppermute | solution.py:390
  87.0 0.7 collective-permute-start.25
  87.6 3.3 %collective-permute-done.20 = bf16[128,1024]{1,0:T(8,128)(2,1)S(1)} collective-permute-done((bf16[128,1024]{1,0:T(8,128)(2,1)S(1)}, bf16[128,1024]{1,0:T(8,128)(2,1)S(1)}, u32[]{:S(2)}, u32[]{:S(2)}) %collective-permute-start.20) | collective-permute-done | bytes 262176 | tf_op jit(solution)/shard_map/ppermute | solution.py:390
  91.0 1.5 %collective-permute-start.24 = (bf16[128,1024]{1,0:T(8,128)(2,1)S(1)}, bf16[128,1024]{1,0:T(8,128)(2,1)S(1)}, u32[]{:S(2)}, u32[]{:S(2)}) collective-permute-start(bf16[128,1024]{1,0:T(8,128)(2,1)S(1)} %add_convert_fusion.7), channel_id=1, source_target_pairs={{0,1},{1,2},{2,3},{3,0},{4,5},{5,6},{6,7},{7,4},{8,9},{9,10},{10,1... | collective-permute-start | bytes 786440 | tf_op jit(solution)/shard_map/ppermute | solution.py:390
  92.6 0.7 collective-permute-start.29
  93.3 3.3 %collective-permute-done.26 = bf16[128,1024]{1,0:T(8,128)(2,1)S(1)} collective-permute-done((bf16[128,1024]{1,0:T(8,128)(2,1)S(1)}, bf16[128,1024]{1,0:T(8,128)(2,1)S(1)}, u32[]{:S(2)}, u32[]{:S(2)}) %collective-permute-start.26) | collective-permute-done | bytes 262176 | tf_op jit(solution)/shard_map/ppermute | solution.py:390
  96.6 1.5 %collective-permute-start.28 = (bf16[128,1024]{1,0:T(8,128)(2,1)S(1)}, bf16[128,1024]{1,0:T(8,128)(2,1)S(1)}, u32[]{:S(2)}, u32[]{:S(2)}) collective-permute-start(bf16[128,1024]{1,0:T(8,128)(2,1)S(1)} %add_convert_fusion.5), channel_id=1, source_target_pairs={{0,1},{1,2},{2,3},{3,0},{4,5},{5,6},{6,7},{7,4},{8,9},{9,10},{10,1... | collective-permute-start | bytes 786440 | tf_op jit(solution)/shard_map/ppermute | solution.py:390
  98.2 0.7 collective-permute-start.30
  98.9 3.3 %collective-permute-done.24 = bf16[128,1024]{1,0:T(8,128)(2,1)S(1)} collective-permute-done((bf16[128,1024]{1,0:T(8,128)(2,1)S(1)}, bf16[128,1024]{1,0:T(8,128)(2,1)S(1)}, u32[]{:S(2)}, u32[]{:S(2)}) %collective-permute-start.24) | collective-permute-done | bytes 262176 | tf_op jit(solution)/shard_map/ppermute | solution.py:390
  102.3 1.4 %collective-permute-done.29 = bf16[128,1024]{1,0:T(8,128)(2,1)S(1)} collective-permute-done((bf16[128,1024]{1,0:T(8,128)(2,1)S(1)}, bf16[128,1024]{1,0:T(8,128)(2,1)S(1)}, u32[]{:S(2)}, u32[]{:S(2)}) %collective-permute-start.29) | collective-permute-done | bytes 262176 | tf_op jit(solution)/shard_map/ppermute | solution.py:390
  103.8 3.2 %collective-permute-done.28 = bf16[128,1024]{1,0:T(8,128)(2,1)S(1)} collective-permute-done((bf16[128,1024]{1,0:T(8,128)(2,1)S(1)}, bf16[128,1024]{1,0:T(8,128)(2,1)S(1)}, u32[]{:S(2)}, u32[]{:S(2)}) %collective-permute-start.28) | collective-permute-done | bytes 262176 | tf_op jit(solution)/shard_map/ppermute | solution.py:390
  107.0 1.4 %collective-permute-done.30 = bf16[128,1024]{1,0:T(8,128)(2,1)S(1)} collective-permute-done((bf16[128,1024]{1,0:T(8,128)(2,1)S(1)}, bf16[128,1024]{1,0:T(8,128)(2,1)S(1)}, u32[]{:S(2)}, u32[]{:S(2)}) %collective-permute-start.30) | collective-permute-done | bytes 262176 | tf_op jit(solution)/shard_map/ppermute | solution.py:390
  108.5 1.0 pad_maximum_fusion
  (80 shorter events, 11.2 us)
Async XLA Ops:
  9.3 6.6 %collective-permute-start = (bf16[4,128,256]{2,1,0:T(8,128)(2,1)S(1)}, bf16[4,128,256]{2,1,0:T(8,128)(2,1)S(1)}, u32[]{:S(2)}, u32[]{:S(2)}) collective-permute-start(bf16[4,128,256]{2,1,0:T(8,128)(2,1)S(1)} %get-tuple-element.45.refs_0_), channel_id=1, source_target_pairs={{0,4},{4,0},{8,12},{12,8},{16,20},{20,16},{24,28},{28,24},{32,36},... | collective-permute-start | bytes 786440 | tf_op jit(solution)/shard_map/ppermute | solution.py:362
  15.2 8.5 %collective-permute-start.1 = (bf16[2,128,256]{2,1,0:T(8,128)(2,1)S(1)}, bf16[2,128,256]{2,1,0:T(8,128)(2,1)S(1)}, u32[]{:S(2)}, u32[]{:S(2)}) collective-permute-start(bf16[2,128,256]{2,1,0:T(8,128)(2,1)S(1)} %get-tuple-element.50.refs_0_), channel_id=1, source_target_pairs={{0,4},{4,0},{8,12},{12,8},{16,20},{20,16},{24,28},{28,24},{32,36},... | collective-permute-start | bytes 393224 | tf_op jit(solution)/shard_map/ppermute | solution.py:362
  22.5 1.3 %collective-permute-start.2 = (bf16[2,128,256]{2,1,0:T(8,128)(2,1)S(1)}, bf16[2,128,256]{2,1,0:T(8,128)(2,1)S(1)}, u32[]{:S(2)}, u32[]{:S(2)}) collective-permute-start(bf16[2,128,256]{2,1,0:T(8,128)(2,1)S(1)} %get-tuple-element.51.refs_1_), channel_id=1, source_target_pairs={{0,4},{4,0},{8,12},{12,8},{16,20},{20,16},{24,28},{28,24},{32,36},... | collective-permute-start | bytes 393224 | tf_op jit(solution)/shard_map/ppermute | solution.py:362
  22.5 6.4 %collective-permute-start.11 = (bf16[2,128,256]{2,1,0:T(8,128)(2,1)S(1)}, bf16[2,128,256]{2,1,0:T(8,128)(2,1)S(1)}, u32[]{:S(2)}, u32[]{:S(2)}) collective-permute-start(bf16[2,128,256]{2,1,0:T(8,128)(2,1)S(1)} %shard_map.93.refs_1_), channel_id=1, source_target_pairs={{0,8},{4,12},{8,0},{12,4},{16,24},{20,28},{24,16},{28,20},{32,40},... | collective-permute-start | bytes 393224 | tf_op jit(solution)/shard_map/ppermute | solution.py:362
  24.6 6.6 %collective-permute-start.3 = (bf16[2,128,256]{2,1,0:T(8,128)(2,1)S(1)}, bf16[2,128,256]{2,1,0:T(8,128)(2,1)S(1)}, u32[]{:S(2)}, u32[]{:S(2)}) collective-permute-start(bf16[2,128,256]{2,1,0:T(8,128)(2,1)S(1)} %shard_map.95.refs_1_), channel_id=1, source_target_pairs={{0,8},{4,12},{8,0},{12,4},{16,24},{20,28},{24,16},{28,20},{32,40},... | collective-permute-start | bytes 393224 | tf_op jit(solution)/shard_map/ppermute | solution.py:362
  29.6 6.7 %collective-permute-start.12 = (bf16[2,128,256]{2,1,0:T(8,128)(2,1)S(1)}, bf16[2,128,256]{2,1,0:T(8,128)(2,1)S(1)}, u32[]{:S(2)}, u32[]{:S(2)}) collective-permute-start(bf16[2,128,256]{2,1,0:T(8,128)(2,1)S(1)} %get-tuple-element.64.refs_1_), channel_id=1, source_target_pairs={{0,16},{4,20},{8,24},{12,28},{16,0},{20,4},{24,8},{28,12},{32,48},... | collective-permute-start | bytes 393224 | tf_op jit(solution)/shard_map/ppermute | solution.py:362
  32.0 7.2 %collective-permute-start.4 = (bf16[2,128,256]{2,1,0:T(8,128)(2,1)S(1)}, bf16[2,128,256]{2,1,0:T(8,128)(2,1)S(1)}, u32[]{:S(2)}, u32[]{:S(2)}) collective-permute-start(bf16[2,128,256]{2,1,0:T(8,128)(2,1)S(1)} %get-tuple-element.53.refs_1_), channel_id=1, source_target_pairs={{0,16},{4,20},{8,24},{12,28},{16,0},{20,4},{24,8},{28,12},{32,48},... | collective-permute-start | bytes 393224 | tf_op jit(solution)/shard_map/ppermute | solution.py:362
  37.1 5.6 %collective-permute-start.13 = (bf16[2,128,256]{2,1,0:T(8,128)(2,1)S(1)}, bf16[2,128,256]{2,1,0:T(8,128)(2,1)S(1)}, u32[]{:S(2)}, u32[]{:S(2)}) collective-permute-start(bf16[2,128,256]{2,1,0:T(8,128)(2,1)S(1)} %get-tuple-element.67.refs_1_), channel_id=1, source_target_pairs={{0,32},{4,36},{8,40},{12,44},{16,48},{20,52},{24,56},{28,60},{32,0... | collective-permute-start | bytes 393224 | tf_op jit(solution)/shard_map/ppermute | solution.py:362
  39.9 7.7 %collective-permute-start.5 = (bf16[2,128,256]{2,1,0:T(8,128)(2,1)S(1)}, bf16[2,128,256]{2,1,0:T(8,128)(2,1)S(1)}, u32[]{:S(2)}, u32[]{:S(2)}) collective-permute-start(bf16[2,128,256]{2,1,0:T(8,128)(2,1)S(1)} %get-tuple-element.56.refs_1_), channel_id=1, source_target_pairs={{0,32},{4,36},{8,40},{12,44},{16,48},{20,52},{24,56},{28,60},{32,0... | collective-permute-start | bytes 393224 | tf_op jit(solution)/shard_map/ppermute | solution.py:362
  43.5 7.4 %collective-permute-start.14 = (bf16[2,128,128]{2,1,0:T(8,128)(2,1)S(1)}, bf16[2,128,128]{2,1,0:T(8,128)(2,1)S(1)}, u32[]{:S(2)}, u32[]{:S(2)}) collective-permute-start(bf16[2,128,128]{2,1,0:T(8,128)(2,1)S(1)} %slice.13), channel_id=1, source_target_pairs={{0,64},{4,68},{8,72},{12,76},{16,80},{20,84},{24,88},{28,92},{32,9... | collective-permute-start | bytes 196616 | tf_op jit(solution)/shard_map/ppermute | solution.py:362
  48.4 5.8 %collective-permute-start.6 = (bf16[2,128,128]{2,1,0:T(8,128)(2,1)S(1)}, bf16[2,128,128]{2,1,0:T(8,128)(2,1)S(1)}, u32[]{:S(2)}, u32[]{:S(2)}) collective-permute-start(bf16[2,128,128]{2,1,0:T(8,128)(2,1)S(1)} %slice.12), channel_id=1, source_target_pairs={{0,64},{4,68},{8,72},{12,76},{16,80},{20,84},{24,88},{28,92},{32,9... | collective-permute-start | bytes 196616 | tf_op jit(solution)/shard_map/ppermute | solution.py:362
  50.4 4.4 %collective-permute-start.15 = (bf16[2,128,128]{2,1,0:T(8,128)(2,1)S(1)}, bf16[2,128,128]{2,1,0:T(8,128)(2,1)S(1)}, u32[]{:S(2)}, u32[]{:S(2)}) collective-permute-start(bf16[2,128,128]{2,1,0:T(8,128)(2,1)S(1)} %get-tuple-element.63.refs_5_), channel_id=1, source_target_pairs={{0,4},{4,0},{8,12},{12,8},{16,20},{20,16},{24,28},{28,24},{32,36},... | collective-permute-start | bytes 196616 | tf_op jit(solution)/shard_map/ppermute | solution.py:362
  50.4 5.0 %collective-permute-start.16 = (bf16[2,128,128]{2,1,0:T(8,128)(2,1)S(1)}, bf16[2,128,128]{2,1,0:T(8,128)(2,1)S(1)}, u32[]{:S(2)}, u32[]{:S(2)}) collective-permute-start(bf16[2,128,128]{2,1,0:T(8,128)(2,1)S(1)} %get-tuple-element.66.refs_6_), channel_id=1, source_target_pairs={{0,4},{4,0},{8,12},{12,8},{16,20},{20,16},{24,28},{28,24},{32,36},... | collective-permute-start | bytes 196616 | tf_op jit(solution)/shard_map/ppermute | solution.py:362
  50.9 4.6 %collective-permute-start.17 = (bf16[2,128,128]{2,1,0:T(8,128)(2,1)S(1)}, bf16[2,128,128]{2,1,0:T(8,128)(2,1)S(1)}, u32[]{:S(2)}, u32[]{:S(2)}) collective-permute-start(bf16[2,128,128]{2,1,0:T(8,128)(2,1)S(1)} %get-tuple-element.69.refs_7_), channel_id=1, source_target_pairs={{0,4},{4,0},{8,12},{12,8},{16,20},{20,16},{24,28},{28,24},{32,36},... | collective-permute-start | bytes 196616 | tf_op jit(solution)/shard_map/ppermute | solution.py:362
  50.9 5.0 %copy-start = (f32[1024]{0:T(1024)S(1)}, f32[1024]{0:T(1024)}, u32[]{:S(2)}) copy-start(f32[1024]{0:T(1024)} %param.16) | copy-start | bytes 12292
  50.9 5.0 %copy-start.1 = (f32[512,512]{1,0:T(8,128)S(1)}, f32[512,512]{1,0:T(8,128)}, u32[]{:S(2)}) copy-start(f32[512,512]{1,0:T(8,128)} %get-tuple-element.61.refs_0_) | copy-start | bytes 3145732
  50.9 5.0 %copy-start.4 = (bf16[512,512]{1,0:T(8,128)(2,1)S(1)}, bf16[512,512]{1,0:T(8,128)(2,1)}, u32[]{:S(2)}) copy-start(bf16[512,512]{1,0:T(8,128)(2,1)} %get-tuple-element.62.refs_1_) | copy-start | bytes 1572868
  51.5 4.4 %collective-permute-start.18 = (bf16[2,128,128]{2,1,0:T(8,128)(2,1)S(1)}, bf16[2,128,128]{2,1,0:T(8,128)(2,1)S(1)}, u32[]{:S(2)}, u32[]{:S(2)}) collective-permute-start(bf16[2,128,128]{2,1,0:T(8,128)(2,1)S(1)} %shard_map.103.refs_8_), channel_id=1, source_target_pairs={{0,4},{4,0},{8,12},{12,8},{16,20},{20,16},{24,28},{28,24},{32,36},... | collective-permute-start | bytes 196616 | tf_op jit(solution)/shard_map/ppermute | solution.py:362
  54.2 5.6 %collective-permute-start.7 = (bf16[2,128,128]{2,1,0:T(8,128)(2,1)S(1)}, bf16[2,128,128]{2,1,0:T(8,128)(2,1)S(1)}, u32[]{:S(2)}, u32[]{:S(2)}) collective-permute-start(bf16[2,128,128]{2,1,0:T(8,128)(2,1)S(1)} %get-tuple-element.52.refs_8_), channel_id=1, source_target_pairs={{0,4},{4,0},{8,12},{12,8},{16,20},{20,16},{24,28},{28,24},{32,36},... | collective-permute-start | bytes 196616 | tf_op jit(solution)/shard_map/ppermute | solution.py:362
  54.8 5.0 %collective-permute-start.8 = (bf16[2,128,128]{2,1,0:T(8,128)(2,1)S(1)}, bf16[2,128,128]{2,1,0:T(8,128)(2,1)S(1)}, u32[]{:S(2)}, u32[]{:S(2)}) collective-permute-start(bf16[2,128,128]{2,1,0:T(8,128)(2,1)S(1)} %get-tuple-element.55.refs_9_), channel_id=1, source_target_pairs={{0,4},{4,0},{8,12},{12,8},{16,20},{20,16},{24,28},{28,24},{32,36},... | collective-permute-start | bytes 196616 | tf_op jit(solution)/shard_map/ppermute | solution.py:362
  55.4 4.4 %collective-permute-start.9 = (bf16[2,128,128]{2,1,0:T(8,128)(2,1)S(1)}, bf16[2,128,128]{2,1,0:T(8,128)(2,1)S(1)}, u32[]{:S(2)}, u32[]{:S(2)}) collective-permute-start(bf16[2,128,128]{2,1,0:T(8,128)(2,1)S(1)} %get-tuple-element.58.refs_10_), channel_id=1, source_target_pairs={{0,4},{4,0},{8,12},{12,8},{16,20},{20,16},{24,28},{28,24},{32,36},... | collective-permute-start | bytes 196616 | tf_op jit(solution)/shard_map/ppermute | solution.py:362
  55.5 4.3 %collective-permute-start.10 = (bf16[2,128,128]{2,1,0:T(8,128)(2,1)S(1)}, bf16[2,128,128]{2,1,0:T(8,128)(2,1)S(1)}, u32[]{:S(2)}, u32[]{:S(2)}) collective-permute-start(bf16[2,128,128]{2,1,0:T(8,128)(2,1)S(1)} %shard_map.99.refs_11_), channel_id=1, source_target_pairs={{0,4},{4,0},{8,12},{12,8},{16,20},{20,16},{24,28},{28,24},{32,36},... | collective-permute-start | bytes 196616 | tf_op jit(solution)/shard_map/ppermute | solution.py:362
  55.9 3.9 %copy-start.2 = (f32[512,256]{1,0:T(8,128)S(1)}, f32[512,256]{1,0:T(8,128)}, u32[]{:S(2)}) copy-start(f32[512,256]{1,0:T(8,128)} %get-tuple-element.44.refs_0_) | copy-start | bytes 1572868
  56.0 3.9 %copy-start.3 = (f32[512,256]{1,0:T(8,128)S(1)}, f32[512,256]{1,0:T(8,128)}, u32[]{:S(2)}) copy-start(f32[512,256]{1,0:T(8,128)} %get-tuple-element.47.refs_1_) | copy-start | bytes 1572868
  56.0 3.9 %copy-start.5 = (bf16[512,256]{1,0:T(8,128)(2,1)S(1)}, bf16[512,256]{1,0:T(8,128)(2,1)}, u32[]{:S(2)}) copy-start(bf16[512,256]{1,0:T(8,128)(2,1)} %get-tuple-element.48.refs_2_) | copy-start | bytes 786436
  56.0 3.9 %copy-start.6 = (bf16[512,256]{1,0:T(8,128)(2,1)S(1)}, bf16[512,256]{1,0:T(8,128)(2,1)}, u32[]{:S(2)}) copy-start(bf16[512,256]{1,0:T(8,128)(2,1)} %get-tuple-element.49.refs_3_) | copy-start | bytes 786436
  56.0 7.6 %slice-start = ((s8[8388608]{0:T(1024)(128)(4,1)}), s8[4194304]{0:T(1024)(128)(4,1)S(1)}, s32[]{:S(2)}) async-start(s8[8388608]{0:T(1024)(128)(4,1)} %bitcast.8), calls=%async_computation | async-start | bytes 8388608
  59.8 3.8 %slice-start.1 = ((s8[8388608]{0:T(1024)(128)(4,1)}), s8[4194304]{0:T(1024)(128)(4,1)S(1)}, s32[]{:S(2)}) async-start(s8[8388608]{0:T(1024)(128)(4,1)} %bitcast.8), calls=%async_computation.1 | async-start | bytes 8388608
  70.5 9.2 %collective-permute-start.19 = (bf16[128,1024]{1,0:T(8,128)(2,1)S(1)}, bf16[128,1024]{1,0:T(8,128)(2,1)S(1)}, u32[]{:S(2)}, u32[]{:S(2)}) collective-permute-start(bf16[128,1024]{1,0:T(8,128)(2,1)S(1)} %fusion.32), channel_id=1, source_target_pairs={{0,1},{1,2},{2,3},{3,0},{4,5},{5,6},{6,7},{7,4},{8,9},{9,10},{10,1... | collective-permute-start | bytes 786440 | tf_op jit(solution)/shard_map/ppermute | solution.py:390
  70.8 10.5 %collective-permute-start.23 = (bf16[128,1024]{1,0:T(8,128)(2,1)S(1)}, bf16[128,1024]{1,0:T(8,128)(2,1)S(1)}, u32[]{:S(2)}, u32[]{:S(2)}) collective-permute-start(bf16[128,1024]{1,0:T(8,128)(2,1)S(1)} %fusion.68), channel_id=1, source_target_pairs={{0,3},{1,0},{2,1},{3,2},{4,7},{5,4},{6,5},{7,6},{8,11},{9,8},{10,9... | collective-permute-start | bytes 786440 | tf_op jit(solution)/shard_map/ppermute | solution.py:390
  73.0 12.3 %collective-permute-start.22 = (bf16[128,1024]{1,0:T(8,128)(2,1)S(1)}, bf16[128,1024]{1,0:T(8,128)(2,1)S(1)}, u32[]{:S(2)}, u32[]{:S(2)}) collective-permute-start(bf16[128,1024]{1,0:T(8,128)(2,1)S(1)} %fusion.56), channel_id=1, source_target_pairs={{0,1},{1,2},{2,3},{3,0},{4,5},{5,6},{6,7},{7,4},{8,9},{9,10},{10,1... | collective-permute-start | bytes 786440 | tf_op jit(solution)/shard_map/ppermute | solution.py:390
  74.6 12.3 %collective-permute-start.21 = (bf16[128,1024]{1,0:T(8,128)(2,1)S(1)}, bf16[128,1024]{1,0:T(8,128)(2,1)S(1)}, u32[]{:S(2)}, u32[]{:S(2)}) collective-permute-start(bf16[128,1024]{1,0:T(8,128)(2,1)S(1)} %fusion.44), channel_id=1, source_target_pairs={{0,3},{1,0},{2,1},{3,2},{4,7},{5,4},{6,5},{7,6},{8,11},{9,8},{10,9... | collective-permute-start | bytes 786440 | tf_op jit(solution)/shard_map/ppermute | solution.py:390
  79.8 11.2 %collective-permute-start.20 = (bf16[128,1024]{1,0:T(8,128)(2,1)S(1)}, bf16[128,1024]{1,0:T(8,128)(2,1)S(1)}, u32[]{:S(2)}, u32[]{:S(2)}) collective-permute-start(bf16[128,1024]{1,0:T(8,128)(2,1)S(1)} %add_convert_fusion.11), channel_id=1, source_target_pairs={{0,1},{1,2},{2,3},{3,0},{4,5},{5,6},{6,7},{7,4},{8,9},{9,10},{10,1... | collective-permute-start | bytes 786440 | tf_op jit(solution)/shard_map/ppermute | solution.py:390
  81.4 11.2 %collective-permute-start.27 = (bf16[128,1024]{1,0:T(8,128)(2,1)S(1)}, bf16[128,1024]{1,0:T(8,128)(2,1)S(1)}, u32[]{:S(2)}, u32[]{:S(2)}) collective-permute-start(bf16[128,1024]{1,0:T(8,128)(2,1)S(1)} %add_convert_fusion.10), channel_id=1, source_target_pairs={{0,3},{1,0},{2,1},{3,2},{4,7},{5,4},{6,5},{7,6},{8,11},{9,8},{10,9... | collective-permute-start | bytes 786440 | tf_op jit(solution)/shard_map/ppermute | solution.py:390
  85.4 11.2 %collective-permute-start.26 = (bf16[128,1024]{1,0:T(8,128)(2,1)S(1)}, bf16[128,1024]{1,0:T(8,128)(2,1)S(1)}, u32[]{:S(2)}, u32[]{:S(2)}) collective-permute-start(bf16[128,1024]{1,0:T(8,128)(2,1)S(1)} %add_convert_fusion.9), channel_id=1, source_target_pairs={{0,1},{1,2},{2,3},{3,0},{4,5},{5,6},{6,7},{7,4},{8,9},{9,10},{10,1... | collective-permute-start | bytes 786440 | tf_op jit(solution)/shard_map/ppermute | solution.py:390
  87.0 11.2 %collective-permute-start.25 = (bf16[128,1024]{1,0:T(8,128)(2,1)S(1)}, bf16[128,1024]{1,0:T(8,128)(2,1)S(1)}, u32[]{:S(2)}, u32[]{:S(2)}) collective-permute-start(bf16[128,1024]{1,0:T(8,128)(2,1)S(1)} %add_convert_fusion.8), channel_id=1, source_target_pairs={{0,3},{1,0},{2,1},{3,2},{4,7},{5,4},{6,5},{7,6},{8,11},{9,8},{10,9... | collective-permute-start | bytes 786440 | tf_op jit(solution)/shard_map/ppermute | solution.py:390
  91.0 11.2 %collective-permute-start.24 = (bf16[128,1024]{1,0:T(8,128)(2,1)S(1)}, bf16[128,1024]{1,0:T(8,128)(2,1)S(1)}, u32[]{:S(2)}, u32[]{:S(2)}) collective-permute-start(bf16[128,1024]{1,0:T(8,128)(2,1)S(1)} %add_convert_fusion.7), channel_id=1, source_target_pairs={{0,1},{1,2},{2,3},{3,0},{4,5},{5,6},{6,7},{7,4},{8,9},{9,10},{10,1... | collective-permute-start | bytes 786440 | tf_op jit(solution)/shard_map/ppermute | solution.py:390
  92.6 11.1 %collective-permute-start.29 = (bf16[128,1024]{1,0:T(8,128)(2,1)S(1)}, bf16[128,1024]{1,0:T(8,128)(2,1)S(1)}, u32[]{:S(2)}, u32[]{:S(2)}) collective-permute-start(bf16[128,1024]{1,0:T(8,128)(2,1)S(1)} %add_convert_fusion.6), channel_id=1, source_target_pairs={{0,3},{1,0},{2,1},{3,2},{4,7},{5,4},{6,5},{7,6},{8,11},{9,8},{10,9... | collective-permute-start | bytes 786440 | tf_op jit(solution)/shard_map/ppermute | solution.py:390
  96.6 10.3 %collective-permute-start.28 = (bf16[128,1024]{1,0:T(8,128)(2,1)S(1)}, bf16[128,1024]{1,0:T(8,128)(2,1)S(1)}, u32[]{:S(2)}, u32[]{:S(2)}) collective-permute-start(bf16[128,1024]{1,0:T(8,128)(2,1)S(1)} %add_convert_fusion.5), channel_id=1, source_target_pairs={{0,1},{1,2},{2,3},{3,0},{4,5},{5,6},{6,7},{7,4},{8,9},{9,10},{10,1... | collective-permute-start | bytes 786440 | tf_op jit(solution)/shard_map/ppermute | solution.py:390
  98.2 10.2 %collective-permute-start.30 = (bf16[128,1024]{1,0:T(8,128)(2,1)S(1)}, bf16[128,1024]{1,0:T(8,128)(2,1)S(1)}, u32[]{:S(2)}, u32[]{:S(2)}) collective-permute-start(bf16[128,1024]{1,0:T(8,128)(2,1)S(1)} %add_convert_fusion.4), channel_id=1, source_target_pairs={{0,3},{1,0},{2,1},{3,2},{4,7},{5,4},{6,5},{7,6},{8,11},{9,8},{10,9... | collective-permute-start | bytes 786440 | tf_op jit(solution)/shard_map/ppermute | solution.py:390

commit v4 on v3

--- a/solution.py
+++ b/solution.py
@@ -12,7 +12,8 @@
 HEAD_DIM = 128
 LOCAL_LEVELS = 4
 TOGETHER = 2
-CHUNKS = 2
+GROUP = 8
+CHIPS = 4
 PIECES = 2
 EPS = 1e-06
 F32 = jnp.float32
@@ -23,7 +24,7 @@
     return jnp.dot(a, b, preferred_element_type=F32)
 
 
-def local_kernel(base, stride, flags, q_ref, k_ref, v_ref, log_ref, beta_ref, weight_ref,
+def local_kernel(flags, q_ref, k_ref, v_ref, log_ref, beta_ref, weight_ref,
                  near_ref, far_ref, map_ref, rows_ref):
     step = pl.program_id(0)
     tokens = q_ref.shape[0]
@@ -59,7 +60,7 @@
     units = [(g, s) for g in range(TOGETHER) for s in range(supers)]
     cols, cum_rows, tail_rows, beta_rows = [], [], [], []
     for g in range(TOGETHER):
-        head = TOGETHER * (base + stride * step) + g
+        head = TOGETHER * step + g
         take = pl.ds(head, 1)
         beta_row = beta_ref[take, :]
         wanted = [rows_ref[0, take, :], rows_ref[2, take, :], beta_row]
@@ -158,17 +159,18 @@
         map_ref[g] = jnp.concatenate([total, eye * decay - erase], axis=1).astype(BF16)
 
 
-def local_part(base, stride, steps, flags, queries, keys, values, log_decay, beta, weights):
+def local_part(flags, queries, keys, values, log_decay, beta, weights):
     tokens = queries.shape[0]
     heads = log_decay.shape[0]
     wide = TOGETHER * HEAD_DIM
-    block = pl.BlockSpec((tokens, wide), lambda h, f: (0, base + stride * h))
-    out = pl.BlockSpec((tokens, wide), lambda h, f: (0, h))
+    steps = heads // TOGETHER
+    block = pl.BlockSpec((tokens, wide), lambda h, f: (0, h))
+    out = block
     whole2 = pl.BlockSpec((heads, tokens), lambda h, f: (0, 0))
     whole3 = pl.BlockSpec(weights.shape, lambda h, f: (0, 0, 0))
     part = steps * TOGETHER
     return pl.pallas_call(
-        functools.partial(local_kernel, base, stride),
+        local_kernel,
         grid_spec=pltpu.PrefetchScalarGridSpec(
             num_scalar_prefetch=1,
             grid=(steps,),
@@ -184,84 +186,78 @@
         ],
         compiler_params=pltpu.CompilerParams(vmem_limit_bytes=14 << 20),
         cost_estimate=pl.CostEstimate(flops=part * 1500000000, bytes_accessed=8 << 20, transcendentals=0),
+        name="local",
     )(flags, queries, keys, values, log_decay, beta, weights)
 
 
-def pair_kernel(bits, *refs):
+def join(later, first):
+    both = mm(later[:, HEAD_DIM:], first)
+    return jnp.concatenate([both[:, :HEAD_DIM] + later[:, :HEAD_DIM].astype(F32), both[:, HEAD_DIM:]], axis=1)
+
+
+def pair_kernel(bits, mine_ref, sib_ref, *outs):
     core = bits[0]
-    cur_ref = refs[-1]
-    half = cur_ref.shape[0]
-    parts = (len(refs) - 1) // 2
-    mine, sib = refs[:parts], refs[parts:2 * parts]
-
-    def run(first, second, offset):
-        for g in range(half):
-            later = second[offset + g]
-            both = mm(later[:, HEAD_DIM:], first[offset + g])
-            cur_ref[g, :, :HEAD_DIM] = (both[:, :HEAD_DIM] + later[:, :HEAD_DIM].astype(F32)).astype(BF16)
-            cur_ref[g, :, HEAD_DIM:] = both[:, HEAD_DIM:].astype(BF16)
+    chip = bits[1] + 2 * bits[2]
+
+    def run(first, second):
+        for d in range(CHIPS):
+            h = CHIPS * core + (chip ^ d)
+            outs[d][...] = join(second[h], first[h]).astype(BF16)
 
     @pl.when(core == 1)
     def _():
-        run(sib[-1], mine[-1], half if parts == 1 else 0)
+        run(sib_ref, mine_ref)
 
     @pl.when(core == 0)
     def _():
-        run(mine[0], sib[0], 0)
-
-
-def level_kernel(level, bits, *refs):
-    if level == 1:
-        sib_ref, cur_ref, new_ref, x_ref, carry_ref = refs
-    else:
-        sib_ref, cur_ref, carried_ref, new_ref, x_ref, carry_ref = refs
-    bit = bits[level]
-    half = cur_ref.shape[0]
-
-    def store(g, both, later):
-        new_ref[g, :, :HEAD_DIM] = (both[:, :HEAD_DIM] + later[:, :HEAD_DIM].astype(F32)).astype(BF16)
-        new_ref[g, :, HEAD_DIM:] = both[:, HEAD_DIM:].astype(BF16)
-
-    @pl.when(bit == 1)
-    def _():
-        for g in range(half):
-            later, sib = cur_ref[g], sib_ref[g]
-            if level == 1:
-                store(g, mm(later[:, HEAD_DIM:], sib), later)
-                x_ref[g] = sib[:, :HEAD_DIM]
-                carry_ref[g] = sib[:, HEAD_DIM:]
-            else:
-                both = mm(jnp.concatenate([later[:, HEAD_DIM:], carried_ref[g]], axis=0), sib)
-                store(g, both[:HEAD_DIM], later)
-                x_ref[g] = both[HEAD_DIM:, :HEAD_DIM].astype(BF16)
-                carry_ref[g] = both[HEAD_DIM:, HEAD_DIM:].astype(BF16)
-
-    @pl.when(bit == 0)
-    def _():
-        row_i = lax.broadcasted_iota(jnp.int32, (HEAD_DIM, HEAD_DIM), 0)
-        col_i = lax.broadcasted_iota(jnp.int32, (HEAD_DIM, HEAD_DIM), 1)
-        eye = (row_i == col_i).astype(F32).astype(BF16)
-        for g in range(half):
-            later = sib_ref[g]
-            store(g, mm(later[:, HEAD_DIM:], cur_ref[g]), later)
-            x_ref[g] = jnp.zeros((HEAD_DIM, HEAD_DIM), BF16)
-            carry_ref[g] = eye if level == 1 else carried_ref[g]
-
-
-def top_kernel(level, bits, sib_ref, carried_ref, x_ref):
-    bit = bits[level]
-
-    @pl.when(bit == 1)
-    def _():
-        for g in range(x_ref.shape[0]):
-            x_ref[g] = mm(carried_ref[g], sib_ref[g]).astype(BF16)
-
-    @pl.when(bit == 0)
-    def _():
-        x_ref[...] = jnp.zeros(x_ref.shape, BF16)
-
-
-def small_call(kernel, bits, args, outs):
+        run(mine_ref, sib_ref)
+
+
+def group_kernel(bits, *refs):
+    taken, (total_ref, *back_refs), (maps, backs) = refs[:CHIPS], refs[CHIPS:2 * CHIPS + 1], refs[2 * CHIPS + 1:]
+    chip = bits[1] + 2 * bits[2]
+    for d in range(CHIPS):
+        maps[chip ^ d] = taken[d][...]
+    row_i = lax.broadcasted_iota(jnp.int32, (HEAD_DIM, HEAD_DIM), 0)
+    col_i = lax.broadcasted_iota(jnp.int32, (HEAD_DIM, HEAD_DIM), 1)
+    eye = (row_i == col_i).astype(F32).astype(BF16)
+    none = jnp.zeros((HEAD_DIM, HEAD_DIM), BF16)
+    m0, m1, m2, m3 = (maps[i] for i in range(CHIPS))
+    low = join(m1, m0).astype(BF16)
+    high = join(m3, m2)
+    both = mm(jnp.concatenate([m2[:, HEAD_DIM:], high[:, HEAD_DIM:].astype(BF16)], axis=0), low)
+    third = both[:HEAD_DIM].astype(BF16)
+    total_ref[:, :HEAD_DIM] = (both[HEAD_DIM:, :HEAD_DIM] + high[:, :HEAD_DIM]).astype(BF16)
+    total_ref[:, HEAD_DIM:] = both[HEAD_DIM:, HEAD_DIM:].astype(BF16)
+    backs[0] = jnp.concatenate([none, none, eye], axis=1)
+    backs[1] = jnp.concatenate([m0[:, :HEAD_DIM], none, m0[:, HEAD_DIM:]], axis=1)
+    backs[2] = jnp.concatenate([none, low], axis=1)
+    backs[3] = jnp.concatenate([m2[:, :HEAD_DIM], third], axis=1)
+    for d in range(CHIPS):
+        back_refs[d][...] = backs[chip ^ d]
+
+
+def near_kernel(bits, sib_ref, cur_ref, state_ref, x_ref, carry_ref):
+    bit = bits[3]
+    row_i = lax.broadcasted_iota(jnp.int32, (HEAD_DIM, HEAD_DIM), 0)
+    col_i = lax.broadcasted_iota(jnp.int32, (HEAD_DIM, HEAD_DIM), 1)
+    eye = (row_i == col_i).astype(F32).astype(BF16)
+    sib, cur = sib_ref[...], cur_ref[...]
+    upper = bit == 1
+    first = jnp.where(upper, sib, cur)
+    later = jnp.where(upper, cur, sib)
+    state = mm(later[:, HEAD_DIM:], first[:, :HEAD_DIM]) + later[:, :HEAD_DIM].astype(F32)
+    state_ref[...] = state.astype(BF16)
+    x_ref[...] = jnp.where(upper, sib[:, :HEAD_DIM], jnp.zeros((HEAD_DIM, HEAD_DIM), BF16))
+    carry_ref[...] = jnp.where(upper, sib[:, HEAD_DIM:], eye)
+
+
+def top_kernel(bits, sib_ref, carried_ref, x_ref):
+    x = mm(carried_ref[...], sib_ref[...])
+    x_ref[...] = jnp.where(bits[4] == 1, x, 0.0).astype(BF16)
+
+
+def small_call(kernel, bits, args, outs, scratch=()):
     return pl.pallas_call(
         kernel,
         grid_spec=pltpu.PrefetchScalarGridSpec(
@@ -269,6 +265,7 @@
             grid=(1,),
             in_specs=[pl.BlockSpec(a.shape, lambda i, b, n=a.ndim: (0,) * n) for a in args],
             out_specs=[pl.BlockSpec(o.shape, lambda i, b, n=len(o.shape): (0,) * n) for o in outs],
+            scratch_shapes=list(scratch),
         ),
         out_shape=outs,
         compiler_params=pltpu.CompilerParams(vmem_limit_bytes=3 << 20),
@@ -276,90 +273,89 @@
     )(bits, *args)
 
 
-def final_kernel(levels, parts, chunk, bits, *refs):
+def final_kernel(base, bits, near_ref, far_ref, sib_ref, weight_ref, gain_ref, *refs):
     core = bits[0]
-    refs = list(refs)
-    near_refs = [refs.pop(0) for _ in range(parts)]
-    far_refs = [refs.pop(0) for _ in range(parts)]
-    sib_refs = [refs.pop(0) for _ in range(parts)]
-    weight_ref, gain_ref = refs[:2]
-    mine, other, z_ref = refs[2:2 + levels], refs[2 + levels:2 + 2 * levels], refs[-1]
-    tokens = near_refs[0].shape[0]
-    side = pl.program_id(0)
-    is_mine = side == core
+    chip = bits[1] + 2 * bits[2]
+    backs, nexts, tops = refs[:GROUP], refs[GROUP:2 * GROUP], refs[2 * GROUP:3 * GROUP]
+    z_ref, all_back, all_far = refs[-3:]
+    tokens = near_ref.shape[0]
+    step = pl.program_id(0)
     upper = core == 1
     first = LOCAL_LEVELS
 
+    @pl.when(step == 0)
+    def _():
+        for k in range(GROUP):
+            head = CHIPS * (core ^ (k & 1)) + (chip ^ (k >> 1))
+            all_back[head] = backs[k][...]
+            all_far[head, :, :HEAD_DIM] = nexts[k][...]
+            all_far[head, :, HEAD_DIM:] = tops[k][...]
+
     def lanes(g):
         return slice(g * HEAD_DIM, (g + 1) * HEAD_DIM)
 
-    def pick(group, where):
-        if parts == 1:
-            return group[0][where]
-        return jnp.where(side == 0, group[0][where], group[1][where])
-
+    heads = [TOGETHER * (base + step) + g for g in range(TOGETHER)]
+    back = [all_back[h] for h in heads]
+    outer = [mm(back[g][:, 2 * HEAD_DIM:], all_far[h]).astype(BF16) for g, h in enumerate(heads)]
+    states = [jnp.concatenate([back[g][:, :2 * HEAD_DIM], outer[g]], axis=1) for g in range(TOGETHER)]
+    moved = [mm(sib_ref[g, :, HEAD_DIM:], states[g]).astype(BF16) for g in range(TOGETHER)]
     stacks = []
     for g in range(TOGETHER):
-        sib = pick(sib_refs, g)
-        states = jnp.concatenate([jnp.where(is_mine, m[g], o[g]) for m, o in zip(mine, other)], axis=1)
-        states = jnp.where(upper, mm(sib[:, HEAD_DIM:], states).astype(BF16), states)
-        low = jnp.where(upper, sib[:, :HEAD_DIM], jnp.zeros((HEAD_DIM, HEAD_DIM), BF16))
-        stacks.append(jnp.transpose(jnp.concatenate([low, states], axis=1)))
-    step = 2 * SUPER
-    units = [(g, t) for g in range(TOGETHER) for t in range(0, tokens, step)]
-    reads = [lax.dot_general(stacks[g], pick(far_refs, (slice(t, t + step), lanes(g))),
+        low = jnp.where(upper, sib_ref[g, :, :HEAD_DIM], jnp.zeros((HEAD_DIM, HEAD_DIM), BF16))
+        stacks.append(jnp.transpose(jnp.concatenate([low, jnp.where(upper, moved[g], states[g])], axis=1)))
+    levels = stacks[0].shape[0] // HEAD_DIM
+    size = 2 * SUPER
+    units = [(g, t) for g in range(TOGETHER) for t in range(0, tokens, size)]
+    reads = [lax.dot_general(stacks[g], far_ref[t:t + size, lanes(g)],
                              (((1,), (1,)), ((), ())), preferred_element_type=F32) for g, t in units]
     for u, (g, t) in enumerate(units):
-        head = TOGETHER * (CHUNKS * side + chunk) + g
         turned = None
-        for i in range(levels + 1):
-            term = weight_ref[first + i, pl.ds(head, 1), t:t + step] * reads[u][i * HEAD_DIM:(i + 1) * HEAD_DIM]
+        for i in range(levels):
+            row = weight_ref[first + i, pl.ds(heads[g], 1), t:t + size]
+            term = row * reads[u][i * HEAD_DIM:(i + 1) * HEAD_DIM]
             turned = term if turned is None else turned + term
-        y = pick(near_refs, (slice(t, t + step), lanes(g))) + jnp.transpose(turned)
+        y = near_ref[t:t + size, lanes(g)] + jnp.transpose(turned)
         scale = lax.rsqrt(jnp.mean(y * y, axis=1, keepdims=True) + EPS)
-        z_ref[t:t + step, lanes(g)] = (y * scale * gain_ref[:, lanes(g)]).astype(BF16)
-
-
-def final_part(chunk, bits, nears, fars, sibs, weights, gain, mine, other, before):
-    tokens = nears[0].shape[0]
+        z_ref[t:t + size, lanes(g)] = (y * scale * gain_ref[:, lanes(g)]).astype(BF16)
+
+
+def final_part(base, steps, bits, near, far, sib, weights, gain, backs, nexts, tops, before=None):
+    tokens, width = near.shape
     wide = TOGETHER * HEAD_DIM
-    levels = len(mine)
-    parts = len(nears)
-    placed = lambda h, b: (0, CHUNKS * h + chunk)
-    state = pl.BlockSpec((TOGETHER, HEAD_DIM, HEAD_DIM), lambda h, b: (0, 0, 0))
-    if parts == 1:
-        block = pl.BlockSpec((tokens, wide), lambda h, b: (0, h))
-        maps = pl.BlockSpec((TOGETHER, HEAD_DIM, 2 * HEAD_DIM), lambda h, b: (h, 0, 0))
-    else:
-        block = pl.BlockSpec((tokens, wide), lambda h, b: (0, 0))
-        maps = pl.BlockSpec((TOGETHER, HEAD_DIM, 2 * HEAD_DIM), lambda h, b: (0, 0, 0))
-    in_specs = [block] * (2 * parts) + [maps] * parts
-    in_specs += [pl.BlockSpec(weights.shape, lambda h, b: (0, 0, 0)), pl.BlockSpec((1, wide), placed)]
-    in_specs += [state] * (2 * levels)
-    args = [bits, *nears, *fars, *sibs, weights, gain, *mine, *other]
+    block = pl.BlockSpec((tokens, wide), lambda h, b: (0, base + h))
+
+    def whole(a):
+        return pl.BlockSpec(a.shape, lambda h, b, n=a.ndim: (0,) * n)
+
+    rest = [*backs, *nexts, *tops]
+    in_specs = [block, block, pl.BlockSpec((TOGETHER, HEAD_DIM, 2 * HEAD_DIM), lambda h, b: (base + h, 0, 0)),
+                whole(weights), pl.BlockSpec((1, wide), lambda h, b: (0, base + h))] + [whole(a) for a in rest]
+    args = [bits, near, far, sib, weights, gain, *rest]
     aliases = {}
     if before is not None:
         aliases = {len(args): 0}
         args.append(before)
         in_specs.append(pl.BlockSpec(memory_space=pl.ANY))
     return pl.pallas_call(
-        functools.partial(final_kernel, levels, parts, chunk),
+        functools.partial(final_kernel, base),
         grid_spec=pltpu.PrefetchScalarGridSpec(
             num_scalar_prefetch=1,
-            grid=(2,),
+            grid=(steps,),
             in_specs=in_specs,
-            out_specs=pl.BlockSpec((tokens, wide), placed),
+            out_specs=block,
+            scratch_shapes=[pltpu.VMEM((GROUP, HEAD_DIM, 3 * HEAD_DIM), BF16),
+                            pltpu.VMEM((GROUP, HEAD_DIM, 2 * HEAD_DIM), BF16)],
         ),
-        out_shape=jax.ShapeDtypeStruct((tokens, gain.shape[1]), BF16),
+        out_shape=jax.ShapeDtypeStruct((tokens, width), BF16),
         input_output_aliases=aliases,
         compiler_params=pltpu.CompilerParams(vmem_limit_bytes=14 << 20),
         cost_estimate=pl.CostEstimate(flops=2400000000, bytes_accessed=4 << 20, transcendentals=0),
     )(*args)
 
 
-def partner(value, bit):
+def partner(value, mask):
     size = lax.axis_size("seq")
-    return lax.ppermute(value, "seq", [(i, i ^ (1 << bit)) for i in range(size)])
+    return lax.ppermute(value, "seq", [(i, i ^ mask) for i in range(size)])
 
 
 def order_pieces():
@@ -398,48 +394,35 @@
 
 
 def layer(queries, keys, values, log_decay, beta, level_weights, doc_start, norm_gain, out_weight):
-    heads = log_decay.shape[0]
-    mine_heads = heads // (2 * CHUNKS)
     nbits = lax.axis_size("seq").bit_length() - 1
     index = lax.axis_index("seq")
     bits = jnp.stack([(index >> b) & 1 for b in range(nbits)]).astype(jnp.int32)
-    gain = norm_gain.reshape(1, -1)
-    wide = jax.ShapeDtypeStruct((mine_heads, HEAD_DIM, 2 * HEAD_DIM), BF16)
-    square = jax.ShapeDtypeStruct((mine_heads, HEAD_DIM, HEAD_DIM), BF16)
     in_hbm = lambda x: pltpu.with_memory_space_constraint(x, pltpu.HBM)
-    given = [in_hbm(x) for x in (queries, keys, values, log_decay, beta, level_weights)]
-    doc_start = in_hbm(doc_start)
-
-    def local(base, stride, steps, flags):
-        near, far, maps = local_part(base, stride, steps, flags, *given)
-        return near, far, maps, partner(maps, 0)
-
-    front = local(0, CHUNKS, 2, doc_start)
-    low = local(1, CHUNKS, 1, doc_start)
-    cur = small_call(pair_kernel, bits, [front[2], front[3]], [wide])[0]
-    flags = lax.optimization_barrier((doc_start, cur))[0]
-    high = local(3, CHUNKS, 1, flags)
-    curs = [cur, small_call(pair_kernel, bits, [low[2], high[2], low[3], high[3]], [wide])[0]]
-    sources = [[front], [low, high]]
-    carried = [None] * CHUNKS
-    states = [[] for _ in range(CHUNKS)]
-    others = [[] for _ in range(CHUNKS)]
-    for level in range(1, nbits):
-        for c in range(CHUNKS):
-            if level < nbits - 1:
-                sib = partner(curs[c], level)
-                args = [sib, curs[c]] if level == 1 else [sib, curs[c], carried[c]]
-                curs[c], x, carried[c] = small_call(
-                    functools.partial(level_kernel, level), bits, args, [wide, square, square])
-            else:
-                sib = partner(curs[c][:, :, :HEAD_DIM], level)
-                x = small_call(functools.partial(top_kernel, level), bits, [sib, carried[c]], [square])[0]
-            states[c].append(x)
-            others[c].append(partner(x, 0))
+    given = [in_hbm(x) for x in (doc_start, queries, keys, values, log_decay, beta, level_weights)]
+    wide = jax.ShapeDtypeStruct((HEAD_DIM, 2 * HEAD_DIM), BF16)
+    square = jax.ShapeDtypeStruct((HEAD_DIM, HEAD_DIM), BF16)
+    back = jax.ShapeDtypeStruct((HEAD_DIM, 3 * HEAD_DIM), BF16)
+    near, far, maps = local_part(*given)
+    sib = partner(maps, 1)
+    sends = small_call(pair_kernel, bits, [maps, sib], [wide] * CHIPS)
+    taken = [sends[0]] + [partner(sends[d], 2 * d) for d in range(1, CHIPS)]
+    total, *outs = small_call(
+        group_kernel, bits, taken, [wide] + [back] * CHIPS,
+        [pltpu.VMEM((CHIPS, HEAD_DIM, 2 * HEAD_DIM), BF16), pltpu.VMEM((CHIPS, HEAD_DIM, 3 * HEAD_DIM), BF16)])
+    got = partner(total, GROUP)
+    state, x_near, carried = small_call(near_kernel, bits, [got, total], [square] * 3)
+    got = partner(state, 2 * GROUP)
+    x_top = small_call(top_kernel, bits, [got, carried], [square])[0]
+    backs = []
+    for d in range(CHIPS):
+        mine = outs[d] if d == 0 else partner(outs[d], 2 * d)
+        backs += [mine, partner(mine, 1)]
+    nexts = [x_near] + [partner(x_near, k) for k in range(1, GROUP)]
+    tops = [x_top] + [partner(x_top, k) for k in range(1, GROUP)]
     z = None
-    for c in range(CHUNKS):
-        nears, fars, _, sibs = zip(*sources[c])
-        z = final_part(c, bits, nears, fars, sibs, given[5], gain, states[c], others[c], z)
+    for base in (0, 2):
+        z = final_part(base, 2, bits, in_hbm(near), in_hbm(far), sib, given[6], norm_gain.reshape(1, -1),
+                       backs, nexts, tops, z)
     return project(z, out_weight)
 
 

time: 110 us -> 123 us (1.12)
  the two profiles are of different devices: /device:TPU:28 before, /device:TPU:0 now
where the time goes in v4:
time: 123 us
  starting transfers between devices  52.4 us (43%)
  waiting for transfers between devices  34.4 us (28%)
  Pallas kernels  27.1 us (22%)
  matrix products  7.14 us (6%)
  other arithmetic  1.85 us (2%)
    ppermute x27, starting transfers between devices, partner(): return lax.ppermute(value, 'seq', [(i, i ^ mask) for i in range(size)])  32.3 us
    ppermute x12, starting transfers between devices, project(): got[p] = lax.ppermute(sums[p], 'head', up if p < PIECES else down)  20.1 us
    ppermute x27, waiting for transfers between devices, partner(): return lax.ppermute(value, 'seq', [(i, i ^ mask) for i in range(size)])  19.5 us
    pallas_call x1, Pallas kernels, local_part(): pl.pallas_call(local_kernel, grid_spec=pltpu.PrefetchScalarGridSpec(num_s...  15.4 us
    ppermute x12, waiting for transfers between devices, project(): got[p] = lax.ppermute(sums[p], 'head', up if p < PIECES else down)  14.9 us
    pallas_call x2, Pallas kernels, final_part(): pl.pallas_call(functools.partial(final_kernel, base), grid_spec=pltpu.Pre...  8.64 us
    dot_general x16, matrix products, term(): return jnp.dot(part, w, preferred_element_type=F32).astype(BF16)  7.14 us
    pallas_call x4, Pallas kernels, small_call(): pl.pallas_call(kernel, grid_spec=pltpu.PrefetchScalarGridSpec(num_scalar_...  3.04 us
  transfers between devices with their start and end apart: 39, of which 17 were waited for; matrix products, arithmetic and copies ran while one was open for 1% of the time, Pallas kernels for 1%

profile of v4, /device:TPU:0, one launch (start us, length us, event | category | flops | bytes accessed | tf_op | source)
XLA Modules:
  0.0 123.3 jit_solution(8348223549825698840)
XLA Ops:
  0.0 15.4 %local.1 = (f32[512,1024]{1,0:T(8,128)}, bf16[512,1024]{1,0:T(8,128)(2,1)}, bf16[8,128,256]{2,1,0:T(8,128)(2,1)S(1)}) custom-call(s32[8]{0:T(128)} %flags.1, bf16[512,1024]{1,0:T(8,128)(2,1)} %q_ref.1, bf16[512,1024]{1,0:T(8,128)(2,1)} %k_ref.1, bf16[512,1024]{1,0:T(8,128)(2,1)} %v_ref.1, f32[8,512]{1,0:T(8,128)} %log_ref.1, f32[8,512]{1,0:T(8,128)} %beta_ref.1, ...), custom_call_target="tpu_custom_call" | custom-call | flops 12000000000 | bytes 8388608 | tf_op jit(solution)/shard_map/local/pallas_call | solution.py:172
  15.5 1.8 %collective-permute-done.sib_ref = bf16[8,128,256]{2,1,0:T(8,128)(2,1)S(1)} collective-permute-done((bf16[8,128,256]{2,1,0:T(8,128)(2,1)S(1)}, bf16[8,128,256]{2,1,0:T(8,128)(2,1)S(1)}, u32[]{:S(2)}, u32[]{:S(2)}) %collective-permute-start) | collective-permute-done | bytes 524320 | tf_op jit(solution)/shard_map/ppermute | solution.py:358
  17.3 0.8 shard_map.91
  18.1 1.7 %collective-permute-start.1 = (bf16[128,256]{1,0:T(8,128)(2,1)S(1)}, bf16[128,256]{1,0:T(8,128)(2,1)S(1)}, u32[]{:S(2)}, u32[]{:S(2)}) collective-permute-start(bf16[128,256]{1,0:T(8,128)(2,1)S(1)} %get-tuple-element.35), channel_id=1, source_target_pairs={{0,8},{4,12},{8,0},{12,4},{16,24},{20,28},{24,16},{28,20},{32,40},... | collective-permute-start | bytes 196616 | tf_op jit(solution)/shard_map/ppermute | solution.py:358
  19.8 2.7 %collective-permute-start.2 = (bf16[128,256]{1,0:T(8,128)(2,1)S(1)}, bf16[128,256]{1,0:T(8,128)(2,1)S(1)}, u32[]{:S(2)}, u32[]{:S(2)}) collective-permute-start(bf16[128,256]{1,0:T(8,128)(2,1)S(1)} %get-tuple-element.36), channel_id=1, source_target_pairs={{0,16},{4,20},{8,24},{12,28},{16,0},{20,4},{24,8},{28,12},{32,48},... | collective-permute-start | bytes 196616 | tf_op jit(solution)/shard_map/ppermute | solution.py:358
  22.9 3.2 %collective-permute-done.2.refs_2_ = bf16[128,256]{1,0:T(8,128)(2,1)S(1)} collective-permute-done((bf16[128,256]{1,0:T(8,128)(2,1)S(1)}, bf16[128,256]{1,0:T(8,128)(2,1)S(1)}, u32[]{:S(2)}, u32[]{:S(2)}) %collective-permute-start.2) | collective-permute-done | bytes 65568 | tf_op jit(solution)/shard_map/ppermute | solution.py:358
  26.0 2.0 %collective-permute-done.3.refs_3_ = bf16[128,256]{1,0:T(8,128)(2,1)S(1)} collective-permute-done((bf16[128,256]{1,0:T(8,128)(2,1)S(1)}, bf16[128,256]{1,0:T(8,128)(2,1)S(1)}, u32[]{:S(2)}, u32[]{:S(2)}) %collective-permute-start.3) | collective-permute-done | bytes 65568 | tf_op jit(solution)/shard_map/ppermute | solution.py:358
  28.0 0.9 shard_map.92
  28.9 2.0 %collective-permute-start.11 = (bf16[128,256]{1,0:T(8,128)(2,1)S(1)}, bf16[128,256]{1,0:T(8,128)(2,1)S(1)}, u32[]{:S(2)}, u32[]{:S(2)}) collective-permute-start(bf16[128,256]{1,0:T(8,128)(2,1)S(1)} %get-tuple-element.42.cur_ref), channel_id=1, source_target_pairs={{0,32},{4,36},{8,40},{12,44},{16,48},{20,52},{24,56},{28,60},{32,0... | collective-permute-start | bytes 196616 | tf_op jit(solution)/shard_map/ppermute | solution.py:358
  30.9 2.3 %collective-permute-done.11.sib_ref = bf16[128,256]{1,0:T(8,128)(2,1)S(1)} collective-permute-done((bf16[128,256]{1,0:T(8,128)(2,1)S(1)}, bf16[128,256]{1,0:T(8,128)(2,1)S(1)}, u32[]{:S(2)}, u32[]{:S(2)}) %collective-permute-start.11) | collective-permute-done | bytes 65568 | tf_op jit(solution)/shard_map/ppermute | solution.py:358
  33.3 0.7 shard_map.93
  33.9 3.9 %collective-permute-start.19 = (bf16[128,128]{1,0:T(8,128)(2,1)S(1)}, bf16[128,128]{1,0:T(8,128)(2,1)S(1)}, u32[]{:S(2)}, u32[]{:S(2)}) collective-permute-start(bf16[128,128]{1,0:T(8,128)(2,1)S(1)} %get-tuple-element.44), channel_id=1, source_target_pairs={{0,64},{4,68},{8,72},{12,76},{16,80},{20,84},{24,88},{28,92},{32,9... | collective-permute-start | bytes 98312 | tf_op jit(solution)/shard_map/ppermute | solution.py:358
  37.9 1.9 %collective-permute-start.14 = (bf16[128,128]{1,0:T(8,128)(2,1)S(1)}, bf16[128,128]{1,0:T(8,128)(2,1)S(1)}, u32[]{:S(2)}, u32[]{:S(2)}) collective-permute-start(bf16[128,128]{1,0:T(8,128)(2,1)S(1)} %get-tuple-element.43.refs_8_), channel_id=1, source_target_pairs={{0,12},{4,8},{8,4},{12,0},{16,28},{20,24},{24,20},{28,16},{32,44},... | collective-permute-start | bytes 98312 | tf_op jit(solution)/shard_map/ppermute | solution.py:358
  39.7 0.6 collective-permute-start.15
  40.3 2.6 %collective-permute-start.16 = (bf16[128,128]{1,0:T(8,128)(2,1)S(1)}, bf16[128,128]{1,0:T(8,128)(2,1)S(1)}, u32[]{:S(2)}, u32[]{:S(2)}) collective-permute-start(bf16[128,128]{1,0:T(8,128)(2,1)S(1)} %get-tuple-element.43.refs_8_), channel_id=1, source_target_pairs={{0,20},{4,16},{8,28},{12,24},{16,4},{20,0},{24,12},{28,8},{32,52},... | collective-permute-start | bytes 98312 | tf_op jit(solution)/shard_map/ppermute | solution.py:358
  42.9 0.7 collective-permute-start.17
  43.5 2.6 %collective-permute-start.9 = (bf16[128,384]{1,0:T(8,128)(2,1)S(1)}, bf16[128,384]{1,0:T(8,128)(2,1)S(1)}, u32[]{:S(2)}, u32[]{:S(2)}) collective-permute-start(bf16[128,384]{1,0:T(8,128)(2,1)S(1)} %get-tuple-element.41), channel_id=1, source_target_pairs={{0,24},{4,28},{8,16},{12,20},{16,8},{20,12},{24,0},{28,4},{32,56},... | collective-permute-start | bytes 294920 | tf_op jit(solution)/shard_map/ppermute | solution.py:358
  46.1 2.1 %collective-permute-start.7 = (bf16[128,384]{1,0:T(8,128)(2,1)S(1)}, bf16[128,384]{1,0:T(8,128)(2,1)S(1)}, u32[]{:S(2)}, u32[]{:S(2)}) collective-permute-start(bf16[128,384]{1,0:T(8,128)(2,1)S(1)} %get-tuple-element.40), channel_id=1, source_target_pairs={{0,16},{4,20},{8,24},{12,28},{16,0},{20,4},{24,8},{28,12},{32,48},... | collective-permute-start | bytes 294920 | tf_op jit(solution)/shard_map/ppermute | solution.py:358
  48.3 2.6 %collective-permute-start.18 = (bf16[128,128]{1,0:T(8,128)(2,1)S(1)}, bf16[128,128]{1,0:T(8,128)(2,1)S(1)}, u32[]{:S(2)}, u32[]{:S(2)}) collective-permute-start(bf16[128,128]{1,0:T(8,128)(2,1)S(1)} %get-tuple-element.43.refs_8_), channel_id=1, source_target_pairs={{0,28},{4,24},{8,20},{12,16},{16,12},{20,8},{24,4},{28,0},{32,60},... | collective-permute-start | bytes 98312 | tf_op jit(solution)/shard_map/ppermute | solution.py:358
  50.9 0.7 shard_map.94.refs_16_
  51.6 1.9 %collective-permute-done.18.refs_15_ = bf16[128,128]{1,0:T(8,128)(2,1)S(1)} collective-permute-done((bf16[128,128]{1,0:T(8,128)(2,1)S(1)}, bf16[128,128]{1,0:T(8,128)(2,1)S(1)}, u32[]{:S(2)}, u32[]{:S(2)}) %collective-permute-start.18) | collective-permute-done | bytes 32800 | tf_op jit(solution)/shard_map/ppermute | solution.py:358
  53.6 0.8 collective-permute-start.21
  54.4 1.0 collective-permute-start.22
  56.3 1.4 %collective-permute-done.21.refs_18_ = bf16[128,128]{1,0:T(8,128)(2,1)S(1)} collective-permute-done((bf16[128,128]{1,0:T(8,128)(2,1)S(1)}, bf16[128,128]{1,0:T(8,128)(2,1)S(1)}, u32[]{:S(2)}, u32[]{:S(2)}) %collective-permute-start.21) | collective-permute-done | bytes 32800 | tf_op jit(solution)/shard_map/ppermute | solution.py:358
  57.7 1.9 %collective-permute-start.23 = (bf16[128,128]{1,0:T(8,128)(2,1)S(1)}, bf16[128,128]{1,0:T(8,128)(2,1)S(1)}, u32[]{:S(2)}, u32[]{:S(2)}) collective-permute-start(bf16[128,128]{1,0:T(8,128)(2,1)S(1)} %shard_map.94.refs_16_), channel_id=1, source_target_pairs={{0,16},{4,20},{8,24},{12,28},{16,0},{20,4},{24,8},{28,12},{32,48},... | collective-permute-start | bytes 98312 | tf_op jit(solution)/shard_map/ppermute | solution.py:358
  59.6 1.2 collective-permute-start.24
  60.8 2.3 %collective-permute-done.23.refs_20_ = bf16[128,128]{1,0:T(8,128)(2,1)S(1)} collective-permute-done((bf16[128,128]{1,0:T(8,128)(2,1)S(1)}, bf16[128,128]{1,0:T(8,128)(2,1)S(1)}, u32[]{:S(2)}, u32[]{:S(2)}) %collective-permute-start.23) | collective-permute-done | bytes 32800 | tf_op jit(solution)/shard_map/ppermute | solution.py:358
  63.1 2.7 %collective-permute-start.25 = (bf16[128,128]{1,0:T(8,128)(2,1)S(1)}, bf16[128,128]{1,0:T(8,128)(2,1)S(1)}, u32[]{:S(2)}, u32[]{:S(2)}) collective-permute-start(bf16[128,128]{1,0:T(8,128)(2,1)S(1)} %shard_map.94.refs_16_), channel_id=1, source_target_pairs={{0,24},{4,28},{8,16},{12,20},{16,8},{20,12},{24,0},{28,4},{32,56},... | collective-permute-start | bytes 98312 | tf_op jit(solution)/shard_map/ppermute | solution.py:358
  65.9 2.3 %collective-permute-done.25.refs_22_ = bf16[128,128]{1,0:T(8,128)(2,1)S(1)} collective-permute-done((bf16[128,128]{1,0:T(8,128)(2,1)S(1)}, bf16[128,128]{1,0:T(8,128)(2,1)S(1)}, u32[]{:S(2)}, u32[]{:S(2)}) %collective-permute-start.25) | collective-permute-done | bytes 32800 | tf_op jit(solution)/shard_map/ppermute | solution.py:358
  68.2 2.1 %collective-permute-done.26.refs_23_ = bf16[128,128]{1,0:T(8,128)(2,1)S(1)} collective-permute-done((bf16[128,128]{1,0:T(8,128)(2,1)S(1)}, bf16[128,128]{1,0:T(8,128)(2,1)S(1)}, u32[]{:S(2)}, u32[]{:S(2)}) %collective-permute-start.26) | collective-permute-done | bytes 32800 | tf_op jit(solution)/shard_map/ppermute | solution.py:358
  70.4 4.3 %shard_map.95.refs_24_ = bf16[512,1024]{1,0:T(8,128)(2,1)S(1)} custom-call(s32[5]{0:T(128)S(1)} %stack.23.bits, f32[512,1024]{1,0:T(8,128)} %get-tuple-element.31.near_ref, bf16[512,1024]{1,0:T(8,128)(2,1)} %get-tuple-element.32.far_ref, bf16[8,128,256]{2,1,0:T(8,128)(2,1)S(1)} %collective-permute-done.sib_ref, f32[10,8,512]{2,1,0:T(8,128)} %weight_ref.5, ...), custom_call_target="tpu_custom_call" | custom-call | flops 2400000000 | bytes 4194304 | tf_op jit(solution)/shard_map/pallas_call | solution.py:339
  74.8 4.3 %shard_map.96 = bf16[512,1024]{1,0:T(8,128)(2,1)S(1)} custom-call(s32[5]{0:T(128)S(1)} %stack.23.bits, f32[512,1024]{1,0:T(8,128)} %get-tuple-element.31.near_ref, bf16[512,1024]{1,0:T(8,128)(2,1)} %get-tuple-element.32.far_ref, bf16[8,128,256]{2,1,0:T(8,128)(2,1)S(1)} %collective-permute-done.sib_ref, ...), custom_call_target="tpu_custom_call", output_to_operand_aliasing={{}: (30, {})} | custom-call | flops 2400000000 | bytes 4194304 | tf_op jit(solution)/shard_map/pallas_call | solution.py:339
  85.9 1.6 %collective-permute-start.27 = (bf16[128,1024]{1,0:T(8,128)(2,1)S(1)}, bf16[128,1024]{1,0:T(8,128)(2,1)S(1)}, u32[]{:S(2)}, u32[]{:S(2)}) collective-permute-start(bf16[128,1024]{1,0:T(8,128)(2,1)S(1)} %fusion.32), channel_id=1, source_target_pairs={{0,1},{1,2},{2,3},{3,0},{4,5},{5,6},{6,7},{7,4},{8,9},{9,10},{10,1... | collective-permute-start | bytes 786440 | tf_op jit(solution)/shard_map/ppermute | solution.py:386
  87.6 1.7 %collective-permute-start.31 = (bf16[128,1024]{1,0:T(8,128)(2,1)S(1)}, bf16[128,1024]{1,0:T(8,128)(2,1)S(1)}, u32[]{:S(2)}, u32[]{:S(2)}) collective-permute-start(bf16[128,1024]{1,0:T(8,128)(2,1)S(1)} %fusion.68), channel_id=1, source_target_pairs={{0,3},{1,0},{2,1},{3,2},{4,7},{5,4},{6,5},{7,6},{8,11},{9,8},{10,9... | collective-permute-start | bytes 786440 | tf_op jit(solution)/shard_map/ppermute | solution.py:386
  90.1 2.9 %collective-permute-start.29 = (bf16[128,1024]{1,0:T(8,128)(2,1)S(1)}, bf16[128,1024]{1,0:T(8,128)(2,1)S(1)}, u32[]{:S(2)}, u32[]{:S(2)}) collective-permute-start(bf16[128,1024]{1,0:T(8,128)(2,1)S(1)} %fusion.44), channel_id=1, source_target_pairs={{0,3},{1,0},{2,1},{3,2},{4,7},{5,4},{6,5},{7,6},{8,11},{9,8},{10,9... | collective-permute-start | bytes 786440 | tf_op jit(solution)/shard_map/ppermute | solution.py:386
  93.0 3.4 %collective-permute-done.27 = bf16[128,1024]{1,0:T(8,128)(2,1)S(1)} collective-permute-done((bf16[128,1024]{1,0:T(8,128)(2,1)S(1)}, bf16[128,1024]{1,0:T(8,128)(2,1)S(1)}, u32[]{:S(2)}, u32[]{:S(2)}) %collective-permute-start.27) | collective-permute-done | bytes 262176 | tf_op jit(solution)/shard_map/ppermute | solution.py:386
  96.4 0.5 collective-permute-start.28
  97.0 2.9 %collective-permute-start.35 = (bf16[128,1024]{1,0:T(8,128)(2,1)S(1)}, bf16[128,1024]{1,0:T(8,128)(2,1)S(1)}, u32[]{:S(2)}, u32[]{:S(2)}) collective-permute-start(bf16[128,1024]{1,0:T(8,128)(2,1)S(1)} %add_convert_fusion.10), channel_id=1, source_target_pairs={{0,3},{1,0},{2,1},{3,2},{4,7},{5,4},{6,5},{7,6},{8,11},{9,8},{10,9... | collective-permute-start | bytes 786440 | tf_op jit(solution)/shard_map/ppermute | solution.py:386
  99.9 2.1 %collective-permute-done.30 = bf16[128,1024]{1,0:T(8,128)(2,1)S(1)} collective-permute-done((bf16[128,1024]{1,0:T(8,128)(2,1)S(1)}, bf16[128,1024]{1,0:T(8,128)(2,1)S(1)}, u32[]{:S(2)}, u32[]{:S(2)}) %collective-permute-start.30) | collective-permute-done | bytes 262176 | tf_op jit(solution)/shard_map/ppermute | solution.py:386
  102.6 2.9 %collective-permute-start.33 = (bf16[128,1024]{1,0:T(8,128)(2,1)S(1)}, bf16[128,1024]{1,0:T(8,128)(2,1)S(1)}, u32[]{:S(2)}, u32[]{:S(2)}) collective-permute-start(bf16[128,1024]{1,0:T(8,128)(2,1)S(1)} %add_convert_fusion.8), channel_id=1, source_target_pairs={{0,3},{1,0},{2,1},{3,2},{4,7},{5,4},{6,5},{7,6},{8,11},{9,8},{10,9... | collective-permute-start | bytes 786440 | tf_op jit(solution)/shard_map/ppermute | solution.py:386
  105.5 2.1 %collective-permute-done.28 = bf16[128,1024]{1,0:T(8,128)(2,1)S(1)} collective-permute-done((bf16[128,1024]{1,0:T(8,128)(2,1)S(1)}, bf16[128,1024]{1,0:T(8,128)(2,1)S(1)}, u32[]{:S(2)}, u32[]{:S(2)}) %collective-permute-start.28) | collective-permute-done | bytes 262176 | tf_op jit(solution)/shard_map/ppermute | solution.py:386
  107.7 0.5 collective-permute-start.32
  108.2 2.9 %collective-permute-start.37 = (bf16[128,1024]{1,0:T(8,128)(2,1)S(1)}, bf16[128,1024]{1,0:T(8,128)(2,1)S(1)}, u32[]{:S(2)}, u32[]{:S(2)}) collective-permute-start(bf16[128,1024]{1,0:T(8,128)(2,1)S(1)} %add_convert_fusion.6), channel_id=1, source_target_pairs={{0,3},{1,0},{2,1},{3,2},{4,7},{5,4},{6,5},{7,6},{8,11},{9,8},{10,9... | collective-permute-start | bytes 786440 | tf_op jit(solution)/shard_map/ppermute | solution.py:386
  111.1 2.1 %collective-permute-done.34 = bf16[128,1024]{1,0:T(8,128)(2,1)S(1)} collective-permute-done((bf16[128,1024]{1,0:T(8,128)(2,1)S(1)}, bf16[128,1024]{1,0:T(8,128)(2,1)S(1)}, u32[]{:S(2)}, u32[]{:S(2)}) %collective-permute-start.34) | collective-permute-done | bytes 262176 | tf_op jit(solution)/shard_map/ppermute | solution.py:386
  113.8 2.9 %collective-permute-start.38 = (bf16[128,1024]{1,0:T(8,128)(2,1)S(1)}, bf16[128,1024]{1,0:T(8,128)(2,1)S(1)}, u32[]{:S(2)}, u32[]{:S(2)}) collective-permute-start(bf16[128,1024]{1,0:T(8,128)(2,1)S(1)} %add_convert_fusion.4), channel_id=1, source_target_pairs={{0,3},{1,0},{2,1},{3,2},{4,7},{5,4},{6,5},{7,6},{8,11},{9,8},{10,9... | collective-permute-start | bytes 786440 | tf_op jit(solution)/shard_map/ppermute | solution.py:386
  116.7 2.1 %collective-permute-done.32 = bf16[128,1024]{1,0:T(8,128)(2,1)S(1)} collective-permute-done((bf16[128,1024]{1,0:T(8,128)(2,1)S(1)}, bf16[128,1024]{1,0:T(8,128)(2,1)S(1)}, u32[]{:S(2)}, u32[]{:S(2)}) %collective-permute-start.32) | collective-permute-done | bytes 262176 | tf_op jit(solution)/shard_map/ppermute | solution.py:386
  119.3 2.8 %collective-permute-done.36 = bf16[128,1024]{1,0:T(8,128)(2,1)S(1)} collective-permute-done((bf16[128,1024]{1,0:T(8,128)(2,1)S(1)}, bf16[128,1024]{1,0:T(8,128)(2,1)S(1)}, u32[]{:S(2)}, u32[]{:S(2)}) %collective-permute-start.36) | collective-permute-done | bytes 262176 | tf_op jit(solution)/shard_map/ppermute | solution.py:386
  122.3 1.0 pad_maximum_fusion
  (74 shorter events, 11.4 us)
Async XLA Ops:
  15.4 1.9 %collective-permute-start = (bf16[8,128,256]{2,1,0:T(8,128)(2,1)S(1)}, bf16[8,128,256]{2,1,0:T(8,128)(2,1)S(1)}, u32[]{:S(2)}, u32[]{:S(2)}) collective-permute-start(bf16[8,128,256]{2,1,0:T(8,128)(2,1)S(1)} %get-tuple-element.33.mine_ref), channel_id=1, source_target_pairs={{0,4},{4,0},{8,12},{12,8},{16,20},{20,16},{24,28},{28,24},{32,36},... | collective-permute-start | bytes 1572872 | tf_op jit(solution)/shard_map/ppermute | solution.py:358
  18.1 4.8 %collective-permute-start.1 = (bf16[128,256]{1,0:T(8,128)(2,1)S(1)}, bf16[128,256]{1,0:T(8,128)(2,1)S(1)}, u32[]{:S(2)}, u32[]{:S(2)}) collective-permute-start(bf16[128,256]{1,0:T(8,128)(2,1)S(1)} %get-tuple-element.35), channel_id=1, source_target_pairs={{0,8},{4,12},{8,0},{12,4},{16,24},{20,28},{24,16},{28,20},{32,40},... | collective-permute-start | bytes 196616 | tf_op jit(solution)/shard_map/ppermute | solution.py:358
  19.8 6.2 %collective-permute-start.2 = (bf16[128,256]{1,0:T(8,128)(2,1)S(1)}, bf16[128,256]{1,0:T(8,128)(2,1)S(1)}, u32[]{:S(2)}, u32[]{:S(2)}) collective-permute-start(bf16[128,256]{1,0:T(8,128)(2,1)S(1)} %get-tuple-element.36), channel_id=1, source_target_pairs={{0,16},{4,20},{8,24},{12,28},{16,0},{20,4},{24,8},{28,12},{32,48},... | collective-permute-start | bytes 196616 | tf_op jit(solution)/shard_map/ppermute | solution.py:358
  22.5 5.5 %collective-permute-start.3 = (bf16[128,256]{1,0:T(8,128)(2,1)S(1)}, bf16[128,256]{1,0:T(8,128)(2,1)S(1)}, u32[]{:S(2)}, u32[]{:S(2)}) collective-permute-start(bf16[128,256]{1,0:T(8,128)(2,1)S(1)} %get-tuple-element.37), channel_id=1, source_target_pairs={{0,24},{4,28},{8,16},{12,20},{16,8},{20,12},{24,0},{28,4},{32,56},... | collective-permute-start | bytes 196616 | tf_op jit(solution)/shard_map/ppermute | solution.py:358
  28.9 41.5 %copy-start = (f32[1024]{0:T(1024)S(1)}, f32[1024]{0:T(1024)}, u32[]{:S(2)}) copy-start(f32[1024]{0:T(1024)} %param.16) | copy-start | bytes 12292
  28.9 4.3 %collective-permute-start.11 = (bf16[128,256]{1,0:T(8,128)(2,1)S(1)}, bf16[128,256]{1,0:T(8,128)(2,1)S(1)}, u32[]{:S(2)}, u32[]{:S(2)}) collective-permute-start(bf16[128,256]{1,0:T(8,128)(2,1)S(1)} %get-tuple-element.42.cur_ref), channel_id=1, source_target_pairs={{0,32},{4,36},{8,40},{12,44},{16,48},{20,52},{24,56},{28,60},{32,0... | collective-permute-start | bytes 196616 | tf_op jit(solution)/shard_map/ppermute | solution.py:358
  33.9 6.4 %collective-permute-start.19 = (bf16[128,128]{1,0:T(8,128)(2,1)S(1)}, bf16[128,128]{1,0:T(8,128)(2,1)S(1)}, u32[]{:S(2)}, u32[]{:S(2)}) collective-permute-start(bf16[128,128]{1,0:T(8,128)(2,1)S(1)} %get-tuple-element.44), channel_id=1, source_target_pairs={{0,64},{4,68},{8,72},{12,76},{16,80},{20,84},{24,88},{28,92},{32,9... | collective-permute-start | bytes 98312 | tf_op jit(solution)/shard_map/ppermute | solution.py:358
  37.9 5.0 %collective-permute-start.12 = (bf16[128,128]{1,0:T(8,128)(2,1)S(1)}, bf16[128,128]{1,0:T(8,128)(2,1)S(1)}, u32[]{:S(2)}, u32[]{:S(2)}) collective-permute-start(bf16[128,128]{1,0:T(8,128)(2,1)S(1)} %get-tuple-element.43.refs_8_), channel_id=1, source_target_pairs={{0,4},{4,0},{8,12},{12,8},{16,20},{20,16},{24,28},{28,24},{32,36},... | collective-permute-start | bytes 98312 | tf_op jit(solution)/shard_map/ppermute | solution.py:358
  37.9 5.7 %collective-permute-start.13 = (bf16[128,128]{1,0:T(8,128)(2,1)S(1)}, bf16[128,128]{1,0:T(8,128)(2,1)S(1)}, u32[]{:S(2)}, u32[]{:S(2)}) collective-permute-start(bf16[128,128]{1,0:T(8,128)(2,1)S(1)} %get-tuple-element.43.refs_8_), channel_id=1, source_target_pairs={{0,8},{4,12},{8,0},{12,4},{16,24},{20,28},{24,16},{28,20},{32,40},... | collective-permute-start | bytes 98312 | tf_op jit(solution)/shard_map/ppermute | solution.py:358
  37.9 8.2 %collective-permute-start.14 = (bf16[128,128]{1,0:T(8,128)(2,1)S(1)}, bf16[128,128]{1,0:T(8,128)(2,1)S(1)}, u32[]{:S(2)}, u32[]{:S(2)}) collective-permute-start(bf16[128,128]{1,0:T(8,128)(2,1)S(1)} %get-tuple-element.43.refs_8_), channel_id=1, source_target_pairs={{0,12},{4,8},{8,4},{12,0},{16,28},{20,24},{24,20},{28,16},{32,44},... | collective-permute-start | bytes 98312 | tf_op jit(solution)/shard_map/ppermute | solution.py:358
  39.7 6.4 %collective-permute-start.15 = (bf16[128,128]{1,0:T(8,128)(2,1)S(1)}, bf16[128,128]{1,0:T(8,128)(2,1)S(1)}, u32[]{:S(2)}, u32[]{:S(2)}) collective-permute-start(bf16[128,128]{1,0:T(8,128)(2,1)S(1)} %get-tuple-element.43.refs_8_), channel_id=1, source_target_pairs={{0,16},{4,20},{8,24},{12,28},{16,0},{20,4},{24,8},{28,12},{32,48},... | collective-permute-start | bytes 98312 | tf_op jit(solution)/shard_map/ppermute | solution.py:358
  40.3 7.9 %collective-permute-start.16 = (bf16[128,128]{1,0:T(8,128)(2,1)S(1)}, bf16[128,128]{1,0:T(8,128)(2,1)S(1)}, u32[]{:S(2)}, u32[]{:S(2)}) collective-permute-start(bf16[128,128]{1,0:T(8,128)(2,1)S(1)} %get-tuple-element.43.refs_8_), channel_id=1, source_target_pairs={{0,20},{4,16},{8,28},{12,24},{16,4},{20,0},{24,12},{28,8},{32,52},... | collective-permute-start | bytes 98312 | tf_op jit(solution)/shard_map/ppermute | solution.py:358
  42.9 5.5 %collective-permute-start.17 = (bf16[128,128]{1,0:T(8,128)(2,1)S(1)}, bf16[128,128]{1,0:T(8,128)(2,1)S(1)}, u32[]{:S(2)}, u32[]{:S(2)}) collective-permute-start(bf16[128,128]{1,0:T(8,128)(2,1)S(1)} %get-tuple-element.43.refs_8_), channel_id=1, source_target_pairs={{0,24},{4,28},{8,16},{12,20},{16,8},{20,12},{24,0},{28,4},{32,56},... | collective-permute-start | bytes 98312 | tf_op jit(solution)/shard_map/ppermute | solution.py:358
  43.5 10.1 %collective-permute-start.9 = (bf16[128,384]{1,0:T(8,128)(2,1)S(1)}, bf16[128,384]{1,0:T(8,128)(2,1)S(1)}, u32[]{:S(2)}, u32[]{:S(2)}) collective-permute-start(bf16[128,384]{1,0:T(8,128)(2,1)S(1)} %get-tuple-element.41), channel_id=1, source_target_pairs={{0,24},{4,28},{8,16},{12,20},{16,8},{20,12},{24,0},{28,4},{32,56},... | collective-permute-start | bytes 294920 | tf_op jit(solution)/shard_map/ppermute | solution.py:358
  46.1 8.3 %collective-permute-start.5 = (bf16[128,384]{1,0:T(8,128)(2,1)S(1)}, bf16[128,384]{1,0:T(8,128)(2,1)S(1)}, u32[]{:S(2)}, u32[]{:S(2)}) collective-permute-start(bf16[128,384]{1,0:T(8,128)(2,1)S(1)} %get-tuple-element.39), channel_id=1, source_target_pairs={{0,8},{4,12},{8,0},{12,4},{16,24},{20,28},{24,16},{28,20},{32,40},... | collective-permute-start | bytes 294920 | tf_op jit(solution)/shard_map/ppermute | solution.py:358
  46.1 9.2 %collective-permute-start.7 = (bf16[128,384]{1,0:T(8,128)(2,1)S(1)}, bf16[128,384]{1,0:T(8,128)(2,1)S(1)}, u32[]{:S(2)}, u32[]{:S(2)}) collective-permute-start(bf16[128,384]{1,0:T(8,128)(2,1)S(1)} %get-tuple-element.40), channel_id=1, source_target_pairs={{0,16},{4,20},{8,24},{12,28},{16,0},{20,4},{24,8},{28,12},{32,48},... | collective-permute-start | bytes 294920 | tf_op jit(solution)/shard_map/ppermute | solution.py:358
  48.3 7.5 %collective-permute-start.4 = (bf16[128,384]{1,0:T(8,128)(2,1)S(1)}, bf16[128,384]{1,0:T(8,128)(2,1)S(1)}, u32[]{:S(2)}, u32[]{:S(2)}) collective-permute-start(bf16[128,384]{1,0:T(8,128)(2,1)S(1)} %get-tuple-element.38.refs_0_), channel_id=1, source_target_pairs={{0,4},{4,0},{8,12},{12,8},{16,20},{20,16},{24,28},{28,24},{32,36},... | collective-permute-start | bytes 294920 | tf_op jit(solution)/shard_map/ppermute | solution.py:358
  48.3 5.2 %collective-permute-start.18 = (bf16[128,128]{1,0:T(8,128)(2,1)S(1)}, bf16[128,128]{1,0:T(8,128)(2,1)S(1)}, u32[]{:S(2)}, u32[]{:S(2)}) collective-permute-start(bf16[128,128]{1,0:T(8,128)(2,1)S(1)} %get-tuple-element.43.refs_8_), channel_id=1, source_target_pairs={{0,28},{4,24},{8,20},{12,16},{16,12},{20,8},{24,4},{28,0},{32,60},... | collective-permute-start | bytes 98312 | tf_op jit(solution)/shard_map/ppermute | solution.py:358
  53.5 2.4 %collective-permute-start.20 = (bf16[128,128]{1,0:T(8,128)(2,1)S(1)}, bf16[128,128]{1,0:T(8,128)(2,1)S(1)}, u32[]{:S(2)}, u32[]{:S(2)}) collective-permute-start(bf16[128,128]{1,0:T(8,128)(2,1)S(1)} %shard_map.94.refs_16_), channel_id=1, source_target_pairs={{0,4},{4,0},{8,12},{12,8},{16,20},{20,16},{24,28},{28,24},{32,36},... | collective-permute-start | bytes 98312 | tf_op jit(solution)/shard_map/ppermute | solution.py:358
  53.6 4.1 %collective-permute-start.21 = (bf16[128,128]{1,0:T(8,128)(2,1)S(1)}, bf16[128,128]{1,0:T(8,128)(2,1)S(1)}, u32[]{:S(2)}, u32[]{:S(2)}) collective-permute-start(bf16[128,128]{1,0:T(8,128)(2,1)S(1)} %shard_map.94.refs_16_), channel_id=1, source_target_pairs={{0,8},{4,12},{8,0},{12,4},{16,24},{20,28},{24,16},{28,20},{32,40},... | collective-permute-start | bytes 98312 | tf_op jit(solution)/shard_map/ppermute | solution.py:358
  54.4 5.2 %collective-permute-start.22 = (bf16[128,128]{1,0:T(8,128)(2,1)S(1)}, bf16[128,128]{1,0:T(8,128)(2,1)S(1)}, u32[]{:S(2)}, u32[]{:S(2)}) collective-permute-start(bf16[128,128]{1,0:T(8,128)(2,1)S(1)} %shard_map.94.refs_16_), channel_id=1, source_target_pairs={{0,12},{4,8},{8,4},{12,0},{16,28},{20,24},{24,20},{28,16},{32,44},... | collective-permute-start | bytes 98312 | tf_op jit(solution)/shard_map/ppermute | solution.py:358
  55.4 15.0 %collective-permute-start.10 = (bf16[128,384]{1,0:T(8,128)(2,1)S(1)}, bf16[128,384]{1,0:T(8,128)(2,1)S(1)}, u32[]{:S(2)}, u32[]{:S(2)}) collective-permute-start(bf16[128,384]{1,0:T(8,128)(2,1)S(1)} %collective-permute-done.9.refs_6_), channel_id=1, source_target_pairs={{0,4},{4,0},{8,12},{12,8},{16,20},{20,16},{24,28},{28,24},{32,36},... | collective-permute-start | bytes 294920 | tf_op jit(solution)/shard_map/ppermute | solution.py:358
  55.8 14.6 %collective-permute-start.6 = (bf16[128,384]{1,0:T(8,128)(2,1)S(1)}, bf16[128,384]{1,0:T(8,128)(2,1)S(1)}, u32[]{:S(2)}, u32[]{:S(2)}) collective-permute-start(bf16[128,384]{1,0:T(8,128)(2,1)S(1)} %collective-permute-done.5.refs_2_), channel_id=1, source_target_pairs={{0,4},{4,0},{8,12},{12,8},{16,20},{20,16},{24,28},{28,24},{32,36},... | collective-permute-start | bytes 294920 | tf_op jit(solution)/shard_map/ppermute | solution.py:358
  55.9 14.5 %collective-permute-start.8 = (bf16[128,384]{1,0:T(8,128)(2,1)S(1)}, bf16[128,384]{1,0:T(8,128)(2,1)S(1)}, u32[]{:S(2)}, u32[]{:S(2)}) collective-permute-start(bf16[128,384]{1,0:T(8,128)(2,1)S(1)} %collective-permute-done.7.refs_4_), channel_id=1, source_target_pairs={{0,4},{4,0},{8,12},{12,8},{16,20},{20,16},{24,28},{28,24},{32,36},... | collective-permute-start | bytes 294920 | tf_op jit(solution)/shard_map/ppermute | solution.py:358
  57.7 5.4 %collective-permute-start.23 = (bf16[128,128]{1,0:T(8,128)(2,1)S(1)}, bf16[128,128]{1,0:T(8,128)(2,1)S(1)}, u32[]{:S(2)}, u32[]{:S(2)}) collective-permute-start(bf16[128,128]{1,0:T(8,128)(2,1)S(1)} %shard_map.94.refs_16_), channel_id=1, source_target_pairs={{0,16},{4,20},{8,24},{12,28},{16,0},{20,4},{24,8},{28,12},{32,48},... | collective-permute-start | bytes 98312 | tf_op jit(solution)/shard_map/ppermute | solution.py:358
  59.6 6.2 %collective-permute-start.24 = (bf16[128,128]{1,0:T(8,128)(2,1)S(1)}, bf16[128,128]{1,0:T(8,128)(2,1)S(1)}, u32[]{:S(2)}, u32[]{:S(2)}) collective-permute-start(bf16[128,128]{1,0:T(8,128)(2,1)S(1)} %shard_map.94.refs_16_), channel_id=1, source_target_pairs={{0,20},{4,16},{8,28},{12,24},{16,4},{20,0},{24,12},{28,8},{32,52},... | collective-permute-start | bytes 98312 | tf_op jit(solution)/shard_map/ppermute | solution.py:358
  63.1 5.1 %collective-permute-start.25 = (bf16[128,128]{1,0:T(8,128)(2,1)S(1)}, bf16[128,128]{1,0:T(8,128)(2,1)S(1)}, u32[]{:S(2)}, u32[]{:S(2)}) collective-permute-start(bf16[128,128]{1,0:T(8,128)(2,1)S(1)} %shard_map.94.refs_16_), channel_id=1, source_target_pairs={{0,24},{4,28},{8,16},{12,20},{16,8},{20,12},{24,0},{28,4},{32,56},... | collective-permute-start | bytes 98312 | tf_op jit(solution)/shard_map/ppermute | solution.py:358
  65.8 4.6 %collective-permute-start.26 = (bf16[128,128]{1,0:T(8,128)(2,1)S(1)}, bf16[128,128]{1,0:T(8,128)(2,1)S(1)}, u32[]{:S(2)}, u32[]{:S(2)}) collective-permute-start(bf16[128,128]{1,0:T(8,128)(2,1)S(1)} %shard_map.94.refs_16_), channel_id=1, source_target_pairs={{0,28},{4,24},{8,20},{12,16},{16,12},{20,8},{24,4},{28,0},{32,60},... | collective-permute-start | bytes 98312 | tf_op jit(solution)/shard_map/ppermute | solution.py:358
  70.4 8.7 %slice-start = ((s8[8388608]{0:T(1024)(128)(4,1)}), s8[4194304]{0:T(1024)(128)(4,1)S(1)}, s32[]{:S(2)}) async-start(s8[8388608]{0:T(1024)(128)(4,1)} %bitcast.8), calls=%async_computation | async-start | bytes 8388608
  74.7 4.4 %slice-start.1 = ((s8[8388608]{0:T(1024)(128)(4,1)}), s8[4194304]{0:T(1024)(128)(4,1)S(1)}, s32[]{:S(2)}) async-start(s8[8388608]{0:T(1024)(128)(4,1)} %bitcast.8), calls=%async_computation.1 | async-start | bytes 8388608
  85.9 10.4 %collective-permute-start.27 = (bf16[128,1024]{1,0:T(8,128)(2,1)S(1)}, bf16[128,1024]{1,0:T(8,128)(2,1)S(1)}, u32[]{:S(2)}, u32[]{:S(2)}) collective-permute-start(bf16[128,1024]{1,0:T(8,128)(2,1)S(1)} %fusion.32), channel_id=1, source_target_pairs={{0,1},{1,2},{2,3},{3,0},{4,5},{5,6},{6,7},{7,4},{8,9},{9,10},{10,1... | collective-permute-start | bytes 786440 | tf_op jit(solution)/shard_map/ppermute | solution.py:386
  87.6 9.3 %collective-permute-start.31 = (bf16[128,1024]{1,0:T(8,128)(2,1)S(1)}, bf16[128,1024]{1,0:T(8,128)(2,1)S(1)}, u32[]{:S(2)}, u32[]{:S(2)}) collective-permute-start(bf16[128,1024]{1,0:T(8,128)(2,1)S(1)} %fusion.68), channel_id=1, source_target_pairs={{0,3},{1,0},{2,1},{3,2},{4,7},{5,4},{6,5},{7,6},{8,11},{9,8},{10,9... | collective-permute-start | bytes 786440 | tf_op jit(solution)/shard_map/ppermute | solution.py:386
  89.7 12.3 %collective-permute-start.30 = (bf16[128,1024]{1,0:T(8,128)(2,1)S(1)}, bf16[128,1024]{1,0:T(8,128)(2,1)S(1)}, u32[]{:S(2)}, u32[]{:S(2)}) collective-permute-start(bf16[128,1024]{1,0:T(8,128)(2,1)S(1)} %fusion.56), channel_id=1, source_target_pairs={{0,1},{1,2},{2,3},{3,0},{4,5},{5,6},{6,7},{7,4},{8,9},{9,10},{10,1... | collective-permute-start | bytes 786440 | tf_op jit(solution)/shard_map/ppermute | solution.py:386
  90.1 12.4 %collective-permute-start.29 = (bf16[128,1024]{1,0:T(8,128)(2,1)S(1)}, bf16[128,1024]{1,0:T(8,128)(2,1)S(1)}, u32[]{:S(2)}, u32[]{:S(2)}) collective-permute-start(bf16[128,1024]{1,0:T(8,128)(2,1)S(1)} %fusion.44), channel_id=1, source_target_pairs={{0,3},{1,0},{2,1},{3,2},{4,7},{5,4},{6,5},{7,6},{8,11},{9,8},{10,9... | collective-permute-start | bytes 786440 | tf_op jit(solution)/shard_map/ppermute | solution.py:386
  96.4 11.2 %collective-permute-start.28 = (bf16[128,1024]{1,0:T(8,128)(2,1)S(1)}, bf16[128,1024]{1,0:T(8,128)(2,1)S(1)}, u32[]{:S(2)}, u32[]{:S(2)}) collective-permute-start(bf16[128,1024]{1,0:T(8,128)(2,1)S(1)} %add_convert_fusion.11), channel_id=1, source_target_pairs={{0,1},{1,2},{2,3},{3,0},{4,5},{5,6},{6,7},{7,4},{8,9},{9,10},{10,1... | collective-permute-start | bytes 786440 | tf_op jit(solution)/shard_map/ppermute | solution.py:386
  97.0 11.2 %collective-permute-start.35 = (bf16[128,1024]{1,0:T(8,128)(2,1)S(1)}, bf16[128,1024]{1,0:T(8,128)(2,1)S(1)}, u32[]{:S(2)}, u32[]{:S(2)}) collective-permute-start(bf16[128,1024]{1,0:T(8,128)(2,1)S(1)} %add_convert_fusion.10), channel_id=1, source_target_pairs={{0,3},{1,0},{2,1},{3,2},{4,7},{5,4},{6,5},{7,6},{8,11},{9,8},{10,9... | collective-permute-start | bytes 786440 | tf_op jit(solution)/shard_map/ppermute | solution.py:386
  102.1 11.2 %collective-permute-start.34 = (bf16[128,1024]{1,0:T(8,128)(2,1)S(1)}, bf16[128,1024]{1,0:T(8,128)(2,1)S(1)}, u32[]{:S(2)}, u32[]{:S(2)}) collective-permute-start(bf16[128,1024]{1,0:T(8,128)(2,1)S(1)} %add_convert_fusion.9), channel_id=1, source_target_pairs={{0,1},{1,2},{2,3},{3,0},{4,5},{5,6},{6,7},{7,4},{8,9},{9,10},{10,1... | collective-permute-start | bytes 786440 | tf_op jit(solution)/shard_map/ppermute | solution.py:386
  102.6 11.2 %collective-permute-start.33 = (bf16[128,1024]{1,0:T(8,128)(2,1)S(1)}, bf16[128,1024]{1,0:T(8,128)(2,1)S(1)}, u32[]{:S(2)}, u32[]{:S(2)}) collective-permute-start(bf16[128,1024]{1,0:T(8,128)(2,1)S(1)} %add_convert_fusion.8), channel_id=1, source_target_pairs={{0,3},{1,0},{2,1},{3,2},{4,7},{5,4},{6,5},{7,6},{8,11},{9,8},{10,9... | collective-permute-start | bytes 786440 | tf_op jit(solution)/shard_map/ppermute | solution.py:386
  107.7 11.2 %collective-permute-start.32 = (bf16[128,1024]{1,0:T(8,128)(2,1)S(1)}, bf16[128,1024]{1,0:T(8,128)(2,1)S(1)}, u32[]{:S(2)}, u32[]{:S(2)}) collective-permute-start(bf16[128,1024]{1,0:T(8,128)(2,1)S(1)} %add_convert_fusion.7), channel_id=1, source_target_pairs={{0,1},{1,2},{2,3},{3,0},{4,5},{5,6},{6,7},{7,4},{8,9},{9,10},{10,1... | collective-permute-start | bytes 786440 | tf_op jit(solution)/shard_map/ppermute | solution.py:386
  108.2 11.0 %collective-permute-start.37 = (bf16[128,1024]{1,0:T(8,128)(2,1)S(1)}, bf16[128,1024]{1,0:T(8,128)(2,1)S(1)}, u32[]{:S(2)}, u32[]{:S(2)}) collective-permute-start(bf16[128,1024]{1,0:T(8,128)(2,1)S(1)} %add_convert_fusion.6), channel_id=1, source_target_pairs={{0,3},{1,0},{2,1},{3,2},{4,7},{5,4},{6,5},{7,6},{8,11},{9,8},{10,9... | collective-permute-start | bytes 786440 | tf_op jit(solution)/shard_map/ppermute | solution.py:386
  113.3 8.8 %collective-permute-start.36 = (bf16[128,1024]{1,0:T(8,128)(2,1)S(1)}, bf16[128,1024]{1,0:T(8,128)(2,1)S(1)}, u32[]{:S(2)}, u32[]{:S(2)}) collective-permute-start(bf16[128,1024]{1,0:T(8,128)(2,1)S(1)} %add_convert_fusion.5), channel_id=1, source_target_pairs={{0,1},{1,2},{2,3},{3,0},{4,5},{5,6},{6,7},{7,4},{8,9},{9,10},{10,1... | collective-permute-start | bytes 786440 | tf_op jit(solution)/shard_map/ppermute | solution.py:386
  113.8 8.4 %collective-permute-start.38 = (bf16[128,1024]{1,0:T(8,128)(2,1)S(1)}, bf16[128,1024]{1,0:T(8,128)(2,1)S(1)}, u32[]{:S(2)}, u32[]{:S(2)}) collective-permute-start(bf16[128,1024]{1,0:T(8,128)(2,1)S(1)} %add_convert_fusion.4), channel_id=1, source_target_pairs={{0,3},{1,0},{2,1},{3,2},{4,7},{5,4},{6,5},{7,6},{8,11},{9,8},{10,9... | collective-permute-start | bytes 786440 | tf_op jit(solution)/shard_map/ppermute | solution.py:386

commit v5 on v3

--- a/solution.py
+++ b/solution.py
@@ -13,6 +13,7 @@
 LOCAL_LEVELS = 4
 TOGETHER = 2
 CHUNKS = 2
+TOP = 4
 PIECES = 2
 EPS = 1e-06
 F32 = jnp.float32
@@ -23,7 +24,7 @@
     return jnp.dot(a, b, preferred_element_type=F32)
 
 
-def local_kernel(base, stride, flags, q_ref, k_ref, v_ref, log_ref, beta_ref, weight_ref,
+def local_kernel(flags, q_ref, k_ref, v_ref, log_ref, beta_ref, weight_ref,
                  near_ref, far_ref, map_ref, rows_ref):
     step = pl.program_id(0)
     tokens = q_ref.shape[0]
@@ -59,7 +60,7 @@
     units = [(g, s) for g in range(TOGETHER) for s in range(supers)]
     cols, cum_rows, tail_rows, beta_rows = [], [], [], []
     for g in range(TOGETHER):
-        head = TOGETHER * (base + stride * step) + g
+        head = TOGETHER * step + g
         take = pl.ds(head, 1)
         beta_row = beta_ref[take, :]
         wanted = [rows_ref[0, take, :], rows_ref[2, take, :], beta_row]
@@ -158,17 +159,18 @@
         map_ref[g] = jnp.concatenate([total, eye * decay - erase], axis=1).astype(BF16)
 
 
-def local_part(base, stride, steps, flags, queries, keys, values, log_decay, beta, weights):
+def local_part(flags, queries, keys, values, log_decay, beta, weights):
     tokens = queries.shape[0]
     heads = log_decay.shape[0]
     wide = TOGETHER * HEAD_DIM
-    block = pl.BlockSpec((tokens, wide), lambda h, f: (0, base + stride * h))
-    out = pl.BlockSpec((tokens, wide), lambda h, f: (0, h))
+    steps = heads // TOGETHER
+    block = pl.BlockSpec((tokens, wide), lambda h, f: (0, h))
+    out = block
     whole2 = pl.BlockSpec((heads, tokens), lambda h, f: (0, 0))
     whole3 = pl.BlockSpec(weights.shape, lambda h, f: (0, 0, 0))
     part = steps * TOGETHER
     return pl.pallas_call(
-        functools.partial(local_kernel, base, stride),
+        local_kernel,
         grid_spec=pltpu.PrefetchScalarGridSpec(
             num_scalar_prefetch=1,
             grid=(steps,),
@@ -184,33 +186,37 @@
         ],
         compiler_params=pltpu.CompilerParams(vmem_limit_bytes=14 << 20),
         cost_estimate=pl.CostEstimate(flops=part * 1500000000, bytes_accessed=8 << 20, transcendentals=0),
+        name="local",
     )(flags, queries, keys, values, log_decay, beta, weights)
 
 
-def pair_kernel(bits, *refs):
+def pair_kernel(bits, mine_ref, sib_ref, *outs):
     core = bits[0]
-    cur_ref = refs[-1]
-    half = cur_ref.shape[0]
-    parts = (len(refs) - 1) // 2
-    mine, sib = refs[:parts], refs[parts:2 * parts]
-
-    def run(first, second, offset):
-        for g in range(half):
-            later = second[offset + g]
-            both = mm(later[:, HEAD_DIM:], first[offset + g])
-            cur_ref[g, :, :HEAD_DIM] = (both[:, :HEAD_DIM] + later[:, :HEAD_DIM].astype(F32)).astype(BF16)
-            cur_ref[g, :, HEAD_DIM:] = both[:, HEAD_DIM:].astype(BF16)
+    half = outs[0].shape[0]
+
+    def run(first, second):
+        for c, cur_ref in enumerate(outs):
+            for g in range(half):
+                h = half * (len(outs) * core + c) + g
+                later = second[h]
+                both = mm(later[:, HEAD_DIM:], first[h])
+                cur_ref[g, :, :HEAD_DIM] = (both[:, :HEAD_DIM] + later[:, :HEAD_DIM].astype(F32)).astype(BF16)
+                cur_ref[g, :, HEAD_DIM:] = both[:, HEAD_DIM:].astype(BF16)
 
     @pl.when(core == 1)
     def _():
-        run(sib[-1], mine[-1], half if parts == 1 else 0)
+        run(sib_ref, mine_ref)
 
     @pl.when(core == 0)
     def _():
-        run(mine[0], sib[0], 0)
-
-
-def level_kernel(level, bits, *refs):
+        run(mine_ref, sib_ref)
+
+
+def level_kernel(level, packs, bits, *refs):
+    refs = list(refs)
+    if packs:
+        gathered = refs[:2 * (TOP - 1) - 1]
+        refs, pack = refs[len(gathered):-1], refs[-1]
     if level == 1:
         sib_ref, cur_ref, new_ref, x_ref, carry_ref = refs
     else:
@@ -247,21 +253,46 @@
             x_ref[g] = jnp.zeros((HEAD_DIM, HEAD_DIM), BF16)
             carry_ref[g] = eye if level == 1 else carried_ref[g]
 
-
-def top_kernel(level, bits, sib_ref, carried_ref, x_ref):
-    bit = bits[level]
-
-    @pl.when(bit == 1)
-    def _():
-        for g in range(x_ref.shape[0]):
-            x_ref[g] = mm(carried_ref[g], sib_ref[g]).astype(BF16)
-
-    @pl.when(bit == 0)
+    if packs:
+        for i, source in enumerate([*gathered, x_ref]):
+            for g in range(half):
+                pack[i * half + g] = source[g]
+
+
+def top_kernel(bits, *refs):
+    x_ref = refs[-1]
+    half = x_ref.shape[0] // CHUNKS
+
+    @pl.when(bits[TOP] == 1)
+    def _():
+        for c in range(CHUNKS):
+            for g in range(half):
+                x_ref[c * half + g] = mm(refs[CHUNKS + c][g], refs[c][g]).astype(BF16)
+
+    @pl.when(bits[TOP] == 0)
     def _():
         x_ref[...] = jnp.zeros(x_ref.shape, BF16)
 
 
-def small_call(kernel, bits, args, outs):
+def state_kernel(bits, sib_ref, mine_ref, other_ref, mine_top, other_top, stack_ref):
+    core = bits[0]
+    upper = core == 1
+    heads = sib_ref.shape[0]
+    half = heads // 2
+    per = half // CHUNKS
+    for h in range(heads):
+        is_mine = core == h // half
+        j = h % half
+        rows = [(j // per) * (TOP - 1) * per + level * per + j % per for level in range(TOP - 1)]
+        parts = [jnp.where(is_mine, mine_ref[r], other_ref[r]) for r in rows]
+        parts.append(jnp.where(is_mine, mine_top[j], other_top[j]))
+        states = jnp.concatenate(parts, axis=1)
+        moved = mm(sib_ref[h, :, HEAD_DIM:], states).astype(BF16)
+        low = jnp.where(upper, sib_ref[h, :, :HEAD_DIM], jnp.zeros((HEAD_DIM, HEAD_DIM), BF16))
+        stack_ref[h] = jnp.transpose(jnp.concatenate([low, jnp.where(upper, moved, states)], axis=1))
+
+
+def small_call(kernel, bits, args, outs, scratch=()):
     return pl.pallas_call(
         kernel,
         grid_spec=pltpu.PrefetchScalarGridSpec(
@@ -269,126 +300,99 @@
             grid=(1,),
             in_specs=[pl.BlockSpec(a.shape, lambda i, b, n=a.ndim: (0,) * n) for a in args],
             out_specs=[pl.BlockSpec(o.shape, lambda i, b, n=len(o.shape): (0,) * n) for o in outs],
+            scratch_shapes=list(scratch),
         ),
         out_shape=outs,
-        compiler_params=pltpu.CompilerParams(vmem_limit_bytes=3 << 20),
+        compiler_params=pltpu.CompilerParams(vmem_limit_bytes=8 << 20),
         cost_estimate=pl.CostEstimate(flops=600000000, bytes_accessed=1 << 20, transcendentals=0),
     )(bits, *args)
 
 
-def final_kernel(levels, parts, chunk, bits, *refs):
-    core = bits[0]
-    refs = list(refs)
-    near_refs = [refs.pop(0) for _ in range(parts)]
-    far_refs = [refs.pop(0) for _ in range(parts)]
-    sib_refs = [refs.pop(0) for _ in range(parts)]
-    weight_ref, gain_ref = refs[:2]
-    mine, other, z_ref = refs[2:2 + levels], refs[2 + levels:2 + 2 * levels], refs[-1]
-    tokens = near_refs[0].shape[0]
-    side = pl.program_id(0)
-    is_mine = side == core
-    upper = core == 1
-    first = LOCAL_LEVELS
+def read_kernel(bits, near_a, near_b, far_a, far_b, weight_a, weight_b, stack_ref, gain_ref, z_ref):
+    step = pl.program_id(0)
+    levels = stack_ref.shape[1] // HEAD_DIM
 
     def lanes(g):
         return slice(g * HEAD_DIM, (g + 1) * HEAD_DIM)
 
-    def pick(group, where):
-        if parts == 1:
-            return group[0][where]
-        return jnp.where(side == 0, group[0][where], group[1][where])
-
-    stacks = []
-    for g in range(TOGETHER):
-        sib = pick(sib_refs, g)
-        states = jnp.concatenate([jnp.where(is_mine, m[g], o[g]) for m, o in zip(mine, other)], axis=1)
-        states = jnp.where(upper, mm(sib[:, HEAD_DIM:], states).astype(BF16), states)
-        low = jnp.where(upper, sib[:, :HEAD_DIM], jnp.zeros((HEAD_DIM, HEAD_DIM), BF16))
-        stacks.append(jnp.transpose(jnp.concatenate([low, states], axis=1)))
-    step = 2 * SUPER
-    units = [(g, t) for g in range(TOGETHER) for t in range(0, tokens, step)]
-    reads = [lax.dot_general(stacks[g], pick(far_refs, (slice(t, t + step), lanes(g))),
-                             (((1,), (1,)), ((), ())), preferred_element_type=F32) for g, t in units]
-    for u, (g, t) in enumerate(units):
-        head = TOGETHER * (CHUNKS * side + chunk) + g
+    count = range(gain_ref.shape[1] // HEAD_DIM)
+    reads = [lax.dot_general(stack_ref[g], jnp.concatenate([far_a[:, lanes(g)], far_b[:, lanes(g)]], axis=0),
+                             (((1,), (1,)), ((), ())), preferred_element_type=F32) for g in count]
+    for g in count:
+        head = pl.ds(len(count) * step + g, 1)
         turned = None
-        for i in range(levels + 1):
-            term = weight_ref[first + i, pl.ds(head, 1), t:t + step] * reads[u][i * HEAD_DIM:(i + 1) * HEAD_DIM]
+        for i in range(levels):
+            row = jnp.concatenate([weight_a[LOCAL_LEVELS + i, head, :], weight_b[LOCAL_LEVELS + i, head, :]], axis=1)
+            term = row * reads[g][i * HEAD_DIM:(i + 1) * HEAD_DIM]
             turned = term if turned is None else turned + term
-        y = pick(near_refs, (slice(t, t + step), lanes(g))) + jnp.transpose(turned)
+        y = jnp.concatenate([near_a[:, lanes(g)], near_b[:, lanes(g)]], axis=0) + jnp.transpose(turned)
         scale = lax.rsqrt(jnp.mean(y * y, axis=1, keepdims=True) + EPS)
-        z_ref[t:t + step, lanes(g)] = (y * scale * gain_ref[:, lanes(g)]).astype(BF16)
-
-
-def final_part(chunk, bits, nears, fars, sibs, weights, gain, mine, other, before):
-    tokens = nears[0].shape[0]
-    wide = TOGETHER * HEAD_DIM
-    levels = len(mine)
-    parts = len(nears)
-    placed = lambda h, b: (0, CHUNKS * h + chunk)
-    state = pl.BlockSpec((TOGETHER, HEAD_DIM, HEAD_DIM), lambda h, b: (0, 0, 0))
-    if parts == 1:
-        block = pl.BlockSpec((tokens, wide), lambda h, b: (0, h))
-        maps = pl.BlockSpec((TOGETHER, HEAD_DIM, 2 * HEAD_DIM), lambda h, b: (h, 0, 0))
-    else:
-        block = pl.BlockSpec((tokens, wide), lambda h, b: (0, 0))
-        maps = pl.BlockSpec((TOGETHER, HEAD_DIM, 2 * HEAD_DIM), lambda h, b: (0, 0, 0))
-    in_specs = [block] * (2 * parts) + [maps] * parts
-    in_specs += [pl.BlockSpec(weights.shape, lambda h, b: (0, 0, 0)), pl.BlockSpec((1, wide), placed)]
-    in_specs += [state] * (2 * levels)
-    args = [bits, *nears, *fars, *sibs, weights, gain, *mine, *other]
-    aliases = {}
-    if before is not None:
-        aliases = {len(args): 0}
-        args.append(before)
-        in_specs.append(pl.BlockSpec(memory_space=pl.ANY))
+        z_ref[:, lanes(g)] = (y * scale * gain_ref[:, lanes(g)]).astype(BF16)
+
+
+def read_part(offsets, blocks, bits, near, far, weights, stacks, gain):
+    tokens, width = near.shape
+    rows = tokens // blocks
+    heads = stacks.shape[0] // 2
+    wide = heads * HEAD_DIM
+    place = bits.shape[0] - 1
+
+    def token_block(offset):
+        return pl.BlockSpec((rows, wide), lambda h, b: ((b[place] + offset) & (blocks - 1), h))
+
+    def weight_block(offset):
+        return pl.BlockSpec((*weights.shape[:2], rows), lambda h, b: (0, 0, (b[place] + offset) & (blocks - 1)))
+
     return pl.pallas_call(
-        functools.partial(final_kernel, levels, parts, chunk),
+        read_kernel,
         grid_spec=pltpu.PrefetchScalarGridSpec(
             num_scalar_prefetch=1,
             grid=(2,),
-            in_specs=in_specs,
-            out_specs=pl.BlockSpec((tokens, wide), placed),
+            in_specs=[token_block(o) for o in offsets] * 2 + [weight_block(o) for o in offsets]
+                     + [pl.BlockSpec((heads, *stacks.shape[1:]), lambda h, b: (h, 0, 0)),
+                        pl.BlockSpec((1, wide), lambda h, b: (0, h))],
+            out_specs=pl.BlockSpec((2 * rows, wide), lambda h, b: (0, h)),
         ),
-        out_shape=jax.ShapeDtypeStruct((tokens, gain.shape[1]), BF16),
-        input_output_aliases=aliases,
+        out_shape=jax.ShapeDtypeStruct((2 * rows, width), BF16),
         compiler_params=pltpu.CompilerParams(vmem_limit_bytes=14 << 20),
         cost_estimate=pl.CostEstimate(flops=2400000000, bytes_accessed=4 << 20, transcendentals=0),
-    )(*args)
-
-
-def partner(value, bit):
+    )(bits, near, near, far, far, weights, weights, stacks, gain)
+
+
+def partner(value, mask):
     size = lax.axis_size("seq")
-    return lax.ppermute(value, "seq", [(i, i ^ (1 << bit)) for i in range(size)])
+    return lax.ppermute(value, "seq", [(i, i ^ mask) for i in range(size)])
 
 
 def order_pieces():
     return [p for i in range(PIECES) for p in (i, PIECES + i)]
 
 
-def project(z, out_weight):
+def project(first_rows, make_last, out_weight):
     size = lax.axis_size("head")
-    me = lax.axis_index("head")
-    rows = z.shape[0] // size
+    rows = first_rows.shape[0] // 2
     cols = out_weight.shape[1] // (2 * PIECES)
-    up = [(j, (j + 1) % size) for j in range(size)]
-    down = [(j, (j - 1) % size) for j in range(size)]
+    ring = [[(j, (j + 1) % size) for j in range(size)], [(j, (j - 1) % size) for j in range(size)]]
 
     def term(block, piece):
-        part = lax.dynamic_slice_in_dim(z, (block % size) * rows, rows, 0)
         w = out_weight[:, piece * cols:(piece + 1) * cols]
-        return jnp.dot(part, w, preferred_element_type=F32).astype(BF16)
+        return jnp.dot(block, w, preferred_element_type=F32).astype(BF16)
 
     order = order_pieces()
+    before, after = first_rows[:rows], first_rows[rows:]
     sums = {}
     for p in order:
-        sums[p] = term(me + size - 1 if p < PIECES else me + 1, p)
+        sums[p] = term(before if p < PIECES else after, p)
+    last_rows = make_last()
+    across, own_rows = last_rows[:rows], last_rows[rows:]
+    sources = [(across, across), (after, before), (own_rows, own_rows)]
     last = None
     for s in range(size - 1):
         got, own = {}, {}
         for p in order:
-            got[p] = lax.ppermute(sums[p], "head", up if p < PIECES else down)
-            own[p] = term(me + 2 * size - 2 - s if p < PIECES else me + 2 + s, p)
+            side = int(p >= PIECES)
+            got[p] = lax.ppermute(sums[p], "head", ring[side])
+            own[p] = term(sources[s][side], p)
         for p in order:
             keep = (own[p],) if last is None else (own[p], last)
             mine = lax.optimization_barrier(keep)[0]
@@ -398,49 +402,49 @@
 
 
 def layer(queries, keys, values, log_decay, beta, level_weights, doc_start, norm_gain, out_weight):
+    nbits = lax.axis_size("seq").bit_length() - 1
+    blocks = lax.axis_size("head")
+    index = lax.axis_index("seq")
+    place = lax.axis_index("head")
+    bits = jnp.stack([(index >> b) & 1 for b in range(nbits)] + [place]).astype(jnp.int32)
+    gain = norm_gain.reshape(1, -1)
+    in_hbm = lambda x: pltpu.with_memory_space_constraint(x, pltpu.HBM)
+    given = [in_hbm(x) for x in (doc_start, queries, keys, values, log_decay, beta, level_weights)]
     heads = log_decay.shape[0]
-    mine_heads = heads // (2 * CHUNKS)
-    nbits = lax.axis_size("seq").bit_length() - 1
-    index = lax.axis_index("seq")
-    bits = jnp.stack([(index >> b) & 1 for b in range(nbits)]).astype(jnp.int32)
-    gain = norm_gain.reshape(1, -1)
-    wide = jax.ShapeDtypeStruct((mine_heads, HEAD_DIM, 2 * HEAD_DIM), BF16)
-    square = jax.ShapeDtypeStruct((mine_heads, HEAD_DIM, HEAD_DIM), BF16)
-    in_hbm = lambda x: pltpu.with_memory_space_constraint(x, pltpu.HBM)
-    given = [in_hbm(x) for x in (queries, keys, values, log_decay, beta, level_weights)]
-    doc_start = in_hbm(doc_start)
-
-    def local(base, stride, steps, flags):
-        near, far, maps = local_part(base, stride, steps, flags, *given)
-        return near, far, maps, partner(maps, 0)
-
-    front = local(0, CHUNKS, 2, doc_start)
-    low = local(1, CHUNKS, 1, doc_start)
-    cur = small_call(pair_kernel, bits, [front[2], front[3]], [wide])[0]
-    flags = lax.optimization_barrier((doc_start, cur))[0]
-    high = local(3, CHUNKS, 1, flags)
-    curs = [cur, small_call(pair_kernel, bits, [low[2], high[2], low[3], high[3]], [wide])[0]]
-    sources = [[front], [low, high]]
+    per = heads // (2 * CHUNKS)
+    wide = jax.ShapeDtypeStruct((per, HEAD_DIM, 2 * HEAD_DIM), BF16)
+    square = jax.ShapeDtypeStruct((per, HEAD_DIM, HEAD_DIM), BF16)
+    near, far, maps = local_part(*given)
+    sib = partner(maps, 1)
+    curs = list(small_call(pair_kernel, bits, [maps, sib], [wide] * CHUNKS))
     carried = [None] * CHUNKS
-    states = [[] for _ in range(CHUNKS)]
-    others = [[] for _ in range(CHUNKS)]
-    for level in range(1, nbits):
+    found = [[] for _ in range(CHUNKS)]
+    packed = None
+    for level in range(1, TOP):
         for c in range(CHUNKS):
-            if level < nbits - 1:
-                sib = partner(curs[c], level)
-                args = [sib, curs[c]] if level == 1 else [sib, curs[c], carried[c]]
-                curs[c], x, carried[c] = small_call(
-                    functools.partial(level_kernel, level), bits, args, [wide, square, square])
-            else:
-                sib = partner(curs[c][:, :, :HEAD_DIM], level)
-                x = small_call(functools.partial(top_kernel, level), bits, [sib, carried[c]], [square])[0]
-            states[c].append(x)
-            others[c].append(partner(x, 0))
-    z = None
-    for c in range(CHUNKS):
-        nears, fars, _, sibs = zip(*sources[c])
-        z = final_part(c, bits, nears, fars, sibs, given[5], gain, states[c], others[c], z)
-    return project(z, out_weight)
+            got = partner(curs[c], 1 << level)
+            args = [got, curs[c]] if level == 1 else [got, curs[c], carried[c]]
+            outs = [wide, square, square]
+            packs = level == TOP - 1 and c == CHUNKS - 1
+            if packs:
+                args = [*found[0], *found[1], *args]
+                outs = outs + [jax.ShapeDtypeStruct((CHUNKS * (TOP - 1) * per, HEAD_DIM, HEAD_DIM), BF16)]
+            curs[c], x, carried[c], *packed = small_call(
+                functools.partial(level_kernel, level, packs), bits, args, outs)
+            found[c].append(x)
+    got = [partner(curs[c][:, :, :HEAD_DIM], 1 << TOP) for c in range(CHUNKS)]
+    top = small_call(top_kernel, bits, [*got, *carried],
+                     [jax.ShapeDtypeStruct((CHUNKS * per, HEAD_DIM, HEAD_DIM), BF16)])[0]
+    stacks = small_call(
+        state_kernel, bits,
+        [sib, packed[0], partner(packed[0], 1), top, partner(top, 1)],
+        [jax.ShapeDtypeStruct((heads, (TOP + 1) * HEAD_DIM, HEAD_DIM), BF16)])[0]
+    near, far = in_hbm(near), in_hbm(far)
+
+    def read(offsets):
+        return read_part(offsets, blocks, bits, near, far, given[6], stacks, gain)
+
+    return project(read((blocks - 1, 1)), lambda: read((2, 0)), out_weight)
 
 
 def solution(mesh):

time: 110 us -> 110 us (level)
  waiting for transfers between devices: 33.4 us -> 43 us
  Pallas kernels: 35.7 us -> 30.1 us
  starting transfers between devices: 30.9 us -> 26.2 us
    ppermute x31 -> x23, waiting for transfers between devices: 33.4 us -> 43 us  [the longest x12 22.5 us: project(): got[p] = lax.ppermute(sums[p], 'head', ring[side])]
    pallas_call x5 -> x3, Pallas kernels: 28.7 us -> 22.6 us  [the longest x1 15.4 us: local_part(): pl.pallas_call(local_kernel, grid_spec=pltpu.PrefetchScalarGridSpec(num_s...]
    ppermute x31 -> x23, starting transfers between devices: 30.9 us -> 26.2 us  [the longest x12 14.1 us: project(): got[p] = lax.ppermute(sums[p], 'head', ring[side])]
    pallas_call x10 -> x9, Pallas kernels: 6.95 us -> 7.5 us  [small_call(): pl.pallas_call(kernel, grid_spec=pltpu.PrefetchScalarGridSpec(num_scalar_...]
  transfers between devices with their start and end apart: 31 -> 23, of which waited for: 14 -> 17; matrix products, arithmetic and copies ran while one was open for 1% -> 1% of each run, Pallas kernels for 21% -> 4%
where the time goes in v5:
time: 110 us; the launch traced here: 109 us
  waiting for transfers between devices  43 us (39%)
  Pallas kernels  30.1 us (27%)
  starting transfers between devices  26.2 us (24%)
  matrix products  7.21 us (7%)
  other arithmetic  1.84 us (2%)
    ppermute x12, waiting for transfers between devices, project(): got[p] = lax.ppermute(sums[p], 'head', ring[side])  22.5 us
    ppermute x11, waiting for transfers between devices, partner(): return lax.ppermute(value, 'seq', [(i, i ^ mask) for i in range(size)])  20.5 us
    pallas_call x1, Pallas kernels, local_part(): pl.pallas_call(local_kernel, grid_spec=pltpu.PrefetchScalarGridSpec(num_s...  15.4 us
    ppermute x12, starting transfers between devices, project(): got[p] = lax.ppermute(sums[p], 'head', ring[side])  14.1 us
    ppermute x11, starting transfers between devices, partner(): return lax.ppermute(value, 'seq', [(i, i ^ mask) for i in range(size)])  12.1 us
    pallas_call x9, Pallas kernels, small_call(): pl.pallas_call(kernel, grid_spec=pltpu.PrefetchScalarGridSpec(num_scalar_...  7.5 us
    pallas_call x2, Pallas kernels, read_part(): pl.pallas_call(read_kernel, grid_spec=pltpu.PrefetchScalarGridSpec(num_sc...  7.24 us
    dot_general x16, matrix products, term(): return jnp.dot(block, w, preferred_element_type=F32).astype(BF16)  7.21 us
  transfers between devices with their start and end apart: 23, of which 17 were waited for; matrix products, arithmetic and copies ran while one was open for 1% of the time, Pallas kernels for 4%

profile of v5, /device:TPU:28, one launch (start us, length us, event | category | flops | bytes accessed | tf_op | source)
XLA Modules:
  0.0 108.8 jit_solution(8474828172565655946)
XLA Ops:
  0.0 15.4 %local.1 = (f32[512,1024]{1,0:T(8,128)}, bf16[512,1024]{1,0:T(8,128)(2,1)}, bf16[8,128,256]{2,1,0:T(8,128)(2,1)S(1)}) custom-call(s32[8]{0:T(128)} %flags.1, bf16[512,1024]{1,0:T(8,128)(2,1)} %q_ref.1, bf16[512,1024]{1,0:T(8,128)(2,1)} %k_ref.1, bf16[512,1024]{1,0:T(8,128)(2,1)} %v_ref.1, f32[8,512]{1,0:T(8,128)} %log_ref.1, f32[8,512]{1,0:T(8,128)} %beta_ref.1, ...), custom_call_target="tpu_custom_call" | custom-call | flops 12000000000 | bytes 8388608 | tf_op jit(solution)/shard_map/local/pallas_call | solution.py:172
  15.5 1.8 %collective-permute-done.sib_ref = bf16[8,128,256]{2,1,0:T(8,128)(2,1)S(1)} collective-permute-done((bf16[8,128,256]{2,1,0:T(8,128)(2,1)S(1)}, bf16[8,128,256]{2,1,0:T(8,128)(2,1)S(1)}, u32[]{:S(2)}, u32[]{:S(2)}) %collective-permute-start) | collective-permute-done | bytes 524320 | tf_op jit(solution)/shard_map/ppermute | solution.py:364
  17.3 0.8 shard_map.91
  18.1 1.3 %collective-permute-start.1 = (bf16[2,128,256]{2,1,0:T(8,128)(2,1)S(1)}, bf16[2,128,256]{2,1,0:T(8,128)(2,1)S(1)}, u32[]{:S(2)}, u32[]{:S(2)}) collective-permute-start(bf16[2,128,256]{2,1,0:T(8,128)(2,1)S(1)} %get-tuple-element.42.refs_1_), channel_id=1, source_target_pairs={{0,8},{4,12},{8,0},{12,4},{16,24},{20,28},{24,16},{28,20},{32,40},... | collective-permute-start | bytes 393224 | tf_op jit(solution)/shard_map/ppermute | solution.py:364
  19.4 0.8 collective-permute-start.4
  20.2 4.3 %collective-permute-done.1.refs_0_ = bf16[2,128,256]{2,1,0:T(8,128)(2,1)S(1)} collective-permute-done((bf16[2,128,256]{2,1,0:T(8,128)(2,1)S(1)}, bf16[2,128,256]{2,1,0:T(8,128)(2,1)S(1)}, u32[]{:S(2)}, u32[]{:S(2)}) %collective-permute-start.1) | collective-permute-done | bytes 131104 | tf_op jit(solution)/shard_map/ppermute | solution.py:364
  24.5 0.7 shard_map.92
  25.3 0.6 collective-permute-start.2
  25.9 0.7 collective-permute-done.4.refs_0_
  26.5 0.7 shard_map.95
  27.3 2.5 %collective-permute-start.5 = (bf16[2,128,256]{2,1,0:T(8,128)(2,1)S(1)}, bf16[2,128,256]{2,1,0:T(8,128)(2,1)S(1)}, u32[]{:S(2)}, u32[]{:S(2)}) collective-permute-start(bf16[2,128,256]{2,1,0:T(8,128)(2,1)S(1)} %get-tuple-element.52.refs_1_), channel_id=1, source_target_pairs={{0,16},{4,20},{8,24},{12,28},{16,0},{20,4},{24,8},{28,12},{32,48},... | collective-permute-start | bytes 393224 | tf_op jit(solution)/shard_map/ppermute | solution.py:364
  29.7 3.3 %collective-permute-done.2.refs_0_ = bf16[2,128,256]{2,1,0:T(8,128)(2,1)S(1)} collective-permute-done((bf16[2,128,256]{2,1,0:T(8,128)(2,1)S(1)}, bf16[2,128,256]{2,1,0:T(8,128)(2,1)S(1)}, u32[]{:S(2)}, u32[]{:S(2)}) %collective-permute-start.2) | collective-permute-done | bytes 131104 | tf_op jit(solution)/shard_map/ppermute | solution.py:364
  33.0 0.8 shard_map.93
  33.7 2.0 %collective-permute-start.3 = (bf16[2,128,256]{2,1,0:T(8,128)(2,1)S(1)}, bf16[2,128,256]{2,1,0:T(8,128)(2,1)S(1)}, u32[]{:S(2)}, u32[]{:S(2)}) collective-permute-start(bf16[2,128,256]{2,1,0:T(8,128)(2,1)S(1)} %get-tuple-element.47.refs_1_), channel_id=1, source_target_pairs={{0,32},{4,36},{8,40},{12,44},{16,48},{20,52},{24,56},{28,60},{32,0... | collective-permute-start | bytes 393224 | tf_op jit(solution)/shard_map/ppermute | solution.py:364
  35.7 0.8 shard_map.96
  36.5 0.9 collective-permute-start.6
  37.4 2.6 %collective-permute-done.3.refs_0_ = bf16[2,128,256]{2,1,0:T(8,128)(2,1)S(1)} collective-permute-done((bf16[2,128,256]{2,1,0:T(8,128)(2,1)S(1)}, bf16[2,128,256]{2,1,0:T(8,128)(2,1)S(1)}, u32[]{:S(2)}, u32[]{:S(2)}) %collective-permute-start.3) | collective-permute-done | bytes 131104 | tf_op jit(solution)/shard_map/ppermute | solution.py:364
  40.0 0.7 shard_map.94
  40.8 0.8 collective-permute-done.6.refs_5_
  41.5 1.4 %shard_map.97 = (bf16[2,128,256]{2,1,0:T(8,128)(2,1)S(1)}, bf16[2,128,128]{2,1,0:T(8,128)(2,1)}, bf16[2,128,128]{2,1,0:T(8,128)(2,1)S(1)}, bf16[12,128,128]{2,1,0:T(8,128)(2,1)S(1)}) custom-call(s32[6]{0:T(128)S(1)} %stack.27.bits, bf16[2,128,128]{2,1,0:T(8,128)(2,1)S(1)} %get-tuple-element.43.refs_0_, bf16[2,128,128]{2,1,0:T(8,128)(2,1)S(1)} %get-tuple-element.46.refs_1_, ...), custom_call_target="tpu_custom_call" | custom-call | flops 600000000 | bytes 1048576 | tf_op jit(solution)/shard_map/pallas_call | solution.py:296
  42.9 3.7 %collective-permute-start.8 = (bf16[2,128,128]{2,1,0:T(8,128)(2,1)S(1)}, bf16[2,128,128]{2,1,0:T(8,128)(2,1)S(1)}, u32[]{:S(2)}, u32[]{:S(2)}) collective-permute-start(bf16[2,128,128]{2,1,0:T(8,128)(2,1)S(1)} %slice.20), channel_id=1, source_target_pairs={{0,64},{4,68},{8,72},{12,76},{16,80},{20,84},{24,88},{28,92},{32,9... | collective-permute-start | bytes 196616 | tf_op jit(solution)/shard_map/ppermute | solution.py:364
  46.7 2.6 %collective-permute-done.8.refs_0_ = bf16[2,128,128]{2,1,0:T(8,128)(2,1)S(1)} collective-permute-done((bf16[2,128,128]{2,1,0:T(8,128)(2,1)S(1)}, bf16[2,128,128]{2,1,0:T(8,128)(2,1)S(1)}, u32[]{:S(2)}, u32[]{:S(2)}) %collective-permute-start.8) | collective-permute-done | bytes 65568 | tf_op jit(solution)/shard_map/ppermute | solution.py:364
  49.3 3.1 %collective-permute-done.9.refs_1_ = bf16[2,128,128]{2,1,0:T(8,128)(2,1)S(1)} collective-permute-done((bf16[2,128,128]{2,1,0:T(8,128)(2,1)S(1)}, bf16[2,128,128]{2,1,0:T(8,128)(2,1)S(1)}, u32[]{:S(2)}, u32[]{:S(2)}) %collective-permute-start.9) | collective-permute-done | bytes 65568 | tf_op jit(solution)/shard_map/ppermute | solution.py:364
  52.4 0.6 shard_map.98.mine_top
  53.2 1.3 %collective-permute-done.10.other_top = bf16[4,128,128]{2,1,0:T(8,128)(2,1)S(1)} collective-permute-done((bf16[4,128,128]{2,1,0:T(8,128)(2,1)S(1)}, bf16[4,128,128]{2,1,0:T(8,128)(2,1)S(1)}, u32[]{:S(2)}, u32[]{:S(2)}) %collective-permute-start.10) | collective-permute-done | bytes 131104 | tf_op jit(solution)/shard_map/ppermute | solution.py:364
  54.6 1.1 %shard_map.99.stack_ref = bf16[8,640,128]{2,1,0:T(8,128)(2,1)S(1)} custom-call(s32[6]{0:T(128)S(1)} %stack.27.bits, bf16[8,128,256]{2,1,0:T(8,128)(2,1)S(1)} %collective-permute-done.sib_ref, bf16[12,128,128]{2,1,0:T(8,128)(2,1)S(1)} %get-tuple-element.57.mine_ref, bf16[12,128,128]{2,1,0:T(8,128)(2,1)S(1)} %collective-permute-done.7.other_ref, ...), custom_call_target="tpu_custom_call" | custom-call | flops 600000000 | bytes 1048576 | tf_op jit(solution)/shard_map/pallas_call | solution.py:296
  55.7 3.6 %shard_map.101 = bf16[256,1024]{1,0:T(8,128)(2,1)S(1)} custom-call(s32[6]{0:T(128)S(1)} %stack.27.bits, f32[512,1024]{1,0:T(8,128)} %get-tuple-element.39.near_a.near_b, f32[512,1024]{1,0:T(8,128)} %get-tuple-element.39.near_a.near_b, bf16[512,1024]{1,0:T(8,128)(2,1)} %get-tuple-element.40.far_a.far_b, bf16[512,1024]{1,0:T(8,128)(2,1)} %get-tuple-element.40.far_a.far_b, ...), custom_call_target="tpu_custom_call" | custom-call | flops 2400000000 | bytes 4194304 | tf_op jit(solution)/shard_map/pallas_call | solution.py:346
  59.4 3.6 %shard_map.100 = bf16[256,1024]{1,0:T(8,128)(2,1)S(1)} custom-call(s32[6]{0:T(128)S(1)} %stack.27.bits, f32[512,1024]{1,0:T(8,128)} %get-tuple-element.39.near_a.near_b, f32[512,1024]{1,0:T(8,128)} %get-tuple-element.39.near_a.near_b, bf16[512,1024]{1,0:T(8,128)(2,1)} %get-tuple-element.40.far_a.far_b, bf16[512,1024]{1,0:T(8,128)(2,1)} %get-tuple-element.40.far_a.far_b, ...), custom_call_target="tpu_custom_call" | custom-call | flops 2400000000 | bytes 4194304 | tf_op jit(solution)/shard_map/pallas_call | solution.py:346
  70.2 1.8 %collective-permute-start.15 = (bf16[128,1024]{1,0:T(8,128)(2,1)S(1)}, bf16[128,1024]{1,0:T(8,128)(2,1)S(1)}, u32[]{:S(2)}, u32[]{:S(2)}) collective-permute-start(bf16[128,1024]{1,0:T(8,128)(2,1)S(1)} %fusion.68), channel_id=1, source_target_pairs={{0,3},{1,0},{2,1},{3,2},{4,7},{5,4},{6,5},{7,6},{8,11},{9,8},{10,9... | collective-permute-start | bytes 786440 | tf_op jit(solution)/shard_map/ppermute | solution.py:394
  72.5 0.8 collective-permute-start.13
  73.3 2.5 %collective-permute-start.14 = (bf16[128,1024]{1,0:T(8,128)(2,1)S(1)}, bf16[128,1024]{1,0:T(8,128)(2,1)S(1)}, u32[]{:S(2)}, u32[]{:S(2)}) collective-permute-start(bf16[128,1024]{1,0:T(8,128)(2,1)S(1)} %fusion.56), channel_id=1, source_target_pairs={{0,1},{1,2},{2,3},{3,0},{4,5},{5,6},{6,7},{7,4},{8,9},{9,10},{10,1... | collective-permute-start | bytes 786440 | tf_op jit(solution)/shard_map/ppermute | solution.py:394
  75.8 3.4 %collective-permute-done.11 = bf16[128,1024]{1,0:T(8,128)(2,1)S(1)} collective-permute-done((bf16[128,1024]{1,0:T(8,128)(2,1)S(1)}, bf16[128,1024]{1,0:T(8,128)(2,1)S(1)}, u32[]{:S(2)}, u32[]{:S(2)}) %collective-permute-start.11) | collective-permute-done | bytes 262176 | tf_op jit(solution)/shard_map/ppermute | solution.py:394
  79.2 1.5 %collective-permute-start.12 = (bf16[128,1024]{1,0:T(8,128)(2,1)S(1)}, bf16[128,1024]{1,0:T(8,128)(2,1)S(1)}, u32[]{:S(2)}, u32[]{:S(2)}) collective-permute-start(bf16[128,1024]{1,0:T(8,128)(2,1)S(1)} %add_convert_fusion.11), channel_id=1, source_target_pairs={{0,1},{1,2},{2,3},{3,0},{4,5},{5,6},{6,7},{7,4},{8,9},{9,10},{10,1... | collective-permute-start | bytes 786440 | tf_op jit(solution)/shard_map/ppermute | solution.py:394
  80.8 0.7 collective-permute-start.19
  81.5 3.3 %collective-permute-done.14 = bf16[128,1024]{1,0:T(8,128)(2,1)S(1)} collective-permute-done((bf16[128,1024]{1,0:T(8,128)(2,1)S(1)}, bf16[128,1024]{1,0:T(8,128)(2,1)S(1)}, u32[]{:S(2)}, u32[]{:S(2)}) %collective-permute-start.14) | collective-permute-done | bytes 262176 | tf_op jit(solution)/shard_map/ppermute | solution.py:394
  84.8 1.5 %collective-permute-start.18 = (bf16[128,1024]{1,0:T(8,128)(2,1)S(1)}, bf16[128,1024]{1,0:T(8,128)(2,1)S(1)}, u32[]{:S(2)}, u32[]{:S(2)}) collective-permute-start(bf16[128,1024]{1,0:T(8,128)(2,1)S(1)} %add_convert_fusion.9), channel_id=1, source_target_pairs={{0,1},{1,2},{2,3},{3,0},{4,5},{5,6},{6,7},{7,4},{8,9},{9,10},{10,1... | collective-permute-start | bytes 786440 | tf_op jit(solution)/shard_map/ppermute | solution.py:394
  86.4 0.7 collective-permute-start.17
  87.1 3.3 %collective-permute-done.12 = bf16[128,1024]{1,0:T(8,128)(2,1)S(1)} collective-permute-done((bf16[128,1024]{1,0:T(8,128)(2,1)S(1)}, bf16[128,1024]{1,0:T(8,128)(2,1)S(1)}, u32[]{:S(2)}, u32[]{:S(2)}) %collective-permute-start.12) | collective-permute-done | bytes 262176 | tf_op jit(solution)/shard_map/ppermute | solution.py:394
  90.5 1.5 %collective-permute-start.16 = (bf16[128,1024]{1,0:T(8,128)(2,1)S(1)}, bf16[128,1024]{1,0:T(8,128)(2,1)S(1)}, u32[]{:S(2)}, u32[]{:S(2)}) collective-permute-start(bf16[128,1024]{1,0:T(8,128)(2,1)S(1)} %add_convert_fusion.7), channel_id=1, source_target_pairs={{0,1},{1,2},{2,3},{3,0},{4,5},{5,6},{6,7},{7,4},{8,9},{9,10},{10,1... | collective-permute-start | bytes 786440 | tf_op jit(solution)/shard_map/ppermute | solution.py:394
  92.0 0.7 collective-permute-start.21
  92.7 3.3 %collective-permute-done.18 = bf16[128,1024]{1,0:T(8,128)(2,1)S(1)} collective-permute-done((bf16[128,1024]{1,0:T(8,128)(2,1)S(1)}, bf16[128,1024]{1,0:T(8,128)(2,1)S(1)}, u32[]{:S(2)}, u32[]{:S(2)}) %collective-permute-start.18) | collective-permute-done | bytes 262176 | tf_op jit(solution)/shard_map/ppermute | solution.py:394
  96.1 1.5 %collective-permute-start.20 = (bf16[128,1024]{1,0:T(8,128)(2,1)S(1)}, bf16[128,1024]{1,0:T(8,128)(2,1)S(1)}, u32[]{:S(2)}, u32[]{:S(2)}) collective-permute-start(bf16[128,1024]{1,0:T(8,128)(2,1)S(1)} %add_convert_fusion.5), channel_id=1, source_target_pairs={{0,1},{1,2},{2,3},{3,0},{4,5},{5,6},{6,7},{7,4},{8,9},{9,10},{10,1... | collective-permute-start | bytes 786440 | tf_op jit(solution)/shard_map/ppermute | solution.py:394
  97.7 0.7 collective-permute-start.22
  98.3 3.3 %collective-permute-done.16 = bf16[128,1024]{1,0:T(8,128)(2,1)S(1)} collective-permute-done((bf16[128,1024]{1,0:T(8,128)(2,1)S(1)}, bf16[128,1024]{1,0:T(8,128)(2,1)S(1)}, u32[]{:S(2)}, u32[]{:S(2)}) %collective-permute-start.16) | collective-permute-done | bytes 262176 | tf_op jit(solution)/shard_map/ppermute | solution.py:394
  101.7 1.4 %collective-permute-done.21 = bf16[128,1024]{1,0:T(8,128)(2,1)S(1)} collective-permute-done((bf16[128,1024]{1,0:T(8,128)(2,1)S(1)}, bf16[128,1024]{1,0:T(8,128)(2,1)S(1)}, u32[]{:S(2)}, u32[]{:S(2)}) %collective-permute-start.21) | collective-permute-done | bytes 262176 | tf_op jit(solution)/shard_map/ppermute | solution.py:394
  103.1 3.3 %collective-permute-done.20 = bf16[128,1024]{1,0:T(8,128)(2,1)S(1)} collective-permute-done((bf16[128,1024]{1,0:T(8,128)(2,1)S(1)}, bf16[128,1024]{1,0:T(8,128)(2,1)S(1)}, u32[]{:S(2)}, u32[]{:S(2)}) %collective-permute-start.20) | collective-permute-done | bytes 262176 | tf_op jit(solution)/shard_map/ppermute | solution.py:394
  106.5 1.2 %collective-permute-done.22 = bf16[128,1024]{1,0:T(8,128)(2,1)S(1)} collective-permute-done((bf16[128,1024]{1,0:T(8,128)(2,1)S(1)}, bf16[128,1024]{1,0:T(8,128)(2,1)S(1)}, u32[]{:S(2)}, u32[]{:S(2)}) %collective-permute-start.22) | collective-permute-done | bytes 262176 | tf_op jit(solution)/shard_map/ppermute | solution.py:394
  107.8 1.0 pad_maximum_fusion
  (49 shorter events, 8.8 us)
Async XLA Ops:
  15.4 1.9 %collective-permute-start = (bf16[8,128,256]{2,1,0:T(8,128)(2,1)S(1)}, bf16[8,128,256]{2,1,0:T(8,128)(2,1)S(1)}, u32[]{:S(2)}, u32[]{:S(2)}) collective-permute-start(bf16[8,128,256]{2,1,0:T(8,128)(2,1)S(1)} %get-tuple-element.41.mine_ref), channel_id=1, source_target_pairs={{0,4},{4,0},{8,12},{12,8},{16,20},{20,16},{24,28},{28,24},{32,36},... | collective-permute-start | bytes 1572872 | tf_op jit(solution)/shard_map/ppermute | solution.py:364
  18.1 6.5 %collective-permute-start.1 = (bf16[2,128,256]{2,1,0:T(8,128)(2,1)S(1)}, bf16[2,128,256]{2,1,0:T(8,128)(2,1)S(1)}, u32[]{:S(2)}, u32[]{:S(2)}) collective-permute-start(bf16[2,128,256]{2,1,0:T(8,128)(2,1)S(1)} %get-tuple-element.42.refs_1_), channel_id=1, source_target_pairs={{0,8},{4,12},{8,0},{12,4},{16,24},{20,28},{24,16},{28,20},{32,40},... | collective-permute-start | bytes 393224 | tf_op jit(solution)/shard_map/ppermute | solution.py:364
  19.4 7.2 %collective-permute-start.4 = (bf16[2,128,256]{2,1,0:T(8,128)(2,1)S(1)}, bf16[2,128,256]{2,1,0:T(8,128)(2,1)S(1)}, u32[]{:S(2)}, u32[]{:S(2)}) collective-permute-start(bf16[2,128,256]{2,1,0:T(8,128)(2,1)S(1)} %get-tuple-element.50.refs_1_), channel_id=1, source_target_pairs={{0,8},{4,12},{8,0},{12,4},{16,24},{20,28},{24,16},{28,20},{32,40},... | collective-permute-start | bytes 393224 | tf_op jit(solution)/shard_map/ppermute | solution.py:364
  25.3 7.7 %collective-permute-start.2 = (bf16[2,128,256]{2,1,0:T(8,128)(2,1)S(1)}, bf16[2,128,256]{2,1,0:T(8,128)(2,1)S(1)}, u32[]{:S(2)}, u32[]{:S(2)}) collective-permute-start(bf16[2,128,256]{2,1,0:T(8,128)(2,1)S(1)} %get-tuple-element.44.refs_1_), channel_id=1, source_target_pairs={{0,16},{4,20},{8,24},{12,28},{16,0},{20,4},{24,8},{28,12},{32,48},... | collective-permute-start | bytes 393224 | tf_op jit(solution)/shard_map/ppermute | solution.py:364
  27.3 8.5 %collective-permute-start.5 = (bf16[2,128,256]{2,1,0:T(8,128)(2,1)S(1)}, bf16[2,128,256]{2,1,0:T(8,128)(2,1)S(1)}, u32[]{:S(2)}, u32[]{:S(2)}) collective-permute-start(bf16[2,128,256]{2,1,0:T(8,128)(2,1)S(1)} %get-tuple-element.52.refs_1_), channel_id=1, source_target_pairs={{0,16},{4,20},{8,24},{12,28},{16,0},{20,4},{24,8},{28,12},{32,48},... | collective-permute-start | bytes 393224 | tf_op jit(solution)/shard_map/ppermute | solution.py:364
  33.7 6.3 %collective-permute-start.3 = (bf16[2,128,256]{2,1,0:T(8,128)(2,1)S(1)}, bf16[2,128,256]{2,1,0:T(8,128)(2,1)S(1)}, u32[]{:S(2)}, u32[]{:S(2)}) collective-permute-start(bf16[2,128,256]{2,1,0:T(8,128)(2,1)S(1)} %get-tuple-element.47.refs_1_), channel_id=1, source_target_pairs={{0,32},{4,36},{8,40},{12,44},{16,48},{20,52},{24,56},{28,60},{32,0... | collective-permute-start | bytes 393224 | tf_op jit(solution)/shard_map/ppermute | solution.py:364
  36.5 5.0 %collective-permute-start.6 = (bf16[2,128,256]{2,1,0:T(8,128)(2,1)S(1)}, bf16[2,128,256]{2,1,0:T(8,128)(2,1)S(1)}, u32[]{:S(2)}, u32[]{:S(2)}) collective-permute-start(bf16[2,128,256]{2,1,0:T(8,128)(2,1)S(1)} %get-tuple-element.55.refs_6_), channel_id=1, source_target_pairs={{0,32},{4,36},{8,40},{12,44},{16,48},{20,52},{24,56},{28,60},{32,0... | collective-permute-start | bytes 393224 | tf_op jit(solution)/shard_map/ppermute | solution.py:364
  42.9 11.7 %collective-permute-start.7 = (bf16[12,128,128]{2,1,0:T(8,128)(2,1)S(1)}, bf16[12,128,128]{2,1,0:T(8,128)(2,1)S(1)}, u32[]{:S(2)}, u32[]{:S(2)}) collective-permute-start(bf16[12,128,128]{2,1,0:T(8,128)(2,1)S(1)} %get-tuple-element.57.mine_ref), channel_id=1, source_target_pairs={{0,4},{4,0},{8,12},{12,8},{16,20},{20,16},{24,28},{28,24},{32,36},... | collective-permute-start | bytes 1179656 | tf_op jit(solution)/shard_map/ppermute | solution.py:364
  42.9 6.4 %collective-permute-start.8 = (bf16[2,128,128]{2,1,0:T(8,128)(2,1)S(1)}, bf16[2,128,128]{2,1,0:T(8,128)(2,1)S(1)}, u32[]{:S(2)}, u32[]{:S(2)}) collective-permute-start(bf16[2,128,128]{2,1,0:T(8,128)(2,1)S(1)} %slice.20), channel_id=1, source_target_pairs={{0,64},{4,68},{8,72},{12,76},{16,80},{20,84},{24,88},{28,92},{32,9... | collective-permute-start | bytes 196616 | tf_op jit(solution)/shard_map/ppermute | solution.py:364
  46.6 5.8 %collective-permute-start.9 = (bf16[2,128,128]{2,1,0:T(8,128)(2,1)S(1)}, bf16[2,128,128]{2,1,0:T(8,128)(2,1)S(1)}, u32[]{:S(2)}, u32[]{:S(2)}) collective-permute-start(bf16[2,128,128]{2,1,0:T(8,128)(2,1)S(1)} %slice.21), channel_id=1, source_target_pairs={{0,64},{4,68},{8,72},{12,76},{16,80},{20,84},{24,88},{28,92},{32,9... | collective-permute-start | bytes 196616 | tf_op jit(solution)/shard_map/ppermute | solution.py:364
  52.4 3.3 %copy-start = (f32[1024]{0:T(1024)S(1)}, f32[1024]{0:T(1024)}, u32[]{:S(2)}) copy-start(f32[1024]{0:T(1024)} %param.16) | copy-start | bytes 12292
  53.0 1.6 %collective-permute-start.10 = (bf16[4,128,128]{2,1,0:T(8,128)(2,1)S(1)}, bf16[4,128,128]{2,1,0:T(8,128)(2,1)S(1)}, u32[]{:S(2)}, u32[]{:S(2)}) collective-permute-start(bf16[4,128,128]{2,1,0:T(8,128)(2,1)S(1)} %shard_map.98.mine_top), channel_id=1, source_target_pairs={{0,4},{4,0},{8,12},{12,8},{16,20},{20,16},{24,28},{28,24},{32,36},... | collective-permute-start | bytes 393224 | tf_op jit(solution)/shard_map/ppermute | solution.py:364
  55.7 7.3 %slice-start = ((s8[8388608]{0:T(1024)(128)(4,1)}), s8[4194304]{0:T(1024)(128)(4,1)S(1)}, s32[]{:S(2)}) async-start(s8[8388608]{0:T(1024)(128)(4,1)} %bitcast.9), calls=%async_computation | async-start | bytes 8388608
  59.4 3.7 %slice-start.1 = ((s8[8388608]{0:T(1024)(128)(4,1)}), s8[4194304]{0:T(1024)(128)(4,1)S(1)}, s32[]{:S(2)}) async-start(s8[8388608]{0:T(1024)(128)(4,1)} %bitcast.9), calls=%async_computation.1 | async-start | bytes 8388608
  69.9 9.2 %collective-permute-start.11 = (bf16[128,1024]{1,0:T(8,128)(2,1)S(1)}, bf16[128,1024]{1,0:T(8,128)(2,1)S(1)}, u32[]{:S(2)}, u32[]{:S(2)}) collective-permute-start(bf16[128,1024]{1,0:T(8,128)(2,1)S(1)} %fusion.32), channel_id=1, source_target_pairs={{0,1},{1,2},{2,3},{3,0},{4,5},{5,6},{6,7},{7,4},{8,9},{9,10},{10,1... | collective-permute-start | bytes 786440 | tf_op jit(solution)/shard_map/ppermute | solution.py:394
  70.2 10.5 %collective-permute-start.15 = (bf16[128,1024]{1,0:T(8,128)(2,1)S(1)}, bf16[128,1024]{1,0:T(8,128)(2,1)S(1)}, u32[]{:S(2)}, u32[]{:S(2)}) collective-permute-start(bf16[128,1024]{1,0:T(8,128)(2,1)S(1)} %fusion.68), channel_id=1, source_target_pairs={{0,3},{1,0},{2,1},{3,2},{4,7},{5,4},{6,5},{7,6},{8,11},{9,8},{10,9... | collective-permute-start | bytes 786440 | tf_op jit(solution)/shard_map/ppermute | solution.py:394
  72.5 13.9 %collective-permute-start.13 = (bf16[128,1024]{1,0:T(8,128)(2,1)S(1)}, bf16[128,1024]{1,0:T(8,128)(2,1)S(1)}, u32[]{:S(2)}, u32[]{:S(2)}) collective-permute-start(bf16[128,1024]{1,0:T(8,128)(2,1)S(1)} %fusion.44), channel_id=1, source_target_pairs={{0,3},{1,0},{2,1},{3,2},{4,7},{5,4},{6,5},{7,6},{8,11},{9,8},{10,9... | collective-permute-start | bytes 786440 | tf_op jit(solution)/shard_map/ppermute | solution.py:394
  73.3 11.5 %collective-permute-start.14 = (bf16[128,1024]{1,0:T(8,128)(2,1)S(1)}, bf16[128,1024]{1,0:T(8,128)(2,1)S(1)}, u32[]{:S(2)}, u32[]{:S(2)}) collective-permute-start(bf16[128,1024]{1,0:T(8,128)(2,1)S(1)} %fusion.56), channel_id=1, source_target_pairs={{0,1},{1,2},{2,3},{3,0},{4,5},{5,6},{6,7},{7,4},{8,9},{9,10},{10,1... | collective-permute-start | bytes 786440 | tf_op jit(solution)/shard_map/ppermute | solution.py:394
  79.2 11.2 %collective-permute-start.12 = (bf16[128,1024]{1,0:T(8,128)(2,1)S(1)}, bf16[128,1024]{1,0:T(8,128)(2,1)S(1)}, u32[]{:S(2)}, u32[]{:S(2)}) collective-permute-start(bf16[128,1024]{1,0:T(8,128)(2,1)S(1)} %add_convert_fusion.11), channel_id=1, source_target_pairs={{0,1},{1,2},{2,3},{3,0},{4,5},{5,6},{6,7},{7,4},{8,9},{9,10},{10,1... | collective-permute-start | bytes 786440 | tf_op jit(solution)/shard_map/ppermute | solution.py:394
  80.8 11.2 %collective-permute-start.19 = (bf16[128,1024]{1,0:T(8,128)(2,1)S(1)}, bf16[128,1024]{1,0:T(8,128)(2,1)S(1)}, u32[]{:S(2)}, u32[]{:S(2)}) collective-permute-start(bf16[128,1024]{1,0:T(8,128)(2,1)S(1)} %add_convert_fusion.10), channel_id=1, source_target_pairs={{0,3},{1,0},{2,1},{3,2},{4,7},{5,4},{6,5},{7,6},{8,11},{9,8},{10,9... | collective-permute-start | bytes 786440 | tf_op jit(solution)/shard_map/ppermute | solution.py:394
  84.8 11.2 %collective-permute-start.18 = (bf16[128,1024]{1,0:T(8,128)(2,1)S(1)}, bf16[128,1024]{1,0:T(8,128)(2,1)S(1)}, u32[]{:S(2)}, u32[]{:S(2)}) collective-permute-start(bf16[128,1024]{1,0:T(8,128)(2,1)S(1)} %add_convert_fusion.9), channel_id=1, source_target_pairs={{0,1},{1,2},{2,3},{3,0},{4,5},{5,6},{6,7},{7,4},{8,9},{9,10},{10,1... | collective-permute-start | bytes 786440 | tf_op jit(solution)/shard_map/ppermute | solution.py:394
  86.4 11.2 %collective-permute-start.17 = (bf16[128,1024]{1,0:T(8,128)(2,1)S(1)}, bf16[128,1024]{1,0:T(8,128)(2,1)S(1)}, u32[]{:S(2)}, u32[]{:S(2)}) collective-permute-start(bf16[128,1024]{1,0:T(8,128)(2,1)S(1)} %add_convert_fusion.8), channel_id=1, source_target_pairs={{0,3},{1,0},{2,1},{3,2},{4,7},{5,4},{6,5},{7,6},{8,11},{9,8},{10,9... | collective-permute-start | bytes 786440 | tf_op jit(solution)/shard_map/ppermute | solution.py:394
  90.5 11.2 %collective-permute-start.16 = (bf16[128,1024]{1,0:T(8,128)(2,1)S(1)}, bf16[128,1024]{1,0:T(8,128)(2,1)S(1)}, u32[]{:S(2)}, u32[]{:S(2)}) collective-permute-start(bf16[128,1024]{1,0:T(8,128)(2,1)S(1)} %add_convert_fusion.7), channel_id=1, source_target_pairs={{0,1},{1,2},{2,3},{3,0},{4,5},{5,6},{6,7},{7,4},{8,9},{9,10},{10,1... | collective-permute-start | bytes 786440 | tf_op jit(solution)/shard_map/ppermute | solution.py:394
  92.0 11.0 %collective-permute-start.21 = (bf16[128,1024]{1,0:T(8,128)(2,1)S(1)}, bf16[128,1024]{1,0:T(8,128)(2,1)S(1)}, u32[]{:S(2)}, u32[]{:S(2)}) collective-permute-start(bf16[128,1024]{1,0:T(8,128)(2,1)S(1)} %add_convert_fusion.6), channel_id=1, source_target_pairs={{0,3},{1,0},{2,1},{3,2},{4,7},{5,4},{6,5},{7,6},{8,11},{9,8},{10,9... | collective-permute-start | bytes 786440 | tf_op jit(solution)/shard_map/ppermute | solution.py:394
  96.1 10.3 %collective-permute-start.20 = (bf16[128,1024]{1,0:T(8,128)(2,1)S(1)}, bf16[128,1024]{1,0:T(8,128)(2,1)S(1)}, u32[]{:S(2)}, u32[]{:S(2)}) collective-permute-start(bf16[128,1024]{1,0:T(8,128)(2,1)S(1)} %add_convert_fusion.5), channel_id=1, source_target_pairs={{0,1},{1,2},{2,3},{3,0},{4,5},{5,6},{6,7},{7,4},{8,9},{9,10},{10,1... | collective-permute-start | bytes 786440 | tf_op jit(solution)/shard_map/ppermute | solution.py:394
  97.7 10.1 %collective-permute-start.22 = (bf16[128,1024]{1,0:T(8,128)(2,1)S(1)}, bf16[128,1024]{1,0:T(8,128)(2,1)S(1)}, u32[]{:S(2)}, u32[]{:S(2)}) collective-permute-start(bf16[128,1024]{1,0:T(8,128)(2,1)S(1)} %add_convert_fusion.4), channel_id=1, source_target_pairs={{0,3},{1,0},{2,1},{3,2},{4,7},{5,4},{6,5},{7,6},{8,11},{9,8},{10,9... | collective-permute-start | bytes 786440 | tf_op jit(solution)/shard_map/ppermute | solution.py:394

commit v6 on v5

--- a/solution.py
+++ b/solution.py
@@ -91,13 +91,15 @@
         rq = lax.rsqrt(jnp.sum(qf * qf, axis=1, keepdims=True) + EPS)
         rk = lax.rsqrt(jnp.sum(kf * kf, axis=1, keepdims=True) + EPS)
         rk_row = lax.rsqrt(jnp.sum(ktf * ktf, axis=0, keepdims=True) + EPS)
-        spread = col(g, s, 0) - cum_rows[g][:, cut(s)]
+        level = jnp.broadcast_to(col(g, s, 0), (SUPER, SUPER))
+        spread = level - cum_rows[g][:, cut(s)]
         ratio = jnp.exp(jnp.where(lower, spread, -1e30)) * rk_row
         scores.append((ratio * (rq * grams[:SUPER])).astype(BF16))
         power = jnp.where(strict, (-col(g, s, 2) * rk) * ratio * grams[SUPER:], 0.0)
         inverses.append(eye + power)
         powers.append(power.astype(BF16))
-        decay = col(g, s, 1)
+        kept = [(1 - flags[s * (SUPER // SPAN) + i]).astype(F32) for i in range(SUPER // SPAN)]
+        decay = jnp.exp(level) * jnp.where(row_i < SPAN, kept[0], kept[1])
         right.append(jnp.concatenate([v_ref[cut(s), lanes(g)], (decay * rk * kf).astype(BF16)], axis=1))
         tails.append((ktf * (rk_row * tail_rows[g][:, cut(s)])).astype(BF16))
         queries.append(decay * rq * qf)
@@ -398,7 +400,10 @@
             mine = lax.optimization_barrier(keep)[0]
             last = (got[p].astype(F32) + mine.astype(F32)).astype(BF16)
             sums[p] = last
-    return jnp.concatenate([sums[p] for p in range(2 * PIECES)], axis=1)
+    out = lax.optimization_barrier(jnp.zeros((rows, out_weight.shape[1]), BF16))
+    for p in order:
+        out = lax.dynamic_update_slice(out, sums[p], (0, p * cols))
+    return out
 
 
 def layer(queries, keys, values, log_decay, beta, level_weights, doc_start, norm_gain, out_weight):

time: 110 us -> 110 us (level)
  starting transfers between devices: 26.2 us -> 25 us
  waiting for transfers between devices: 43 us -> 44.1 us
    ppermute x12, starting transfers between devices: 14.1 us -> 12.8 us  [project(): got[p] = lax.ppermute(sums[p], 'head', ring[side])]
where the time goes in v6:
time: 110 us; the launch traced here: 108 us
  waiting for transfers between devices  44.1 us (40%)
  Pallas kernels  30 us (27%)
  starting transfers between devices  25 us (23%)
  matrix products  7.21 us (7%)
  other arithmetic  1.51 us (1%)
    ppermute x12, waiting for transfers between devices, project(): got[p] = lax.ppermute(sums[p], 'head', ring[side])  23.6 us
    ppermute x11, waiting for transfers between devices, partner(): return lax.ppermute(value, 'seq', [(i, i ^ mask) for i in range(size)])  20.5 us
    pallas_call x1, Pallas kernels, local_part(): pl.pallas_call(local_kernel, grid_spec=pltpu.PrefetchScalarGridSpec(num_s...  15.2 us
    ppermute x12, starting transfers between devices, project(): got[p] = lax.ppermute(sums[p], 'head', ring[side])  12.8 us
    ppermute x11, starting transfers between devices, partner(): return lax.ppermute(value, 'seq', [(i, i ^ mask) for i in range(size)])  12.1 us
    pallas_call x9, Pallas kernels, small_call(): pl.pallas_call(kernel, grid_spec=pltpu.PrefetchScalarGridSpec(num_scalar_...  7.5 us
    pallas_call x2, Pallas kernels, read_part(): pl.pallas_call(read_kernel, grid_spec=pltpu.PrefetchScalarGridSpec(num_sc...  7.24 us
    dot_general x16, matrix products, term(): return jnp.dot(block, w, preferred_element_type=F32).astype(BF16)  7.21 us
  transfers between devices with their start and end apart: 23, of which 17 were waited for; matrix products, arithmetic and copies ran while one was open for 1% of the time, Pallas kernels for 4%

profile of v6, /device:TPU:28, one launch (start us, length us, event | category | flops | bytes accessed | tf_op | source)
XLA Modules:
  0.0 108.3 jit_solution(205454960546882239)
XLA Ops:
  0.0 15.2 %local.1 = (f32[512,1024]{1,0:T(8,128)}, bf16[512,1024]{1,0:T(8,128)(2,1)}, bf16[8,128,256]{2,1,0:T(8,128)(2,1)S(1)}) custom-call(s32[8]{0:T(128)} %flags.1, bf16[512,1024]{1,0:T(8,128)(2,1)} %q_ref.1, bf16[512,1024]{1,0:T(8,128)(2,1)} %k_ref.1, bf16[512,1024]{1,0:T(8,128)(2,1)} %v_ref.1, f32[8,512]{1,0:T(8,128)} %log_ref.1, f32[8,512]{1,0:T(8,128)} %beta_ref.1, ...), custom_call_target="tpu_custom_call" | custom-call | flops 12000000000 | bytes 8388608 | tf_op jit(solution)/shard_map/local/pallas_call | solution.py:174
  15.3 1.8 %collective-permute-done.sib_ref = bf16[8,128,256]{2,1,0:T(8,128)(2,1)S(1)} collective-permute-done((bf16[8,128,256]{2,1,0:T(8,128)(2,1)S(1)}, bf16[8,128,256]{2,1,0:T(8,128)(2,1)S(1)}, u32[]{:S(2)}, u32[]{:S(2)}) %collective-permute-start) | collective-permute-done | bytes 524320 | tf_op jit(solution)/shard_map/ppermute | solution.py:366
  17.1 0.8 shard_map.91
  17.9 1.3 %collective-permute-start.1 = (bf16[2,128,256]{2,1,0:T(8,128)(2,1)S(1)}, bf16[2,128,256]{2,1,0:T(8,128)(2,1)S(1)}, u32[]{:S(2)}, u32[]{:S(2)}) collective-permute-start(bf16[2,128,256]{2,1,0:T(8,128)(2,1)S(1)} %get-tuple-element.42.refs_1_), channel_id=1, source_target_pairs={{0,8},{4,12},{8,0},{12,4},{16,24},{20,28},{24,16},{28,20},{32,40},... | collective-permute-start | bytes 393224 | tf_op jit(solution)/shard_map/ppermute | solution.py:366
  19.2 0.8 collective-permute-start.4
  20.0 4.3 %collective-permute-done.1.refs_0_ = bf16[2,128,256]{2,1,0:T(8,128)(2,1)S(1)} collective-permute-done((bf16[2,128,256]{2,1,0:T(8,128)(2,1)S(1)}, bf16[2,128,256]{2,1,0:T(8,128)(2,1)S(1)}, u32[]{:S(2)}, u32[]{:S(2)}) %collective-permute-start.1) | collective-permute-done | bytes 131104 | tf_op jit(solution)/shard_map/ppermute | solution.py:366
  24.4 0.7 shard_map.92
  25.1 0.6 collective-permute-start.2
  25.7 0.7 collective-permute-done.4.refs_0_
  26.4 0.7 shard_map.95
  27.1 2.5 %collective-permute-start.5 = (bf16[2,128,256]{2,1,0:T(8,128)(2,1)S(1)}, bf16[2,128,256]{2,1,0:T(8,128)(2,1)S(1)}, u32[]{:S(2)}, u32[]{:S(2)}) collective-permute-start(bf16[2,128,256]{2,1,0:T(8,128)(2,1)S(1)} %get-tuple-element.52.refs_1_), channel_id=1, source_target_pairs={{0,16},{4,20},{8,24},{12,28},{16,0},{20,4},{24,8},{28,12},{32,48},... | collective-permute-start | bytes 393224 | tf_op jit(solution)/shard_map/ppermute | solution.py:366
  29.5 3.3 %collective-permute-done.2.refs_0_ = bf16[2,128,256]{2,1,0:T(8,128)(2,1)S(1)} collective-permute-done((bf16[2,128,256]{2,1,0:T(8,128)(2,1)S(1)}, bf16[2,128,256]{2,1,0:T(8,128)(2,1)S(1)}, u32[]{:S(2)}, u32[]{:S(2)}) %collective-permute-start.2) | collective-permute-done | bytes 131104 | tf_op jit(solution)/shard_map/ppermute | solution.py:366
  32.8 0.8 shard_map.93
  33.5 2.0 %collective-permute-start.3 = (bf16[2,128,256]{2,1,0:T(8,128)(2,1)S(1)}, bf16[2,128,256]{2,1,0:T(8,128)(2,1)S(1)}, u32[]{:S(2)}, u32[]{:S(2)}) collective-permute-start(bf16[2,128,256]{2,1,0:T(8,128)(2,1)S(1)} %get-tuple-element.47.refs_1_), channel_id=1, source_target_pairs={{0,32},{4,36},{8,40},{12,44},{16,48},{20,52},{24,56},{28,60},{32,0... | collective-permute-start | bytes 393224 | tf_op jit(solution)/shard_map/ppermute | solution.py:366
  35.6 0.8 shard_map.96
  36.3 0.9 collective-permute-start.6
  37.2 2.6 %collective-permute-done.3.refs_0_ = bf16[2,128,256]{2,1,0:T(8,128)(2,1)S(1)} collective-permute-done((bf16[2,128,256]{2,1,0:T(8,128)(2,1)S(1)}, bf16[2,128,256]{2,1,0:T(8,128)(2,1)S(1)}, u32[]{:S(2)}, u32[]{:S(2)}) %collective-permute-start.3) | collective-permute-done | bytes 131104 | tf_op jit(solution)/shard_map/ppermute | solution.py:366
  39.9 0.7 shard_map.94
  40.6 0.8 collective-permute-done.6.refs_5_
  41.4 1.4 %shard_map.97 = (bf16[2,128,256]{2,1,0:T(8,128)(2,1)S(1)}, bf16[2,128,128]{2,1,0:T(8,128)(2,1)}, bf16[2,128,128]{2,1,0:T(8,128)(2,1)S(1)}, bf16[12,128,128]{2,1,0:T(8,128)(2,1)S(1)}) custom-call(s32[6]{0:T(128)S(1)} %stack.27.bits, bf16[2,128,128]{2,1,0:T(8,128)(2,1)S(1)} %get-tuple-element.43.refs_0_, bf16[2,128,128]{2,1,0:T(8,128)(2,1)S(1)} %get-tuple-element.46.refs_1_, ...), custom_call_target="tpu_custom_call" | custom-call | flops 600000000 | bytes 1048576 | tf_op jit(solution)/shard_map/pallas_call | solution.py:298
  42.7 3.7 %collective-permute-start.9 = (bf16[2,128,128]{2,1,0:T(8,128)(2,1)S(1)}, bf16[2,128,128]{2,1,0:T(8,128)(2,1)S(1)}, u32[]{:S(2)}, u32[]{:S(2)}) collective-permute-start(bf16[2,128,128]{2,1,0:T(8,128)(2,1)S(1)} %slice.21), channel_id=1, source_target_pairs={{0,64},{4,68},{8,72},{12,76},{16,80},{20,84},{24,88},{28,92},{32,9... | collective-permute-start | bytes 196616 | tf_op jit(solution)/shard_map/ppermute | solution.py:366
  46.6 2.6 %collective-permute-done.9.refs_1_ = bf16[2,128,128]{2,1,0:T(8,128)(2,1)S(1)} collective-permute-done((bf16[2,128,128]{2,1,0:T(8,128)(2,1)S(1)}, bf16[2,128,128]{2,1,0:T(8,128)(2,1)S(1)}, u32[]{:S(2)}, u32[]{:S(2)}) %collective-permute-start.9) | collective-permute-done | bytes 65568 | tf_op jit(solution)/shard_map/ppermute | solution.py:366
  49.1 3.1 %collective-permute-done.8.refs_0_ = bf16[2,128,128]{2,1,0:T(8,128)(2,1)S(1)} collective-permute-done((bf16[2,128,128]{2,1,0:T(8,128)(2,1)S(1)}, bf16[2,128,128]{2,1,0:T(8,128)(2,1)S(1)}, u32[]{:S(2)}, u32[]{:S(2)}) %collective-permute-start.8) | collective-permute-done | bytes 65568 | tf_op jit(solution)/shard_map/ppermute | solution.py:366
  52.2 0.6 shard_map.98.mine_top
  53.1 1.3 %collective-permute-done.10.other_top = bf16[4,128,128]{2,1,0:T(8,128)(2,1)S(1)} collective-permute-done((bf16[4,128,128]{2,1,0:T(8,128)(2,1)S(1)}, bf16[4,128,128]{2,1,0:T(8,128)(2,1)S(1)}, u32[]{:S(2)}, u32[]{:S(2)}) %collective-permute-start.10) | collective-permute-done | bytes 131104 | tf_op jit(solution)/shard_map/ppermute | solution.py:366
  54.4 1.1 %shard_map.99.stack_ref = bf16[8,640,128]{2,1,0:T(8,128)(2,1)S(1)} custom-call(s32[6]{0:T(128)S(1)} %stack.27.bits, bf16[8,128,256]{2,1,0:T(8,128)(2,1)S(1)} %collective-permute-done.sib_ref, bf16[12,128,128]{2,1,0:T(8,128)(2,1)S(1)} %get-tuple-element.57.mine_ref, bf16[12,128,128]{2,1,0:T(8,128)(2,1)S(1)} %collective-permute-done.7.other_ref, ...), custom_call_target="tpu_custom_call" | custom-call | flops 600000000 | bytes 1048576 | tf_op jit(solution)/shard_map/pallas_call | solution.py:298
  55.6 3.6 %shard_map.100 = bf16[256,1024]{1,0:T(8,128)(2,1)S(1)} custom-call(s32[6]{0:T(128)S(1)} %stack.27.bits, f32[512,1024]{1,0:T(8,128)} %get-tuple-element.39.near_a.near_b, f32[512,1024]{1,0:T(8,128)} %get-tuple-element.39.near_a.near_b, bf16[512,1024]{1,0:T(8,128)(2,1)} %get-tuple-element.40.far_a.far_b, bf16[512,1024]{1,0:T(8,128)(2,1)} %get-tuple-element.40.far_a.far_b, ...), custom_call_target="tpu_custom_call" | custom-call | flops 2400000000 | bytes 4194304 | tf_op jit(solution)/shard_map/pallas_call | solution.py:348
  59.2 3.6 %shard_map.101 = bf16[256,1024]{1,0:T(8,128)(2,1)S(1)} custom-call(s32[6]{0:T(128)S(1)} %stack.27.bits, f32[512,1024]{1,0:T(8,128)} %get-tuple-element.39.near_a.near_b, f32[512,1024]{1,0:T(8,128)} %get-tuple-element.39.near_a.near_b, bf16[512,1024]{1,0:T(8,128)(2,1)} %get-tuple-element.40.far_a.far_b, bf16[512,1024]{1,0:T(8,128)(2,1)} %get-tuple-element.40.far_a.far_b, ...), custom_call_target="tpu_custom_call" | custom-call | flops 2400000000 | bytes 4194304 | tf_op jit(solution)/shard_map/pallas_call | solution.py:348
  70.0 1.8 %collective-permute-start.15 = (bf16[128,1024]{1,0:T(8,128)(2,1)S(1)}, bf16[128,1024]{1,0:T(8,128)(2,1)S(1)}, u32[]{:S(2)}, u32[]{:S(2)}) collective-permute-start(bf16[128,1024]{1,0:T(8,128)(2,1)S(1)} %fusion.68), channel_id=1, source_target_pairs={{0,3},{1,0},{2,1},{3,2},{4,7},{5,4},{6,5},{7,6},{8,11},{9,8},{10,9... | collective-permute-start | bytes 786440 | tf_op jit(solution)/shard_map/ppermute | solution.py:396
  72.3 1.5 %collective-permute-start.14 = (bf16[128,1024]{1,0:T(8,128)(2,1)S(1)}, bf16[128,1024]{1,0:T(8,128)(2,1)S(1)}, u32[]{:S(2)}, u32[]{:S(2)}) collective-permute-start(bf16[128,1024]{1,0:T(8,128)(2,1)S(1)} %fusion.56), channel_id=1, source_target_pairs={{0,1},{1,2},{2,3},{3,0},{4,5},{5,6},{6,7},{7,4},{8,9},{9,10},{10,1... | collective-permute-start | bytes 786440 | tf_op jit(solution)/shard_map/ppermute | solution.py:396
  73.8 0.6 collective-permute-start.13
  74.4 4.6 %collective-permute-done.11 = bf16[128,1024]{1,0:T(8,128)(2,1)S(1)} collective-permute-done((bf16[128,1024]{1,0:T(8,128)(2,1)S(1)}, bf16[128,1024]{1,0:T(8,128)(2,1)S(1)}, u32[]{:S(2)}, u32[]{:S(2)}) %collective-permute-start.11) | collective-permute-done | bytes 262176 | tf_op jit(solution)/shard_map/ppermute | solution.py:396
  79.1 1.5 %collective-permute-start.12 = (bf16[128,1024]{1,0:T(8,128)(2,1)S(1)}, bf16[128,1024]{1,0:T(8,128)(2,1)S(1)}, u32[]{:S(2)}, u32[]{:S(2)}) collective-permute-start(bf16[128,1024]{1,0:T(8,128)(2,1)S(1)} %add_convert_fusion.11), channel_id=1, source_target_pairs={{0,1},{1,2},{2,3},{3,0},{4,5},{5,6},{6,7},{7,4},{8,9},{9,10},{10,1... | collective-permute-start | bytes 786440 | tf_op jit(solution)/shard_map/ppermute | solution.py:396
  80.6 0.7 collective-permute-start.19
  81.3 3.3 %collective-permute-done.14 = bf16[128,1024]{1,0:T(8,128)(2,1)S(1)} collective-permute-done((bf16[128,1024]{1,0:T(8,128)(2,1)S(1)}, bf16[128,1024]{1,0:T(8,128)(2,1)S(1)}, u32[]{:S(2)}, u32[]{:S(2)}) %collective-permute-start.14) | collective-permute-done | bytes 262176 | tf_op jit(solution)/shard_map/ppermute | solution.py:396
  84.7 1.5 %collective-permute-start.18 = (bf16[128,1024]{1,0:T(8,128)(2,1)S(1)}, bf16[128,1024]{1,0:T(8,128)(2,1)S(1)}, u32[]{:S(2)}, u32[]{:S(2)}) collective-permute-start(bf16[128,1024]{1,0:T(8,128)(2,1)S(1)} %add_convert_fusion.9), channel_id=1, source_target_pairs={{0,1},{1,2},{2,3},{3,0},{4,5},{5,6},{6,7},{7,4},{8,9},{9,10},{10,1... | collective-permute-start | bytes 786440 | tf_op jit(solution)/shard_map/ppermute | solution.py:396
  86.2 0.7 collective-permute-start.17
  86.9 3.3 %collective-permute-done.12 = bf16[128,1024]{1,0:T(8,128)(2,1)S(1)} collective-permute-done((bf16[128,1024]{1,0:T(8,128)(2,1)S(1)}, bf16[128,1024]{1,0:T(8,128)(2,1)S(1)}, u32[]{:S(2)}, u32[]{:S(2)}) %collective-permute-start.12) | collective-permute-done | bytes 262176 | tf_op jit(solution)/shard_map/ppermute | solution.py:396
  90.3 1.5 %collective-permute-start.16 = (bf16[128,1024]{1,0:T(8,128)(2,1)S(1)}, bf16[128,1024]{1,0:T(8,128)(2,1)S(1)}, u32[]{:S(2)}, u32[]{:S(2)}) collective-permute-start(bf16[128,1024]{1,0:T(8,128)(2,1)S(1)} %add_convert_fusion.7), channel_id=1, source_target_pairs={{0,1},{1,2},{2,3},{3,0},{4,5},{5,6},{6,7},{7,4},{8,9},{9,10},{10,1... | collective-permute-start | bytes 786440 | tf_op jit(solution)/shard_map/ppermute | solution.py:396
  91.9 0.7 collective-permute-start.20
  92.5 3.3 %collective-permute-done.18 = bf16[128,1024]{1,0:T(8,128)(2,1)S(1)} collective-permute-done((bf16[128,1024]{1,0:T(8,128)(2,1)S(1)}, bf16[128,1024]{1,0:T(8,128)(2,1)S(1)}, u32[]{:S(2)}, u32[]{:S(2)}) %collective-permute-start.18) | collective-permute-done | bytes 262176 | tf_op jit(solution)/shard_map/ppermute | solution.py:396
  95.9 1.5 %collective-permute-start.21 = (bf16[128,1024]{1,0:T(8,128)(2,1)S(1)}, bf16[128,1024]{1,0:T(8,128)(2,1)S(1)}, u32[]{:S(2)}, u32[]{:S(2)}) collective-permute-start(bf16[128,1024]{1,0:T(8,128)(2,1)S(1)} %add_convert_fusion.5), channel_id=1, source_target_pairs={{0,1},{1,2},{2,3},{3,0},{4,5},{5,6},{6,7},{7,4},{8,9},{9,10},{10,1... | collective-permute-start | bytes 786440 | tf_op jit(solution)/shard_map/ppermute | solution.py:396
  97.5 0.7 collective-permute-start.22
  98.1 3.3 %collective-permute-done.16 = bf16[128,1024]{1,0:T(8,128)(2,1)S(1)} collective-permute-done((bf16[128,1024]{1,0:T(8,128)(2,1)S(1)}, bf16[128,1024]{1,0:T(8,128)(2,1)S(1)}, u32[]{:S(2)}, u32[]{:S(2)}) %collective-permute-start.16) | collective-permute-done | bytes 262176 | tf_op jit(solution)/shard_map/ppermute | solution.py:396
  101.6 1.3 %collective-permute-done.20 = bf16[128,1024]{1,0:T(8,128)(2,1)S(1)} collective-permute-done((bf16[128,1024]{1,0:T(8,128)(2,1)S(1)}, bf16[128,1024]{1,0:T(8,128)(2,1)S(1)}, u32[]{:S(2)}, u32[]{:S(2)}) %collective-permute-start.20) | collective-permute-done | bytes 262176 | tf_op jit(solution)/shard_map/ppermute | solution.py:396
  103.0 3.3 %collective-permute-done.21 = bf16[128,1024]{1,0:T(8,128)(2,1)S(1)} collective-permute-done((bf16[128,1024]{1,0:T(8,128)(2,1)S(1)}, bf16[128,1024]{1,0:T(8,128)(2,1)S(1)}, u32[]{:S(2)}, u32[]{:S(2)}) %collective-permute-start.21) | collective-permute-done | bytes 262176 | tf_op jit(solution)/shard_map/ppermute | solution.py:396
  106.3 1.2 %collective-permute-done.22 = bf16[128,1024]{1,0:T(8,128)(2,1)S(1)} collective-permute-done((bf16[128,1024]{1,0:T(8,128)(2,1)S(1)}, bf16[128,1024]{1,0:T(8,128)(2,1)S(1)}, u32[]{:S(2)}, u32[]{:S(2)}) %collective-permute-start.22) | collective-permute-done | bytes 262176 | tf_op jit(solution)/shard_map/ppermute | solution.py:396
  107.5 0.8 fusion.80
  (51 shorter events, 8.8 us)
Async XLA Ops:
  15.2 1.9 %collective-permute-start = (bf16[8,128,256]{2,1,0:T(8,128)(2,1)S(1)}, bf16[8,128,256]{2,1,0:T(8,128)(2,1)S(1)}, u32[]{:S(2)}, u32[]{:S(2)}) collective-permute-start(bf16[8,128,256]{2,1,0:T(8,128)(2,1)S(1)} %get-tuple-element.41.mine_ref), channel_id=1, source_target_pairs={{0,4},{4,0},{8,12},{12,8},{16,20},{20,16},{24,28},{28,24},{32,36},... | collective-permute-start | bytes 1572872 | tf_op jit(solution)/shard_map/ppermute | solution.py:366
  17.9 6.5 %collective-permute-start.1 = (bf16[2,128,256]{2,1,0:T(8,128)(2,1)S(1)}, bf16[2,128,256]{2,1,0:T(8,128)(2,1)S(1)}, u32[]{:S(2)}, u32[]{:S(2)}) collective-permute-start(bf16[2,128,256]{2,1,0:T(8,128)(2,1)S(1)} %get-tuple-element.42.refs_1_), channel_id=1, source_target_pairs={{0,8},{4,12},{8,0},{12,4},{16,24},{20,28},{24,16},{28,20},{32,40},... | collective-permute-start | bytes 393224 | tf_op jit(solution)/shard_map/ppermute | solution.py:366
  19.2 7.1 %collective-permute-start.4 = (bf16[2,128,256]{2,1,0:T(8,128)(2,1)S(1)}, bf16[2,128,256]{2,1,0:T(8,128)(2,1)S(1)}, u32[]{:S(2)}, u32[]{:S(2)}) collective-permute-start(bf16[2,128,256]{2,1,0:T(8,128)(2,1)S(1)} %get-tuple-element.50.refs_1_), channel_id=1, source_target_pairs={{0,8},{4,12},{8,0},{12,4},{16,24},{20,28},{24,16},{28,20},{32,40},... | collective-permute-start | bytes 393224 | tf_op jit(solution)/shard_map/ppermute | solution.py:366
  25.1 7.7 %collective-permute-start.2 = (bf16[2,128,256]{2,1,0:T(8,128)(2,1)S(1)}, bf16[2,128,256]{2,1,0:T(8,128)(2,1)S(1)}, u32[]{:S(2)}, u32[]{:S(2)}) collective-permute-start(bf16[2,128,256]{2,1,0:T(8,128)(2,1)S(1)} %get-tuple-element.44.refs_1_), channel_id=1, source_target_pairs={{0,16},{4,20},{8,24},{12,28},{16,0},{20,4},{24,8},{28,12},{32,48},... | collective-permute-start | bytes 393224 | tf_op jit(solution)/shard_map/ppermute | solution.py:366
  27.1 8.5 %collective-permute-start.5 = (bf16[2,128,256]{2,1,0:T(8,128)(2,1)S(1)}, bf16[2,128,256]{2,1,0:T(8,128)(2,1)S(1)}, u32[]{:S(2)}, u32[]{:S(2)}) collective-permute-start(bf16[2,128,256]{2,1,0:T(8,128)(2,1)S(1)} %get-tuple-element.52.refs_1_), channel_id=1, source_target_pairs={{0,16},{4,20},{8,24},{12,28},{16,0},{20,4},{24,8},{28,12},{32,48},... | collective-permute-start | bytes 393224 | tf_op jit(solution)/shard_map/ppermute | solution.py:366
  33.5 6.3 %collective-permute-start.3 = (bf16[2,128,256]{2,1,0:T(8,128)(2,1)S(1)}, bf16[2,128,256]{2,1,0:T(8,128)(2,1)S(1)}, u32[]{:S(2)}, u32[]{:S(2)}) collective-permute-start(bf16[2,128,256]{2,1,0:T(8,128)(2,1)S(1)} %get-tuple-element.47.refs_1_), channel_id=1, source_target_pairs={{0,32},{4,36},{8,40},{12,44},{16,48},{20,52},{24,56},{28,60},{32,0... | collective-permute-start | bytes 393224 | tf_op jit(solution)/shard_map/ppermute | solution.py:366
  36.3 5.0 %collective-permute-start.6 = (bf16[2,128,256]{2,1,0:T(8,128)(2,1)S(1)}, bf16[2,128,256]{2,1,0:T(8,128)(2,1)S(1)}, u32[]{:S(2)}, u32[]{:S(2)}) collective-permute-start(bf16[2,128,256]{2,1,0:T(8,128)(2,1)S(1)} %get-tuple-element.55.refs_6_), channel_id=1, source_target_pairs={{0,32},{4,36},{8,40},{12,44},{16,48},{20,52},{24,56},{28,60},{32,0... | collective-permute-start | bytes 393224 | tf_op jit(solution)/shard_map/ppermute | solution.py:366
  42.7 11.7 %collective-permute-start.7 = (bf16[12,128,128]{2,1,0:T(8,128)(2,1)S(1)}, bf16[12,128,128]{2,1,0:T(8,128)(2,1)S(1)}, u32[]{:S(2)}, u32[]{:S(2)}) collective-permute-start(bf16[12,128,128]{2,1,0:T(8,128)(2,1)S(1)} %get-tuple-element.57.mine_ref), channel_id=1, source_target_pairs={{0,4},{4,0},{8,12},{12,8},{16,20},{20,16},{24,28},{28,24},{32,36},... | collective-permute-start | bytes 1179656 | tf_op jit(solution)/shard_map/ppermute | solution.py:366
  42.7 6.4 %collective-permute-start.9 = (bf16[2,128,128]{2,1,0:T(8,128)(2,1)S(1)}, bf16[2,128,128]{2,1,0:T(8,128)(2,1)S(1)}, u32[]{:S(2)}, u32[]{:S(2)}) collective-permute-start(bf16[2,128,128]{2,1,0:T(8,128)(2,1)S(1)} %slice.21), channel_id=1, source_target_pairs={{0,64},{4,68},{8,72},{12,76},{16,80},{20,84},{24,88},{28,92},{32,9... | collective-permute-start | bytes 196616 | tf_op jit(solution)/shard_map/ppermute | solution.py:366
  46.5 5.8 %collective-permute-start.8 = (bf16[2,128,128]{2,1,0:T(8,128)(2,1)S(1)}, bf16[2,128,128]{2,1,0:T(8,128)(2,1)S(1)}, u32[]{:S(2)}, u32[]{:S(2)}) collective-permute-start(bf16[2,128,128]{2,1,0:T(8,128)(2,1)S(1)} %slice.20), channel_id=1, source_target_pairs={{0,64},{4,68},{8,72},{12,76},{16,80},{20,84},{24,88},{28,92},{32,9... | collective-permute-start | bytes 196616 | tf_op jit(solution)/shard_map/ppermute | solution.py:366
  52.2 3.3 %copy-start = (f32[1024]{0:T(1024)S(1)}, f32[1024]{0:T(1024)}, u32[]{:S(2)}) copy-start(f32[1024]{0:T(1024)} %param.16) | copy-start | bytes 12292
  52.8 1.6 %collective-permute-start.10 = (bf16[4,128,128]{2,1,0:T(8,128)(2,1)S(1)}, bf16[4,128,128]{2,1,0:T(8,128)(2,1)S(1)}, u32[]{:S(2)}, u32[]{:S(2)}) collective-permute-start(bf16[4,128,128]{2,1,0:T(8,128)(2,1)S(1)} %shard_map.98.mine_top), channel_id=1, source_target_pairs={{0,4},{4,0},{8,12},{12,8},{16,20},{20,16},{24,28},{28,24},{32,36},... | collective-permute-start | bytes 393224 | tf_op jit(solution)/shard_map/ppermute | solution.py:366
  55.6 7.3 %slice-start = ((s8[8388608]{0:T(1024)(128)(4,1)}), s8[4194304]{0:T(1024)(128)(4,1)S(1)}, s32[]{:S(2)}) async-start(s8[8388608]{0:T(1024)(128)(4,1)} %bitcast.9), calls=%async_computation | async-start | bytes 8388608
  59.2 3.7 %slice-start.1 = ((s8[8388608]{0:T(1024)(128)(4,1)}), s8[4194304]{0:T(1024)(128)(4,1)S(1)}, s32[]{:S(2)}) async-start(s8[8388608]{0:T(1024)(128)(4,1)} %bitcast.9), calls=%async_computation.1 | async-start | bytes 8388608
  69.7 9.2 %collective-permute-start.11 = (bf16[128,1024]{1,0:T(8,128)(2,1)S(1)}, bf16[128,1024]{1,0:T(8,128)(2,1)S(1)}, u32[]{:S(2)}, u32[]{:S(2)}) collective-permute-start(bf16[128,1024]{1,0:T(8,128)(2,1)S(1)} %fusion.32), channel_id=1, source_target_pairs={{0,1},{1,2},{2,3},{3,0},{4,5},{5,6},{6,7},{7,4},{8,9},{9,10},{10,1... | collective-permute-start | bytes 786440 | tf_op jit(solution)/shard_map/ppermute | solution.py:396
  70.0 10.5 %collective-permute-start.15 = (bf16[128,1024]{1,0:T(8,128)(2,1)S(1)}, bf16[128,1024]{1,0:T(8,128)(2,1)S(1)}, u32[]{:S(2)}, u32[]{:S(2)}) collective-permute-start(bf16[128,1024]{1,0:T(8,128)(2,1)S(1)} %fusion.68), channel_id=1, source_target_pairs={{0,3},{1,0},{2,1},{3,2},{4,7},{5,4},{6,5},{7,6},{8,11},{9,8},{10,9... | collective-permute-start | bytes 786440 | tf_op jit(solution)/shard_map/ppermute | solution.py:396
  72.3 12.3 %collective-permute-start.14 = (bf16[128,1024]{1,0:T(8,128)(2,1)S(1)}, bf16[128,1024]{1,0:T(8,128)(2,1)S(1)}, u32[]{:S(2)}, u32[]{:S(2)}) collective-permute-start(bf16[128,1024]{1,0:T(8,128)(2,1)S(1)} %fusion.56), channel_id=1, source_target_pairs={{0,1},{1,2},{2,3},{3,0},{4,5},{5,6},{6,7},{7,4},{8,9},{9,10},{10,1... | collective-permute-start | bytes 786440 | tf_op jit(solution)/shard_map/ppermute | solution.py:396
  73.8 12.4 %collective-permute-start.13 = (bf16[128,1024]{1,0:T(8,128)(2,1)S(1)}, bf16[128,1024]{1,0:T(8,128)(2,1)S(1)}, u32[]{:S(2)}, u32[]{:S(2)}) collective-permute-start(bf16[128,1024]{1,0:T(8,128)(2,1)S(1)} %fusion.44), channel_id=1, source_target_pairs={{0,3},{1,0},{2,1},{3,2},{4,7},{5,4},{6,5},{7,6},{8,11},{9,8},{10,9... | collective-permute-start | bytes 786440 | tf_op jit(solution)/shard_map/ppermute | solution.py:396
  79.1 11.2 %collective-permute-start.12 = (bf16[128,1024]{1,0:T(8,128)(2,1)S(1)}, bf16[128,1024]{1,0:T(8,128)(2,1)S(1)}, u32[]{:S(2)}, u32[]{:S(2)}) collective-permute-start(bf16[128,1024]{1,0:T(8,128)(2,1)S(1)} %add_convert_fusion.11), channel_id=1, source_target_pairs={{0,1},{1,2},{2,3},{3,0},{4,5},{5,6},{6,7},{7,4},{8,9},{9,10},{10,1... | collective-permute-start | bytes 786440 | tf_op jit(solution)/shard_map/ppermute | solution.py:396
  80.6 11.2 %collective-permute-start.19 = (bf16[128,1024]{1,0:T(8,128)(2,1)S(1)}, bf16[128,1024]{1,0:T(8,128)(2,1)S(1)}, u32[]{:S(2)}, u32[]{:S(2)}) collective-permute-start(bf16[128,1024]{1,0:T(8,128)(2,1)S(1)} %add_convert_fusion.10), channel_id=1, source_target_pairs={{0,3},{1,0},{2,1},{3,2},{4,7},{5,4},{6,5},{7,6},{8,11},{9,8},{10,9... | collective-permute-start | bytes 786440 | tf_op jit(solution)/shard_map/ppermute | solution.py:396
  84.7 11.2 %collective-permute-start.18 = (bf16[128,1024]{1,0:T(8,128)(2,1)S(1)}, bf16[128,1024]{1,0:T(8,128)(2,1)S(1)}, u32[]{:S(2)}, u32[]{:S(2)}) collective-permute-start(bf16[128,1024]{1,0:T(8,128)(2,1)S(1)} %add_convert_fusion.9), channel_id=1, source_target_pairs={{0,1},{1,2},{2,3},{3,0},{4,5},{5,6},{6,7},{7,4},{8,9},{9,10},{10,1... | collective-permute-start | bytes 786440 | tf_op jit(solution)/shard_map/ppermute | solution.py:396
  86.2 11.2 %collective-permute-start.17 = (bf16[128,1024]{1,0:T(8,128)(2,1)S(1)}, bf16[128,1024]{1,0:T(8,128)(2,1)S(1)}, u32[]{:S(2)}, u32[]{:S(2)}) collective-permute-start(bf16[128,1024]{1,0:T(8,128)(2,1)S(1)} %add_convert_fusion.8), channel_id=1, source_target_pairs={{0,3},{1,0},{2,1},{3,2},{4,7},{5,4},{6,5},{7,6},{8,11},{9,8},{10,9... | collective-permute-start | bytes 786440 | tf_op jit(solution)/shard_map/ppermute | solution.py:396
  90.3 11.2 %collective-permute-start.16 = (bf16[128,1024]{1,0:T(8,128)(2,1)S(1)}, bf16[128,1024]{1,0:T(8,128)(2,1)S(1)}, u32[]{:S(2)}, u32[]{:S(2)}) collective-permute-start(bf16[128,1024]{1,0:T(8,128)(2,1)S(1)} %add_convert_fusion.7), channel_id=1, source_target_pairs={{0,1},{1,2},{2,3},{3,0},{4,5},{5,6},{6,7},{7,4},{8,9},{9,10},{10,1... | collective-permute-start | bytes 786440 | tf_op jit(solution)/shard_map/ppermute | solution.py:396
  91.9 11.0 %collective-permute-start.20 = (bf16[128,1024]{1,0:T(8,128)(2,1)S(1)}, bf16[128,1024]{1,0:T(8,128)(2,1)S(1)}, u32[]{:S(2)}, u32[]{:S(2)}) collective-permute-start(bf16[128,1024]{1,0:T(8,128)(2,1)S(1)} %add_convert_fusion.6), channel_id=1, source_target_pairs={{0,3},{1,0},{2,1},{3,2},{4,7},{5,4},{6,5},{7,6},{8,11},{9,8},{10,9... | collective-permute-start | bytes 786440 | tf_op jit(solution)/shard_map/ppermute | solution.py:396
  95.9 10.3 %collective-permute-start.21 = (bf16[128,1024]{1,0:T(8,128)(2,1)S(1)}, bf16[128,1024]{1,0:T(8,128)(2,1)S(1)}, u32[]{:S(2)}, u32[]{:S(2)}) collective-permute-start(bf16[128,1024]{1,0:T(8,128)(2,1)S(1)} %add_convert_fusion.5), channel_id=1, source_target_pairs={{0,1},{1,2},{2,3},{3,0},{4,5},{5,6},{6,7},{7,4},{8,9},{9,10},{10,1... | collective-permute-start | bytes 786440 | tf_op jit(solution)/shard_map/ppermute | solution.py:396
  97.5 10.1 %collective-permute-start.22 = (bf16[128,1024]{1,0:T(8,128)(2,1)S(1)}, bf16[128,1024]{1,0:T(8,128)(2,1)S(1)}, u32[]{:S(2)}, u32[]{:S(2)}) collective-permute-start(bf16[128,1024]{1,0:T(8,128)(2,1)S(1)} %add_convert_fusion.4), channel_id=1, source_target_pairs={{0,3},{1,0},{2,1},{3,2},{4,7},{5,4},{6,5},{7,6},{8,11},{9,8},{10,9... | collective-permute-start | bytes 786440 | tf_op jit(solution)/shard_map/ppermute | solution.py:396
  106.3 1.2 %copy-start.1 = (bf16[128,4096]{1,0:T(8,128)(2,1)}, bf16[128,4096]{1,0:T(8,128)(2,1)S(1)}, u32[]{:S(2)}) copy-start(bf16[128,4096]{1,0:T(8,128)(2,1)S(1)} %constant_dynamic-update-slice_fusion) | copy-start | bytes 3145732
